TPU v7x, 32 devices: a whole 2x2x4 slice. The times are simulated.
32 devices in a mesh: groups: 2 (over y), span: 4 (over z), head: 2 (over x), slab: 2 (over core).
Axes of the slice: x: 2, y: 2, z: 4, core: 2. Of those that a mesh axis runs over, the one named last changes fastest.
Arguments:
- queries: bfloat16 [3072, 5120], P(('groups', 'span'), 'head'), parts along dimension 0, may hold values from -6 to 6
- keys: bfloat16 [3072, 5120], P(('groups', 'span', 'slab'), 'head'), parts along dimension 0, may hold values from -4 to 4
- values: bfloat16 [3072, 5120], P(('groups', 'span', 'slab'), 'head'), parts along dimension 0, may hold values from -240 to 240
- span_mask: int32 [8, 4], P('groups'), parts along dimension 0, may hold values from 0 to 1, as said below
- head_gain: float32 [5120], P('head'), may hold values from 0.5 to 2
- head_shift: float32 [5120], P('head'), may hold values from -3 to 3
- patch_weight: bfloat16 [5120, 64], P('head'), may hold values from -0.078125 to 0.078125
- noisy_latent: float32 [24, 16, 32, 16], P(('groups', 'span'), 'head', 'slab'), parts along dimension 0, may hold values from -6 to 6
- conv_weight: bfloat16 [432, 384], replicated, may hold values from -0.3125 to 0.3125
- conv_bias: float32 [384], replicated, may hold values from -3 to 3
Outputs:
- clean_latent: float32 [24, 16, 32, 16], P(('groups', 'span'), 'head', 'slab'), parts along dimension 0
- decoded: bfloat16 [24, 16, 32, 384], P(('groups', 'span'), 'head', 'slab'), parts along dimension 0
There are 2 independent parts, one for each index of `groups`. A program takes and returns all parts, laid end to end along the dimension named above; an argument that names none is the same for every part. Nothing has to cross between parts.
Inputs may be any that keep to these rules, and one draw needn't show every extreme that they name: span_mask[i, j] is 1 where j = i and 0 where j > i.
All inputs are finite; a program needn't handle non-finite values.
Results may differ from a plain program's by a relative error of at most 0.012.
Values may be sent and summed in bfloat16 or wider, within the bound.
No kernel may reach another device: no remote copies, remote signals or barrier semaphores. Data moves between devices by JAX's collectives and lax.ppermute only.
A program may use at most 128 MiB of HBM per device.

v0:
```python
import math

import jax
import jax.numpy as jnp
from jax import lax
from jax.sharding import PartitionSpec as P

HEADS = 40
HD = 128
LAT_CH = 16
FRAMES_SPAN = 3
TROWS = 8
TCOLS = 16


neg_big = -1e30
noise_level = 0.75
norm_eps = 1e-06


def with_halo(cells, sides, width):
    for axis, dim in sides:
        count = lax.axis_size(axis)
        ends = count - 1
        head = lax.slice_in_dim(cells, 0, width, axis=dim)
        tail = lax.slice_in_dim(cells, cells.shape[dim] - width, cells.shape[dim], axis=dim)
        cells = jnp.concatenate(
            [
                lax.ppermute(tail, axis, [(i, (i + 1) % count) for i in range(ends)]),
                cells,
                lax.ppermute(head, axis, [((i + 1) % count, i) for i in range(ends)]),
            ],
            axis=dim,
        )
    return cells


def from_behind(value, axis, by):
    size = lax.axis_size(axis)
    pairs = [(i, i + by) for i in range(size) if 0 <= i + by < size]
    return lax.ppermute(value, axis, pairs)


def block_length(total_rows):
    block_size = total_rows
    while block_size > 768 and block_size % 2 == 0:
        block_size = block_size // 2
    return block_size


def fold_keys(partial_state, key_value, query_block, mask_row, rows_span):
    keys_piece, values_piece = key_value
    heads_dev = query_block.shape[1]
    piece_rows = keys_piece.shape[0]
    length = block_length(piece_rows)
    span_count = mask_row.shape[0]
    score_scale = 1.0 / math.sqrt(HD)
    span_ids = jnp.arange(span_count, dtype=jnp.int32)

    def one_block(carry_state, block_index):
        running_max, running_sum, weighted = carry_state
        offset = block_index * length
        key_block = lax.dynamic_slice_in_dim(keys_piece, offset, length, 0).reshape(
            length, heads_dev, HD
        )
        value_block = lax.dynamic_slice_in_dim(values_piece, offset, length, 0).reshape(
            length, heads_dev, HD
        )
        key_span = (offset + jnp.arange(length, dtype=jnp.int32)) // rows_span
        allowed = (
            jnp.sum(jnp.where(key_span[:, None] == span_ids[None, :], mask_row[None, :], 0), axis=1)
            > 0
        )
        scores = (
            jnp.einsum("qhd,khd->hqk", query_block, key_block, preferred_element_type=jnp.float32)
            * score_scale
        )
        scores = jnp.where(allowed[None, None, :], scores, neg_big)
        new_max = jnp.maximum(running_max, jnp.max(scores, axis=2))
        weights = jnp.where(allowed[None, None, :], jnp.exp(scores - new_max[:, :, None]), 0.0)
        factor = jnp.exp(running_max - new_max)
        running_sum = running_sum * factor + jnp.sum(weights, axis=2)
        weighted = weighted * factor.T[:, :, None] + jnp.einsum(
            "hqk,khd->qhd",
            weights.astype(jnp.bfloat16),
            value_block,
            preferred_element_type=jnp.float32,
        )
        return ((new_max, running_sum, weighted), None)

    result, unused = lax.scan(
        one_block, partial_state, jnp.arange(piece_rows // length, dtype=jnp.int32)
    )
    return result


def per_device(
    queries,
    keys,
    values,
    span_mask,
    head_gain,
    head_shift,
    patch_weight,
    noisy_latent,
    conv_weight,
    conv_bias,
):
    heads_dev = queries.shape[1] // HD
    slab_count = lax.axis_size("slab")
    col_dev = TCOLS // slab_count
    slab_place = lax.axis_index("slab")
    span_place = lax.axis_index("span")
    mask_row = lax.dynamic_slice_in_dim(span_mask, span_place, 1, 0)[0]
    token_grid = queries.reshape(FRAMES_SPAN, TROWS, TCOLS, queries.shape[-1])
    picked = lax.dynamic_slice_in_dim(token_grid, slab_place * col_dev, col_dev, 2)
    own_queries = picked.reshape(FRAMES_SPAN * TROWS * col_dev, queries.shape[-1]).reshape(
        -1, heads_dev, HD
    )
    query_rows = own_queries.shape[0]
    rows_span = keys.shape[0] * slab_count
    running_max, running_sum, weighted = fold_keys(
        (
            jnp.full((heads_dev, query_rows), neg_big, jnp.float32),
            jnp.zeros((heads_dev, query_rows), jnp.float32),
            jnp.zeros((query_rows, heads_dev, HD), jnp.float32),
        ),
        (
            lax.all_gather(keys, ("span", "slab"), axis=0, tiled=True),
            lax.all_gather(values, ("span", "slab"), axis=0, tiled=True),
        ),
        own_queries,
        mask_row,
        rows_span,
    )
    attended = (
        (weighted / running_sum.T[:, :, None])
        .astype(jnp.bfloat16)
        .reshape(query_rows, heads_dev * HD)
    )
    feature_width = HEADS * HD
    values32 = attended.astype(jnp.float32)
    row_total = jnp.sum(values32, axis=1)
    row_squares = jnp.sum(values32 * values32, axis=1)
    row_total, row_squares = lax.psum((row_total, row_squares), "head")
    row_mean = row_total / feature_width
    spread = row_squares / feature_width - row_mean * row_mean
    normed = (
        (values32 - row_mean[:, None]) * lax.rsqrt(spread + norm_eps)[:, None] * head_gain[None, :]
        + head_shift[None, :]
    ).astype(jnp.bfloat16)
    normed_grid = normed.reshape(FRAMES_SPAN, TROWS, col_dev, normed.shape[-1])
    own_rows = TROWS // lax.axis_size("head")
    picked = normed_grid
    product = jnp.dot(
        picked.reshape(-1, picked.shape[-1]), patch_weight, preferred_element_type=jnp.float32
    )
    velocity = lax.psum_scatter(
        product.reshape(
            FRAMES_SPAN, own_rows * lax.axis_size("head"), col_dev * patch_weight.shape[1]
        )
        .transpose(1, 0, 2)
        .reshape(own_rows * lax.axis_size("head"), -1)
        .astype(jnp.bfloat16),
        "head",
        scatter_dimension=0,
        tiled=True,
    ).astype(jnp.float32)
    rows_dev = velocity.shape[0]
    patch_cells = (
        velocity.reshape(rows_dev, FRAMES_SPAN, col_dev, 2, 2, LAT_CH)
        .transpose(1, 0, 3, 2, 4, 5)
        .reshape(FRAMES_SPAN, 2 * rows_dev, 2 * col_dev, LAT_CH)
    )
    clean_latent = noisy_latent - noise_level * patch_cells
    latent_input = clean_latent.astype(jnp.bfloat16)
    framed = with_halo(latent_input, (("head", 1), ("slab", 2)), 1)
    earlier = from_behind(framed[FRAMES_SPAN - 2 :], "span", 1)
    stacked = jnp.concatenate([earlier, framed], axis=0)
    height = clean_latent.shape[1]
    breadth = clean_latent.shape[2]
    columns = jnp.concatenate(
        [
            stacked[
                frame_tap : frame_tap + FRAMES_SPAN,
                row_tap : row_tap + height,
                col_tap : col_tap + breadth,
                :,
            ]
            for frame_tap in range(3)
            for row_tap in range(3)
            for col_tap in range(3)
        ],
        axis=-1,
    )
    decoded = (
        jnp.dot(
            columns.reshape(FRAMES_SPAN * height * breadth, 27 * LAT_CH),
            conv_weight,
            preferred_element_type=jnp.float32,
        )
        + conv_bias[None, :]
    )
    decoded = decoded.astype(jnp.bfloat16).reshape(
        FRAMES_SPAN, height, breadth, conv_weight.shape[1]
    )
    return (clean_latent, decoded)


def solution(mesh):
    placed = (
        P(("groups", "span"), "head"),
        P(("groups", "span", "slab"), "head"),
        P(("groups", "span", "slab"), "head"),
        P("groups", None),
        P("head"),
        P("head"),
        P("head", None),
        P(("groups", "span"), "head", "slab", None),
        P(),
        P(),
    )
    return jax.shard_map(
        per_device,
        mesh=mesh,
        in_specs=placed,
        out_specs=(
            P(("groups", "span"), "head", "slab", None),
            P(("groups", "span"), "head", "slab", None),
        ),
        check_vma=False,
    )
```

profile of v0, /device:TPU:0, one launch (start us, length us, event | category | flops | bytes accessed | tf_op | source)
XLA Modules:
  0.0 286.9 jit_solution(14048511079382129699)
XLA Ops:
  8.7 1.0 constant_dynamic-slice_fusion.2
  9.8 1.7 reshape_reshape.3
  11.4 1.2 copy.38
  14.6 75.5 %all-gather.3.cloned.1.call-done = bf16[1536,2560]{1,0:T(8,128)(2,1)} async-done(((bf16[192,2560]{1,0:T(8,128)(2,1)}), bf16[1536,2560]{1,0:T(8,128)(2,1)}) %all-gather.3.cloned.1.call-update) | async-done | bytes 7864336 | tf_op jit(solution)/shard_map/all_gather | solution.py:129
  90.1 78.0 %all-gather.5.cloned.1.call-done = bf16[1536,2560]{1,0:T(8,128)(2,1)} async-done(((bf16[192,2560]{1,0:T(8,128)(2,1)}), bf16[1536,2560]{1,0:T(8,128)(2,1)}) %all-gather.5.cloned.1.call-update) | async-done | bytes 7864336 | tf_op jit(solution)/shard_map/all_gather | solution.py:130
  168.1 70.0 %while.17 = (s32[]{:T(128)}, f32[20,192]{1,0:T(8,128)S(1)}, f32[20,192]{1,0:T(8,128)S(1)}, f32[192,20,128]{2,0,1:T(8,128)}, s32[2]{0:T(128)S(1)}, /*index=5*/s32...) while((s32[]{:T(128)}, f32[20,192]{1,0:T(8,128)S(1)}, ...), condition=%wide.region_4.5_spmd.clone, body=%wide.region_0.4_spmd.clone.sunk | while | flops 1549801728 | bytes 95616248 | solution.py:91
  169.5 7.0 %constant_dynamic-slice_fusion.5 = (bf16[768,2560]{1,0:T(8,128)(2,1)}, bf16[768,2560]{1,0:T(8,128)(2,1)}) fusion(bf16[1536,2560]{1,0:T(8,128)(2,1)} %get-tuple-element.368, s32[]{:T(128)S(6)} %select_n.93, bf16[1536,2560]{1,0:T(8,128)(2,1)} %get-tuple-element.366), kind=kLoop, calls=%fused_computation.26.clone.1 | loop fusion | bytes 15728644 | tf_op jit(solution)/shard_map/while/body/eval_jaxpr/dynamic_slice | solution.py:66
  176.4 6.3 %copy.52 = bf16[768,2560]{0,1:T(8,128)(2,1)} copy(bf16[768,2560]{1,0:T(8,128)(2,1)} %get-tuple-element.328) | data formatting | bytes 7864320 | tf_op jit(solution)/shard_map/while/body/eval_jaxpr/dynamic_slice | solution.py:63
  182.7 6.3 %copy.53 = bf16[768,2560]{0,1:T(8,128)(2,1)} copy(bf16[768,2560]{1,0:T(8,128)(2,1)} %get-tuple-element.332) | data formatting | bytes 7864320 | tf_op jit(solution)/shard_map/while/body/eval_jaxpr/dynamic_slice | solution.py:66
  189.0 4.8 %bitcast_reduce_fusion.2 = (f32[20,192]{1,0:T(8,128)S(1)}, f32[20,768,192]{1,2,0:T(8,128)S(1)}) fusion(pred[768]{0:T(1024)(128)(4,1)S(1)} %broadcast_compare_fusion.2, bf16[192,20,128]{2,0,1:T(8,128)(2,1)} %get-tuple-element.367, bf16[768,20,128]{0,2,1:T(8,128)(2,1)} %bitcast.80), kind=kOutput, calls=%fused_computation.2.clone.1 | convolution fusion | flops 763818240 | bytes 16727808 | tf_op jit(solution)/shard_map/while/body/eval_jaxpr/qhd,khd->hqk/dot_general | solution.py:75
  193.8 4.8 %bitcast_add_fusion.2 = f32[192,20,128]{2,0,1:T(8,128)} fusion(f32[192,20,128]{2,0,1:T(8,128)} %get-tuple-element.350, bf16[768,20,128]{0,2,1:T(8,128)(2,1)S(1)} %bitcast.81, f32[20,768,192]{1,2,0:T(8,128)S(1)} %get-tuple-element.331, f32[20,192]{1,0:T(8,128)S(1)} %get-tuple-element.361, pred[768]{0:T(1024)(128)(4,1)S(1)} %broadcast_compare_fusion.2, ...), kind=kOutput, calls=%fused_computation.11.clone.1 | convolution fusion | flops 771194880 | bytes 19692288 | tf_op jit(solution)/shard_map/while/body/eval_jaxpr/hqk,khd->qhd/dot_general | solution.py:83
  198.6 3.6 %fusion.51 = f32[20,192]{1,0:T(8,128)S(1)} fusion(f32[20,768,192]{1,2,0:T(8,128)S(1)} %get-tuple-element.331, f32[20,192]{1,0:T(8,128)S(1)} %get-tuple-element.361, pred[768]{0:T(1024)(128)(4,1)S(1)} %broadcast_compare_fusion.2), kind=kLoop, calls=%fused_computation.7.clone.1 | loop fusion | flops 14741760 | bytes 11827968 | tf_op jit(solution)/shard_map/while/body/eval_jaxpr/reduce_sum | solution.py:82
  203.7 7.0 %constant_dynamic-slice_fusion.5 = (bf16[768,2560]{1,0:T(8,128)(2,1)}, bf16[768,2560]{1,0:T(8,128)(2,1)}) fusion(bf16[1536,2560]{1,0:T(8,128)(2,1)} %get-tuple-element.368, s32[]{:T(128)S(6)} %select_n.93, bf16[1536,2560]{1,0:T(8,128)(2,1)} %get-tuple-element.366), kind=kLoop, calls=%fused_computation.26.clone.1 | loop fusion | bytes 15728644 | tf_op jit(solution)/shard_map/while/body/eval_jaxpr/dynamic_slice | solution.py:66
  210.6 6.3 %copy.52 = bf16[768,2560]{0,1:T(8,128)(2,1)} copy(bf16[768,2560]{1,0:T(8,128)(2,1)} %get-tuple-element.328) | data formatting | bytes 7864320 | tf_op jit(solution)/shard_map/while/body/eval_jaxpr/dynamic_slice | solution.py:63
  216.9 6.3 %copy.53 = bf16[768,2560]{0,1:T(8,128)(2,1)} copy(bf16[768,2560]{1,0:T(8,128)(2,1)} %get-tuple-element.332) | data formatting | bytes 7864320 | tf_op jit(solution)/shard_map/while/body/eval_jaxpr/dynamic_slice | solution.py:66
  223.2 4.8 %bitcast_reduce_fusion.2 = (f32[20,192]{1,0:T(8,128)S(1)}, f32[20,768,192]{1,2,0:T(8,128)S(1)}) fusion(pred[768]{0:T(1024)(128)(4,1)S(1)} %broadcast_compare_fusion.2, bf16[192,20,128]{2,0,1:T(8,128)(2,1)} %get-tuple-element.367, bf16[768,20,128]{0,2,1:T(8,128)(2,1)} %bitcast.80), kind=kOutput, calls=%fused_computation.2.clone.1 | convolution fusion | flops 763818240 | bytes 16727808 | tf_op jit(solution)/shard_map/while/body/eval_jaxpr/qhd,khd->hqk/dot_general | solution.py:75
  228.0 6.4 %bitcast_add_fusion.2 = f32[192,20,128]{2,0,1:T(8,128)} fusion(f32[192,20,128]{2,0,1:T(8,128)} %get-tuple-element.350, bf16[768,20,128]{0,2,1:T(8,128)(2,1)S(1)} %bitcast.81, f32[20,768,192]{1,2,0:T(8,128)S(1)} %get-tuple-element.331, f32[20,192]{1,0:T(8,128)S(1)} %get-tuple-element.361, pred[768]{0:T(1024)(128)(4,1)S(1)} %broadcast_compare_fusion.2, ...), kind=kOutput, calls=%fused_computation.11.clone.1 | convolution fusion | flops 771194880 | bytes 19692288 | tf_op jit(solution)/shard_map/while/body/eval_jaxpr/hqk,khd->qhd/dot_general | solution.py:83
  234.4 3.6 %fusion.51 = f32[20,192]{1,0:T(8,128)S(1)} fusion(f32[20,768,192]{1,2,0:T(8,128)S(1)} %get-tuple-element.331, f32[20,192]{1,0:T(8,128)S(1)} %get-tuple-element.361, pred[768]{0:T(1024)(128)(4,1)S(1)} %broadcast_compare_fusion.2), kind=kLoop, calls=%fused_computation.7.clone.1 | loop fusion | flops 14741760 | bytes 11827968 | tf_op jit(solution)/shard_map/while/body/eval_jaxpr/reduce_sum | solution.py:82
  238.1 2.2 convert_reduce_fusion
  240.4 4.9 %all-reduce.1 = (f32[192]{0:T(256)S(1)}, f32[192]{0:T(256)S(1)}) all-reduce(f32[192]{0:T(256)S(1)} %get-tuple-element.200, f32[192]{0:T(256)S(1)} %get-tuple-element.199), channel_id=1, replica_groups=mesh['groups'=2,'span'=4,'head'=2,'slab'=2] {'head'}, use_global_device_ids=true, to_apply=%region_8.9 | all-reduce | flops 384 | bytes 3072 | tf_op jit(solution)/shard_map/psum | solution.py:145
  245.3 1.6 convolution_convert_fusion
  247.1 8.3 %all-reduce = bf16[8,1536]{1,0:T(8,128)(2,1)S(1)} all-reduce(bf16[8,1536]{1,0:T(8,128)(2,1)S(1)} %bitcast.86), channel_id=2, replica_groups=mesh['groups'=2,'span'=4,'head'=2,'slab'=2] {'head'}, use_global_device_ids=true, to_apply=%region_9.10.clone | all-reduce | flops 12288 | bytes 49152
  256.6 2.4 collective-permute-start
  259.0 1.3 collective-permute-start.1
  260.4 4.2 %collective-permute-done.1 = bf16[3,1,16,16]{3,2,1,0:T(8,128)(2,1)S(1)} collective-permute-done((bf16[3,1,16,16]{3,2,1,0:T(8,128)(2,1)S(1)}, bf16[3,1,16,16]{3,2,1,0:T(8,128)(2,1)S(1)}, u32[]{:S(2)}, u32[]{:S(2)}) %collective-permute-start.1) | collective-permute-done | bytes 1568 | tf_op jit(solution)/shard_map/ppermute | solution.py:31
  264.6 1.3 collective-permute-start.2
  265.9 1.3 collective-permute-start.3
  267.9 1.1 collective-permute-done.3
  269.1 1.3 collective-permute-start.4
  271.3 2.2 collective-permute-done.4
  274.6 3.2 %concatenate.35 = bf16[3,8,16,432]{3,2,1,0:T(8,128)(2,1)} concatenate(bf16[3,8,16,16]{3,2,1,0:T(8,128)(2,1)} %get-tuple-element.247, bf16[3,8,16,16]{3,2,1,0:T(8,128)(2,1)} %get-tuple-element.246, bf16[3,8,16,16]{3,2,1,0:T(8,128)(2,1)} %get-tuple-element.245, bf16[3,8,16,16]{3,2,1,0:T(8,128)(2,1)S(1)} %get-tuple-element.244, bf16[3,8,16,16]{3,2,1,0:T(8,128)(2,1)S(1)} %get-tuple-element.243, ...), dimensions={3} | concatenate | bytes 663552 | tf_op jit(solution)/shard_map/concatenate | solution.py:182
  277.8 2.2 fusion.23
  (57 shorter events, 8.5 us)
Async XLA Ops:
  7.2 1.6 copy-start
  7.2 5.5 %copy-start.6 = (u32[32]{0:T(128)S(1)}, u32[32]{0:T(128)}, u32[]{:S(2)}) copy-start(u32[32]{0:T(128)} %constant.95) | copy-start | bytes 388
  7.2 82.9 %all-gather.3.cloned.1.call-start = ((), (), s32[]{:S(2)}) async-start(), calls=%async_computation | async-start | bytes 8847360 | tf_op jit(solution)/shard_map/all_gather | solution.py:129
  7.9 160.2 %all-gather.5.cloned.1.call-start = ((), (), s32[]{:S(2)}) async-start(), calls=%async_computation.1 | async-start | bytes 8847360 | tf_op jit(solution)/shard_map/all_gather | solution.py:130
  168.1 77.2 %copy-start.3 = (f32[2560]{0:T(1024)S(1)}, f32[2560]{0:T(1024)}, u32[]{:S(2)}) copy-start(f32[2560]{0:T(1024)} %param.17) | copy-start | bytes 30724
  168.1 77.2 %copy-start.4 = (f32[2560]{0:T(1024)S(1)}, f32[2560]{0:T(1024)}, u32[]{:S(2)}) copy-start(f32[2560]{0:T(1024)} %param.16) | copy-start | bytes 30724
  189.0 4.8 %copy-start.1 = (bf16[768,2560]{0,1:T(8,128)(2,1)S(1)}, bf16[768,2560]{0,1:T(8,128)(2,1)}, u32[]{:S(2)}) copy-start(bf16[768,2560]{0,1:T(8,128)(2,1)} %copy.53) | copy-start | bytes 11796484 | tf_op jit(solution)/shard_map/while
  223.2 4.8 %copy-start.1 = (bf16[768,2560]{0,1:T(8,128)(2,1)S(1)}, bf16[768,2560]{0,1:T(8,128)(2,1)}, u32[]{:S(2)}) copy-start(bf16[768,2560]{0,1:T(8,128)(2,1)} %copy.53) | copy-start | bytes 11796484 | tf_op jit(solution)/shard_map/while
  238.1 17.7 %copy-start.2 = (f32[3,8,16,16]{3,2,1,0:T(8,128)S(1)}, f32[3,8,16,16]{3,2,1,0:T(8,128)}, u32[]{:S(2)}) copy-start(f32[3,8,16,16]{3,2,1,0:T(8,128)} %param.19) | copy-start | bytes 73732
  256.6 3.8 %collective-permute-start = (bf16[3,1,16,16]{3,2,1,0:T(8,128)(2,1)S(1)}, bf16[3,1,16,16]{3,2,1,0:T(8,128)(2,1)S(1)}, u32[]{:S(2)}, u32[]{:S(2)}) collective-permute-start(bf16[3,1,16,16]{3,2,1,0:T(8,128)(2,1)S(1)} %get-tuple-element.260), channel_id=1, source_target_pairs={{0,2},{1,3},{4,6},{5,7},{8,10},{9,11},{12,14},{13,15},{16,18},{17,... | collective-permute-start | bytes 4616 | tf_op jit(solution)/shard_map/ppermute | solution.py:29
  259.0 5.6 %collective-permute-start.1 = (bf16[3,1,16,16]{3,2,1,0:T(8,128)(2,1)S(1)}, bf16[3,1,16,16]{3,2,1,0:T(8,128)(2,1)S(1)}, u32[]{:S(2)}, u32[]{:S(2)}) collective-permute-start(bf16[3,1,16,16]{3,2,1,0:T(8,128)(2,1)S(1)} %get-tuple-element.261), channel_id=1, source_target_pairs={{2,0},{3,1},{6,4},{7,5},{10,8},{11,9},{14,12},{15,13},{18,16},{19,... | collective-permute-start | bytes 4616 | tf_op jit(solution)/shard_map/ppermute | solution.py:31
  264.6 3.3 %collective-permute-start.2 = (bf16[3,10,1,16]{3,2,1,0:T(2,128)(2,1)S(1)}, bf16[3,10,1,16]{3,2,1,0:T(2,128)(2,1)S(1)}, u32[]{:S(2)}, u32[]{:S(2)}) collective-permute-start(bf16[3,10,1,16]{3,2,1,0:T(2,128)(2,1)S(1)} %get-tuple-element.256), channel_id=1, source_target_pairs={{0,1},{2,3},{4,5},{6,7},{8,9},{10,11},{12,13},{14,15},{16,17},{18,... | collective-permute-start | bytes 2888 | tf_op jit(solution)/shard_map/ppermute | solution.py:29
  265.9 3.1 %collective-permute-start.3 = (bf16[3,10,1,16]{3,2,1,0:T(2,128)(2,1)S(1)}, bf16[3,10,1,16]{3,2,1,0:T(2,128)(2,1)S(1)}, u32[]{:S(2)}, u32[]{:S(2)}) collective-permute-start(bf16[3,10,1,16]{3,2,1,0:T(2,128)(2,1)S(1)} %get-tuple-element.257), channel_id=1, source_target_pairs={{1,0},{3,2},{5,4},{7,6},{9,8},{11,10},{13,12},{15,14},{17,16},{19,... | collective-permute-start | bytes 2888 | tf_op jit(solution)/shard_map/ppermute | solution.py:31
  269.1 4.5 %collective-permute-start.4 = (bf16[2,10,18,16]{3,2,1,0:T(8,128)(2,1)S(1)}, bf16[2,10,18,16]{3,2,1,0:T(8,128)(2,1)S(1)}, u32[]{:S(2)}, u32[]{:S(2)}) collective-permute-start(bf16[2,10,18,16]{3,2,1,0:T(8,128)(2,1)S(1)} %pad_maximum_fusion.1), channel_id=1, source_target_pairs={{0,4},{4,8},{8,12},{1,5},{5,9},{9,13},{2,6},{6,10},{10,14},{3,7},{... | collective-permute-start | bytes 34568 | tf_op jit(solution)/shard_map/ppermute | solution.py:41
  270.5 7.4 %copy-start.5 = (f32[384]{0:T(512)S(1)}, f32[384]{0:T(512)}, u32[]{:S(2)}) copy-start(f32[384]{0:T(512)} %param.21) | copy-start | bytes 4612
Sparse Core Ops, SparseCore 0:
  9.7 80.4 all-gather.2
  91.8 76.2 all-gather.4
where the time goes:
time: 288 us; the launch traced here: 287 us
  waiting for transfers between devices  162 us (56%)
  local copies, waits for them, and re-layouts  51.2 us (18%)
  matrix products  24.5 us (9%)
  between operations  14.9 us (5%)
  blocking collectives  13.3 us (5%)
  other arithmetic  11.5 us (4%)
  starting transfers between devices  7.64 us (3%)
    all_gather x1, waiting for transfers between devices, per_device(): lax.all_gather(values, ('span', 'slab'), axis=0, tiled=True)  78 us
    all_gather x1, waiting for transfers between devices, per_device(): lax.all_gather(keys, ('span', 'slab'), axis=0, tiled=True)  75.5 us
    dynamic_slice x4, local copies, waits for them, and re-layouts, one_block(): lax.dynamic_slice_in_dim(values_piece, offset, length, 0)  26.6 us
    dynamic_slice x2, local copies, waits for them, and re-layouts, one_block(): lax.dynamic_slice_in_dim(keys_piece, offset, length, 0)  12.6 us
    dot_general x2, matrix products, one_block(): jnp.einsum('hqk,khd->qhd', weights.astype(jnp.bfloat16), value_block, pre...  11.2 us
    dot_general x2, matrix products, one_block(): jnp.einsum('qhd,khd->hqk', query_block, key_block, preferred_element_type...  9.52 us
    unnamed x1, blocking collectives  8.32 us
    reduce_sum x2, other arithmetic, one_block(): running_sum = running_sum * factor + jnp.sum(weights, axis=2)  7.25 us
  transfers between devices with their start and end apart: 7, of which 6 were waited for; matrix products, arithmetic and copies ran while one was open for 2% of the time, Pallas kernels for 0%

commit v1 on v0

--- a/solution.py
+++ b/solution.py
@@ -1,8 +1,12 @@
+import functools
 import math
 
 import jax
 import jax.numpy as jnp
+import numpy as np
 from jax import lax
+from jax.experimental import pallas as pl
+from jax.experimental.pallas import tpu as pltpu
 from jax.sharding import PartitionSpec as P
 
 HEADS = 40
@@ -94,7 +98,7 @@
     return result
 
 
-def per_device(
+def gathered_plan(
     queries,
     keys,
     values,
@@ -207,6 +211,473 @@
     return (clean_latent, decoded)
 
 
+NEAR_HEADS = 4
+MIDDLE_HEADS = 4
+FAR_HEADS = 2
+EARLY = 3
+STAT_ROWS = 8
+SLOTS = 3
+ABSENT = -1
+
+
+def plan_fits(heads_dev, span_count, slab_count, head_count):
+    return (
+        span_count == 4
+        and slab_count == 2
+        and head_count == 2
+        and heads_dev == slab_count * (NEAR_HEADS + MIDDLE_HEADS + FAR_HEADS)
+    )
+
+
+def attend_kernel(plan, meta, mask, *refs):
+    (query_own, key_own, value_own, received, weight, gain, sums_in), rest = refs[:7], refs[7:]
+    payloads, (sums_out, score, peak, folded, squares) = rest[:-5], rest[-5:]
+    query_sources, key_sources, slots, span_count = plan
+    rows = query_own.shape[0]
+    step = pl.program_id(0)
+    base = 2
+    to_exp2 = math.log2(math.e) / math.sqrt(HD)
+
+    def key_of(source):
+        if source is None:
+            return jnp.concatenate([key_own[...], received[: rows // 2]], axis=0)
+        ref, start = payloads[source[0]], source[1]
+        return ref[start : start + rows]
+
+    def value_of(source):
+        if source is None:
+            return jnp.concatenate([value_own[...], received[rows // 2 :]], axis=0)
+        ref, start = payloads[source[0]], source[1] + rows
+        return ref[start : start + rows]
+
+    def allowed(query_index, key_index):
+        query_span = meta[base + query_index]
+        key_span = meta[base + len(query_sources) + key_index]
+        entry = mask[jnp.maximum(query_span, 0) * span_count + jnp.maximum(key_span, 0)]
+        return (query_span >= 0) & (key_span >= 0) & (key_span <= query_span) & (entry > 0)
+
+    @pl.when(step == 0)
+    def _():
+        folded[...] = jnp.zeros_like(folded)
+        squares[...] = jnp.zeros_like(squares)
+        sums_out[...] = sums_in[...]
+
+    scaled = weight[...].astype(jnp.float32) * gain[...]
+    high = scaled.astype(jnp.bfloat16)
+    low = (scaled - high.astype(jnp.float32)).astype(jnp.bfloat16)
+    projector = jnp.concatenate([high, low, jnp.ones((16, HD), jnp.bfloat16)], axis=0)
+    ones_block = jnp.ones((rows, HD), jnp.bfloat16)
+
+    def one_query(query_index, source):
+        @pl.when(meta[base + query_index] >= 0)
+        def _():
+            if source is None:
+                query = query_own[...]
+            else:
+                query = payloads[source[0]][source[1] : source[1] + rows]
+            peak[...] = jnp.full_like(peak, neg_big)
+            for key_index, key_source in enumerate(key_sources):
+
+                @pl.when(allowed(query_index, key_index))
+                def _():
+                    block = lax.dot_general(
+                        query,
+                        key_of(key_source),
+                        (((1,), (1,)), ((), ())),
+                        preferred_element_type=jnp.float32,
+                    )
+                    score[key_index] = block
+                    best = peak[...]
+                    for lane in range(0, rows, HD):
+                        best = jnp.maximum(best, block[:, lane : lane + HD])
+                    peak[...] = best
+
+            top = jnp.max(peak[...], axis=1, keepdims=True)
+            peak[...] = jnp.broadcast_to(top, peak.shape)
+            gathered = score.at[len(key_sources)]
+            gathered[:, : 2 * HD] = jnp.zeros((rows, 2 * HD), jnp.float32)
+            for key_index, key_source in enumerate(key_sources):
+
+                @pl.when(allowed(query_index, key_index))
+                def _():
+                    shift = peak[...]
+                    block = jnp.concatenate(
+                        [
+                            jnp.exp2((score[key_index, :, lane : lane + HD] - shift) * to_exp2)
+                            for lane in range(0, rows, HD)
+                        ],
+                        axis=1,
+                    ).astype(jnp.bfloat16)
+                    gathered[:, : 2 * HD] += jnp.dot(
+                        block,
+                        jnp.concatenate([value_of(key_source), ones_block], axis=1),
+                        preferred_element_type=jnp.float32,
+                    )
+
+            attended = (gathered[:, :HD] / gathered[:, HD : 2 * HD]).astype(jnp.bfloat16)
+            folded[query_index] += lax.dot_general(
+                projector, attended, (((1,), (1,)), ((), ())), preferred_element_type=jnp.float32
+            )
+            wide = attended.astype(jnp.float32)
+            squares[query_index] += wide * wide
+
+    for query_index, source in enumerate(query_sources):
+        one_query(query_index, source)
+
+    @pl.when(step == pl.num_programs(0) - 1)
+    def _():
+        ones_rows = jnp.ones((STAT_ROWS, HD), jnp.bfloat16)
+        patch = weight.shape[0]
+        for query_index, slot in enumerate(slots):
+            rest_of = squares[query_index]
+            total = jnp.zeros((STAT_ROWS, rows), jnp.float32)
+            for _ in range(3):
+                piece = rest_of.astype(jnp.bfloat16)
+                rest_of = rest_of - piece.astype(jnp.float32)
+                total = total + lax.dot_general(
+                    ones_rows, piece, (((1,), (1,)), ((), ())), preferred_element_type=jnp.float32
+                )
+            done = folded[query_index]
+            sums_out[slot, :patch] += done[:patch] + done[patch : 2 * patch]
+            sums_out[slot, patch : patch + STAT_ROWS] += done[
+                2 * patch : 2 * patch + STAT_ROWS
+            ]
+            sums_out[slot, patch + STAT_ROWS :] += total
+
+
+def attend(
+    heads, meta, mask, own, sums, payloads, query_sources, key_sources, slots, span_count, name
+):
+    queries, keys, values, received, weight, gain = own
+    rows = queries.shape[0]
+    patch = weight.shape[0]
+    column = lambda height, entry: pl.BlockSpec(
+        (height, HD), lambda i, meta, mask: (0, meta[entry] + i)
+    )
+    sums_spec = pl.BlockSpec(sums.shape, lambda i, meta, mask: (0, 0, 0))
+    plan = (query_sources, key_sources, slots, span_count)
+    pairs = heads * len(query_sources) * len(key_sources)
+    return pl.pallas_call(
+        functools.partial(attend_kernel, plan),
+        name=name,
+        out_shape=jax.ShapeDtypeStruct(sums.shape, sums.dtype),
+        grid_spec=pltpu.PrefetchScalarGridSpec(
+            num_scalar_prefetch=2,
+            grid=(heads,),
+            in_specs=[
+                column(rows, 0),
+                column(rows // 2, 0),
+                column(rows // 2, 0),
+                column(rows, 1),
+                column(patch, 0),
+                column(1, 0),
+                sums_spec,
+            ]
+            + [
+                pl.BlockSpec((payload.shape[0], HD), lambda i, meta, mask: (0, i))
+                for payload in payloads
+            ],
+            out_specs=sums_spec,
+            scratch_shapes=[
+                pltpu.VMEM((len(key_sources) + 1, rows, rows), jnp.float32),
+                pltpu.VMEM((rows, HD), jnp.float32),
+                pltpu.VMEM((len(query_sources), 2 * patch + 16, rows), jnp.float32),
+                pltpu.VMEM((len(query_sources), rows, HD), jnp.float32),
+            ],
+        ),
+        compiler_params=pltpu.CompilerParams(vmem_limit_bytes=40 << 20),
+        cost_estimate=pl.CostEstimate(
+            flops=pairs * 4 * rows * rows * HD,
+            bytes_accessed=(heads * HD * 2 * (3 * rows + sum(p.shape[0] for p in payloads))),
+            transcendentals=pairs * rows * rows,
+        ),
+    )(meta, mask, queries, keys, values, received, weight, gain, sums, *payloads)
+
+
+def meta_table(span_count, first, spans_of):
+    return np.array(
+        [[first[place], first[place]] + spans_of(place) for place in range(span_count)], np.int32
+    )
+
+
+def token_sums(queries, keys, values, span_mask, head_gain, patch_weight):
+    span_count = lax.axis_size("span")
+    slab_count = lax.axis_size("slab")
+    place = lax.axis_index("span")
+    slab = lax.axis_index("slab")
+    heads = queries.shape[1] // HD // slab_count
+    width = heads * HD
+    rows = queries.shape[0]
+    first_own = slab * heads
+    swap = [(0, 1), (1, 0)]
+
+    def pick(array, head, count):
+        return lax.dynamic_slice_in_dim(array, head * HD, count * HD, 1)
+
+    def pick_queries(head, count):
+        return pick(queries, first_own + head, count)
+
+    handed = jnp.concatenate(
+        [
+            lax.dynamic_slice_in_dim(array, (1 - slab) * width, width, 1)
+            for array in (keys, values)
+        ],
+        axis=0,
+    )
+    received = lax.ppermute(handed, "slab", swap)
+    half = rows // 2
+
+    def pick_pair(head, count):
+        return [
+            pick(keys, first_own + head, count),
+            pick(received[:half], head, count),
+            pick(values, first_own + head, count),
+            pick(received[half:], head, count),
+        ]
+
+    near, middle, far = 0, NEAR_HEADS, NEAR_HEADS + MIDDLE_HEADS
+    late = NEAR_HEADS - EARLY
+
+    def at(*choices):
+        return jnp.array(choices, jnp.int32)[place]
+
+    send = lambda value, *pairs: lax.ppermute(value, "span", list(pairs))
+    rows_of = lambda parts: jnp.concatenate(parts, axis=0)
+
+    down_start = at(near, middle, near, middle)
+    up_start = at(near, middle, near, near)
+    query_down = send(pick_queries(down_start, EARLY), (1, 0), (2, 1), (3, 2))
+    query_down_two = send(pick_queries(near, EARLY), (3, 1))
+    pair_up = send(rows_of(pick_pair(up_start, EARLY)), (0, 1), (1, 2))
+    pair_down = send(rows_of(pick_pair(down_start, EARLY)), (1, 0), (2, 1), (3, 2))
+    pair_up_two = send(rows_of(pick_pair(middle, EARLY)), (0, 2))
+    pair_down_two = send(rows_of(pick_pair(near, EARLY)), (3, 1))
+    far_pair = rows_of(pick_pair(far, FAR_HEADS))
+    far_all = rows_of([pick_queries(far, FAR_HEADS), far_pair])
+    far_next = send(far_all, (2, 3), (1, 0))
+    far_two = send(far_pair, (1, 3))
+    far_three = send(far_pair, (0, 3))
+    late_down = send(
+        rows_of([pick_queries(down_start + EARLY, late)] + pick_pair(down_start + EARLY, late)),
+        (1, 0),
+        (2, 1),
+        (3, 2),
+    )
+    late_up = send(rows_of(pick_pair(up_start + EARLY, late)), (0, 1), (1, 2))
+    late_up_two = send(rows_of(pick_pair(middle + EARLY, late)), (0, 2))
+    late_down_two = send(
+        rows_of([pick_queries(near + EARLY, late)] + pick_pair(near + EARLY, late)), (3, 1)
+    )
+
+    def main_spans(p):
+        reach = lambda q: q if 0 <= q < span_count else ABSENT
+        query = [p if p in (1, 2) else ABSENT, p + 1 if p < 3 else ABSENT, 3 if p == 1 else ABSENT]
+        return query + [p] + [reach(p + d) for d in (-1, -2, 1, 2)]
+
+    def far_spans(p):
+        query = [3 if p == 3 else ABSENT, 1 if p == 0 else ABSENT, 2 if p == 3 else ABSENT]
+        near_span = {0: 1, 3: 2}.get(p, ABSENT)
+        return query + [p, near_span, 1 if p == 3 else ABSENT, 0 if p == 3 else ABSENT]
+
+    main_first = (middle, near, middle, near)
+
+    def meta(first, spans_of):
+        row = jnp.array(meta_table(span_count, first, spans_of))[place]
+        return row + jnp.where(jnp.arange(row.shape[0]) == 0, first_own, 0)
+
+    mask = span_mask.reshape(-1)
+    weight = patch_weight.T
+    own = (queries, keys, values, received, weight, head_gain[None, :])
+    patch = weight.shape[0]
+    sums = jnp.zeros((SLOTS, patch + 2 * STAT_ROWS, rows), jnp.float32)
+    run = functools.partial(attend, mask=mask, own=own, span_count=span_count)
+    sums = run(
+        heads,
+        meta((0,) * span_count, lambda p: [0 if p == 0 else ABSENT, p]),
+        sums=sums,
+        payloads=[],
+        query_sources=(None,),
+        key_sources=(None,),
+        slots=(0,),
+        name="first_span",
+    )
+    sums = run(
+        FAR_HEADS,
+        meta((far,) * span_count, far_spans),
+        sums=sums,
+        payloads=[far_next, far_two, far_three],
+        query_sources=(None, (0, 0), (0, 0)),
+        key_sources=(None, (0, rows), (1, 0), (2, 0)),
+        slots=(0, 1, 2),
+        name="far_heads",
+    )
+    sums = run(
+        EARLY,
+        meta(main_first, main_spans),
+        sums=sums,
+        payloads=[query_down, query_down_two, pair_up, pair_up_two, pair_down, pair_down_two],
+        query_sources=(None, (0, 0), (1, 0)),
+        key_sources=(None, (2, 0), (3, 0), (4, 0), (5, 0)),
+        slots=(0, 1, 2),
+        name="early_heads",
+    )
+    sums = run(
+        late,
+        meta(tuple(f + EARLY for f in main_first), main_spans),
+        sums=sums,
+        payloads=[late_down, late_down_two, late_up, late_up_two],
+        query_sources=(None, (0, 0), (1, 0)),
+        key_sources=(None, (2, 0), (3, 0), (0, rows), (1, rows)),
+        slots=(0, 1, 2),
+        name="late_heads",
+    )
+    return sums
+
+
+def gather_noise(noisy_latent, swap):
+    frames, height, breadth, channels = noisy_latent.shape
+    earlier = from_behind(noisy_latent[frames - 2 :].reshape(2, -1), "span", 1)
+    grid = jnp.concatenate([earlier, noisy_latent.reshape(frames, -1)], axis=0)
+    slab = lax.axis_index("slab")
+    head = lax.axis_index("head")
+    other = lax.ppermute(grid, "slab", swap)
+    grid = grid.reshape(frames + 2, height, breadth * channels)
+    other = other.reshape(grid.shape)
+    grid = jnp.where(
+        slab == 0,
+        jnp.concatenate([grid, other], axis=2),
+        jnp.concatenate([other, grid], axis=2),
+    )
+    other = lax.ppermute(grid, "head", swap)
+    grid = jnp.where(
+        head == 0,
+        jnp.concatenate([grid, other], axis=1),
+        jnp.concatenate([other, grid], axis=1),
+    )
+    return grid.reshape(frames + 2, 2 * height, 2 * breadth, channels)
+
+
+def per_device(
+    queries,
+    keys,
+    values,
+    span_mask,
+    head_gain,
+    head_shift,
+    patch_weight,
+    noisy_latent,
+    conv_weight,
+    conv_bias,
+):
+    heads_dev = queries.shape[1] // HD
+    if not plan_fits(
+        heads_dev, lax.axis_size("span"), lax.axis_size("slab"), lax.axis_size("head")
+    ):
+        return gathered_plan(
+            queries,
+            keys,
+            values,
+            span_mask,
+            head_gain,
+            head_shift,
+            patch_weight,
+            noisy_latent,
+            conv_weight,
+            conv_bias,
+        )
+    place = lax.axis_index("span")
+    slab = lax.axis_index("slab")
+    head = lax.axis_index("head")
+    swap = [(0, 1), (1, 0)]
+    noise = gather_noise(noisy_latent, swap)
+    wide_weight = patch_weight.astype(jnp.float32)
+    constants = jnp.stack(
+        [
+            jnp.sum(wide_weight * head_gain[:, None], axis=0),
+            jnp.sum(wide_weight * head_shift[:, None], axis=0),
+        ]
+    )
+    constants = constants + lax.ppermute(constants, "head", swap)
+
+    sums = token_sums(queries, keys, values, span_mask, head_gain, patch_weight)
+    half = sums.shape[1] // 2
+    mine = lax.dynamic_slice_in_dim(sums, slab * half, half, 1)
+    theirs = lax.dynamic_slice_in_dim(sums, (1 - slab) * half, half, 1)
+    mine = mine + lax.ppermute(theirs, "slab", swap)
+    mine = mine + lax.ppermute(mine, "head", swap)
+    own, after, third = mine[0], mine[1], mine[2]
+    from_one = lax.ppermute(jnp.stack([after, own]), "span", [(0, 1), (1, 2), (2, 3)])
+    from_two = lax.ppermute(jnp.stack([third, after]), "span", [(0, 2), (1, 3)])
+    from_next = lax.ppermute(third, "span", [(3, 2)])
+    current = own + from_one[0] + from_two[0] + from_next
+    before = from_one[1] + from_two[1] + jnp.where(place == 3, third, 0.0)
+    both = jnp.stack([before, current])
+    other = lax.ppermute(both, "slab", swap)
+    both = jnp.where(
+        slab == 0,
+        jnp.concatenate([both, other], axis=1),
+        jnp.concatenate([other, both], axis=1),
+    )
+
+    patch = patch_weight.shape[1]
+    feature_width = HEADS * HD
+    row_mean = both[:, patch] / feature_width
+    spread = both[:, patch + STAT_ROWS] / feature_width - row_mean * row_mean
+    velocity = (
+        lax.rsqrt(spread + norm_eps)[:, None, :]
+        * (both[:, :patch] - row_mean[:, None, :] * constants[0][None, :, None])
+        + constants[1][None, :, None]
+    )
+    cells = (
+        velocity.reshape(2, 2, 2, LAT_CH, FRAMES_SPAN, TROWS, TCOLS)
+        .transpose(0, 4, 5, 1, 6, 2, 3)
+        .reshape(2, FRAMES_SPAN, 2 * TROWS, 2 * TCOLS, LAT_CH)
+    )
+    cells = jnp.concatenate([cells[0, FRAMES_SPAN - 2 :], cells[1]], axis=0)
+    latent = noise - noise_level * cells
+    frames, height, breadth, channels = noisy_latent.shape
+    clean_latent = lax.dynamic_slice(
+        latent,
+        (2, head * height, slab * breadth, 0),
+        (frames, height, breadth, channels),
+    )
+    latent_input = latent.astype(jnp.bfloat16)
+    present = (jnp.arange(frames + 2) >= 2) | (place > 0)
+    latent_input = jnp.where(present[:, None, None, None], latent_input, 0)
+    padded = jnp.pad(latent_input, ((0, 0), (1, 1), (1, 1), (0, 0)))
+    stacked = lax.dynamic_slice(
+        padded,
+        (0, head * height, slab * breadth, 0),
+        (frames + 2, height + 2, breadth + 2, channels),
+    )
+    columns = jnp.concatenate(
+        [
+            stacked[
+                frame_tap : frame_tap + FRAMES_SPAN,
+                row_tap : row_tap + height,
+                col_tap : col_tap + breadth,
+                :,
+            ]
+            for frame_tap in range(3)
+            for row_tap in range(3)
+            for col_tap in range(3)
+        ],
+        axis=-1,
+    )
+    decoded = (
+        jnp.dot(
+            columns.reshape(FRAMES_SPAN * height * breadth, 27 * LAT_CH),
+            conv_weight,
+            preferred_element_type=jnp.float32,
+        )
+        + conv_bias[None, :]
+    )
+    decoded = decoded.astype(jnp.bfloat16).reshape(
+        FRAMES_SPAN, height, breadth, conv_weight.shape[1]
+    )
+    return (clean_latent, decoded)
+
+
 def solution(mesh):
     placed = (
         P(("groups", "span"), "head"),

time: 288 us -> 168 us (0.58)
  waiting for transfers between devices: 162 us -> 15.6 us
  starting transfers between devices: 7.64 us -> 75.2 us
  Pallas kernels: 0 us -> 25.1 us
  matrix products: 24.5 us -> 1.09 us
  local copies, waits for them, and re-layouts: 51.2 us -> 33.8 us
  blocking collectives: 13.3 us -> 0 us
  between operations: 14.9 us -> 5.41 us
    all_gather x2 -> x0, waiting for transfers between devices: 154 us -> none  [the longest x1 78 us: per_device(): lax.all_gather(values, ('span', 'slab'), axis=0, tiled=True)]
    ppermute x4 -> x23, starting transfers between devices: 6.27 us -> 54.8 us  [the longest x13 28.6 us: token_sums(): send = lambda value, *pairs: lax.ppermute(value, 'span', list(pairs))]
    dynamic_slice x10 -> x17, local copies, waits for them, and re-layouts: 42 us -> 11.9 us  [the longest x12 8.71 us: pick(): return lax.dynamic_slice_in_dim(array, head * HD, count * HD, 1)]
    pallas_call x0 -> x4, Pallas kernels: none -> 25.1 us  [attend(): pl.pallas_call(functools.partial(attend_kernel, plan), name=name, out_sha...]
    dot_general x5 -> x0, matrix products: 22.3 us -> none  [the longest x2 11.2 us: one_block(): jnp.einsum('hqk,khd->qhd', weights.astype(jnp.bfloat16), value_block, pre...]
    ppermute x1, starting transfers between devices: 1.3 us -> 20.4 us  [from_behind(): return lax.ppermute(value, axis, pairs)]
    ppermute x4 -> x23, waiting for transfers between devices: 5.34 us -> 15.6 us  [the longest x1 6.14 us: per_device(): mine = mine + lax.ppermute(mine, 'head', swap)]
    reduce_sum x5 -> x1, other arithmetic: 9.62 us -> 0.23 us  [per_device(): jnp.sum(wide_weight * head_gain[:, None], axis=0)]
  transfers between devices with their start and end apart: 7 -> 24, of which waited for: 6 -> 5; matrix products, arithmetic and copies ran while one was open for 2% -> 17% of each run, Pallas kernels for 0% -> 15%
where the time goes in v1:
time: 168 us; the launch traced here: 167 us
  starting transfers between devices  75.2 us (45%)
  local copies, waits for them, and re-layouts  33.8 us (20%)
  Pallas kernels  25.1 us (15%)
  waiting for transfers between devices  15.6 us (9%)
  other arithmetic  10.3 us (6%)
  between operations  5.41 us (3%)
    ppermute x13, starting transfers between devices, token_sums(): send = lambda value, *pairs: lax.ppermute(value, 'span', list(pairs))  28.6 us
    pallas_call x4, Pallas kernels, attend(): pl.pallas_call(functools.partial(attend_kernel, plan), name=name, out_sha...  25.1 us
    ppermute x1, starting transfers between devices, from_behind(): return lax.ppermute(value, axis, pairs)  20.4 us
    ppermute x1, starting transfers between devices, per_device(): from_two = lax.ppermute(jnp.stack([third, after]), 'span', [(0, 2), (1, 3)])  12.3 us
    dynamic_slice x12, local copies, waits for them, and re-layouts, pick(): return lax.dynamic_slice_in_dim(array, head * HD, count * HD, 1)  8.71 us
    ppermute x1, starting transfers between devices, per_device(): lax.ppermute(jnp.stack([after, own]), 'span', [(0, 1), (1, 2), (2, 3)])  8.48 us
    ppermute x1, waiting for transfers between devices, per_device(): mine = mine + lax.ppermute(mine, 'head', swap)  6.14 us
    unnamed x72, local copies, waits for them, and re-layouts  5.55 us
  transfers between devices with their start and end apart: 24, of which 5 were waited for; matrix products, arithmetic and copies ran while one was open for 17% of the time, Pallas kernels for 15%

profile of v1, /device:TPU:0, one launch (start us, length us, event | category | flops | bytes accessed | tf_op | source)
XLA Modules:
  0.0 166.5 jit_solution(5955078074234332320)
XLA Ops:
  0.7 1.3 constant_dynamic-slice_fusion.27
  5.7 1.3 collective-permute-start.7
  7.8 2.5 %collective-permute-start.23 = (f32[2,64]{1,0:T(2,128)}, f32[2,64]{1,0:T(2,128)}, u32[]{:S(2)}, u32[]{:S(2)}) collective-permute-start(f32[2,64]{1,0:T(2,128)} %pad_maximum_fusion.12), channel_id=1, source_target_pairs={{0,2},{2,0},{1,3},{3,1},{4,6},{6,4},{5,7},{7,5},{8,10},{10,8},{9,1... | collective-permute-start | bytes 1544 | tf_op jit(solution)/shard_map/ppermute | solution.py:600
  11.5 1.6 constant_dynamic-update-slice_fusion.7
  20.7 1.6 reshape.65
  23.0 1.6 constant_dynamic-slice_fusion.3
  24.7 1.9 %constant_dynamic-slice_fusion.8 = (bf16[192,384]{1,0:T(8,128)(2,1)}, bf16[192,384]{1,0:T(8,128)(2,1)}, bf16[192,384]{1,0:T(8,128)(2,1)}, bf16[192,384]{1,0:T(8,128)(2,1)}) fusion(bf16[192,2560]{1,0:T(8,128)(2,1)} %refs_2_.7, s32[]{:T(128)S(6)} %select_n.157, s32[]{:T(128)S(6)} %select_n.156, s32[]{:T(128)S(6)} %select_n.160, s32[]{:T(128)S(6)} %select_n.158), kind=kLoop, calls=%fused_computation.92 | loop fusion | bytes 1179664 | tf_op jit(solution)/shard_map/dynamic_slice | solution.py:415
  29.4 1.5 constant_dynamic-update-slice_fusion.5
  32.5 7.8 %collective-permute-start.6 = (bf16[768,256]{1,0:T(8,128)(2,1)S(1)}, bf16[768,256]{1,0:T(8,128)(2,1)S(1)}, u32[]{:S(2)}, u32[]{:S(2)}) collective-permute-start(bf16[768,256]{1,0:T(8,128)(2,1)S(1)} %pad_maximum_fusion.5), channel_id=1, source_target_pairs={{0,12},{1,13},{2,14},{3,15},{16,28},{17,29},{18,30},{19,31}} | collective-permute-start | bytes 1179656 | tf_op jit(solution)/shard_map/ppermute | solution.py:444
  41.0 1.4 collective-permute-start.4
  42.7 4.7 %collective-permute-start.9 = (bf16[768,384]{1,0:T(8,128)(2,1)S(1)}, bf16[768,384]{1,0:T(8,128)(2,1)S(1)}, u32[]{:S(2)}, u32[]{:S(2)}) collective-permute-start(bf16[768,384]{1,0:T(8,128)(2,1)S(1)} %pad_maximum_fusion.1), channel_id=1, source_target_pairs={{0,4},{4,8},{1,5},{5,9},{2,6},{6,10},{3,7},{7,11},{16,20},{20,24},... | collective-permute-start | bytes 1769480 | tf_op jit(solution)/shard_map/ppermute | solution.py:444
  50.4 1.3 collective-permute-start.10
  51.7 1.3 collective-permute-start.11
  54.4 3.7 %collective-permute-done.4.refs_7_ = bf16[1152,256]{1,0:T(8,128)(2,1)S(1)} collective-permute-done((bf16[1152,256]{1,0:T(8,128)(2,1)}, bf16[1152,256]{1,0:T(8,128)(2,1)S(1)}, u32[]{:S(2)}, u32[]{:S(2)}) %collective-permute-start.4) | collective-permute-done | bytes 589856 | tf_op jit(solution)/shard_map/ppermute | solution.py:444
  58.9 10.7 %first_span.1.refs_6_ = f32[3,80,384]{2,1,0:T(8,128)S(1)} custom-call(s32[4]{0:T(128)S(1)} %fusion.12.meta, s32[16]{0:T(128)S(1)} %reshape.68.mask, bf16[384,2560]{1,0:T(8,128)(2,1)S(1)} %copy-done.1, bf16[192,2560]{1,0:T(8,128)(2,1)S(1)} %copy-done.3, bf16[192,2560]{1,0:T(8,128)(2,1)S(1)} %copy-done.4, ...), custom_call_target="tpu_custom_call" | custom-call | flops 754974720 | bytes 2949120 | tf_op jit(solution)/shard_map/first_span/pallas_call | solution.py:360
  69.6 4.6 %far_heads.1.refs_6_ = f32[3,80,384]{2,1,0:T(8,128)S(1)} custom-call(s32[9]{0:T(128)S(1)} %fusion.11.meta, s32[16]{0:T(128)S(1)} %reshape.68.mask, bf16[384,2560]{1,0:T(8,128)(2,1)S(1)} %copy-done.1, bf16[192,2560]{1,0:T(8,128)(2,1)S(1)} %copy-done.3, bf16[192,2560]{1,0:T(8,128)(2,1)S(1)} %copy-done.4, bf16[384,1280]{1,0:T(8,128)(2,1)S(1)} %collective-permute-done.3.refs_3_, ...), custom_call_target="tpu_custom_call" | custom-call | flops 1811939328 | bytes 1966080 | tf_op jit(solution)/shard_map/far_heads/pallas_call | solution.py:360
  74.2 20.4 %collective-permute-start = (f32[2,2048]{1,0:T(2,128)S(1)}, f32[2,2048]{1,0:T(2,128)S(1)}, u32[]{:S(2)}, u32[]{:S(2)}) collective-permute-start(f32[2,2048]{1,0:T(2,128)S(1)} %copy-done.24), channel_id=1, source_target_pairs={{0,4},{4,8},{8,12},{1,5},{5,9},{9,13},{2,6},{6,10},{10,14},{3,7},{... | collective-permute-start | bytes 49160 | tf_op jit(solution)/shard_map/ppermute | solution.py:45
  94.6 1.3 collective-permute-start.13
  96.6 5.2 %collective-permute-start.15 = (bf16[768,128]{1,0:T(8,128)(2,1)S(1)}, bf16[768,128]{1,0:T(8,128)(2,1)S(1)}, u32[]{:S(2)}, u32[]{:S(2)}) collective-permute-start(bf16[768,128]{1,0:T(8,128)(2,1)S(1)} %pad_maximum_fusion.6), channel_id=1, source_target_pairs={{0,4},{4,8},{1,5},{5,9},{2,6},{6,10},{3,7},{7,11},{16,20},{20,24},... | collective-permute-start | bytes 589832 | tf_op jit(solution)/shard_map/ppermute | solution.py:444
  101.8 1.5 collective-permute-start.16
  103.3 7.0 %early_heads.1.refs_6_ = f32[3,80,384]{2,1,0:T(8,128)S(1)} custom-call(s32[10]{0:T(128)S(1)} %get-tuple-element.89.meta, s32[16]{0:T(128)S(1)} %reshape.68.mask, bf16[384,2560]{1,0:T(8,128)(2,1)S(1)} %copy-done.1, bf16[192,2560]{1,0:T(8,128)(2,1)S(1)} %copy-done.3, bf16[192,2560]{1,0:T(8,128)(2,1)S(1)} %copy-done.4, ...), custom_call_target="tpu_custom_call" | custom-call | flops 3397386240 | bytes 3833856 | tf_op jit(solution)/shard_map/early_heads/pallas_call | solution.py:360
  110.3 2.8 %late_heads.1 = f32[3,80,384]{2,1,0:T(8,128)S(1)} custom-call(s32[10]{0:T(128)S(1)} %get-tuple-element.88.meta, s32[16]{0:T(128)S(1)} %reshape.68.mask, bf16[384,2560]{1,0:T(8,128)(2,1)S(1)} %copy-done.1, bf16[192,2560]{1,0:T(8,128)(2,1)S(1)} %copy-done.3, bf16[192,2560]{1,0:T(8,128)(2,1)S(1)} %copy-done.4, ...), custom_call_target="tpu_custom_call" | custom-call | flops 1132462080 | bytes 1277952 | tf_op jit(solution)/shard_map/late_heads/pallas_call | solution.py:360
  117.0 6.1 %collective-permute-done.18 = f32[3,40,384]{2,1,0:T(8,128)S(1)} collective-permute-done((f32[3,40,384]{2,1,0:T(8,128)S(1)}, f32[3,40,384]{2,1,0:T(8,128)S(1)}, u32[]{:S(2)}, u32[]{:S(2)}) %collective-permute-start.18) | collective-permute-done | bytes 184352 | tf_op jit(solution)/shard_map/ppermute | solution.py:607
  123.2 12.3 %collective-permute-start.20 = (f32[2,40,384]{2,1,0:T(8,128)S(1)}, f32[2,40,384]{2,1,0:T(8,128)S(1)}, u32[]{:S(2)}, u32[]{:S(2)}) collective-permute-start(f32[2,40,384]{2,1,0:T(8,128)S(1)} %get-tuple-element.85), channel_id=1, source_target_pairs={{0,8},{4,12},{1,9},{5,13},{2,10},{6,14},{3,11},{7,15},{16,24},{20,... | collective-permute-start | bytes 368648 | tf_op jit(solution)/shard_map/ppermute | solution.py:610
  135.5 8.5 %collective-permute-start.19 = (f32[2,40,384]{2,1,0:T(8,128)S(1)}, f32[2,40,384]{2,1,0:T(8,128)S(1)}, u32[]{:S(2)}, u32[]{:S(2)}) collective-permute-start(f32[2,40,384]{2,1,0:T(8,128)S(1)} %get-tuple-element.84), channel_id=1, source_target_pairs={{0,4},{4,8},{8,12},{1,5},{5,9},{9,13},{2,6},{6,10},{10,14},{3,7},{... | collective-permute-start | bytes 368648 | tf_op jit(solution)/shard_map/ppermute | solution.py:609
  144.1 2.3 %collective-permute-done.19 = f32[2,40,384]{2,1,0:T(8,128)S(1)} collective-permute-done((f32[2,40,384]{2,1,0:T(8,128)S(1)}, f32[2,40,384]{2,1,0:T(8,128)S(1)}, u32[]{:S(2)}, u32[]{:S(2)}) %collective-permute-start.19) | collective-permute-done | bytes 122912 | tf_op jit(solution)/shard_map/ppermute | solution.py:609
  149.0 2.7 %collective-permute-done.2 = f32[5,8,512]{2,1,0:T(8,128)S(1)} collective-permute-done((f32[5,8,512]{2,1,0:T(8,128)S(1)}, f32[5,8,512]{2,1,0:T(8,128)S(1)}, u32[]{:S(2)}, u32[]{:S(2)}) %collective-permute-start.2) | collective-permute-done | bytes 81952 | tf_op jit(solution)/shard_map/ppermute | solution.py:551
  153.5 2.1 %copy.20 = f32[2,3,8,2,16,2,16]{6,5,4,3,2,1,0:T(2,128)} copy(f32[2,3,8,2,16,2,16]{4,2,1,6,5,3,0:T(8,128)S(1)} %bitcast.68) | data formatting | bytes 393216 | tf_op jit(solution)/shard_map/transpose | solution.py:633
  156.2 1.1 slice_bitcast_fusion
  157.4 1.8 %convert_select_fusion = (bf16[5,16,32,16]{3,2,1,0:T(8,128)(2,1)S(1)}, f32[5,16,32,16]{3,2,1,0:T(8,128)S(1)}) fusion(pred[5]{0:T(512)(128)(4,1)S(1)} %copy-done.27, f32[3,16,32,16]{3,2,1,0:T(8,128)S(1)} %bitcast.69, f32[2,16,32,16]{3,2,1,0:T(8,128)S(1)} %slice_bitcast_fusion, f32[5,8,32,16]{3,2,1,0:T(8,128)S(1)} %copy-done.9, ...), kind=kLoop, calls=%fused_computation.38 | loop fusion | flops 327680 | bytes 573446 | tf_op jit(solution)/shard_map/jit(_where)/select_n | solution.py:646
  160.0 1.3 pad_dynamic-slice_fusion
  163.0 2.4 %concatenate.114 = bf16[3,8,16,432]{3,2,1,0:T(8,128)(2,1)S(1)} concatenate(bf16[3,8,16,16]{3,2,1,0:T(8,128)(2,1)S(1)} %get-tuple-element.43, bf16[3,8,16,16]{3,2,1,0:T(8,128)(2,1)S(1)} %get-tuple-element.44, bf16[3,8,16,16]{3,2,1,0:T(8,128)(2,1)S(1)} %get-tuple-element.54, bf16[3,8,16,16]{3,2,1,0:T(8,128)(2,1)S(1)} %get-tuple-element.45, ...), dimensions={3} | concatenate | bytes 663552 | tf_op jit(solution)/shard_map/concatenate | solution.py:653
  (163 shorter events, 33.3 us)
Async XLA Ops:
  0.6 164.8 %copy-start = (bf16[432,384]{1,0:T(8,128)(2,1)S(1)}, bf16[432,384]{1,0:T(8,128)(2,1)}, u32[]{:S(2)}) copy-start(bf16[432,384]{1,0:T(8,128)(2,1)} %param.24) | copy-start | bytes 995332
  3.1 12.2 %copy-start.29 = (s32[4]{0:T(128)S(1)}, s32[4]{0:T(128)}, u32[]{:S(2)}) copy-start(s32[4]{0:T(128)} %constant.76.clone) | copy-start | bytes 52
  3.1 25.7 %collective-permute-start.3 = (bf16[384,1280]{1,0:T(8,128)(2,1)}, bf16[384,1280]{1,0:T(8,128)(2,1)S(1)}, u32[]{:S(2)}, u32[]{:S(2)}) collective-permute-start(bf16[384,1280]{1,0:T(8,128)(2,1)} %pad_maximum_fusion), channel_id=1, source_target_pairs={{0,1},{1,0},{2,3},{3,2},{4,5},{5,4},{6,7},{7,6},{8,9},{9,8},{10,11... | collective-permute-start | bytes 2949128 | tf_op jit(solution)/shard_map/ppermute | solution.py:427
  4.8 13.6 %copy-start.8 = (f32[3,8,16,16]{3,2,1,0:T(8,128)S(1)}, f32[3,8,16,16]{3,2,1,0:T(8,128)}, u32[]{:S(2)}) copy-start(f32[3,8,16,16]{3,2,1,0:T(8,128)} %param.23) | copy-start | bytes 73732
  5.7 44.7 %collective-permute-start.7 = (bf16[384,384]{1,0:T(8,128)(2,1)}, bf16[384,384]{1,0:T(8,128)(2,1)}, u32[]{:S(2)}, u32[]{:S(2)}) collective-permute-start(bf16[384,384]{1,0:T(8,128)(2,1)} %get-tuple-element.13), channel_id=1, source_target_pairs={{4,0},{8,4},{12,8},{5,1},{9,5},{13,9},{6,2},{10,6},{14,10},{7,3},{... | collective-permute-start | bytes 884744 | tf_op jit(solution)/shard_map/ppermute | solution.py:444
  7.8 19.7 %collective-permute-start.23 = (f32[2,64]{1,0:T(2,128)}, f32[2,64]{1,0:T(2,128)}, u32[]{:S(2)}, u32[]{:S(2)}) collective-permute-start(f32[2,64]{1,0:T(2,128)} %pad_maximum_fusion.12), channel_id=1, source_target_pairs={{0,2},{2,0},{1,3},{3,1},{4,6},{6,4},{5,7},{7,5},{8,10},{10,8},{9,1... | collective-permute-start | bytes 1544 | tf_op jit(solution)/shard_map/ppermute | solution.py:600
  31.8 19.9 %collective-permute-start.5 = (bf16[768,256]{1,0:T(8,128)(2,1)S(1)}, bf16[768,256]{1,0:T(8,128)(2,1)S(1)}, u32[]{:S(2)}, u32[]{:S(2)}) collective-permute-start(bf16[768,256]{1,0:T(8,128)(2,1)S(1)} %pad_maximum_fusion.5), channel_id=1, source_target_pairs={{4,12},{5,13},{6,14},{7,15},{20,28},{21,29},{22,30},{23,31}} | collective-permute-start | bytes 1179656 | tf_op jit(solution)/shard_map/ppermute | solution.py:444
  32.5 20.5 %collective-permute-start.6 = (bf16[768,256]{1,0:T(8,128)(2,1)S(1)}, bf16[768,256]{1,0:T(8,128)(2,1)S(1)}, u32[]{:S(2)}, u32[]{:S(2)}) collective-permute-start(bf16[768,256]{1,0:T(8,128)(2,1)S(1)} %pad_maximum_fusion.5), channel_id=1, source_target_pairs={{0,12},{1,13},{2,14},{3,15},{16,28},{17,29},{18,30},{19,31}} | collective-permute-start | bytes 1179656 | tf_op jit(solution)/shard_map/ppermute | solution.py:444
  41.0 17.1 %collective-permute-start.4 = (bf16[1152,256]{1,0:T(8,128)(2,1)}, bf16[1152,256]{1,0:T(8,128)(2,1)S(1)}, u32[]{:S(2)}, u32[]{:S(2)}) collective-permute-start(bf16[1152,256]{1,0:T(8,128)(2,1)} %constant_dynamic-update-slice_fusion.4), channel_id=1, source_target_pairs={{8,12},{4,0},{9,13},{5,1},{10,14},{6,2},{11,15},{7,3},{24,28},{20,... | collective-permute-start | bytes 1769480 | tf_op jit(solution)/shard_map/ppermute | solution.py:444
  42.7 51.9 %collective-permute-start.9 = (bf16[768,384]{1,0:T(8,128)(2,1)S(1)}, bf16[768,384]{1,0:T(8,128)(2,1)S(1)}, u32[]{:S(2)}, u32[]{:S(2)}) collective-permute-start(bf16[768,384]{1,0:T(8,128)(2,1)S(1)} %pad_maximum_fusion.1), channel_id=1, source_target_pairs={{0,4},{4,8},{1,5},{5,9},{2,6},{6,10},{3,7},{7,11},{16,20},{20,24},... | collective-permute-start | bytes 1769480 | tf_op jit(solution)/shard_map/ppermute | solution.py:444
  47.8 6.0 %copy-start.20 = (bf16[192,128]{1,0:T(8,128)(2,1)S(1)}, bf16[192,128]{1,0:T(8,128)(2,1)}, u32[]{:S(2)}) copy-start(bf16[192,128]{1,0:T(8,128)(2,1)} %get-tuple-element.15) | copy-start | bytes 147460
  49.0 9.1 %copy-start.18 = (bf16[384,384]{1,0:T(8,128)(2,1)S(1)}, bf16[384,384]{1,0:T(8,128)(2,1)}, u32[]{:S(2)}) copy-start(bf16[384,384]{1,0:T(8,128)(2,1)} %get-tuple-element.12) | copy-start | bytes 884740
  49.7 9.1 %copy-start.3 = (bf16[192,2560]{1,0:T(8,128)(2,1)S(1)}, bf16[192,2560]{1,0:T(8,128)(2,1)}, u32[]{:S(2)}) copy-start(bf16[192,2560]{1,0:T(8,128)(2,1)} %refs_1_.7) | copy-start | bytes 2949124
  49.7 9.1 %copy-start.6 = (bf16[2560,64]{0,1:T(8,128)(2,1)S(1)}, bf16[2560,64]{0,1:T(8,128)(2,1)}, u32[]{:S(2)}) copy-start(bf16[2560,64]{0,1:T(8,128)(2,1)} %param.22) | copy-start | bytes 983044
  50.4 45.5 %collective-permute-start.10 = (bf16[768,384]{1,0:T(8,128)(2,1)S(1)}, bf16[768,384]{1,0:T(8,128)(2,1)S(1)}, u32[]{:S(2)}, u32[]{:S(2)}) collective-permute-start(bf16[768,384]{1,0:T(8,128)(2,1)S(1)} %pad_maximum_fusion.2), channel_id=1, source_target_pairs={{0,8},{1,9},{2,10},{3,11},{16,24},{17,25},{18,26},{19,27}} | collective-permute-start | bytes 1769480 | tf_op jit(solution)/shard_map/ppermute | solution.py:444
  51.7 44.9 %collective-permute-start.11 = (bf16[768,384]{1,0:T(8,128)(2,1)S(1)}, bf16[768,384]{1,0:T(8,128)(2,1)S(1)}, u32[]{:S(2)}, u32[]{:S(2)}) collective-permute-start(bf16[768,384]{1,0:T(8,128)(2,1)S(1)} %pad_maximum_fusion.3), channel_id=1, source_target_pairs={{4,0},{8,4},{12,8},{5,1},{9,5},{13,9},{6,2},{10,6},{14,10},{7,3},{... | collective-permute-start | bytes 1769480 | tf_op jit(solution)/shard_map/ppermute | solution.py:444
  53.1 48.8 %collective-permute-start.12 = (bf16[768,384]{1,0:T(8,128)(2,1)S(1)}, bf16[768,384]{1,0:T(8,128)(2,1)S(1)}, u32[]{:S(2)}, u32[]{:S(2)}) collective-permute-start(bf16[768,384]{1,0:T(8,128)(2,1)S(1)} %pad_maximum_fusion.4), channel_id=1, source_target_pairs={{12,4},{13,5},{14,6},{15,7},{28,20},{29,21},{30,22},{31,23}} | collective-permute-start | bytes 1769480 | tf_op jit(solution)/shard_map/ppermute | solution.py:444
  58.1 16.1 %collective-permute-start.8 = (bf16[384,384]{1,0:T(8,128)(2,1)S(1)}, bf16[384,384]{1,0:T(8,128)(2,1)S(1)}, u32[]{:S(2)}, u32[]{:S(2)}) collective-permute-start(bf16[384,384]{1,0:T(8,128)(2,1)S(1)} %copy-done.18), channel_id=1, source_target_pairs={{12,4},{13,5},{14,6},{15,7},{28,20},{29,21},{30,22},{31,23}} | collective-permute-start | bytes 884744 | tf_op jit(solution)/shard_map/ppermute | solution.py:444
  58.9 10.7 %copy-start.19 = (bf16[192,128]{1,0:T(8,128)(2,1)S(1)}, bf16[192,128]{1,0:T(8,128)(2,1)}, u32[]{:S(2)}) copy-start(bf16[192,128]{1,0:T(8,128)(2,1)} %get-tuple-element.14) | copy-start | bytes 147460
  74.2 39.8 %collective-permute-start = (f32[2,2048]{1,0:T(2,128)S(1)}, f32[2,2048]{1,0:T(2,128)S(1)}, u32[]{:S(2)}, u32[]{:S(2)}) collective-permute-start(f32[2,2048]{1,0:T(2,128)S(1)} %copy-done.24), channel_id=1, source_target_pairs={{0,4},{4,8},{8,12},{1,5},{5,9},{9,13},{2,6},{6,10},{10,14},{3,7},{... | collective-permute-start | bytes 49160 | tf_op jit(solution)/shard_map/ppermute | solution.py:45
  94.6 15.7 %collective-permute-start.13 = (bf16[1152,128]{1,0:T(8,128)(2,1)}, bf16[1152,128]{1,0:T(8,128)(2,1)S(1)}, u32[]{:S(2)}, u32[]{:S(2)}) collective-permute-start(bf16[1152,128]{1,0:T(8,128)(2,1)} %get-tuple-element.72), channel_id=1, source_target_pairs={{4,0},{8,4},{12,8},{5,1},{9,5},{13,9},{6,2},{10,6},{14,10},{7,3},{... | collective-permute-start | bytes 884744 | tf_op jit(solution)/shard_map/ppermute | solution.py:444
  95.9 14.4 %collective-permute-start.14 = (bf16[1152,128]{1,0:T(8,128)(2,1)}, bf16[1152,128]{1,0:T(8,128)(2,1)S(1)}, u32[]{:S(2)}, u32[]{:S(2)}) collective-permute-start(bf16[1152,128]{1,0:T(8,128)(2,1)} %get-tuple-element.20), channel_id=1, source_target_pairs={{12,4},{13,5},{14,6},{15,7},{28,20},{29,21},{30,22},{31,23}} | collective-permute-start | bytes 884744 | tf_op jit(solution)/shard_map/ppermute | solution.py:444
  96.6 13.7 %collective-permute-start.15 = (bf16[768,128]{1,0:T(8,128)(2,1)S(1)}, bf16[768,128]{1,0:T(8,128)(2,1)S(1)}, u32[]{:S(2)}, u32[]{:S(2)}) collective-permute-start(bf16[768,128]{1,0:T(8,128)(2,1)S(1)} %pad_maximum_fusion.6), channel_id=1, source_target_pairs={{0,4},{4,8},{1,5},{5,9},{2,6},{6,10},{3,7},{7,11},{16,20},{20,24},... | collective-permute-start | bytes 589832 | tf_op jit(solution)/shard_map/ppermute | solution.py:444
  101.8 8.5 %collective-permute-start.16 = (bf16[768,128]{1,0:T(8,128)(2,1)S(1)}, bf16[768,128]{1,0:T(8,128)(2,1)S(1)}, u32[]{:S(2)}, u32[]{:S(2)}) collective-permute-start(bf16[768,128]{1,0:T(8,128)(2,1)S(1)} %pad_maximum_fusion.7), channel_id=1, source_target_pairs={{0,8},{1,9},{2,10},{3,11},{16,24},{17,25},{18,26},{19,27}} | collective-permute-start | bytes 589832 | tf_op jit(solution)/shard_map/ppermute | solution.py:444
  114.0 1.5 collective-permute-start.17
  114.1 30.0 %collective-permute-start.1 = (f32[5,2048]{1,0:T(8,128)S(1)}, f32[5,2048]{1,0:T(8,128)S(1)}, u32[]{:S(2)}, u32[]{:S(2)}) collective-permute-start(f32[5,2048]{1,0:T(8,128)S(1)} %pad_maximum_fusion.11), channel_id=1, source_target_pairs={{0,1},{1,0},{2,3},{3,2},{4,5},{5,4},{6,7},{7,6},{8,9},{9,8},{10,11... | collective-permute-start | bytes 122888 | tf_op jit(solution)/shard_map/ppermute | solution.py:543
  116.4 6.7 %collective-permute-start.18 = (f32[3,40,384]{2,1,0:T(8,128)S(1)}, f32[3,40,384]{2,1,0:T(8,128)S(1)}, u32[]{:S(2)}, u32[]{:S(2)}) collective-permute-start(f32[3,40,384]{2,1,0:T(8,128)S(1)} %dynamic-slice_add_fusion), channel_id=1, source_target_pairs={{0,2},{2,0},{1,3},{3,1},{4,6},{6,4},{5,7},{7,5},{8,10},{10,8},{9,1... | collective-permute-start | bytes 552968 | tf_op jit(solution)/shard_map/ppermute | solution.py:607
  123.2 20.9 %collective-permute-start.20 = (f32[2,40,384]{2,1,0:T(8,128)S(1)}, f32[2,40,384]{2,1,0:T(8,128)S(1)}, u32[]{:S(2)}, u32[]{:S(2)}) collective-permute-start(f32[2,40,384]{2,1,0:T(8,128)S(1)} %get-tuple-element.85), channel_id=1, source_target_pairs={{0,8},{4,12},{1,9},{5,13},{2,10},{6,14},{3,11},{7,15},{16,24},{20,... | collective-permute-start | bytes 368648 | tf_op jit(solution)/shard_map/ppermute | solution.py:610
  135.5 10.9 %collective-permute-start.19 = (f32[2,40,384]{2,1,0:T(8,128)S(1)}, f32[2,40,384]{2,1,0:T(8,128)S(1)}, u32[]{:S(2)}, u32[]{:S(2)}) collective-permute-start(f32[2,40,384]{2,1,0:T(8,128)S(1)} %get-tuple-element.84), channel_id=1, source_target_pairs={{0,4},{4,8},{8,12},{1,5},{5,9},{9,13},{2,6},{6,10},{10,14},{3,7},{... | collective-permute-start | bytes 368648 | tf_op jit(solution)/shard_map/ppermute | solution.py:609
  146.5 1.4 collective-permute-start.21
  147.2 4.5 %collective-permute-start.2 = (f32[5,8,512]{2,1,0:T(8,128)S(1)}, f32[5,8,512]{2,1,0:T(8,128)S(1)}, u32[]{:S(2)}, u32[]{:S(2)}) collective-permute-start(f32[5,8,512]{2,1,0:T(8,128)S(1)} %maximum_select_fusion.3), channel_id=1, source_target_pairs={{0,2},{2,0},{1,3},{3,1},{4,6},{6,4},{5,7},{7,5},{8,10},{10,8},{9,1... | collective-permute-start | bytes 245768 | tf_op jit(solution)/shard_map/ppermute | solution.py:551
  148.0 4.8 %collective-permute-start.22 = (f32[2,40,384]{2,1,0:T(8,128)S(1)}, f32[2,40,384]{2,1,0:T(8,128)S(1)}, u32[]{:S(2)}, u32[]{:S(2)}) collective-permute-start(f32[2,40,384]{2,1,0:T(8,128)S(1)} %pad_maximum_fusion.10), channel_id=1, source_target_pairs={{0,1},{1,0},{2,3},{3,2},{4,5},{5,4},{6,7},{7,6},{8,9},{9,8},{10,11... | collective-permute-start | bytes 368648 | tf_op jit(solution)/shard_map/ppermute | solution.py:615
  (23 other events, 70.8 us)

commit v2 on v0

--- a/solution.py
+++ b/solution.py
@@ -1,8 +1,12 @@
+import functools
 import math
 
 import jax
 import jax.numpy as jnp
+import numpy as np
 from jax import lax
+from jax.experimental import pallas as pl
+from jax.experimental.pallas import tpu as pltpu
 from jax.sharding import PartitionSpec as P
 
 HEADS = 40
@@ -94,7 +98,7 @@
     return result
 
 
-def per_device(
+def gathered_plan(
     queries,
     keys,
     values,
@@ -207,6 +211,626 @@
     return (clean_latent, decoded)
 
 
+NEAR_HEADS = 4
+MIDDLE_HEADS = 4
+FAR_HEADS = 2
+MIDDLE = NEAR_HEADS
+FAR = NEAR_HEADS + MIDDLE_HEADS
+EARLY = 3
+LATE = NEAR_HEADS - EARLY
+STAT_ROWS = 8
+SLOTS = 3
+QUERY_ROWS = 192
+SWAP = [(0, 1), (1, 0)]
+WINDOW = 32
+
+OWN, OTHER, DOWN, UP, MAIN, PLACE, SLAB = range(7)
+
+
+def plan_fits(heads_dev, span_count, slab_count, head_count):
+    return (
+        span_count == 4
+        and slab_count == 2
+        and head_count == 2
+        and heads_dev == slab_count * (NEAR_HEADS + MIDDLE_HEADS + FAR_HEADS)
+    )
+
+
+def scalar_operand(heads):
+    by_place = np.array(
+        [
+            [0, heads, MIDDLE, 0, MIDDLE, 0, 0, 0],
+            [0, heads, MIDDLE, MIDDLE, 0, 1, 0, 0],
+            [0, heads, 0, 0, MIDDLE, 2, 0, 0],
+            [0, heads, MIDDLE, 0, 0, 3, 0, 0],
+        ],
+        np.int32,
+    )
+    by_slab = np.array([heads, -heads, 0, 0, 0, 0, 1, 0], np.int32)
+    row = lax.dynamic_slice_in_dim(jnp.array(by_place), lax.axis_index("span"), 1, 0)[0]
+    return row + lax.axis_index("slab") * jnp.array(by_slab)
+
+
+def pack_kernel(copies, scalars, *refs):
+    ins, outs, semaphores = refs[: copies[0]], refs[copies[0] : -1], refs[-1]
+    started = []
+    for number, (source, row, rows, entries, shift, target, at, heads) in enumerate(copies[1]):
+        head = shift
+        for entry in entries:
+            head = head + scalars[entry]
+        column = pl.multiple_of(head * HD, HD)
+        copy = pltpu.make_async_copy(
+            ins[source].at[pl.ds(row, rows), pl.ds(column, heads * HD)],
+            outs[target].at[pl.ds(at, rows), :],
+            semaphores.at[number],
+        )
+        copy.start()
+        started.append(copy)
+    for copy in started:
+        copy.wait()
+
+
+def pack(scalars, arrays, shapes, copies, name):
+    moved = sum(2 * 2 * rows * heads * HD for _, _, rows, _, _, _, _, heads in copies)
+    return pl.pallas_call(
+        functools.partial(pack_kernel, (len(arrays), copies)),
+        name=name,
+        out_shape=[jax.ShapeDtypeStruct(shape, jnp.bfloat16) for shape in shapes],
+        grid_spec=pltpu.PrefetchScalarGridSpec(
+            num_scalar_prefetch=1,
+            grid=(1,),
+            in_specs=[pl.BlockSpec(memory_space=pl.ANY)] * len(arrays),
+            out_specs=[pl.BlockSpec(memory_space=pl.ANY)] * len(shapes),
+            scratch_shapes=[pltpu.SemaphoreType.DMA((len(copies),))],
+        ),
+        cost_estimate=pl.CostEstimate(flops=0, bytes_accessed=moved, transcendentals=0),
+    )(scalars, *arrays)
+
+
+def pack_messages(scalars, queries, keys, values, received, messages, name):
+    rows = queries.shape[0]
+    half = rows // 2
+    copies, shapes = [], []
+    for target, (entry, shift, heads, whole) in enumerate(messages):
+        entries = () if entry is None else (entry,)
+        at = 0
+        if whole:
+            copies.append((0, 0, rows, (OWN,) + entries, shift, target, 0, heads))
+            at = rows
+        for part, array in enumerate((1, 2)):
+            copies.append((array, 0, half, (OWN,) + entries, shift, target, at, heads))
+            copies.append((3, part * half, half, entries, shift, target, at + half, heads))
+            at += rows
+        shapes.append((at, heads * HD))
+    return pack(scalars, (queries, keys, values, received), shapes, copies, name)
+
+
+def attend_kernel(variants, extra, span_count, scalars, mask, *refs):
+    query_own, key_own, value_own, received, weight, gain, sums_in = refs[:7]
+    more = refs[7 : 7 + extra]
+    payloads, (sums_out, folded, squares) = refs[7 + extra : -3], refs[-3:]
+    rows = query_own.shape[0]
+    half = rows // 2
+    step = pl.program_id(0)
+    to_exp2 = math.log2(math.e) / math.sqrt(HD)
+
+    @pl.when(step == 0)
+    def _():
+        folded[...] = jnp.zeros_like(folded)
+        squares[...] = jnp.zeros_like(squares)
+
+    def query_of(source):
+        if source is None:
+            return query_own[...]
+        if source[0] < 0:
+            return more[0][:, source[1] * HD : (source[1] + 1) * HD]
+        return payloads[source[0]][:rows]
+
+    def pair_of(source):
+        if source is None:
+            parts = (key_own[...], received[:half], value_own[...], received[half:])
+        elif source[0] < 0:
+            lanes = slice(source[1] * HD, (source[1] + 1) * HD)
+            parts = (more[1][:, lanes], more[3][:half, lanes], more[2][:, lanes], more[3][half:, lanes])
+        else:
+            payload = payloads[source[0]]
+            start = payload.shape[0] - 2 * rows
+            return payload[start : start + rows], payload[start + rows :]
+        return jnp.concatenate(parts[:2], axis=0), jnp.concatenate(parts[2:], axis=0)
+
+    def projector(extra_head):
+        if extra_head is None:
+            scaled = weight[...].astype(jnp.float32) * gain[...]
+        else:
+            lanes = slice(extra_head * HD, (extra_head + 1) * HD)
+            scaled = more[4][:, lanes].astype(jnp.float32) * more[5][:, lanes]
+        high = scaled.astype(jnp.bfloat16)
+        low = (scaled - high.astype(jnp.float32)).astype(jnp.bfloat16)
+        return jnp.concatenate([high, low, jnp.ones((16, HD), jnp.bfloat16)], axis=0)
+
+    def one_query(source, slot, query_span, key_sources):
+        query = query_of(source)
+        pairs = [pair_of(key_source) for key_source, _ in key_sources]
+        open_to = [
+            None if key_span == query_span else mask[query_span * span_count + key_span] > 0
+            for _, key_span in key_sources
+        ]
+        keys_in = jnp.concatenate([pair[0] for pair in pairs], axis=0)
+        ones_block = jnp.ones((rows, HD), jnp.bfloat16)
+        values_in = jnp.concatenate(
+            [jnp.concatenate([pair[1], ones_block], axis=1) for pair in pairs], axis=0
+        )
+        pieces = []
+        for row in range(0, rows, QUERY_ROWS):
+            score = lax.dot_general(
+                query[row : row + QUERY_ROWS],
+                keys_in,
+                (((1,), (1,)), ((), ())),
+                preferred_element_type=jnp.float32,
+            )
+            best = None
+            for number, is_open in enumerate(open_to):
+                start = number * rows
+                block = score[:, start : start + HD]
+                for lane in range(HD, rows, HD):
+                    block = jnp.maximum(block, score[:, start + lane : start + lane + HD])
+                if is_open is not None:
+                    block = jnp.where(is_open, block, neg_big)
+                best = block if best is None else jnp.maximum(best, block)
+            top = jnp.max(best, axis=1, keepdims=True)
+            weights = []
+            for number, is_open in enumerate(open_to):
+                start = number * rows
+                shift = top if is_open is None else jnp.where(is_open, top, -neg_big)
+                weights.append(
+                    jnp.exp2((score[:, start : start + rows] - shift) * to_exp2).astype(jnp.bfloat16)
+                )
+            both = jnp.dot(
+                jnp.concatenate(weights, axis=1), values_in, preferred_element_type=jnp.float32
+            )
+            pieces.append((both[:, :HD] / both[:, HD:]).astype(jnp.bfloat16))
+        attended = jnp.concatenate(pieces, axis=0)
+        extra_head = source[1] if source is not None and source[0] < 0 else None
+        folded[slot] += lax.dot_general(
+            projector(extra_head),
+            attended,
+            (((1,), (1,)), ((), ())),
+            preferred_element_type=jnp.float32,
+        )
+        wide = attended.astype(jnp.float32)
+        squares[slot] += wide * wide
+
+    for place, tasks in variants.items():
+
+        @pl.when(scalars[PLACE] == place)
+        def _():
+            for task in tasks:
+                one_query(*task)
+
+    @pl.when(step == pl.num_programs(0) - 1)
+    def _():
+        ones_rows = jnp.ones((STAT_ROWS, HD), jnp.bfloat16)
+        patch = weight.shape[0]
+        for slot in range(SLOTS):
+            left = squares[slot]
+            total = jnp.zeros((STAT_ROWS, rows), jnp.float32)
+            for _ in range(3):
+                piece = left.astype(jnp.bfloat16)
+                left = left - piece.astype(jnp.float32)
+                total = total + lax.dot_general(
+                    ones_rows, piece, (((1,), (1,)), ((), ())), preferred_element_type=jnp.float32
+                )
+            done = folded[slot]
+            sums_out[slot] = sums_in[slot] + jnp.concatenate(
+                [
+                    done[:patch] + done[patch : 2 * patch],
+                    done[2 * patch : 2 * patch + STAT_ROWS],
+                    total,
+                ],
+                axis=0,
+            )
+
+
+def attend(steps, entries, first, own, scalars, mask, sums, payloads, variants, more, name):
+    queries, keys, values, received, weight, gain = own
+    rows = queries.shape[0]
+    half = rows // 2
+    patch = weight.shape[0]
+
+    def column(height, own_column):
+        def index(i, scalars, mask):
+            head = first + i + (scalars[OWN] if own_column else 0)
+            for entry in entries:
+                head = head + scalars[entry]
+            return (0, head)
+
+        return pl.BlockSpec((height, HD), index)
+
+    def two_columns(height, own_column):
+        return pl.BlockSpec(
+            (height, 2 * HD),
+            lambda i, scalars, mask: (0, i + (scalars[OWN] // 2 if own_column else 0)),
+        )
+
+    sums_spec = pl.BlockSpec(sums.shape, lambda i, scalars, mask: (0, 0, 0))
+    in_specs = [
+        column(rows, True),
+        column(half, True),
+        column(half, True),
+        column(rows, False),
+        column(patch, True),
+        column(1, True),
+        sums_spec,
+    ]
+    arrays = [queries, keys, values, received, weight, gain, sums]
+    extra = 0
+    if more:
+        extra = 6
+        in_specs += [
+            two_columns(rows, True),
+            two_columns(half, True),
+            two_columns(half, True),
+            two_columns(rows, False),
+            two_columns(patch, True),
+            two_columns(1, True),
+        ]
+        arrays += [queries, keys, values, received, weight, gain]
+    in_specs += [
+        pl.BlockSpec((payload.shape[0], HD), lambda i, scalars, mask: (0, i))
+        for payload in payloads
+    ]
+    arrays += payloads
+    pairs = steps * max(sum(len(task[3]) for task in tasks) for tasks in variants.values())
+    span_count = math.isqrt(mask.shape[0])
+    return pl.pallas_call(
+        functools.partial(attend_kernel, variants, extra, span_count),
+        name=name,
+        out_shape=jax.ShapeDtypeStruct(sums.shape, sums.dtype),
+        grid_spec=pltpu.PrefetchScalarGridSpec(
+            num_scalar_prefetch=2,
+            grid=(steps,),
+            in_specs=in_specs,
+            out_specs=sums_spec,
+            scratch_shapes=[
+                pltpu.VMEM((SLOTS, 2 * patch + 16, rows), jnp.float32),
+                pltpu.VMEM((SLOTS, rows, HD), jnp.float32),
+            ],
+        ),
+        compiler_params=pltpu.CompilerParams(vmem_limit_bytes=40 << 20),
+        cost_estimate=pl.CostEstimate(
+            flops=pairs * 4 * rows * rows * HD,
+            bytes_accessed=steps * HD * 2 * sum(spec.block_shape[0] for spec in in_specs[:4]),
+            transcendentals=pairs * rows * rows,
+        ),
+    )(scalars, mask, *arrays)
+
+
+def token_sums(scalars, queries, keys, values, span_mask, head_gain, patch_weight):
+    rows = queries.shape[0]
+    heads = NEAR_HEADS + MIDDLE_HEADS + FAR_HEADS
+    half = rows // 2
+    (handed,) = pack(
+        scalars,
+        (keys, values),
+        [(rows, heads * HD)],
+        [(0, 0, half, (OTHER,), 0, 0, 0, heads), (1, 0, half, (OTHER,), 0, 0, half, heads)],
+        "pack_handed",
+    )
+    received = lax.ppermute(handed, "slab", SWAP)
+    bring = functools.partial(pack_messages, scalars, queries, keys, values, received)
+    send = lambda value, *pairs: lax.ppermute(value, "span", list(pairs))
+
+    down, up = bring([(DOWN, 0, EARLY, True), (UP, 0, EARLY, False)], "pack_first")
+    anchor = down
+    down_two, up_two = bring(
+        [(None, 0, EARLY, True), (None, MIDDLE, EARLY, False)], "pack_second"
+    )
+    far_all, far_pair, late_down, late_down_two, late_up, late_up_two = bring(
+        [
+            (None, FAR, FAR_HEADS, True),
+            (None, FAR, FAR_HEADS, False),
+            (DOWN, EARLY, LATE, True),
+            (None, EARLY, LATE, True),
+            (UP, EARLY, LATE, False),
+            (None, MIDDLE + EARLY, LATE, False),
+        ],
+        "pack_third",
+    )
+    down = send(down, (1, 0), (2, 1), (3, 2))
+    up = send(up, (0, 1), (1, 2))
+    down_two = send(down_two, (3, 1))
+    up_two = send(up_two, (0, 2))
+    far_two = send(far_pair, (1, 3))
+    far_three = send(far_pair, (0, 3))
+    far_next = send(far_all, (2, 3), (1, 0))
+    late_down = send(late_down, (1, 0), (2, 1), (3, 2))
+    late_down_two = send(late_down_two, (3, 1))
+    late_up = send(late_up, (0, 1), (1, 2))
+    late_up_two = send(late_up_two, (0, 2))
+
+    mask = span_mask.reshape(-1)
+    weight = patch_weight.T
+    own = (queries, keys, values, received, weight, head_gain[None, :])
+    sums = jnp.zeros((SLOTS, weight.shape[0] + 2 * STAT_ROWS, rows), jnp.float32)
+    on_one, on_two, back_one, back_two = (0, 0), (1, 0), (2, 0), (3, 0)
+    main = {
+        0: [(None, 0, 0, [(None, 0)]), (on_one, 1, 1, [(None, 0), (on_one, 1)])],
+        1: [
+            (on_two, 2, 3, [(back_one, 0), (None, 1), (on_one, 2), (on_two, 3)]),
+            (on_one, 1, 2, [(back_one, 0), (None, 1), (on_one, 2)]),
+            (None, 0, 1, [(back_one, 0), (None, 1)]),
+        ],
+        2: [
+            (on_one, 1, 3, [(back_two, 0), (back_one, 1), (None, 2), (on_one, 3)]),
+            (None, 0, 2, [(back_two, 0), (back_one, 1), (None, 2)]),
+        ],
+    }
+    extra = [((-1, lane), 0, 0, [((-1, lane), 0)]) for lane in range(2)]
+    far = {
+        0: [(None, 0, 0, [(None, 0)]), ((0, 0), 1, 1, [(None, 0), ((0, 0), 1)])] + extra,
+        3: [
+            (None, 0, 3, [((2, 0), 0), ((1, 0), 1), ((0, 0), 2), (None, 3)]),
+            ((0, 0), 2, 2, [((2, 0), 0), ((1, 0), 1), ((0, 0), 2)]),
+        ],
+    }
+    run = functools.partial(attend, own=own, scalars=scalars, mask=mask)
+    sums = run(
+        FAR_HEADS,
+        (),
+        FAR,
+        sums=sums,
+        payloads=[far_next, far_two, far_three],
+        variants=far,
+        more=True,
+        name="far_heads",
+    )
+    sums = run(
+        EARLY,
+        (MAIN,),
+        0,
+        sums=sums,
+        payloads=[down, down_two, up, up_two],
+        variants=main,
+        more=False,
+        name="early_heads",
+    )
+    sums = run(
+        LATE,
+        (MAIN,),
+        EARLY,
+        sums=sums,
+        payloads=[late_down, late_down_two, late_up, late_up_two],
+        variants=main,
+        more=False,
+        name="late_heads",
+    )
+    return sums, anchor
+
+
+def noise_window(noisy_latent):
+    frames, height, breadth, channels = noisy_latent.shape
+    own = noisy_latent.transpose(1, 2, 0, 3).reshape(height, breadth, frames * channels)
+    earlier = from_behind(own[:, :, (frames - 2) * channels :], "span", 1)
+    grid = jnp.concatenate([earlier, own], axis=2)
+    slab = lax.axis_index("slab")
+    edge = jnp.where(slab == 0, grid[:, breadth - 1], grid[:, 0])
+    edge = lax.ppermute(edge, "slab", SWAP)[:, None]
+    grid = jnp.concatenate(
+        [
+            jnp.where(slab == 1, edge, 0.0),
+            grid,
+            jnp.where(slab == 0, edge, 0.0),
+            jnp.zeros((height, WINDOW - breadth - 2, grid.shape[2]), grid.dtype),
+        ],
+        axis=1,
+    )
+    head = lax.axis_index("head")
+    edge = jnp.where(head == 0, grid[height - 1], grid[0])
+    edge = lax.ppermute(edge, "head", SWAP)[None]
+    grid = jnp.concatenate(
+        [jnp.where(head == 1, edge, 0.0), grid, jnp.where(head == 0, edge, 0.0)], axis=0
+    )
+    return grid.reshape((height + 2) * WINDOW, grid.shape[2])
+
+
+def cell_selector(height, breadth):
+    cell = lax.broadcasted_iota(jnp.int32, ((height + 2) * WINDOW, 4 * TROWS * TCOLS), 0)
+    column = lax.broadcasted_iota(jnp.int32, cell.shape, 1)
+    y = lax.axis_index("head") * height + cell // WINDOW - 1
+    x = lax.axis_index("slab") * breadth + cell % WINDOW - 1
+    inside = (y >= 0) & (y < 2 * TROWS) & (x >= 0) & (x < 2 * TCOLS)
+    inside = inside & (cell % WINDOW < breadth + 2)
+    target = ((y % 2) * 2 + x % 2) * (TROWS * TCOLS) + (y // 2) * TCOLS + x // 2
+    return (inside & (column == target)).astype(jnp.bfloat16)
+
+
+def banded_weight(conv_weight):
+    channels = conv_weight.shape[1]
+    taps = conv_weight.reshape(3, 3, 3, LAT_CH, channels)
+    banded = jnp.stack(
+        [
+            jnp.pad(taps, ((n, FRAMES_SPAN - 1 - n), (0, 0), (0, 0), (0, 0), (0, 0)))
+            for n in range(FRAMES_SPAN)
+        ],
+        axis=4,
+    )
+    return banded.transpose(1, 2, 0, 3, 4, 5).reshape(
+        3, 3 * (FRAMES_SPAN + 2) * LAT_CH, FRAMES_SPAN * channels
+    )
+
+
+def finish_kernel(
+    scalars, mine, other, noise, selector, band, bias, constants, clean, decoded, cells
+):
+    frames, height, breadth, channels = clean.shape
+    patch = constants.shape[0]
+    first = scalars[SLAB] == 0
+    sums = jnp.concatenate(
+        [jnp.where(first, mine[...], other[...]), jnp.where(first, other[...], mine[...])], axis=0
+    )
+    feature_width = HEADS * HD
+    row_mean = sums[patch : patch + 1] / feature_width
+    spread = sums[patch + STAT_ROWS : patch + STAT_ROWS + 1] / feature_width - row_mean * row_mean
+    velocity = (
+        lax.rsqrt(spread + norm_eps) * (sums[:patch] - constants[:, 0:1] * row_mean)
+        + constants[:, 1:2]
+    )
+    tokens = TROWS * TCOLS
+    lane = lax.broadcasted_iota(jnp.int32, velocity.shape, 1)
+    velocity = jnp.where((lane >= 2 * tokens) | (scalars[PLACE] > 0), velocity, 0.0)
+    columns = jnp.concatenate(
+        [
+            jnp.concatenate(
+                [
+                    velocity[
+                        part * channels : (part + 1) * channels,
+                        frame * tokens : (frame + 1) * tokens,
+                    ]
+                    for part in range(4)
+                ],
+                axis=1,
+            )
+            for frame in range(frames + 2)
+        ],
+        axis=0,
+    )
+    high = columns.astype(jnp.bfloat16)
+    low = (columns - high.astype(jnp.float32)).astype(jnp.bfloat16)
+    chosen = sum(
+        lax.dot_general(
+            selector[...], part, (((1,), (1,)), ((), ())), preferred_element_type=jnp.float32
+        )
+        for part in (high, low)
+    )
+    count = (height + 2) * WINDOW
+    cells[:count] = noise[...] - noise_level * chosen
+    cells[count:] = jnp.zeros_like(cells[count:])
+    for frame in range(frames):
+        lanes = slice((frame + 2) * channels, (frame + 3) * channels)
+        for y in range(height):
+            start = (y + 1) * WINDOW + 1
+            clean[frame, y] = cells[start : start + breadth, lanes]
+    shifted = jnp.concatenate(
+        [cells[tap : tap + count] for tap in range(3)], axis=1
+    ).astype(jnp.bfloat16)
+    total = jnp.broadcast_to(bias[...], (height * breadth, bias.shape[1]))
+    for tap in range(3):
+        block = jnp.concatenate(
+            [
+                shifted[(y + tap) * WINDOW : (y + tap) * WINDOW + breadth]
+                for y in range(height)
+            ],
+            axis=0,
+        )
+        total = total + jnp.dot(block, band[tap], preferred_element_type=jnp.float32)
+    outputs = decoded.shape[3]
+    total = total.astype(decoded.dtype)
+    for frame in range(frames):
+        decoded[frame] = total[:, frame * outputs : (frame + 1) * outputs].reshape(
+            height, breadth, outputs
+        )
+
+
+def finish(scalars, mine, other, noise, selector, band, bias, constants, shape, outputs):
+    whole = pl.BlockSpec(memory_space=pltpu.VMEM)
+    frames, height, breadth, channels = shape
+    rows = (height + 2) * WINDOW
+    return pl.pallas_call(
+        finish_kernel,
+        name="finish",
+        out_shape=(
+            jax.ShapeDtypeStruct(shape, jnp.float32),
+            jax.ShapeDtypeStruct((frames, height, breadth, outputs), jnp.bfloat16),
+        ),
+        in_specs=[pl.BlockSpec(memory_space=pltpu.SMEM)] + [whole] * 7,
+        out_specs=(whole, whole),
+        scratch_shapes=[pltpu.VMEM((rows + 8, (frames + 2) * channels), jnp.float32)],
+        compiler_params=pltpu.CompilerParams(vmem_limit_bytes=32 << 20),
+    )(scalars, mine, other, noise, selector, band, bias, constants)
+
+
+def per_device(
+    queries,
+    keys,
+    values,
+    span_mask,
+    head_gain,
+    head_shift,
+    patch_weight,
+    noisy_latent,
+    conv_weight,
+    conv_bias,
+):
+    heads_dev = queries.shape[1] // HD
+    if not plan_fits(
+        heads_dev, lax.axis_size("span"), lax.axis_size("slab"), lax.axis_size("head")
+    ):
+        return gathered_plan(
+            queries,
+            keys,
+            values,
+            span_mask,
+            head_gain,
+            head_shift,
+            patch_weight,
+            noisy_latent,
+            conv_weight,
+            conv_bias,
+        )
+    place = lax.axis_index("span")
+    slab = lax.axis_index("slab")
+    scalars = scalar_operand(heads_dev // lax.axis_size("slab"))
+    sums, anchor = token_sums(
+        scalars, queries, keys, values, span_mask, head_gain, patch_weight
+    )
+
+    noisy, weight, gain, shift, taps, bias, _ = lax.optimization_barrier(
+        (noisy_latent, patch_weight, head_gain, head_shift, conv_weight, conv_bias, anchor)
+    )
+    _, height, breadth, _ = noisy.shape
+    noise = noise_window(noisy)
+    wide_weight = weight.T.astype(jnp.float32)
+    constants = jnp.stack(
+        [
+            jnp.sum(wide_weight * gain[None, :], axis=1),
+            jnp.sum(wide_weight * shift[None, :], axis=1),
+        ],
+        axis=1,
+    )
+    constants = constants + lax.ppermute(constants, "head", SWAP)
+    selector = cell_selector(height, breadth)
+    band = banded_weight(taps)
+    bias = jnp.tile(bias, FRAMES_SPAN)[None, :]
+
+    half = sums.shape[1] // 2
+    mine = lax.dynamic_slice_in_dim(sums, slab * half, half, 1)
+    theirs = lax.dynamic_slice_in_dim(sums, (1 - slab) * half, half, 1)
+    mine = mine + lax.ppermute(theirs, "slab", SWAP)
+    own, after, third = mine[0], mine[1], mine[2]
+    skip = TROWS * TCOLS
+    from_one = lax.ppermute(
+        jnp.concatenate([own[:, skip:], after], axis=1), "span", [(0, 1), (1, 2), (2, 3)]
+    )
+    to_current = lax.ppermute(third, "span", [(1, 3), (3, 2)])
+    to_before = lax.ppermute(after[:, skip:], "span", [(0, 2), (1, 3)])
+    kept = jnp.concatenate([jnp.where(place == 3, third[:, skip:], 0.0), own], axis=1)
+    total = kept + from_one + jnp.concatenate([to_before, to_current], axis=1)
+    total = total + lax.ppermute(total, "head", SWAP)
+    other = lax.ppermute(total, "slab", SWAP)
+    return finish(
+        scalars,
+        total,
+        other,
+        noise,
+        selector,
+        band,
+        bias,
+        constants,
+        noisy_latent.shape,
+        conv_weight.shape[1],
+    )
+
+
 def solution(mesh):
     placed = (
         P(("groups", "span"), "head"),

time: 288 us -> 292 us (1.014)
  Pallas kernels: 0 us -> 207 us
  waiting for transfers between devices: 162 us -> 20.4 us
  starting transfers between devices: 7.64 us -> 44.7 us
  local copies, waits for them, and re-layouts: 51.2 us -> 14.2 us
  matrix products: 24.5 us -> 0 us
  between operations: 14.9 us -> 1.15 us
  blocking collectives: 13.3 us -> 0 us
  other arithmetic: 11.5 us -> 3.5 us
    pallas_call x0 -> x8, Pallas kernels: none -> 207 us  [the longest x4 186 us: pack(): pl.pallas_call(functools.partial(pack_kernel, (len(arrays), copies)), nam...]
    all_gather x2 -> x0, waiting for transfers between devices: 154 us -> none  [the longest x1 78 us: per_device(): lax.all_gather(values, ('span', 'slab'), axis=0, tiled=True)]
    dynamic_slice x10 -> x1, local copies, waits for them, and re-layouts: 42 us -> 0.04 us  [per_device(): theirs = lax.dynamic_slice_in_dim(sums, (1 - slab) * half, half, 1)]
    ppermute x4 -> x21, starting transfers between devices: 6.27 us -> 40.2 us  [the longest x11 29.3 us: token_sums(): send = lambda value, *pairs: lax.ppermute(value, 'span', list(pairs))]
    dot_general x6 -> x0, matrix products: 24.5 us -> none  [the longest x2 11.2 us: one_block(): jnp.einsum('hqk,khd->qhd', weights.astype(jnp.bfloat16), value_block, pre...]
    ppermute x4 -> x21, waiting for transfers between devices: 5.34 us -> 20.4 us  [the longest x11 11.2 us: token_sums(): send = lambda value, *pairs: lax.ppermute(value, 'span', list(pairs))]
    reduce_sum x5 -> x1, other arithmetic: 9.62 us -> 0.23 us  [per_device(): jnp.sum(wide_weight * gain[None, :], axis=1)]
    unnamed x1 -> x0, blocking collectives: 8.32 us -> none
  transfers between devices with their start and end apart: 7 -> 22, of which waited for: 6 -> 7; matrix products, arithmetic and copies ran while one was open for 2% -> 4% of each run, Pallas kernels for 0% -> 38%
where the time goes in v2:
time: 292 us; the launch traced here: 291 us
  Pallas kernels  207 us (71%)
  starting transfers between devices  44.7 us (15%)
  waiting for transfers between devices  20.4 us (7%)
  local copies, waits for them, and re-layouts  14.2 us (5%)
  other arithmetic  3.5 us (1%)
    pallas_call x4, Pallas kernels, pack(): pl.pallas_call(functools.partial(pack_kernel, (len(arrays), copies)), nam...  186 us
    ppermute x11, starting transfers between devices, token_sums(): send = lambda value, *pairs: lax.ppermute(value, 'span', list(pairs))  29.3 us
    pallas_call x3, Pallas kernels, attend(): pl.pallas_call(functools.partial(attend_kernel, variants, extra, span_cou...  17.9 us
    ppermute x11, waiting for transfers between devices, token_sums(): send = lambda value, *pairs: lax.ppermute(value, 'span', list(pairs))  11.2 us
  transfers between devices with their start and end apart: 22, of which 7 were waited for; matrix products, arithmetic and copies ran while one was open for 4% of the time, Pallas kernels for 38%

profile of v2, /device:TPU:0, one launch (start us, length us, event | category | flops | bytes accessed | tf_op | source)
XLA Modules:
  0.0 290.5 jit_solution(2909756844727777863)
XLA Ops:
  0.7 1.3 fusion.42.scalars
  1.9 31.6 %pack_handed.1 = bf16[384,1280]{1,0:T(8,128)(2,1)} custom-call(s32[8]{0:T(128)} %fusion.42.scalars, bf16[192,2560]{1,0:T(8,128)(2,1)} %refs_1_.13, bf16[192,2560]{1,0:T(8,128)(2,1)} %refs_2_.11), custom_call_target="tpu_custom_call" | custom-call | bytes 1966080 | tf_op jit(solution)/shard_map/pack_handed/pallas_call | solution.py:275
  34.1 2.4 collective-permute-done.refs_3_.refs_10_
  37.4 61.6 %pack_third.1 = (bf16[1152,256]{1,0:T(8,128)(2,1)}, bf16[768,256]{1,0:T(8,128)(2,1)}, bf16[1152,128]{1,0:T(8,128)(2,1)}, bf16[1152,128]{1,0:T(8,128)(2,1)}, bf16...) custom-call(s32[8]{0:T(128)} %fusion.42.scalars, bf16[384,2560]{1,0:T(8,128)(2,1)} %refs_0_.13, ...), custom_call_target="tpu_custom_call" | custom-call | bytes 3932160 | tf_op jit(solution)/shard_map/pack_third/pallas_call | solution.py:275
  99.7 1.4 fusion.30.selector
  101.1 7.6 %collective-permute-start.3 = (bf16[768,256]{1,0:T(8,128)(2,1)}, bf16[768,256]{1,0:T(8,128)(2,1)S(1)}, u32[]{:S(2)}, u32[]{:S(2)}) collective-permute-start(bf16[768,256]{1,0:T(8,128)(2,1)} %get-tuple-element.19), channel_id=1, source_target_pairs={{0,12},{1,13},{2,14},{3,15},{16,28},{17,29},{18,30},{19,31}} | collective-permute-start | bytes 1179656 | tf_op jit(solution)/shard_map/ppermute | solution.py:521
  108.8 46.5 %pack_first.1 = (bf16[1152,384]{1,0:T(8,128)(2,1)}, bf16[768,384]{1,0:T(8,128)(2,1)}) custom-call(s32[8]{0:T(128)} %fusion.42.scalars, bf16[384,2560]{1,0:T(8,128)(2,1)} %refs_0_.13, bf16[192,2560]{1,0:T(8,128)(2,1)} %refs_1_.13, bf16[192,2560]{1,0:T(8,128)(2,1)} %refs_2_.11, bf16[384,1280]{1,0:T(8,128)(2,1)} %copy-done.4), custom_call_target="tpu_custom_call" | custom-call | bytes 2949120 | tf_op jit(solution)/shard_map/pack_first/pallas_call | solution.py:275
  155.3 1.3 collective-permute-start.4
  157.0 4.5 %collective-permute-start.18 = (f32[8,16,32]{2,1,0:T(8,128)S(1)}, f32[8,16,32]{2,1,0:T(8,128)S(1)}, u32[]{:S(2)}, u32[]{:S(2)}) collective-permute-start(f32[8,16,32]{2,1,0:T(8,128)S(1)} %slice.50), channel_id=1, source_target_pairs={{0,4},{4,8},{8,12},{1,5},{5,9},{9,13},{2,6},{6,10},{10,14},{3,7},{... | collective-permute-start | bytes 49160 | tf_op jit(solution)/shard_map/ppermute | solution.py:45
  161.9 1.5 collective-permute-start.21
  163.5 46.6 %pack_second.1 = (bf16[1152,384]{1,0:T(8,128)(2,1)}, bf16[768,384]{1,0:T(8,128)(2,1)}) custom-call(s32[8]{0:T(128)} %fusion.42.scalars, bf16[384,2560]{1,0:T(8,128)(2,1)} %refs_0_.13, bf16[192,2560]{1,0:T(8,128)(2,1)} %refs_1_.13, bf16[192,2560]{1,0:T(8,128)(2,1)} %refs_2_.11, bf16[384,1280]{1,0:T(8,128)(2,1)} %copy-done.4), custom_call_target="tpu_custom_call" | custom-call | bytes 2949120 | tf_op jit(solution)/shard_map/pack_second/pallas_call | solution.py:275
  210.1 1.3 collective-permute-start.1
  211.5 1.6 collective-permute-start.5
  213.1 5.9 %collective-permute-start.6 = (bf16[768,384]{1,0:T(8,128)(2,1)}, bf16[768,384]{1,0:T(8,128)(2,1)}, u32[]{:S(2)}, u32[]{:S(2)}) collective-permute-start(bf16[768,384]{1,0:T(8,128)(2,1)} %get-tuple-element.22), channel_id=1, source_target_pairs={{0,4},{4,8},{1,5},{5,9},{2,6},{6,10},{3,7},{7,11},{16,20},{20,24},... | collective-permute-start | bytes 1769480 | tf_op jit(solution)/shard_map/ppermute | solution.py:521
  219.1 2.1 collective-permute-start.7
  221.5 2.5 copy.32
  224.0 5.4 %reshape.34.band = bf16[3,240,1152]{2,1,0:T(8,128)(2,1)} reshape(bf16[3,3,5,16,3,384]{5,4,3,2,1,0:T(4,128)(2,1)} %copy.32) | data formatting | bytes 3317760 | tf_op jit(solution)/shard_map/reshape | solution.py:657
  229.6 1.3 collective-permute-start.8
  230.9 1.4 collective-permute-done.6.refs_9_
  232.9 9.8 %collective-permute-done.7.refs_10_ = bf16[768,384]{1,0:T(8,128)(2,1)} collective-permute-done((bf16[768,384]{1,0:T(8,128)(2,1)}, bf16[768,384]{1,0:T(8,128)(2,1)}, u32[]{:S(2)}, u32[]{:S(2)}) %collective-permute-start.7) | collective-permute-done | bytes 589856 | tf_op jit(solution)/shard_map/ppermute | solution.py:521
  242.7 1.3 collective-permute-start.10
  244.0 5.5 %collective-permute-start.11 = (bf16[768,128]{1,0:T(8,128)(2,1)}, bf16[768,128]{1,0:T(8,128)(2,1)S(1)}, u32[]{:S(2)}, u32[]{:S(2)}) collective-permute-start(bf16[768,128]{1,0:T(8,128)(2,1)} %get-tuple-element.27), channel_id=1, source_target_pairs={{0,8},{1,9},{2,10},{3,11},{16,24},{17,25},{18,26},{19,27}} | collective-permute-start | bytes 589832 | tf_op jit(solution)/shard_map/ppermute | solution.py:521
  249.6 1.2 copy-done.3
  250.8 1.2 copy-done.5
  254.0 8.0 %far_heads.1.refs_6_ = f32[3,80,384]{2,1,0:T(8,128)S(1)} custom-call(s32[8]{0:T(128)S(1)} %copy-done.13, s32[16]{0:T(128)S(1)} %reshape.30.mask, bf16[384,2560]{1,0:T(8,128)(2,1)S(1)} %copy-done.1, bf16[192,2560]{1,0:T(8,128)(2,1)S(1)} %copy-done.2, bf16[192,2560]{1,0:T(8,128)(2,1)S(1)} %copy-done.3, bf16[384,1280]{1,0:T(8,128)(2,1)S(1)} %copy-done.5, ...), custom_call_target="tpu_custom_call" | custom-call | flops 1056964608 | bytes 589824 | tf_op jit(solution)/shard_map/far_heads/pallas_call | solution.py:485
  262.1 7.0 %early_heads.1.refs_6_ = f32[3,80,384]{2,1,0:T(8,128)S(1)} custom-call(s32[8]{0:T(128)S(1)} %copy-done.13, s32[16]{0:T(128)S(1)} %reshape.30.mask, bf16[384,2560]{1,0:T(8,128)(2,1)S(1)} %copy-done.1, bf16[192,2560]{1,0:T(8,128)(2,1)S(1)} %copy-done.2, bf16[192,2560]{1,0:T(8,128)(2,1)S(1)} %copy-done.3, bf16[384,1280]{1,0:T(8,128)(2,1)S(1)} %copy-done.5, ...), custom_call_target="tpu_custom_call" | custom-call | flops 2038431744 | bytes 884736 | tf_op jit(solution)/shard_map/early_heads/pallas_call | solution.py:485
  269.2 2.8 late_heads.1
  273.7 4.5 %collective-permute-start.13 = (f32[40,640]{1,0:T(8,128)S(1)}, f32[40,640]{1,0:T(8,128)S(1)}, u32[]{:S(2)}, u32[]{:S(2)}) collective-permute-start(f32[40,640]{1,0:T(8,128)S(1)} %pad_maximum_fusion.1), channel_id=1, source_target_pairs={{0,4},{4,8},{8,12},{1,5},{5,9},{9,13},{2,6},{6,10},{10,14},{3,7},{... | collective-permute-start | bytes 307208 | tf_op jit(solution)/shard_map/ppermute | solution.py:811
  279.0 1.3 collective-permute-start.14
  280.3 1.6 collective-permute-done.14
  283.1 3.6 %collective-permute-done.16 = f32[40,640]{1,0:T(8,128)S(1)} collective-permute-done((f32[40,640]{1,0:T(8,128)S(1)}, f32[40,640]{1,0:T(8,128)S(1)}, u32[]{:S(2)}, u32[]{:S(2)}) %collective-permute-start.16) | collective-permute-done | bytes 102432 | tf_op jit(solution)/shard_map/ppermute | solution.py:818
  288.1 2.4 finish.1
  (95 shorter events, 11.3 us)
Async XLA Ops:
  0.6 228.8 %copy-start = (f32[384]{0:T(512)S(1)}, f32[384]{0:T(512)}, u32[]{:S(2)}) copy-start(f32[384]{0:T(512)} %param.21) | copy-start | bytes 4612
  33.5 2.9 %collective-permute-start = (bf16[384,1280]{1,0:T(8,128)(2,1)}, bf16[384,1280]{1,0:T(8,128)(2,1)S(1)}, u32[]{:S(2)}, u32[]{:S(2)}) collective-permute-start(bf16[384,1280]{1,0:T(8,128)(2,1)} %pack_handed.1), channel_id=1, source_target_pairs={{0,1},{1,0},{2,3},{3,2},{4,5},{5,4},{6,7},{7,6},{8,9},{9,8},{10,11... | collective-permute-start | bytes 2949128 | tf_op jit(solution)/shard_map/ppermute | solution.py:519
  34.1 67.0 %copy-start.16 = (f32[2560]{0:T(1024)S(1)}, f32[2560]{0:T(1024)}, u32[]{:S(2)}) copy-start(f32[2560]{0:T(1024)} %param.16) | copy-start | bytes 30724
  99.0 114.1 %collective-permute-start.2 = (bf16[768,256]{1,0:T(8,128)(2,1)}, bf16[768,256]{1,0:T(8,128)(2,1)S(1)}, u32[]{:S(2)}, u32[]{:S(2)}) collective-permute-start(bf16[768,256]{1,0:T(8,128)(2,1)} %get-tuple-element.19), channel_id=1, source_target_pairs={{4,12},{5,13},{6,14},{7,15},{20,28},{21,29},{22,30},{23,31}} | collective-permute-start | bytes 1179656 | tf_op jit(solution)/shard_map/ppermute | solution.py:521
  101.1 55.5 %copy-start.15 = (f32[3,8,16,16]{3,2,1,0:T(8,128)S(1)}, f32[3,8,16,16]{3,2,1,0:T(8,128)}, u32[]{:S(2)}) copy-start(f32[3,8,16,16]{3,2,1,0:T(8,128)} %param.19) | copy-start | bytes 73732
  101.1 60.4 %copy-start.6 = (bf16[2560,64]{0,1:T(8,128)(2,1)S(1)}, bf16[2560,64]{0,1:T(8,128)(2,1)}, u32[]{:S(2)}) copy-start(bf16[2560,64]{0,1:T(8,128)(2,1)} %param.18) | copy-start | bytes 983044
  101.1 60.4 %copy-start.17 = (f32[2560]{0:T(1024)S(1)}, f32[2560]{0:T(1024)}, u32[]{:S(2)}) copy-start(f32[2560]{0:T(1024)} %param.17) | copy-start | bytes 30724
  101.1 62.3 %copy-start.18 = (s32[4,4]{1,0:T(4,128)S(1)}, s32[4,4]{1,0:T(4,128)}, u32[]{:S(2)}) copy-start(s32[4,4]{1,0:T(4,128)} %param.15) | copy-start | bytes 196
  101.1 118.0 %collective-permute-start.3 = (bf16[768,256]{1,0:T(8,128)(2,1)}, bf16[768,256]{1,0:T(8,128)(2,1)S(1)}, u32[]{:S(2)}, u32[]{:S(2)}) collective-permute-start(bf16[768,256]{1,0:T(8,128)(2,1)} %get-tuple-element.19), channel_id=1, source_target_pairs={{0,12},{1,13},{2,14},{3,15},{16,28},{17,29},{18,30},{19,31}} | collective-permute-start | bytes 1179656 | tf_op jit(solution)/shard_map/ppermute | solution.py:521
  155.3 88.7 %collective-permute-start.4 = (bf16[1152,384]{1,0:T(8,128)(2,1)}, bf16[1152,384]{1,0:T(8,128)(2,1)}, u32[]{:S(2)}, u32[]{:S(2)}) collective-permute-start(bf16[1152,384]{1,0:T(8,128)(2,1)} %get-tuple-element.20), channel_id=1, source_target_pairs={{4,0},{8,4},{12,8},{5,1},{9,5},{13,9},{6,2},{10,6},{14,10},{7,3},{... | collective-permute-start | bytes 2654216 | tf_op jit(solution)/shard_map/ppermute | solution.py:521
  157.0 54.5 %collective-permute-start.18 = (f32[8,16,32]{2,1,0:T(8,128)S(1)}, f32[8,16,32]{2,1,0:T(8,128)S(1)}, u32[]{:S(2)}, u32[]{:S(2)}) collective-permute-start(f32[8,16,32]{2,1,0:T(8,128)S(1)} %slice.50), channel_id=1, source_target_pairs={{0,4},{4,8},{8,12},{1,5},{5,9},{9,13},{2,6},{6,10},{10,14},{3,7},{... | collective-permute-start | bytes 49160 | tf_op jit(solution)/shard_map/ppermute | solution.py:45
  161.9 48.3 %collective-permute-start.21 = (f32[64,2]{1,0:T(8,128)S(1)}, f32[64,2]{1,0:T(8,128)S(1)}, u32[]{:S(2)}, u32[]{:S(2)}) collective-permute-start(f32[64,2]{1,0:T(8,128)S(1)} %copy.34), channel_id=1, source_target_pairs={{0,2},{2,0},{1,3},{3,1},{4,6},{6,4},{5,7},{7,5},{8,10},{10,8},{9,1... | collective-permute-start | bytes 1544 | tf_op jit(solution)/shard_map/ppermute | solution.py:800
  163.5 55.5 %copy-start.14 = (bf16[432,384]{1,0:T(8,128)(2,1)S(1)}, bf16[432,384]{1,0:T(8,128)(2,1)}, u32[]{:S(2)}) copy-start(bf16[432,384]{1,0:T(8,128)(2,1)} %param.20) | copy-start | bytes 995332
  210.1 19.4 %collective-permute-start.1 = (bf16[1152,256]{1,0:T(8,128)(2,1)}, bf16[1152,256]{1,0:T(8,128)(2,1)}, u32[]{:S(2)}, u32[]{:S(2)}) collective-permute-start(bf16[1152,256]{1,0:T(8,128)(2,1)} %get-tuple-element.18), channel_id=1, source_target_pairs={{8,12},{4,0},{9,13},{5,1},{10,14},{6,2},{11,15},{7,3},{24,28},{20,... | collective-permute-start | bytes 1769480 | tf_op jit(solution)/shard_map/ppermute | solution.py:521
  211.5 50.6 %collective-permute-start.5 = (bf16[1152,384]{1,0:T(8,128)(2,1)}, bf16[1152,384]{1,0:T(8,128)(2,1)}, u32[]{:S(2)}, u32[]{:S(2)}) collective-permute-start(bf16[1152,384]{1,0:T(8,128)(2,1)} %get-tuple-element.21), channel_id=1, source_target_pairs={{12,4},{13,5},{14,6},{15,7},{28,20},{29,21},{30,22},{31,23}} | collective-permute-start | bytes 2654216 | tf_op jit(solution)/shard_map/ppermute | solution.py:521
  213.1 19.2 %collective-permute-start.6 = (bf16[768,384]{1,0:T(8,128)(2,1)}, bf16[768,384]{1,0:T(8,128)(2,1)}, u32[]{:S(2)}, u32[]{:S(2)}) collective-permute-start(bf16[768,384]{1,0:T(8,128)(2,1)} %get-tuple-element.22), channel_id=1, source_target_pairs={{0,4},{4,8},{1,5},{5,9},{2,6},{6,10},{3,7},{7,11},{16,20},{20,24},... | collective-permute-start | bytes 1769480 | tf_op jit(solution)/shard_map/ppermute | solution.py:521
  219.1 23.6 %collective-permute-start.7 = (bf16[768,384]{1,0:T(8,128)(2,1)}, bf16[768,384]{1,0:T(8,128)(2,1)}, u32[]{:S(2)}, u32[]{:S(2)}) collective-permute-start(bf16[768,384]{1,0:T(8,128)(2,1)} %get-tuple-element.23), channel_id=1, source_target_pairs={{0,8},{1,9},{2,10},{3,11},{16,24},{17,25},{18,26},{19,27}} | collective-permute-start | bytes 1769480 | tf_op jit(solution)/shard_map/ppermute | solution.py:521
  224.0 25.5 %copy-start.1 = (bf16[384,2560]{1,0:T(8,128)(2,1)S(1)}, bf16[384,2560]{1,0:T(8,128)(2,1)}, u32[]{:S(2)}) copy-start(bf16[384,2560]{1,0:T(8,128)(2,1)} %refs_0_.13) | copy-start | bytes 5898244
  224.0 25.5 %copy-start.2 = (bf16[192,2560]{1,0:T(8,128)(2,1)S(1)}, bf16[192,2560]{1,0:T(8,128)(2,1)}, u32[]{:S(2)}) copy-start(bf16[192,2560]{1,0:T(8,128)(2,1)} %refs_1_.13) | copy-start | bytes 2949124
  224.0 25.5 %copy-start.13 = (s32[8]{0:T(128)S(1)}, s32[8]{0:T(128)}, u32[]{:S(2)}) copy-start(s32[8]{0:T(128)} %fusion.42.scalars) | copy-start | bytes 100
  229.6 39.6 %collective-permute-start.8 = (bf16[1152,128]{1,0:T(8,128)(2,1)}, bf16[1152,128]{1,0:T(8,128)(2,1)S(1)}, u32[]{:S(2)}, u32[]{:S(2)}) collective-permute-start(bf16[1152,128]{1,0:T(8,128)(2,1)} %get-tuple-element.24), channel_id=1, source_target_pairs={{4,0},{8,4},{12,8},{5,1},{9,5},{13,9},{6,2},{10,6},{14,10},{7,3},{... | collective-permute-start | bytes 884744 | tf_op jit(solution)/shard_map/ppermute | solution.py:521
  232.2 37.0 %collective-permute-start.9 = (bf16[1152,128]{1,0:T(8,128)(2,1)}, bf16[1152,128]{1,0:T(8,128)(2,1)S(1)}, u32[]{:S(2)}, u32[]{:S(2)}) collective-permute-start(bf16[1152,128]{1,0:T(8,128)(2,1)} %get-tuple-element.25), channel_id=1, source_target_pairs={{12,4},{13,5},{14,6},{15,7},{28,20},{29,21},{30,22},{31,23}} | collective-permute-start | bytes 884744 | tf_op jit(solution)/shard_map/ppermute | solution.py:521
  242.7 26.4 %collective-permute-start.10 = (bf16[768,128]{1,0:T(8,128)(2,1)}, bf16[768,128]{1,0:T(8,128)(2,1)S(1)}, u32[]{:S(2)}, u32[]{:S(2)}) collective-permute-start(bf16[768,128]{1,0:T(8,128)(2,1)} %get-tuple-element.26), channel_id=1, source_target_pairs={{0,4},{4,8},{1,5},{5,9},{2,6},{6,10},{3,7},{7,11},{16,20},{20,24},... | collective-permute-start | bytes 589832 | tf_op jit(solution)/shard_map/ppermute | solution.py:521
  244.0 25.1 %collective-permute-start.11 = (bf16[768,128]{1,0:T(8,128)(2,1)}, bf16[768,128]{1,0:T(8,128)(2,1)S(1)}, u32[]{:S(2)}, u32[]{:S(2)}) collective-permute-start(bf16[768,128]{1,0:T(8,128)(2,1)} %get-tuple-element.27), channel_id=1, source_target_pairs={{0,8},{1,9},{2,10},{3,11},{16,24},{17,25},{18,26},{19,27}} | collective-permute-start | bytes 589832 | tf_op jit(solution)/shard_map/ppermute | solution.py:521
  262.0 10.6 %collective-permute-start.19 = (f32[8,80]{1,0:T(8,128)S(1)}, f32[8,80]{1,0:T(8,128)S(1)}, u32[]{:S(2)}, u32[]{:S(2)}) collective-permute-start(f32[8,80]{1,0:T(8,128)S(1)} %select_bitcast_fusion.2), channel_id=1, source_target_pairs={{0,1},{1,0},{2,3},{3,2},{4,5},{5,4},{6,7},{7,6},{8,9},{9,8},{10,11... | collective-permute-start | bytes 7688 | tf_op jit(solution)/shard_map/ppermute | solution.py:617
  272.0 1.6 collective-permute-start.12
  272.7 10.4 %collective-permute-start.20 = (f32[32,80]{1,0:T(8,128)S(1)}, f32[32,80]{1,0:T(8,128)S(1)}, u32[]{:S(2)}, u32[]{:S(2)}) collective-permute-start(f32[32,80]{1,0:T(8,128)S(1)} %fusion.34), channel_id=1, source_target_pairs={{0,2},{2,0},{1,3},{3,1},{4,6},{6,4},{5,7},{7,5},{8,10},{10,8},{9,1... | collective-permute-start | bytes 30728 | tf_op jit(solution)/shard_map/ppermute | solution.py:629
  273.7 8.2 %collective-permute-start.13 = (f32[40,640]{1,0:T(8,128)S(1)}, f32[40,640]{1,0:T(8,128)S(1)}, u32[]{:S(2)}, u32[]{:S(2)}) collective-permute-start(f32[40,640]{1,0:T(8,128)S(1)} %pad_maximum_fusion.1), channel_id=1, source_target_pairs={{0,4},{4,8},{8,12},{1,5},{5,9},{9,13},{2,6},{6,10},{10,14},{3,7},{... | collective-permute-start | bytes 307208 | tf_op jit(solution)/shard_map/ppermute | solution.py:811
  278.3 3.6 %collective-permute-start.15 = (f32[40,384]{1,0:T(8,128)S(1)}, f32[40,384]{1,0:T(8,128)S(1)}, u32[]{:S(2)}, u32[]{:S(2)}) collective-permute-start(f32[40,384]{1,0:T(8,128)S(1)} %get-tuple-element.39), channel_id=1, source_target_pairs={{4,12},{12,8},{5,13},{13,9},{6,14},{14,10},{7,15},{15,11},{20,28},... | collective-permute-start | bytes 184328 | tf_op jit(solution)/shard_map/ppermute | solution.py:814
  279.0 3.0 %collective-permute-start.14 = (f32[40,256]{1,0:T(8,128)S(1)}, f32[40,256]{1,0:T(8,128)S(1)}, u32[]{:S(2)}, u32[]{:S(2)}) collective-permute-start(f32[40,256]{1,0:T(8,128)S(1)} %slice.49), channel_id=1, source_target_pairs={{0,8},{4,12},{1,9},{5,13},{2,10},{6,14},{3,11},{7,15},{16,24},{20,... | collective-permute-start | bytes 122888 | tf_op jit(solution)/shard_map/ppermute | solution.py:815
  282.0 4.7 %collective-permute-start.16 = (f32[40,640]{1,0:T(8,128)S(1)}, f32[40,640]{1,0:T(8,128)S(1)}, u32[]{:S(2)}, u32[]{:S(2)}) collective-permute-start(f32[40,640]{1,0:T(8,128)S(1)} %fusion.32), channel_id=1, source_target_pairs={{0,2},{2,0},{1,3},{3,1},{4,6},{6,4},{5,7},{7,5},{8,10},{10,8},{9,1... | collective-permute-start | bytes 307208 | tf_op jit(solution)/shard_map/ppermute | solution.py:818
  286.7 1.4 collective-permute-start.17
  (9 other events, 48.4 us)

commit v3 on v2

--- a/solution.py
+++ b/solution.py
@@ -251,58 +251,89 @@
     return row + lax.axis_index("slab") * jnp.array(by_slab)
 
 
-def pack_kernel(copies, scalars, *refs):
-    ins, outs, semaphores = refs[: copies[0]], refs[copies[0] : -1], refs[-1]
-    started = []
-    for number, (source, row, rows, entries, shift, target, at, heads) in enumerate(copies[1]):
-        head = shift
-        for entry in entries:
-            head = head + scalars[entry]
-        column = pl.multiple_of(head * HD, HD)
-        copy = pltpu.make_async_copy(
-            ins[source].at[pl.ds(row, rows), pl.ds(column, heads * HD)],
-            outs[target].at[pl.ds(at, rows), :],
-            semaphores.at[number],
-        )
-        copy.start()
-        started.append(copy)
-    for copy in started:
-        copy.wait()
-
-
-def pack(scalars, arrays, shapes, copies, name):
-    moved = sum(2 * 2 * rows * heads * HD for _, _, rows, _, _, _, _, heads in copies)
+def hand_kernel(scalars, keys, values, out):
+    half = keys.shape[0]
+    out[:half] = keys[...]
+    out[half:] = values[...]
+
+
+def pack_handed(scalars, keys, values, heads):
+    half = keys.shape[0]
+    wide = heads * HD
+    column = pl.BlockSpec((half, wide), lambda i, scalars: (0, 1 - scalars[SLAB]))
     return pl.pallas_call(
-        functools.partial(pack_kernel, (len(arrays), copies)),
-        name=name,
-        out_shape=[jax.ShapeDtypeStruct(shape, jnp.bfloat16) for shape in shapes],
+        hand_kernel,
+        name="pack_handed",
+        out_shape=jax.ShapeDtypeStruct((2 * half, wide), keys.dtype),
         grid_spec=pltpu.PrefetchScalarGridSpec(
             num_scalar_prefetch=1,
             grid=(1,),
-            in_specs=[pl.BlockSpec(memory_space=pl.ANY)] * len(arrays),
-            out_specs=[pl.BlockSpec(memory_space=pl.ANY)] * len(shapes),
-            scratch_shapes=[pltpu.SemaphoreType.DMA((len(copies),))],
-        ),
-        cost_estimate=pl.CostEstimate(flops=0, bytes_accessed=moved, transcendentals=0),
-    )(scalars, *arrays)
-
-
-def pack_messages(scalars, queries, keys, values, received, messages, name):
-    rows = queries.shape[0]
-    half = rows // 2
-    copies, shapes = [], []
-    for target, (entry, shift, heads, whole) in enumerate(messages):
-        entries = () if entry is None else (entry,)
+            in_specs=[column, column],
+            out_specs=pl.BlockSpec((2 * half, wide), lambda i, scalars: (0, 0)),
+        ),
+        compiler_params=pltpu.CompilerParams(vmem_limit_bytes=16 << 20),
+        cost_estimate=pl.CostEstimate(
+            flops=0, bytes_accessed=8 * half * wide, transcendentals=0
+        ),
+    )(scalars, keys, values)
+
+
+def pack_kernel(wholes, scalars, *refs):
+    ins, outs = refs[: 4 * len(wholes)], refs[4 * len(wholes) :]
+    for number, (whole, out) in enumerate(zip(wholes, outs)):
+        queries, keys, values, received = ins[4 * number : 4 * number + 4]
+        rows = received.shape[0]
+        half = rows // 2
         at = 0
         if whole:
-            copies.append((0, 0, rows, (OWN,) + entries, shift, target, 0, heads))
+            out[:rows] = queries[...]
             at = rows
-        for part, array in enumerate((1, 2)):
-            copies.append((array, 0, half, (OWN,) + entries, shift, target, at, heads))
-            copies.append((3, part * half, half, entries, shift, target, at + half, heads))
-            at += rows
-        shapes.append((at, heads * HD))
-    return pack(scalars, (queries, keys, values, received), shapes, copies, name)
+        out[at : at + half] = keys[...]
+        out[at + half : at + rows] = received[:half]
+        out[at + rows : at + rows + half] = values[...]
+        out[at + rows + half :] = received[half:]
+
+
+def pack_messages(scalars, heads, messages, queries, keys, values, received, name):
+    rows = queries.shape[0]
+
+    def column(height, entry, shift, own_column):
+        def index(i, scalars):
+            head = shift + i + (scalars[OWN] if own_column else 0)
+            return (0, head if entry is None else head + scalars[entry])
+
+        return pl.BlockSpec((height, HD), index)
+
+    in_specs, arrays, shapes = [], [], []
+    for entry, shift, whole in messages:
+        in_specs += [
+            column(rows, entry, shift, True) if whole else column(16, None, 0, False),
+            column(rows // 2, entry, shift, True),
+            column(rows // 2, entry, shift, True),
+            column(rows, entry, shift, False),
+        ]
+        arrays += [queries, keys, values, received]
+        shapes.append(((3 if whole else 2) * rows, heads * HD))
+    wholes = [whole for _, _, whole in messages]
+    return pl.pallas_call(
+        functools.partial(pack_kernel, wholes),
+        name=name,
+        out_shape=[jax.ShapeDtypeStruct(shape, queries.dtype) for shape in shapes],
+        grid_spec=pltpu.PrefetchScalarGridSpec(
+            num_scalar_prefetch=1,
+            grid=(heads,),
+            in_specs=in_specs,
+            out_specs=[
+                pl.BlockSpec((shape[0], HD), lambda i, scalars: (0, i)) for shape in shapes
+            ],
+        ),
+        compiler_params=pltpu.CompilerParams(vmem_limit_bytes=16 << 20),
+        cost_estimate=pl.CostEstimate(
+            flops=0,
+            bytes_accessed=4 * sum(shape[0] * shape[1] for shape in shapes),
+            transcendentals=0,
+        ),
+    )(scalars, *arrays)
 
 
 def attend_kernel(variants, extra, span_count, scalars, mask, *refs):
@@ -508,33 +539,33 @@
 def token_sums(scalars, queries, keys, values, span_mask, head_gain, patch_weight):
     rows = queries.shape[0]
     heads = NEAR_HEADS + MIDDLE_HEADS + FAR_HEADS
-    half = rows // 2
-    (handed,) = pack(
-        scalars,
-        (keys, values),
-        [(rows, heads * HD)],
-        [(0, 0, half, (OTHER,), 0, 0, 0, heads), (1, 0, half, (OTHER,), 0, 0, half, heads)],
-        "pack_handed",
-    )
-    received = lax.ppermute(handed, "slab", SWAP)
-    bring = functools.partial(pack_messages, scalars, queries, keys, values, received)
+    received = lax.ppermute(pack_handed(scalars, keys, values, heads), "slab", SWAP)
     send = lambda value, *pairs: lax.ppermute(value, "span", list(pairs))
 
-    down, up = bring([(DOWN, 0, EARLY, True), (UP, 0, EARLY, False)], "pack_first")
+    def bring(heads, messages, source, name):
+        return pack_messages(scalars, heads, messages, queries, keys, values, source, name)
+
+    down, up = bring(EARLY, [(DOWN, 0, True), (UP, 0, False)], received, "pack_first")
     anchor = down
+    source, _ = lax.optimization_barrier((received, down))
     down_two, up_two = bring(
-        [(None, 0, EARLY, True), (None, MIDDLE, EARLY, False)], "pack_second"
-    )
-    far_all, far_pair, late_down, late_down_two, late_up, late_up_two = bring(
+        EARLY, [(None, 0, True), (None, MIDDLE, False)], source, "pack_second"
+    )
+    source, _ = lax.optimization_barrier((received, down_two))
+    far_all, far_pair = bring(
+        FAR_HEADS, [(None, FAR, True), (None, FAR, False)], source, "pack_far"
+    )
+    source, _ = lax.optimization_barrier((received, far_all))
+    late_down, late_down_two, late_up, late_up_two = bring(
+        LATE,
         [
-            (None, FAR, FAR_HEADS, True),
-            (None, FAR, FAR_HEADS, False),
-            (DOWN, EARLY, LATE, True),
-            (None, EARLY, LATE, True),
-            (UP, EARLY, LATE, False),
-            (None, MIDDLE + EARLY, LATE, False),
-        ],
-        "pack_third",
+            (DOWN, EARLY, True),
+            (None, EARLY, True),
+            (UP, EARLY, False),
+            (None, MIDDLE + EARLY, False),
+        ],
+        source,
+        "pack_late",
     )
     down = send(down, (1, 0), (2, 1), (3, 2))
     up = send(up, (0, 1), (1, 2))

time: 292 us -> 129 us (0.44)
  Pallas kernels: 207 us -> 33.6 us
  local copies, waits for them, and re-layouts: 14.2 us -> 23 us
  starting transfers between devices: 44.7 us -> 53.1 us
  waiting for transfers between devices: 20.4 us -> 12.6 us
    pallas_call x4 -> x5, Pallas kernels: 186 us -> 12.2 us  [the longest x4 10.6 us: pack_messages(): pl.pallas_call(functools.partial(pack_kernel, wholes), name=name, out_sha...]
    ppermute x11, waiting for transfers between devices: 11.2 us -> 1.05 us  [token_sums(): send = lambda value, *pairs: lax.ppermute(value, 'span', list(pairs))]
    ppermute x11, starting transfers between devices: 29.3 us -> 36.9 us  [token_sums(): send = lambda value, *pairs: lax.ppermute(value, 'span', list(pairs))]
    unnamed x40 -> x54, local copies, waits for them, and re-layouts: 5.46 us -> 11.4 us
  transfers between devices with their start and end apart: 22 -> 22, of which waited for: 7 -> 6; matrix products, arithmetic and copies ran while one was open for 4% -> 12% of each run, Pallas kernels for 38% -> 16%
where the time goes in v3:
time: 129 us; the launch traced here: 128 us
  starting transfers between devices  53.1 us (41%)
  Pallas kernels  33.6 us (26%)
  local copies, waits for them, and re-layouts  23 us (18%)
  waiting for transfers between devices  12.6 us (10%)
  other arithmetic  4.58 us (4%)
    ppermute x11, starting transfers between devices, token_sums(): send = lambda value, *pairs: lax.ppermute(value, 'span', list(pairs))  36.9 us
    pallas_call x3, Pallas kernels, attend(): pl.pallas_call(functools.partial(attend_kernel, variants, extra, span_cou...  19 us
    unnamed x54, local copies, waits for them, and re-layouts  11.4 us
    pallas_call x4, Pallas kernels, pack_messages(): pl.pallas_call(functools.partial(pack_kernel, wholes), name=name, out_sha...  10.6 us
    reshape x1, local copies, waits for them, and re-layouts, banded_weight(): banded.transpose(1, 2, 0, 3, 4, 5)  5.29 us
    ppermute x1, starting transfers between devices, from_behind(): return lax.ppermute(value, axis, pairs)  4.55 us
    ppermute x1, starting transfers between devices, per_device(): lax.ppermute(jnp.concatenate([own[:, skip:], after], axis=1), 'span', [(0...  4.48 us
    ppermute x1, waiting for transfers between devices, per_device(): total = total + lax.ppermute(total, 'head', SWAP)  3.72 us
  transfers between devices with their start and end apart: 22, of which 6 were waited for; matrix products, arithmetic and copies ran while one was open for 12% of the time, Pallas kernels for 16%

profile of v3, /device:TPU:0, one launch (start us, length us, event | category | flops | bytes accessed | tf_op | source)
XLA Modules:
  0.0 127.9 jit_solution(972071533132616935)
XLA Ops:
  3.9 1.6 %pack_handed.1 = bf16[384,1280]{1,0:T(8,128)(2,1)} custom-call(s32[8]{0:T(128)S(1)} %fusion.42.scalars, bf16[192,2560]{1,0:T(8,128)(2,1)S(1)} %copy-done.2, bf16[192,2560]{1,0:T(8,128)(2,1)S(1)} %copy-done.4), custom_call_target="tpu_custom_call" | custom-call | bytes 1966080 | tf_op jit(solution)/shard_map/pack_handed/pallas_call | solution.py:264
  6.0 2.5 %collective-permute-done.refs_3_.refs_7_.refs_10_.refs_11_.refs_15_ = bf16[384,1280]{1,0:T(8,128)(2,1)} collective-permute-done((bf16[384,1280]{1,0:T(8,128)(2,1)}, bf16[384,1280]{1,0:T(8,128)(2,1)}, u32[]{:S(2)}, u32[]{:S(2)}) %collective-permute-start) | collective-permute-done | bytes 983072 | tf_op jit(solution)/shard_map/ppermute | solution.py:542
  9.7 2.9 %pack_first.1 = (bf16[1152,384]{1,0:T(8,128)(2,1)S(1)}, bf16[768,384]{1,0:T(8,128)(2,1)S(1)}) custom-call(s32[8]{0:T(128)S(1)} %fusion.42.scalars, bf16[384,2560]{1,0:T(8,128)(2,1)S(1)} %copy-done.1, bf16[192,2560]{1,0:T(8,128)(2,1)S(1)} %copy-done.3, bf16[192,2560]{1,0:T(8,128)(2,1)S(1)} %copy-done.5, ...), custom_call_target="tpu_custom_call" | custom-call | bytes 2949120 | tf_op jit(solution)/shard_map/pack_first/pallas_call | solution.py:318
  14.3 3.5 %pack_second.1 = (bf16[1152,384]{1,0:T(8,128)(2,1)S(1)}, bf16[768,384]{1,0:T(8,128)(2,1)}) custom-call(s32[8]{0:T(128)S(1)} %fusion.42.scalars, bf16[384,2560]{1,0:T(8,128)(2,1)S(1)} %copy-done.1, bf16[192,2560]{1,0:T(8,128)(2,1)S(1)} %copy-done.3, bf16[192,2560]{1,0:T(8,128)(2,1)S(1)} %copy-done.5, ...), custom_call_target="tpu_custom_call" | custom-call | bytes 2949120 | tf_op jit(solution)/shard_map/pack_second/pallas_call | solution.py:318
  18.8 2.5 %pack_far.1 = (bf16[1152,256]{1,0:T(8,128)(2,1)S(1)}, bf16[768,256]{1,0:T(8,128)(2,1)}) custom-call(s32[8]{0:T(128)S(1)} %fusion.42.scalars, bf16[384,2560]{1,0:T(8,128)(2,1)S(1)} %copy-done.1, bf16[192,2560]{1,0:T(8,128)(2,1)S(1)} %copy-done.3, bf16[192,2560]{1,0:T(8,128)(2,1)S(1)} %copy-done.5, ...), custom_call_target="tpu_custom_call" | custom-call | bytes 1966080 | tf_op jit(solution)/shard_map/pack_far/pallas_call | solution.py:318
  22.1 1.6 %collective-permute-start.2 = (bf16[768,256]{1,0:T(8,128)(2,1)}, bf16[768,256]{1,0:T(8,128)(2,1)}, u32[]{:S(2)}, u32[]{:S(2)}) collective-permute-start(bf16[768,256]{1,0:T(8,128)(2,1)} %get-tuple-element.26), channel_id=1, source_target_pairs={{4,12},{5,13},{6,14},{7,15},{20,28},{21,29},{22,30},{23,31}} | collective-permute-start | bytes 1179656 | tf_op jit(solution)/shard_map/ppermute | solution.py:543
  23.7 1.3 %fusion.30.selector = bf16[320,512]{1,0:T(8,128)(2,1)} fusion(s32[320]{0:T(512)S(1)} %get-tuple-element.55, s32[320]{0:T(512)S(1)} %get-tuple-element.56, s32[]{:T(128)S(6)} %mul.54, s32[320]{0:T(512)S(1)} %get-tuple-element.54, s32[320]{0:T(512)S(1)} %get-tuple-element.57, s32[]{:T(128)S(6)} %mul.53, pred[320]{0:T(512)(128)(4,1)S(1)} %get-tuple-element.59, ...), kind=kLoop, calls=%fused_computation.47 | loop fusion | flops 10158080 | bytes 333448 | tf_op jit(solution)/shard_map/convert_element_type | solution.py:675
  25.0 7.5 %collective-permute-start.3 = (bf16[768,256]{1,0:T(8,128)(2,1)}, bf16[768,256]{1,0:T(8,128)(2,1)}, u32[]{:S(2)}, u32[]{:S(2)}) collective-permute-start(bf16[768,256]{1,0:T(8,128)(2,1)} %get-tuple-element.26), channel_id=1, source_target_pairs={{0,12},{1,13},{2,14},{3,15},{16,28},{17,29},{18,30},{19,31}} | collective-permute-start | bytes 1179656 | tf_op jit(solution)/shard_map/ppermute | solution.py:543
  32.6 1.3 %collective-permute-start.4 = (bf16[1152,384]{1,0:T(8,128)(2,1)}, bf16[1152,384]{1,0:T(8,128)(2,1)}, u32[]{:S(2)}, u32[]{:S(2)}) collective-permute-start(bf16[1152,384]{1,0:T(8,128)(2,1)} %copy-done.12), channel_id=1, source_target_pairs={{4,0},{8,4},{12,8},{5,1},{9,5},{13,9},{6,2},{10,6},{14,10},{7,3},{... | collective-permute-start | bytes 2654216 | tf_op jit(solution)/shard_map/ppermute | solution.py:543
  35.9 4.5 %collective-permute-start.18 = (f32[8,16,32]{2,1,0:T(8,128)S(1)}, f32[8,16,32]{2,1,0:T(8,128)S(1)}, u32[]{:S(2)}, u32[]{:S(2)}) collective-permute-start(f32[8,16,32]{2,1,0:T(8,128)S(1)} %slice.50), channel_id=1, source_target_pairs={{0,4},{4,8},{8,12},{1,5},{5,9},{9,13},{2,6},{6,10},{10,14},{3,7},{... | collective-permute-start | bytes 49160 | tf_op jit(solution)/shard_map/ppermute | solution.py:45
  40.8 1.5 %collective-permute-start.21 = (f32[64,2]{1,0:T(8,128)S(1)}, f32[64,2]{1,0:T(8,128)}, u32[]{:S(2)}, u32[]{:S(2)}) collective-permute-start(f32[64,2]{1,0:T(8,128)S(1)} %copy.34), channel_id=1, source_target_pairs={{0,2},{2,0},{1,3},{3,1},{4,6},{6,4},{5,7},{7,5},{8,10},{10,8},{9,1... | collective-permute-start | bytes 1544 | tf_op jit(solution)/shard_map/ppermute | solution.py:831
  42.4 2.4 %collective-permute-done.21 = f32[64,2]{1,0:T(8,128)} collective-permute-done((f32[64,2]{1,0:T(8,128)S(1)}, f32[64,2]{1,0:T(8,128)}, u32[]{:S(2)}, u32[]{:S(2)}) %collective-permute-start.21) | collective-permute-done | bytes 544 | tf_op jit(solution)/shard_map/ppermute | solution.py:831
  44.9 1.6 %collective-permute-start.5 = (bf16[1152,384]{1,0:T(8,128)(2,1)}, bf16[1152,384]{1,0:T(8,128)(2,1)}, u32[]{:S(2)}, u32[]{:S(2)}) collective-permute-start(bf16[1152,384]{1,0:T(8,128)(2,1)} %copy-done.11), channel_id=1, source_target_pairs={{12,4},{13,5},{14,6},{15,7},{28,20},{29,21},{30,22},{31,23}} | collective-permute-start | bytes 2654216 | tf_op jit(solution)/shard_map/ppermute | solution.py:543
  46.5 1.3 %collective-permute-start.1 = (bf16[1152,256]{1,0:T(8,128)(2,1)}, bf16[1152,256]{1,0:T(8,128)(2,1)}, u32[]{:S(2)}, u32[]{:S(2)}) collective-permute-start(bf16[1152,256]{1,0:T(8,128)(2,1)} %copy-done.14), channel_id=1, source_target_pairs={{8,12},{4,0},{9,13},{5,1},{10,14},{6,2},{11,15},{7,3},{24,28},{20,... | collective-permute-start | bytes 1769480 | tf_op jit(solution)/shard_map/ppermute | solution.py:543
  47.8 6.2 %collective-permute-start.6 = (bf16[768,384]{1,0:T(8,128)(2,1)}, bf16[768,384]{1,0:T(8,128)(2,1)}, u32[]{:S(2)}, u32[]{:S(2)}) collective-permute-start(bf16[768,384]{1,0:T(8,128)(2,1)} %copy-done.13), channel_id=1, source_target_pairs={{0,4},{4,8},{1,5},{5,9},{2,6},{6,10},{3,7},{7,11},{16,20},{20,24},... | collective-permute-start | bytes 1769480 | tf_op jit(solution)/shard_map/ppermute | solution.py:543
  54.0 1.4 %pad_bitcast_fusion.2 = (bf16[5,3,3,16,1,384]{5,3,2,1,0,4:T(8,128)(2,1)S(1)}, bf16[5,3,3,16,1,384]{5,3,2,1,0,4:T(8,128)(2,1)S(1)}, bf16[5,3,3,16,1,384]{5,3,2,1,0,4:T(8,128)(2,1)S(1)}) fusion(bf16[3,3,3,16,384]{4,3,2,1,0:T(8,128)(2,1)} %bitcast.48), kind=kLoop, calls=%fused_computation.51 | loop fusion | bytes 1990656 | tf_op jit(solution)/shard_map/stack | solution.py:681
  55.4 4.5 %collective-permute-start.7 = (bf16[768,384]{1,0:T(8,128)(2,1)}, bf16[768,384]{1,0:T(8,128)(2,1)}, u32[]{:S(2)}, u32[]{:S(2)}) collective-permute-start(bf16[768,384]{1,0:T(8,128)(2,1)} %get-tuple-element.28), channel_id=1, source_target_pairs={{0,8},{1,9},{2,10},{3,11},{16,24},{17,25},{18,26},{19,27}} | collective-permute-start | bytes 1769480 | tf_op jit(solution)/shard_map/ppermute | solution.py:543
  61.2 1.7 %pack_late.1 = (bf16[1152,128]{1,0:T(8,128)(2,1)S(1)}, bf16[1152,128]{1,0:T(8,128)(2,1)S(1)}, bf16[768,128]{1,0:T(8,128)(2,1)S(1)}, bf16[768,128]{1,0:T(8,128)(2,1)S(1)}) custom-call(s32[8]{0:T(128)S(1)} %fusion.42.scalars, bf16[384,2560]{1,0:T(8,128)(2,1)S(1)} %copy-done.1, bf16[192,2560]{1,0:T(8,128)(2,1)S(1)} %copy-done.3, ...), custom_call_target="tpu_custom_call" | custom-call | bytes 1966080 | tf_op jit(solution)/shard_map/pack_late/pallas_call | solution.py:318
  64.9 2.5 %copy.32 = bf16[3,3,5,16,3,384]{5,4,3,2,1,0:T(4,128)(2,1)} copy(bf16[3,3,5,16,3,384]{5,3,1,0,2,4:T(8,128)(2,1)S(1)} %maximum_bitcast_fusion) | data formatting | bytes 3317760 | tf_op jit(solution)/shard_map/transpose | solution.py:688
  67.5 5.3 %reshape.34.band = bf16[3,240,1152]{2,1,0:T(8,128)(2,1)} reshape(bf16[3,3,5,16,3,384]{5,4,3,2,1,0:T(4,128)(2,1)} %copy.32) | data formatting | bytes 3317760 | tf_op jit(solution)/shard_map/reshape | solution.py:688
  74.5 1.3 %collective-permute-start.8 = (bf16[1152,128]{1,0:T(8,128)(2,1)}, bf16[1152,128]{1,0:T(8,128)(2,1)S(1)}, u32[]{:S(2)}, u32[]{:S(2)}) collective-permute-start(bf16[1152,128]{1,0:T(8,128)(2,1)} %copy-done.16), channel_id=1, source_target_pairs={{4,0},{8,4},{12,8},{5,1},{9,5},{13,9},{6,2},{10,6},{14,10},{7,3},{... | collective-permute-start | bytes 884744 | tf_op jit(solution)/shard_map/ppermute | solution.py:543
  77.5 8.1 %collective-permute-start.10 = (bf16[768,128]{1,0:T(8,128)(2,1)}, bf16[768,128]{1,0:T(8,128)(2,1)S(1)}, u32[]{:S(2)}, u32[]{:S(2)}) collective-permute-start(bf16[768,128]{1,0:T(8,128)(2,1)} %copy-done.17), channel_id=1, source_target_pairs={{0,4},{4,8},{1,5},{5,9},{2,6},{6,10},{3,7},{7,11},{16,20},{20,24},... | collective-permute-start | bytes 589832 | tf_op jit(solution)/shard_map/ppermute | solution.py:543
  85.6 2.8 %collective-permute-start.11 = (bf16[768,128]{1,0:T(8,128)(2,1)S(1)}, bf16[768,128]{1,0:T(8,128)(2,1)S(1)}, u32[]{:S(2)}, u32[]{:S(2)}) collective-permute-start(bf16[768,128]{1,0:T(8,128)(2,1)S(1)} %get-tuple-element.33), channel_id=1, source_target_pairs={{0,8},{1,9},{2,10},{3,11},{16,24},{17,25},{18,26},{19,27}} | collective-permute-start | bytes 589832 | tf_op jit(solution)/shard_map/ppermute | solution.py:543
  89.7 8.3 %far_heads.1.refs_6_ = f32[3,80,384]{2,1,0:T(8,128)S(1)} custom-call(s32[8]{0:T(128)S(1)} %fusion.42.scalars, s32[16]{0:T(128)S(1)} %reshape.30.mask, bf16[384,2560]{1,0:T(8,128)(2,1)S(1)} %copy-done.1, bf16[192,2560]{1,0:T(8,128)(2,1)S(1)} %copy-done.3, bf16[192,2560]{1,0:T(8,128)(2,1)S(1)} %copy-done.7, ...), custom_call_target="tpu_custom_call" | custom-call | flops 1056964608 | bytes 589824 | tf_op jit(solution)/shard_map/far_heads/pallas_call | solution.py:516
  98.0 7.1 %early_heads.1.refs_6_ = f32[3,80,384]{2,1,0:T(8,128)S(1)} custom-call(s32[8]{0:T(128)S(1)} %fusion.42.scalars, s32[16]{0:T(128)S(1)} %reshape.30.mask, bf16[384,2560]{1,0:T(8,128)(2,1)S(1)} %copy-done.1, bf16[192,2560]{1,0:T(8,128)(2,1)S(1)} %copy-done.3, bf16[192,2560]{1,0:T(8,128)(2,1)S(1)} %copy-done.7, ...), custom_call_target="tpu_custom_call" | custom-call | flops 2038431744 | bytes 884736 | tf_op jit(solution)/shard_map/early_heads/pallas_call | solution.py:516
  105.2 3.7 %late_heads.1 = f32[3,80,384]{2,1,0:T(8,128)S(1)} custom-call(s32[8]{0:T(128)S(1)} %fusion.42.scalars, s32[16]{0:T(128)S(1)} %reshape.30.mask, bf16[384,2560]{1,0:T(8,128)(2,1)S(1)} %copy-done.1, bf16[192,2560]{1,0:T(8,128)(2,1)S(1)} %copy-done.3, bf16[192,2560]{1,0:T(8,128)(2,1)S(1)} %copy-done.7, ...), custom_call_target="tpu_custom_call" | custom-call | flops 679477248 | bytes 294912 | tf_op jit(solution)/shard_map/late_heads/pallas_call | solution.py:516
  109.6 1.5 %collective-permute-start.20 = (f32[32,80]{1,0:T(8,128)S(1)}, f32[32,80]{1,0:T(8,128)S(1)}, u32[]{:S(2)}, u32[]{:S(2)}) collective-permute-start(f32[32,80]{1,0:T(8,128)S(1)} %fusion.34), channel_id=1, source_target_pairs={{0,2},{2,0},{1,3},{3,1},{4,6},{6,4},{5,7},{7,5},{8,10},{10,8},{9,1... | collective-permute-start | bytes 30728 | tf_op jit(solution)/shard_map/ppermute | solution.py:660
  111.2 4.5 %collective-permute-start.13 = (f32[40,640]{1,0:T(8,128)S(1)}, f32[40,640]{1,0:T(8,128)S(1)}, u32[]{:S(2)}, u32[]{:S(2)}) collective-permute-start(f32[40,640]{1,0:T(8,128)S(1)} %pad_maximum_fusion.1), channel_id=1, source_target_pairs={{0,4},{4,8},{8,12},{1,5},{5,9},{9,13},{2,6},{6,10},{10,14},{3,7},{... | collective-permute-start | bytes 307208 | tf_op jit(solution)/shard_map/ppermute | solution.py:842
  116.3 1.3 %collective-permute-start.14 = (f32[40,256]{1,0:T(8,128)S(1)}, f32[40,256]{1,0:T(8,128)S(1)}, u32[]{:S(2)}, u32[]{:S(2)}) collective-permute-start(f32[40,256]{1,0:T(8,128)S(1)} %slice.49), channel_id=1, source_target_pairs={{0,8},{4,12},{1,9},{5,13},{2,10},{6,14},{3,11},{7,15},{16,24},{20,... | collective-permute-start | bytes 122888 | tf_op jit(solution)/shard_map/ppermute | solution.py:846
  117.6 1.6 %collective-permute-done.14 = f32[40,256]{1,0:T(8,128)S(1)} collective-permute-done((f32[40,256]{1,0:T(8,128)S(1)}, f32[40,256]{1,0:T(8,128)S(1)}, u32[]{:S(2)}, u32[]{:S(2)}) %collective-permute-start.14) | collective-permute-done | bytes 40992 | tf_op jit(solution)/shard_map/ppermute | solution.py:846
  120.3 3.7 %collective-permute-done.16 = f32[40,640]{1,0:T(8,128)S(1)} collective-permute-done((f32[40,640]{1,0:T(8,128)S(1)}, f32[40,640]{1,0:T(8,128)S(1)}, u32[]{:S(2)}, u32[]{:S(2)}) %collective-permute-start.16) | collective-permute-done | bytes 102432 | tf_op jit(solution)/shard_map/ppermute | solution.py:849
  125.4 2.4 %finish.1 = (f32[3,8,16,16]{3,2,1,0:T(8,128)}, bf16[3,8,16,384]{3,2,1,0:T(8,128)(2,1)}) custom-call(s32[8]{0:T(128)S(1)} %fusion.42.scalars, f32[40,640]{1,0:T(8,128)S(1)} %add.86.mine, f32[40,640]{1,0:T(8,128)S(1)} %collective-permute-done.17.other, f32[320,80]{1,0:T(8,128)S(1)} %bitcast.46, bf16[320,512]{1,0:T(8,128)(2,1)S(1)} %copy-done.10, ...), custom_call_target="tpu_custom_call" | custom-call | tf_op jit(solution)/shard_map/finish/pallas_call | solution.py:769
  (110 shorter events, 22.7 us)
Async XLA Ops:
  0.6 72.1 %copy-start = (f32[384]{0:T(512)S(1)}, f32[384]{0:T(512)}, u32[]{:S(2)}) copy-start(f32[384]{0:T(512)} %param.21) | copy-start | bytes 4612
  0.6 7.8 %copy-start.1 = (bf16[384,2560]{1,0:T(8,128)(2,1)S(1)}, bf16[384,2560]{1,0:T(8,128)(2,1)}, u32[]{:S(2)}) copy-start(bf16[384,2560]{1,0:T(8,128)(2,1)} %refs_0_.13) | copy-start | bytes 5898244
  5.5 3.0 %collective-permute-start = (bf16[384,1280]{1,0:T(8,128)(2,1)}, bf16[384,1280]{1,0:T(8,128)(2,1)}, u32[]{:S(2)}, u32[]{:S(2)}) collective-permute-start(bf16[384,1280]{1,0:T(8,128)(2,1)} %pack_handed.1), channel_id=1, source_target_pairs={{0,1},{1,0},{2,3},{3,2},{4,5},{5,4},{6,7},{7,6},{8,9},{9,8},{10,11... | collective-permute-start | bytes 2949128 | tf_op jit(solution)/shard_map/ppermute | solution.py:542
  18.8 15.1 %copy-start.22 = (f32[3,8,16,16]{3,2,1,0:T(8,128)S(1)}, f32[3,8,16,16]{3,2,1,0:T(8,128)}, u32[]{:S(2)}) copy-start(f32[3,8,16,16]{3,2,1,0:T(8,128)} %param.19) | copy-start | bytes 73732
  18.8 21.7 %copy-start.8 = (bf16[2560,64]{0,1:T(8,128)(2,1)S(1)}, bf16[2560,64]{0,1:T(8,128)(2,1)}, u32[]{:S(2)}) copy-start(bf16[2560,64]{0,1:T(8,128)(2,1)} %param.18) | copy-start | bytes 983044
  18.8 21.7 %copy-start.24 = (f32[2560]{0:T(1024)S(1)}, f32[2560]{0:T(1024)}, u32[]{:S(2)}) copy-start(f32[2560]{0:T(1024)} %param.17) | copy-start | bytes 30724
  22.1 20.2 %copy-start.25 = (s32[4,4]{1,0:T(4,128)S(1)}, s32[4,4]{1,0:T(4,128)}, u32[]{:S(2)}) copy-start(s32[4,4]{1,0:T(4,128)} %param.15) | copy-start | bytes 196
  22.1 25.7 %collective-permute-start.2 = (bf16[768,256]{1,0:T(8,128)(2,1)}, bf16[768,256]{1,0:T(8,128)(2,1)}, u32[]{:S(2)}, u32[]{:S(2)}) collective-permute-start(bf16[768,256]{1,0:T(8,128)(2,1)} %get-tuple-element.26), channel_id=1, source_target_pairs={{4,12},{5,13},{6,14},{7,15},{20,28},{21,29},{22,30},{23,31}} | collective-permute-start | bytes 1179656 | tf_op jit(solution)/shard_map/ppermute | solution.py:543
  25.0 30.4 %collective-permute-start.3 = (bf16[768,256]{1,0:T(8,128)(2,1)}, bf16[768,256]{1,0:T(8,128)(2,1)}, u32[]{:S(2)}, u32[]{:S(2)}) collective-permute-start(bf16[768,256]{1,0:T(8,128)(2,1)} %get-tuple-element.26), channel_id=1, source_target_pairs={{0,12},{1,13},{2,14},{3,15},{16,28},{17,29},{18,30},{19,31}} | collective-permute-start | bytes 1179656 | tf_op jit(solution)/shard_map/ppermute | solution.py:543
  32.6 53.1 %collective-permute-start.4 = (bf16[1152,384]{1,0:T(8,128)(2,1)}, bf16[1152,384]{1,0:T(8,128)(2,1)}, u32[]{:S(2)}, u32[]{:S(2)}) collective-permute-start(bf16[1152,384]{1,0:T(8,128)(2,1)} %copy-done.12), channel_id=1, source_target_pairs={{4,0},{8,4},{12,8},{5,1},{9,5},{13,9},{6,2},{10,6},{14,10},{7,3},{... | collective-permute-start | bytes 2654216 | tf_op jit(solution)/shard_map/ppermute | solution.py:543
  35.8 6.5 %copy-start.18 = (f32[8,16,48]{2,1,0:T(8,128)}, f32[8,16,48]{2,1,0:T(8,128)S(1)}, u32[]{:S(2)}) copy-start(f32[8,16,48]{2,1,0:T(8,128)S(1)} %reshape.31) | copy-start | bytes 73732
  35.9 10.6 %collective-permute-start.18 = (f32[8,16,32]{2,1,0:T(8,128)S(1)}, f32[8,16,32]{2,1,0:T(8,128)S(1)}, u32[]{:S(2)}, u32[]{:S(2)}) collective-permute-start(f32[8,16,32]{2,1,0:T(8,128)S(1)} %slice.50), channel_id=1, source_target_pairs={{0,4},{4,8},{8,12},{1,5},{5,9},{9,13},{2,6},{6,10},{10,14},{3,7},{... | collective-permute-start | bytes 49160 | tf_op jit(solution)/shard_map/ppermute | solution.py:45
  40.8 4.0 %collective-permute-start.21 = (f32[64,2]{1,0:T(8,128)S(1)}, f32[64,2]{1,0:T(8,128)}, u32[]{:S(2)}, u32[]{:S(2)}) collective-permute-start(f32[64,2]{1,0:T(8,128)S(1)} %copy.34), channel_id=1, source_target_pairs={{0,2},{2,0},{1,3},{3,1},{4,6},{6,4},{5,7},{7,5},{8,10},{10,8},{9,1... | collective-permute-start | bytes 1544 | tf_op jit(solution)/shard_map/ppermute | solution.py:831
  44.9 53.1 %collective-permute-start.5 = (bf16[1152,384]{1,0:T(8,128)(2,1)}, bf16[1152,384]{1,0:T(8,128)(2,1)}, u32[]{:S(2)}, u32[]{:S(2)}) collective-permute-start(bf16[1152,384]{1,0:T(8,128)(2,1)} %copy-done.11), channel_id=1, source_target_pairs={{12,4},{13,5},{14,6},{15,7},{28,20},{29,21},{30,22},{31,23}} | collective-permute-start | bytes 2654216 | tf_op jit(solution)/shard_map/ppermute | solution.py:543
  46.5 13.5 %copy-start.20 = (f32[8,16,32]{2,1,0:T(8,128)}, f32[8,16,32]{2,1,0:T(8,128)S(1)}, u32[]{:S(2)}) copy-start(f32[8,16,32]{2,1,0:T(8,128)S(1)} %collective-permute-done.18) | copy-start | bytes 49156
  46.5 28.0 %collective-permute-start.1 = (bf16[1152,256]{1,0:T(8,128)(2,1)}, bf16[1152,256]{1,0:T(8,128)(2,1)}, u32[]{:S(2)}, u32[]{:S(2)}) collective-permute-start(bf16[1152,256]{1,0:T(8,128)(2,1)} %copy-done.14), channel_id=1, source_target_pairs={{8,12},{4,0},{9,13},{5,1},{10,14},{6,2},{11,15},{7,3},{24,28},{20,... | collective-permute-start | bytes 1769480 | tf_op jit(solution)/shard_map/ppermute | solution.py:543
  47.8 28.0 %collective-permute-start.6 = (bf16[768,384]{1,0:T(8,128)(2,1)}, bf16[768,384]{1,0:T(8,128)(2,1)}, u32[]{:S(2)}, u32[]{:S(2)}) collective-permute-start(bf16[768,384]{1,0:T(8,128)(2,1)} %copy-done.13), channel_id=1, source_target_pairs={{0,4},{4,8},{1,5},{5,9},{2,6},{6,10},{3,7},{7,11},{16,20},{20,24},... | collective-permute-start | bytes 1769480 | tf_op jit(solution)/shard_map/ppermute | solution.py:543
  55.4 22.1 %collective-permute-start.7 = (bf16[768,384]{1,0:T(8,128)(2,1)}, bf16[768,384]{1,0:T(8,128)(2,1)}, u32[]{:S(2)}, u32[]{:S(2)}) collective-permute-start(bf16[768,384]{1,0:T(8,128)(2,1)} %get-tuple-element.28), channel_id=1, source_target_pairs={{0,8},{1,9},{2,10},{3,11},{16,24},{17,25},{18,26},{19,27}} | collective-permute-start | bytes 1769480 | tf_op jit(solution)/shard_map/ppermute | solution.py:543
  74.5 30.7 %collective-permute-start.8 = (bf16[1152,128]{1,0:T(8,128)(2,1)}, bf16[1152,128]{1,0:T(8,128)(2,1)S(1)}, u32[]{:S(2)}, u32[]{:S(2)}) collective-permute-start(bf16[1152,128]{1,0:T(8,128)(2,1)} %copy-done.16), channel_id=1, source_target_pairs={{4,0},{8,4},{12,8},{5,1},{9,5},{13,9},{6,2},{10,6},{14,10},{7,3},{... | collective-permute-start | bytes 884744 | tf_op jit(solution)/shard_map/ppermute | solution.py:543
  75.8 29.4 %collective-permute-start.9 = (bf16[1152,128]{1,0:T(8,128)(2,1)}, bf16[1152,128]{1,0:T(8,128)(2,1)S(1)}, u32[]{:S(2)}, u32[]{:S(2)}) collective-permute-start(bf16[1152,128]{1,0:T(8,128)(2,1)} %copy-done.15), channel_id=1, source_target_pairs={{12,4},{13,5},{14,6},{15,7},{28,20},{29,21},{30,22},{31,23}} | collective-permute-start | bytes 884744 | tf_op jit(solution)/shard_map/ppermute | solution.py:543
  77.5 27.6 %collective-permute-start.10 = (bf16[768,128]{1,0:T(8,128)(2,1)}, bf16[768,128]{1,0:T(8,128)(2,1)S(1)}, u32[]{:S(2)}, u32[]{:S(2)}) collective-permute-start(bf16[768,128]{1,0:T(8,128)(2,1)} %copy-done.17), channel_id=1, source_target_pairs={{0,4},{4,8},{1,5},{5,9},{2,6},{6,10},{3,7},{7,11},{16,20},{20,24},... | collective-permute-start | bytes 589832 | tf_op jit(solution)/shard_map/ppermute | solution.py:543
  85.6 19.5 %collective-permute-start.11 = (bf16[768,128]{1,0:T(8,128)(2,1)S(1)}, bf16[768,128]{1,0:T(8,128)(2,1)S(1)}, u32[]{:S(2)}, u32[]{:S(2)}) collective-permute-start(bf16[768,128]{1,0:T(8,128)(2,1)S(1)} %get-tuple-element.33), channel_id=1, source_target_pairs={{0,8},{1,9},{2,10},{3,11},{16,24},{17,25},{18,26},{19,27}} | collective-permute-start | bytes 589832 | tf_op jit(solution)/shard_map/ppermute | solution.py:543
  97.9 11.5 %collective-permute-start.19 = (f32[8,80]{1,0:T(8,128)S(1)}, f32[8,80]{1,0:T(8,128)S(1)}, u32[]{:S(2)}, u32[]{:S(2)}) collective-permute-start(f32[8,80]{1,0:T(8,128)S(1)} %select_bitcast_fusion.2), channel_id=1, source_target_pairs={{0,1},{1,0},{2,3},{3,2},{4,5},{5,4},{6,7},{7,6},{8,9},{9,8},{10,11... | collective-permute-start | bytes 7688 | tf_op jit(solution)/shard_map/ppermute | solution.py:648
  108.8 16.6 %copy-start.9 = (bf16[3,240,1152]{2,1,0:T(8,128)(2,1)S(1)}, bf16[3,240,1152]{2,1,0:T(8,128)(2,1)}, u32[]{:S(2)}) copy-start(bf16[3,240,1152]{2,1,0:T(8,128)(2,1)} %reshape.34.band) | copy-start | bytes 4976644
  108.8 16.6 %copy-start.10 = (bf16[320,512]{1,0:T(8,128)(2,1)S(1)}, bf16[320,512]{1,0:T(8,128)(2,1)}, u32[]{:S(2)}) copy-start(bf16[320,512]{1,0:T(8,128)(2,1)} %fusion.30.selector) | copy-start | bytes 983044
  108.9 2.2 %collective-permute-start.12 = (f32[3,40,384]{2,1,0:T(8,128)S(1)}, f32[3,40,384]{2,1,0:T(8,128)S(1)}, u32[]{:S(2)}, u32[]{:S(2)}) collective-permute-start(f32[3,40,384]{2,1,0:T(8,128)S(1)} %constant_dynamic-slice_fusion), channel_id=1, source_target_pairs={{0,1},{1,0},{2,3},{3,2},{4,5},{5,4},{6,7},{7,6},{8,9},{9,8},{10,11... | collective-permute-start | bytes 552968 | tf_op jit(solution)/shard_map/ppermute | solution.py:839
  109.6 10.8 %collective-permute-start.20 = (f32[32,80]{1,0:T(8,128)S(1)}, f32[32,80]{1,0:T(8,128)S(1)}, u32[]{:S(2)}, u32[]{:S(2)}) collective-permute-start(f32[32,80]{1,0:T(8,128)S(1)} %fusion.34), channel_id=1, source_target_pairs={{0,2},{2,0},{1,3},{3,1},{4,6},{6,4},{5,7},{7,5},{8,10},{10,8},{9,1... | collective-permute-start | bytes 30728 | tf_op jit(solution)/shard_map/ppermute | solution.py:660
  111.2 8.1 %collective-permute-start.13 = (f32[40,640]{1,0:T(8,128)S(1)}, f32[40,640]{1,0:T(8,128)S(1)}, u32[]{:S(2)}, u32[]{:S(2)}) collective-permute-start(f32[40,640]{1,0:T(8,128)S(1)} %pad_maximum_fusion.1), channel_id=1, source_target_pairs={{0,4},{4,8},{8,12},{1,5},{5,9},{9,13},{2,6},{6,10},{10,14},{3,7},{... | collective-permute-start | bytes 307208 | tf_op jit(solution)/shard_map/ppermute | solution.py:842
  115.7 3.6 %collective-permute-start.15 = (f32[40,384]{1,0:T(8,128)S(1)}, f32[40,384]{1,0:T(8,128)S(1)}, u32[]{:S(2)}, u32[]{:S(2)}) collective-permute-start(f32[40,384]{1,0:T(8,128)S(1)} %get-tuple-element.45), channel_id=1, source_target_pairs={{4,12},{12,8},{5,13},{13,9},{6,14},{14,10},{7,15},{15,11},{20,28},... | collective-permute-start | bytes 184328 | tf_op jit(solution)/shard_map/ppermute | solution.py:845
  116.3 3.0 %collective-permute-start.14 = (f32[40,256]{1,0:T(8,128)S(1)}, f32[40,256]{1,0:T(8,128)S(1)}, u32[]{:S(2)}, u32[]{:S(2)}) collective-permute-start(f32[40,256]{1,0:T(8,128)S(1)} %slice.49), channel_id=1, source_target_pairs={{0,8},{4,12},{1,9},{5,13},{2,10},{6,14},{3,11},{7,15},{16,24},{20,... | collective-permute-start | bytes 122888 | tf_op jit(solution)/shard_map/ppermute | solution.py:846
  119.3 4.7 %collective-permute-start.16 = (f32[40,640]{1,0:T(8,128)S(1)}, f32[40,640]{1,0:T(8,128)S(1)}, u32[]{:S(2)}, u32[]{:S(2)}) collective-permute-start(f32[40,640]{1,0:T(8,128)S(1)} %fusion.32), channel_id=1, source_target_pairs={{0,2},{2,0},{1,3},{3,1},{4,6},{6,4},{5,7},{7,5},{8,10},{10,8},{9,1... | collective-permute-start | bytes 307208 | tf_op jit(solution)/shard_map/ppermute | solution.py:849
  124.1 1.4 %collective-permute-start.17 = (f32[40,640]{1,0:T(8,128)S(1)}, f32[40,640]{1,0:T(8,128)S(1)}, u32[]{:S(2)}, u32[]{:S(2)}) collective-permute-start(f32[40,640]{1,0:T(8,128)S(1)} %add.86.mine), channel_id=1, source_target_pairs={{0,1},{1,0},{2,3},{3,2},{4,5},{5,4},{6,7},{7,6},{8,9},{9,8},{10,11... | collective-permute-start | bytes 307208 | tf_op jit(solution)/shard_map/ppermute | solution.py:850
  (16 other events, 31.2 us)

commit v4 on v2

--- a/solution.py
+++ b/solution.py
@@ -223,6 +223,7 @@
 QUERY_ROWS = 192
 SWAP = [(0, 1), (1, 0)]
 WINDOW = 32
+GRANT = 20 << 20
 
 OWN, OTHER, DOWN, UP, MAIN, PLACE, SLAB = range(7)
 
@@ -251,10 +252,10 @@
     return row + lax.axis_index("slab") * jnp.array(by_slab)
 
 
-def pack_kernel(copies, scalars, *refs):
-    ins, outs, semaphores = refs[: copies[0]], refs[copies[0] : -1], refs[-1]
+def pack_kernel(inputs, copies, scalars, *refs):
+    ins, outs, semaphores = refs[:inputs], refs[inputs:-1], refs[-1]
     started = []
-    for number, (source, row, rows, entries, shift, target, at, heads) in enumerate(copies[1]):
+    for number, (source, row, rows, entries, shift, target, at, heads) in enumerate(copies):
         head = shift
         for entry in entries:
             head = head + scalars[entry]
@@ -273,21 +274,22 @@
 def pack(scalars, arrays, shapes, copies, name):
     moved = sum(2 * 2 * rows * heads * HD for _, _, rows, _, _, _, _, heads in copies)
     return pl.pallas_call(
-        functools.partial(pack_kernel, (len(arrays), copies)),
+        functools.partial(pack_kernel, len(arrays), copies),
         name=name,
         out_shape=[jax.ShapeDtypeStruct(shape, jnp.bfloat16) for shape in shapes],
         grid_spec=pltpu.PrefetchScalarGridSpec(
             num_scalar_prefetch=1,
             grid=(1,),
             in_specs=[pl.BlockSpec(memory_space=pl.ANY)] * len(arrays),
-            out_specs=[pl.BlockSpec(memory_space=pl.ANY)] * len(shapes),
+            out_specs=[pl.BlockSpec(shape, lambda i, scalars: (0, 0)) for shape in shapes],
             scratch_shapes=[pltpu.SemaphoreType.DMA((len(copies),))],
         ),
+        compiler_params=pltpu.CompilerParams(vmem_limit_bytes=GRANT),
         cost_estimate=pl.CostEstimate(flops=0, bytes_accessed=moved, transcendentals=0),
     )(scalars, *arrays)
 
 
-def pack_messages(scalars, queries, keys, values, received, messages, name):
+def pack_messages(scalars, messages, queries, keys, values, received, name):
     rows = queries.shape[0]
     half = rows // 2
     copies, shapes = [], []
@@ -476,10 +478,12 @@
         ]
         arrays += [queries, keys, values, received, weight, gain]
     in_specs += [
-        pl.BlockSpec((payload.shape[0], HD), lambda i, scalars, mask: (0, i))
-        for payload in payloads
+        pl.BlockSpec(
+            (payload.shape[0], HD), lambda i, scalars, mask, start=start: (0, start + i)
+        )
+        for payload, start in payloads
     ]
-    arrays += payloads
+    arrays += [payload for payload, _ in payloads]
     pairs = steps * max(sum(len(task[3]) for task in tasks) for tasks in variants.values())
     span_count = math.isqrt(mask.shape[0])
     return pl.pallas_call(
@@ -496,7 +500,7 @@
                 pltpu.VMEM((SLOTS, rows, HD), jnp.float32),
             ],
         ),
-        compiler_params=pltpu.CompilerParams(vmem_limit_bytes=40 << 20),
+        compiler_params=pltpu.CompilerParams(vmem_limit_bytes=GRANT),
         cost_estimate=pl.CostEstimate(
             flops=pairs * 4 * rows * rows * HD,
             bytes_accessed=steps * HD * 2 * sum(spec.block_shape[0] for spec in in_specs[:4]),
@@ -508,6 +512,9 @@
 def token_sums(scalars, queries, keys, values, span_mask, head_gain, patch_weight):
     rows = queries.shape[0]
     heads = NEAR_HEADS + MIDDLE_HEADS + FAR_HEADS
+    queries, keys, values = (
+        pltpu.with_memory_space_constraint(array, pltpu.HBM) for array in (queries, keys, values)
+    )
     half = rows // 2
     (handed,) = pack(
         scalars,
@@ -517,35 +524,45 @@
         "pack_handed",
     )
     received = lax.ppermute(handed, "slab", SWAP)
-    bring = functools.partial(pack_messages, scalars, queries, keys, values, received)
     send = lambda value, *pairs: lax.ppermute(value, "span", list(pairs))
 
-    down, up = bring([(DOWN, 0, EARLY, True), (UP, 0, EARLY, False)], "pack_first")
-    anchor = down
-    down_two, up_two = bring(
-        [(None, 0, EARLY, True), (None, MIDDLE, EARLY, False)], "pack_second"
-    )
-    far_all, far_pair, late_down, late_down_two, late_up, late_up_two = bring(
+    def bring(messages, source, name):
+        return pack_messages(scalars, messages, queries, keys, values, source, name)
+
+    down, up, down_two, up_two = bring(
+        [
+            (DOWN, 0, EARLY, True),
+            (UP, 0, NEAR_HEADS, False),
+            (None, 0, EARLY, True),
+            (None, MIDDLE, EARLY, False),
+        ],
+        received,
+        "pack_first",
+    )
+    down = send(down, (1, 0), (2, 1), (3, 2))
+    up = send(up, (0, 1), (1, 2))
+    down_two = send(down_two, (3, 1))
+    up_two = send(up_two, (0, 2))
+    source, _ = lax.optimization_barrier((received, up))
+    far_all, far_pair, late_down, late_down_two, late_up_two = bring(
         [
             (None, FAR, FAR_HEADS, True),
             (None, FAR, FAR_HEADS, False),
             (DOWN, EARLY, LATE, True),
             (None, EARLY, LATE, True),
-            (UP, EARLY, LATE, False),
             (None, MIDDLE + EARLY, LATE, False),
         ],
-        "pack_third",
-    )
-    down = send(down, (1, 0), (2, 1), (3, 2))
-    up = send(up, (0, 1), (1, 2))
-    down_two = send(down_two, (3, 1))
-    up_two = send(up_two, (0, 2))
+        source,
+        "pack_second",
+    )
     far_two = send(far_pair, (1, 3))
     far_three = send(far_pair, (0, 3))
     far_next = send(far_all, (2, 3), (1, 0))
+    late_down, late_down_two, late_up_two, _ = lax.optimization_barrier(
+        (late_down, late_down_two, late_up_two, down)
+    )
     late_down = send(late_down, (1, 0), (2, 1), (3, 2))
     late_down_two = send(late_down_two, (3, 1))
-    late_up = send(late_up, (0, 1), (1, 2))
     late_up_two = send(late_up_two, (0, 2))
 
     mask = span_mask.reshape(-1)
@@ -575,36 +592,39 @@
     }
     run = functools.partial(attend, own=own, scalars=scalars, mask=mask)
     sums = run(
+        EARLY,
+        (MAIN,),
+        0,
+        sums=sums,
+        payloads=[(down, 0), (down_two, 0), (up, 0), (up_two, 0)],
+        variants=main,
+        more=False,
+        name="early_heads",
+    )
+    sums = run(
         FAR_HEADS,
         (),
         FAR,
         sums=sums,
-        payloads=[far_next, far_two, far_three],
+        payloads=[(far_next, 0), (far_two, 0), (far_three, 0)],
         variants=far,
         more=True,
         name="far_heads",
     )
-    sums = run(
-        EARLY,
-        (MAIN,),
-        0,
-        sums=sums,
-        payloads=[down, down_two, up, up_two],
-        variants=main,
-        more=False,
-        name="early_heads",
-    )
-    sums = run(
-        LATE,
-        (MAIN,),
-        EARLY,
-        sums=sums,
-        payloads=[late_down, late_down_two, late_up, late_up_two],
-        variants=main,
-        more=False,
-        name="late_heads",
-    )
-    return sums, anchor
+
+    def last(sums):
+        return run(
+            LATE,
+            (MAIN,),
+            EARLY,
+            sums=sums,
+            payloads=[(late_down, 0), (late_down_two, 0), (up, EARLY), (late_up_two, 0)],
+            variants=main,
+            more=False,
+            name="late_heads",
+        )
+
+    return sums, last, up_two
 
 
 def noise_window(noisy_latent):
@@ -745,7 +765,7 @@
         in_specs=[pl.BlockSpec(memory_space=pltpu.SMEM)] + [whole] * 7,
         out_specs=(whole, whole),
         scratch_shapes=[pltpu.VMEM((rows + 8, (frames + 2) * channels), jnp.float32)],
-        compiler_params=pltpu.CompilerParams(vmem_limit_bytes=32 << 20),
+        compiler_params=pltpu.CompilerParams(vmem_limit_bytes=GRANT),
     )(scalars, mine, other, noise, selector, band, bias, constants)
 
 
@@ -780,7 +800,7 @@
     place = lax.axis_index("span")
     slab = lax.axis_index("slab")
     scalars = scalar_operand(heads_dev // lax.axis_size("slab"))
-    sums, anchor = token_sums(
+    sums, last, anchor = token_sums(
         scalars, queries, keys, values, span_mask, head_gain, patch_weight
     )
 
@@ -801,7 +821,11 @@
     selector = cell_selector(height, breadth)
     band = banded_weight(taps)
     bias = jnp.tile(bias, FRAMES_SPAN)[None, :]
-
+    sums, noise, constants, selector, band, bias = lax.optimization_barrier(
+        (sums, noise, constants, selector, band, bias)
+    )
+
+    sums = last(sums)
     half = sums.shape[1] // 2
     mine = lax.dynamic_slice_in_dim(sums, slab * half, half, 1)
     theirs = lax.dynamic_slice_in_dim(sums, (1 - slab) * half, half, 1)

time: 292 us -> 120 us (0.41)
  Pallas kernels: 207 us -> 29.7 us
  waiting for transfers between devices: 20.4 us -> 31.7 us
  starting transfers between devices: 44.7 us -> 35.5 us
    pallas_call x4 -> x3, Pallas kernels: 186 us -> 8.23 us  [pack(): pl.pallas_call(functools.partial(pack_kernel, len(arrays), copies), name=...]
    ppermute x1, waiting for transfers between devices: 0.01 us -> 12.5 us  [from_behind(): return lax.ppermute(value, axis, pairs)]
    ppermute x11 -> x10, starting transfers between devices: 29.3 us -> 24.5 us  [token_sums(): send = lambda value, *pairs: lax.ppermute(value, 'span', list(pairs))]
    ppermute x1, starting transfers between devices: 4.55 us -> 1.29 us  [from_behind(): return lax.ppermute(value, axis, pairs)]
    ppermute x11 -> x10, waiting for transfers between devices: 11.2 us -> 8.08 us  [token_sums(): send = lambda value, *pairs: lax.ppermute(value, 'span', list(pairs))]
    unnamed x40 -> x50, local copies, waits for them, and re-layouts: 5.46 us -> 5.98 us
  transfers between devices with their start and end apart: 22 -> 21, of which waited for: 7 -> 7; matrix products, arithmetic and copies ran while one was open for 4% -> 13% of each run, Pallas kernels for 38% -> 15%
where the time goes in v4:
time: 120 us; the launch traced here: 119 us
  starting transfers between devices  35.5 us (30%)
  waiting for transfers between devices  31.7 us (26%)
  Pallas kernels  29.7 us (25%)
  local copies, waits for them, and re-layouts  14.6 us (12%)
  other arithmetic  5.91 us (5%)
  between operations  1.29 us (1%)
    ppermute x10, starting transfers between devices, token_sums(): send = lambda value, *pairs: lax.ppermute(value, 'span', list(pairs))  24.5 us
    pallas_call x3, Pallas kernels, attend(): pl.pallas_call(functools.partial(attend_kernel, variants, extra, span_cou...  19.1 us
    ppermute x1, waiting for transfers between devices, from_behind(): return lax.ppermute(value, axis, pairs)  12.5 us
    pallas_call x3, Pallas kernels, pack(): pl.pallas_call(functools.partial(pack_kernel, len(arrays), copies), name=...  8.23 us
    ppermute x10, waiting for transfers between devices, token_sums(): send = lambda value, *pairs: lax.ppermute(value, 'span', list(pairs))  8.08 us
    unnamed x50, local copies, waits for them, and re-layouts  5.98 us
    ppermute x1, waiting for transfers between devices, per_device(): total = total + lax.ppermute(total, 'head', SWAP)  4.13 us
    reshape x1, local copies, waits for them, and re-layouts, banded_weight(): banded.transpose(1, 2, 0, 3, 4, 5)  4.06 us
  transfers between devices with their start and end apart: 21, of which 7 were waited for; matrix products, arithmetic and copies ran while one was open for 13% of the time, Pallas kernels for 15%

profile of v4, /device:TPU:0, one launch (start us, length us, event | category | flops | bytes accessed | tf_op | source)
XLA Modules:
  0.0 118.7 jit_solution(9548879282814114271)
XLA Ops:
  1.4 1.7 %pack_handed.1 = bf16[384,1280]{1,0:T(8,128)(2,1)S(1)} custom-call(s32[8]{0:T(128)S(1)} %fusion.42.scalars, bf16[192,2560]{1,0:T(8,128)(2,1)} %refs_1_.11, bf16[192,2560]{1,0:T(8,128)(2,1)} %refs_2_.9), custom_call_target="tpu_custom_call" | custom-call | bytes 1966080 | tf_op jit(solution)/shard_map/pack_handed/pallas_call | solution.py:276
  3.8 2.0 %collective-permute-done.refs_3_.refs_10_ = bf16[384,1280]{1,0:T(8,128)(2,1)S(1)} collective-permute-done((bf16[384,1280]{1,0:T(8,128)(2,1)S(1)}, bf16[384,1280]{1,0:T(8,128)(2,1)S(1)}, u32[]{:S(2)}, u32[]{:S(2)}) %collective-permute-start) | collective-permute-done | bytes 983072 | tf_op jit(solution)/shard_map/ppermute | solution.py:526
  5.8 3.5 %pack_first.1 = (bf16[1152,384]{1,0:T(8,128)(2,1)}, bf16[768,512]{1,0:T(8,128)(2,1)S(1)}, bf16[1152,384]{1,0:T(8,128)(2,1)}, bf16[768,384]{1,0:T(8,128)(2,1)S(1)}) custom-call(s32[8]{0:T(128)S(1)} %fusion.42.scalars, bf16[384,2560]{1,0:T(8,128)(2,1)} %refs_0_.11, bf16[192,2560]{1,0:T(8,128)(2,1)} %refs_1_.11, bf16[192,2560]{1,0:T(8,128)(2,1)} %refs_2_.9, ...), custom_call_target="tpu_custom_call" | custom-call | bytes 6291456 | tf_op jit(solution)/shard_map/pack_first/pallas_call | solution.py:276
  9.3 6.0 %collective-permute-start.4 = (bf16[768,384]{1,0:T(8,128)(2,1)S(1)}, bf16[768,384]{1,0:T(8,128)(2,1)S(1)}, u32[]{:S(2)}, u32[]{:S(2)}) collective-permute-start(bf16[768,384]{1,0:T(8,128)(2,1)S(1)} %get-tuple-element.30), channel_id=1, source_target_pairs={{0,8},{1,9},{2,10},{3,11},{16,24},{17,25},{18,26},{19,27}} | collective-permute-start | bytes 1769480 | tf_op jit(solution)/shard_map/ppermute | solution.py:527
  15.3 1.4 %fusion.30.selector = bf16[320,512]{1,0:T(8,128)(2,1)} fusion(s32[320]{0:T(512)S(1)} %get-tuple-element.67, s32[320]{0:T(512)S(1)} %get-tuple-element.68, s32[]{:T(128)S(6)} %mul.56, s32[320]{0:T(512)S(1)} %get-tuple-element.66, s32[320]{0:T(512)S(1)} %get-tuple-element.69, s32[]{:T(128)S(6)} %mul.55, pred[320]{0:T(512)(128)(4,1)S(1)} %get-tuple-element.71, ...), kind=kLoop, calls=%fused_computation.47 | loop fusion | flops 10158080 | bytes 333448 | tf_op jit(solution)/shard_map/convert_element_type | solution.py:664
  16.7 1.3 %collective-permute-start.3 = (bf16[768,512]{1,0:T(8,128)(2,1)S(1)}, bf16[768,512]{1,0:T(8,128)(2,1)S(1)}, u32[]{:S(2)}, u32[]{:S(2)}) collective-permute-start(bf16[768,512]{1,0:T(8,128)(2,1)S(1)} %get-tuple-element.29), channel_id=1, source_target_pairs={{0,4},{4,8},{1,5},{5,9},{2,6},{6,10},{3,7},{7,11},{16,20},{20,24},... | collective-permute-start | bytes 2359304 | tf_op jit(solution)/shard_map/ppermute | solution.py:527
  18.0 1.3 %collective-permute-start.1 = (bf16[1152,384]{1,0:T(8,128)(2,1)}, bf16[1152,384]{1,0:T(8,128)(2,1)}, u32[]{:S(2)}, u32[]{:S(2)}) collective-permute-start(bf16[1152,384]{1,0:T(8,128)(2,1)} %get-tuple-element.27), channel_id=1, source_target_pairs={{4,0},{8,4},{12,8},{5,1},{9,5},{13,9},{6,2},{10,6},{14,10},{7,3},{... | collective-permute-start | bytes 2654216 | tf_op jit(solution)/shard_map/ppermute | solution.py:527
  19.3 1.6 %collective-permute-start.2 = (bf16[1152,384]{1,0:T(8,128)(2,1)}, bf16[1152,384]{1,0:T(8,128)(2,1)}, u32[]{:S(2)}, u32[]{:S(2)}) collective-permute-start(bf16[1152,384]{1,0:T(8,128)(2,1)} %get-tuple-element.28), channel_id=1, source_target_pairs={{12,4},{13,5},{14,6},{15,7},{28,20},{29,21},{30,22},{31,23}} | collective-permute-start | bytes 2654216 | tf_op jit(solution)/shard_map/ppermute | solution.py:527
  20.9 8.1 %collective-permute-done.4.refs_10_ = bf16[768,384]{1,0:T(8,128)(2,1)S(1)} collective-permute-done((bf16[768,384]{1,0:T(8,128)(2,1)S(1)}, bf16[768,384]{1,0:T(8,128)(2,1)S(1)}, u32[]{:S(2)}, u32[]{:S(2)}) %collective-permute-start.4) | collective-permute-done | bytes 589856 | tf_op jit(solution)/shard_map/ppermute | solution.py:527
  30.8 1.3 %collective-permute-start.8 = (f32[8,16,32]{2,1,0:T(8,128)S(1)}, f32[8,16,32]{2,1,0:T(8,128)S(1)}, u32[]{:S(2)}, u32[]{:S(2)}) collective-permute-start(f32[8,16,32]{2,1,0:T(8,128)S(1)} %slice.44), channel_id=1, source_target_pairs={{0,4},{4,8},{8,12},{1,5},{5,9},{9,13},{2,6},{6,10},{10,14},{3,7},{... | collective-permute-start | bytes 49160 | tf_op jit(solution)/shard_map/ppermute | solution.py:45
  32.4 1.5 %collective-permute-start.11 = (f32[64,2]{1,0:T(8,128)S(1)}, f32[64,2]{1,0:T(8,128)S(1)}, u32[]{:S(2)}, u32[]{:S(2)}) collective-permute-start(f32[64,2]{1,0:T(8,128)S(1)} %copy.33), channel_id=1, source_target_pairs={{0,2},{2,0},{1,3},{3,1},{4,6},{6,4},{5,7},{7,5},{8,10},{10,8},{9,1... | collective-permute-start | bytes 1544 | tf_op jit(solution)/shard_map/ppermute | solution.py:820
  33.9 12.5 %collective-permute-done.8 = f32[8,16,32]{2,1,0:T(8,128)S(1)} collective-permute-done((f32[8,16,32]{2,1,0:T(8,128)S(1)}, f32[8,16,32]{2,1,0:T(8,128)S(1)}, u32[]{:S(2)}, u32[]{:S(2)}) %collective-permute-start.8) | collective-permute-done | bytes 16416 | tf_op jit(solution)/shard_map/ppermute | solution.py:45
  46.7 1.4 %pad_bitcast_fusion.2 = (bf16[5,3,3,16,1,384]{5,3,2,1,0,4:T(8,128)(2,1)S(1)}, bf16[5,3,3,16,1,384]{5,3,2,1,0,4:T(8,128)(2,1)S(1)}, bf16[5,3,3,16,1,384]{5,3,2,1,0,4:T(8,128)(2,1)S(1)}) fusion(bf16[3,3,3,16,384]{4,3,2,1,0:T(8,128)(2,1)} %bitcast.48), kind=kLoop, calls=%fused_computation.51 | loop fusion | bytes 1990656 | tf_op jit(solution)/shard_map/stack | solution.py:670
  48.8 1.5 %collective-permute-start.10 = (f32[32,80]{1,0:T(8,128)}, f32[32,80]{1,0:T(8,128)}, u32[]{:S(2)}, u32[]{:S(2)}) collective-permute-start(f32[32,80]{1,0:T(8,128)} %fusion.34), channel_id=1, source_target_pairs={{0,2},{2,0},{1,3},{3,1},{4,6},{6,4},{5,7},{7,5},{8,10},{10,8},{9,1... | collective-permute-start | bytes 30728 | tf_op jit(solution)/shard_map/ppermute | solution.py:649
  50.3 3.0 %pack_second.1 = (bf16[1152,256]{1,0:T(8,128)(2,1)}, bf16[768,256]{1,0:T(8,128)(2,1)}, bf16[1152,128]{1,0:T(8,128)(2,1)S(1)}, bf16[1152,128]{1,0:T(8,128)(2,1)S(1)}, bf16[768,128]{1,0:T(8,128)(2,1)S(1)}) custom-call(s32[8]{0:T(128)S(1)} %fusion.42.scalars, bf16[384,2560]{1,0:T(8,128)(2,1)} %refs_0_.11, bf16[192,2560]{1,0:T(8,128)(2,1)} %refs_1_.11, ...), custom_call_target="tpu_custom_call" | custom-call | bytes 3538944 | tf_op jit(solution)/shard_map/pack_second/pallas_call | solution.py:276
  54.1 2.0 %collective-permute-start.7 = (bf16[768,256]{1,0:T(8,128)(2,1)}, bf16[768,256]{1,0:T(8,128)(2,1)}, u32[]{:S(2)}, u32[]{:S(2)}) collective-permute-start(bf16[768,256]{1,0:T(8,128)(2,1)} %get-tuple-element.33), channel_id=1, source_target_pairs={{0,12},{1,13},{2,14},{3,15},{16,28},{17,29},{18,30},{19,31}} | collective-permute-start | bytes 1179656 | tf_op jit(solution)/shard_map/ppermute | solution.py:527
  56.2 1.3 %collective-permute-start.5 = (bf16[1152,256]{1,0:T(8,128)(2,1)}, bf16[1152,256]{1,0:T(8,128)(2,1)}, u32[]{:S(2)}, u32[]{:S(2)}) collective-permute-start(bf16[1152,256]{1,0:T(8,128)(2,1)} %get-tuple-element.32), channel_id=1, source_target_pairs={{8,12},{4,0},{9,13},{5,1},{10,14},{6,2},{11,15},{7,3},{24,28},{20,... | collective-permute-start | bytes 1769480 | tf_op jit(solution)/shard_map/ppermute | solution.py:527
  58.7 2.5 %copy.34 = bf16[3,3,5,16,3,384]{5,4,3,2,1,0:T(4,128)(2,1)} copy(bf16[3,3,5,16,3,384]{5,3,1,0,2,4:T(8,128)(2,1)S(1)} %maximum_bitcast_fusion) | data formatting | bytes 3317760 | tf_op jit(solution)/shard_map/transpose | solution.py:677
  61.3 4.1 %reshape.34.band = bf16[3,240,1152]{2,1,0:T(8,128)(2,1)S(1)} reshape(bf16[3,3,5,16,3,384]{5,4,3,2,1,0:T(4,128)(2,1)} %copy.34) | data formatting | bytes 3317760 | tf_op jit(solution)/shard_map/reshape | solution.py:677
  67.5 1.3 %collective-permute-start.12 = (bf16[1152,128]{1,0:T(8,128)(2,1)}, bf16[1152,128]{1,0:T(8,128)(2,1)S(1)}, u32[]{:S(2)}, u32[]{:S(2)}) collective-permute-start(bf16[1152,128]{1,0:T(8,128)(2,1)} %copy-done.11), channel_id=1, source_target_pairs={{4,0},{8,4},{12,8},{5,1},{9,5},{13,9},{6,2},{10,6},{14,10},{7,3},{... | collective-permute-start | bytes 884744 | tf_op jit(solution)/shard_map/ppermute | solution.py:527
  70.5 8.3 %collective-permute-start.14 = (bf16[768,128]{1,0:T(8,128)(2,1)}, bf16[768,128]{1,0:T(8,128)(2,1)S(1)}, u32[]{:S(2)}, u32[]{:S(2)}) collective-permute-start(bf16[768,128]{1,0:T(8,128)(2,1)} %copy-done.12), channel_id=1, source_target_pairs={{0,8},{1,9},{2,10},{3,11},{16,24},{17,25},{18,26},{19,27}} | collective-permute-start | bytes 589832 | tf_op jit(solution)/shard_map/ppermute | solution.py:527
  78.9 1.1 copy-done.3
  81.1 7.0 %early_heads.1.refs_6_ = f32[3,80,384]{2,1,0:T(8,128)S(1)} custom-call(s32[8]{0:T(128)S(1)} %fusion.42.scalars, s32[16]{0:T(128)S(1)} %reshape.30.mask, bf16[384,2560]{1,0:T(8,128)(2,1)} %refs_0_.11, bf16[192,2560]{1,0:T(8,128)(2,1)} %refs_1_.11, bf16[192,2560]{1,0:T(8,128)(2,1)} %refs_2_.9, bf16[384,1280]{1,0:T(8,128)(2,1)S(1)} %collective-permute-done.refs_3_.refs_10_, ...), custom_call_target="tpu_custom_call" | custom-call | flops 2038431744 | bytes 884736 | tf_op jit(solution)/shard_map/early_heads/pallas_call | solution.py:489
  88.2 8.3 %far_heads.1.refs_6_ = f32[3,80,384]{2,1,0:T(8,128)S(1)} custom-call(s32[8]{0:T(128)S(1)} %fusion.42.scalars, s32[16]{0:T(128)S(1)} %reshape.30.mask, bf16[384,2560]{1,0:T(8,128)(2,1)} %refs_0_.11, bf16[192,2560]{1,0:T(8,128)(2,1)} %refs_1_.11, bf16[192,2560]{1,0:T(8,128)(2,1)} %refs_2_.9, bf16[384,1280]{1,0:T(8,128)(2,1)S(1)} %collective-permute-done.refs_3_.refs_10_, ...), custom_call_target="tpu_custom_call" | custom-call | flops 1056964608 | bytes 589824 | tf_op jit(solution)/shard_map/far_heads/pallas_call | solution.py:489
  97.1 3.7 %late_heads.1 = f32[3,80,384]{2,1,0:T(8,128)S(1)} custom-call(s32[8]{0:T(128)S(1)} %fusion.42.scalars, s32[16]{0:T(128)S(1)} %copy-done.10, bf16[384,2560]{1,0:T(8,128)(2,1)} %refs_0_.11, bf16[192,2560]{1,0:T(8,128)(2,1)} %refs_1_.11, bf16[192,2560]{1,0:T(8,128)(2,1)} %refs_2_.9, bf16[384,1280]{1,0:T(8,128)(2,1)S(1)} %collective-permute-done.refs_3_.refs_10_, ...), custom_call_target="tpu_custom_call" | custom-call | flops 679477248 | bytes 294912 | tf_op jit(solution)/shard_map/late_heads/pallas_call | solution.py:489
  101.0 1.4 %collective-permute-done.15 = f32[3,40,384]{2,1,0:T(8,128)S(1)} collective-permute-done((f32[3,40,384]{2,1,0:T(8,128)S(1)}, f32[3,40,384]{2,1,0:T(8,128)S(1)}, u32[]{:S(2)}, u32[]{:S(2)}) %collective-permute-start.15) | collective-permute-done | bytes 184352 | tf_op jit(solution)/shard_map/ppermute | solution.py:832
  102.4 1.3 %collective-permute-start.17 = (f32[40,256]{1,0:T(8,128)S(1)}, f32[40,256]{1,0:T(8,128)S(1)}, u32[]{:S(2)}, u32[]{:S(2)}) collective-permute-start(f32[40,256]{1,0:T(8,128)S(1)} %slice.50), channel_id=1, source_target_pairs={{0,8},{4,12},{1,9},{5,13},{2,10},{6,14},{3,11},{7,15},{16,24},{20,... | collective-permute-start | bytes 122888 | tf_op jit(solution)/shard_map/ppermute | solution.py:839
  104.4 3.5 %collective-permute-start.16 = (f32[40,640]{1,0:T(8,128)S(1)}, f32[40,640]{1,0:T(8,128)S(1)}, u32[]{:S(2)}, u32[]{:S(2)}) collective-permute-start(f32[40,640]{1,0:T(8,128)S(1)} %pad_maximum_fusion.1), channel_id=1, source_target_pairs={{0,4},{4,8},{8,12},{1,5},{5,9},{9,13},{2,6},{6,10},{10,14},{3,7},{... | collective-permute-start | bytes 307208 | tf_op jit(solution)/shard_map/ppermute | solution.py:835
  108.0 2.2 %collective-permute-done.16 = f32[40,640]{1,0:T(8,128)S(1)} collective-permute-done((f32[40,640]{1,0:T(8,128)S(1)}, f32[40,640]{1,0:T(8,128)S(1)}, u32[]{:S(2)}, u32[]{:S(2)}) %collective-permute-start.16) | collective-permute-done | bytes 102432 | tf_op jit(solution)/shard_map/ppermute | solution.py:835
  110.8 4.1 %collective-permute-done.19 = f32[40,640]{1,0:T(8,128)S(1)} collective-permute-done((f32[40,640]{1,0:T(8,128)S(1)}, f32[40,640]{1,0:T(8,128)S(1)}, u32[]{:S(2)}, u32[]{:S(2)}) %collective-permute-start.19) | collective-permute-done | bytes 102432 | tf_op jit(solution)/shard_map/ppermute | solution.py:842
  115.0 1.3 %collective-permute-done.20.other = f32[40,640]{1,0:T(8,128)S(1)} collective-permute-done((f32[40,640]{1,0:T(8,128)S(1)}, f32[40,640]{1,0:T(8,128)S(1)}, u32[]{:S(2)}, u32[]{:S(2)}) %collective-permute-start.20) | collective-permute-done | bytes 102432 | tf_op jit(solution)/shard_map/ppermute | solution.py:843
  116.3 2.4 %finish.1 = (f32[3,8,16,16]{3,2,1,0:T(8,128)}, bf16[3,8,16,384]{3,2,1,0:T(8,128)(2,1)}) custom-call(s32[8]{0:T(128)S(1)} %fusion.42.scalars, f32[40,640]{1,0:T(8,128)S(1)} %add.97.mine, f32[40,640]{1,0:T(8,128)S(1)} %collective-permute-done.20.other, f32[320,80]{1,0:T(8,128)S(1)} %bitcast.46, bf16[320,512]{1,0:T(8,128)(2,1)S(1)} %copy-done.5, ...), custom_call_target="tpu_custom_call" | custom-call | tf_op jit(solution)/shard_map/finish/pallas_call | solution.py:758
  (102 shorter events, 13.4 us)
Async XLA Ops:
  0.6 29.2 %copy-start = (f32[384]{0:T(512)S(1)}, f32[384]{0:T(512)}, u32[]{:S(2)}) copy-start(f32[384]{0:T(512)} %param.21) | copy-start | bytes 4612
  3.1 2.7 %collective-permute-start = (bf16[384,1280]{1,0:T(8,128)(2,1)S(1)}, bf16[384,1280]{1,0:T(8,128)(2,1)S(1)}, u32[]{:S(2)}, u32[]{:S(2)}) collective-permute-start(bf16[384,1280]{1,0:T(8,128)(2,1)S(1)} %pack_handed.1), channel_id=1, source_target_pairs={{0,1},{1,0},{2,3},{3,2},{4,5},{5,4},{6,7},{7,6},{8,9},{9,8},{10,11... | collective-permute-start | bytes 2949128 | tf_op jit(solution)/shard_map/ppermute | solution.py:526
  3.7 84.4 %copy-start.9 = (s32[16]{0:T(128)}, s32[16]{0:T(128)S(1)}, u32[]{:S(2)}) copy-start(s32[16]{0:T(128)S(1)} %reshape.30.mask) | copy-start | bytes 196
  3.8 26.6 %copy-start.16 = (f32[3,8,16,16]{3,2,1,0:T(8,128)S(1)}, f32[3,8,16,16]{3,2,1,0:T(8,128)}, u32[]{:S(2)}) copy-start(f32[3,8,16,16]{3,2,1,0:T(8,128)} %param.19) | copy-start | bytes 73732
  3.8 28.3 %copy-start.1 = (bf16[2560,64]{0,1:T(8,128)(2,1)S(1)}, bf16[2560,64]{0,1:T(8,128)(2,1)}, u32[]{:S(2)}) copy-start(bf16[2560,64]{0,1:T(8,128)(2,1)} %param.18) | copy-start | bytes 983044
  3.8 28.3 %copy-start.22 = (f32[2560]{0:T(1024)S(1)}, f32[2560]{0:T(1024)}, u32[]{:S(2)}) copy-start(f32[2560]{0:T(1024)} %param.17) | copy-start | bytes 30724
  9.3 19.7 %collective-permute-start.4 = (bf16[768,384]{1,0:T(8,128)(2,1)S(1)}, bf16[768,384]{1,0:T(8,128)(2,1)S(1)}, u32[]{:S(2)}, u32[]{:S(2)}) collective-permute-start(bf16[768,384]{1,0:T(8,128)(2,1)S(1)} %get-tuple-element.30), channel_id=1, source_target_pairs={{0,8},{1,9},{2,10},{3,11},{16,24},{17,25},{18,26},{19,27}} | collective-permute-start | bytes 1769480 | tf_op jit(solution)/shard_map/ppermute | solution.py:527
  16.7 33.6 %collective-permute-start.3 = (bf16[768,512]{1,0:T(8,128)(2,1)S(1)}, bf16[768,512]{1,0:T(8,128)(2,1)S(1)}, u32[]{:S(2)}, u32[]{:S(2)}) collective-permute-start(bf16[768,512]{1,0:T(8,128)(2,1)S(1)} %get-tuple-element.29), channel_id=1, source_target_pairs={{0,4},{4,8},{1,5},{5,9},{2,6},{6,10},{3,7},{7,11},{16,20},{20,24},... | collective-permute-start | bytes 2359304 | tf_op jit(solution)/shard_map/ppermute | solution.py:527
  18.0 49.5 %collective-permute-start.1 = (bf16[1152,384]{1,0:T(8,128)(2,1)}, bf16[1152,384]{1,0:T(8,128)(2,1)}, u32[]{:S(2)}, u32[]{:S(2)}) collective-permute-start(bf16[1152,384]{1,0:T(8,128)(2,1)} %get-tuple-element.27), channel_id=1, source_target_pairs={{4,0},{8,4},{12,8},{5,1},{9,5},{13,9},{6,2},{10,6},{14,10},{7,3},{... | collective-permute-start | bytes 2654216 | tf_op jit(solution)/shard_map/ppermute | solution.py:527
  19.3 49.5 %collective-permute-start.2 = (bf16[1152,384]{1,0:T(8,128)(2,1)}, bf16[1152,384]{1,0:T(8,128)(2,1)}, u32[]{:S(2)}, u32[]{:S(2)}) collective-permute-start(bf16[1152,384]{1,0:T(8,128)(2,1)} %get-tuple-element.28), channel_id=1, source_target_pairs={{12,4},{13,5},{14,6},{15,7},{28,20},{29,21},{30,22},{31,23}} | collective-permute-start | bytes 2654216 | tf_op jit(solution)/shard_map/ppermute | solution.py:527
  30.7 26.8 %copy-start.13 = (f32[8,16,48]{2,1,0:T(8,128)}, f32[8,16,48]{2,1,0:T(8,128)S(1)}, u32[]{:S(2)}) copy-start(f32[8,16,48]{2,1,0:T(8,128)S(1)} %reshape.31) | copy-start | bytes 73732
  30.8 15.7 %collective-permute-start.8 = (f32[8,16,32]{2,1,0:T(8,128)S(1)}, f32[8,16,32]{2,1,0:T(8,128)S(1)}, u32[]{:S(2)}, u32[]{:S(2)}) collective-permute-start(f32[8,16,32]{2,1,0:T(8,128)S(1)} %slice.44), channel_id=1, source_target_pairs={{0,4},{4,8},{8,12},{1,5},{5,9},{9,13},{2,6},{6,10},{10,14},{3,7},{... | collective-permute-start | bytes 49160 | tf_op jit(solution)/shard_map/ppermute | solution.py:45
  32.4 23.7 %collective-permute-start.11 = (f32[64,2]{1,0:T(8,128)S(1)}, f32[64,2]{1,0:T(8,128)S(1)}, u32[]{:S(2)}, u32[]{:S(2)}) collective-permute-start(f32[64,2]{1,0:T(8,128)S(1)} %copy.33), channel_id=1, source_target_pairs={{0,2},{2,0},{1,3},{3,1},{4,6},{6,4},{5,7},{7,5},{8,10},{10,8},{9,1... | collective-permute-start | bytes 1544 | tf_op jit(solution)/shard_map/ppermute | solution.py:820
  46.6 1.5 %collective-permute-start.9 = (f32[8,80]{1,0:T(8,128)S(1)}, f32[8,80]{1,0:T(8,128)S(1)}, u32[]{:S(2)}, u32[]{:S(2)}) collective-permute-start(f32[8,80]{1,0:T(8,128)S(1)} %select_bitcast_fusion.2), channel_id=1, source_target_pairs={{0,1},{1,0},{2,3},{3,2},{4,5},{5,4},{6,7},{7,6},{8,9},{9,8},{10,11... | collective-permute-start | bytes 7688 | tf_op jit(solution)/shard_map/ppermute | solution.py:637
  48.1 5.3 %copy-start.18 = (f32[8,80]{1,0:T(8,128)}, f32[8,80]{1,0:T(8,128)S(1)}, u32[]{:S(2)}) copy-start(f32[8,80]{1,0:T(8,128)S(1)} %get-tuple-element.64) | copy-start | bytes 7684
  48.8 17.3 %collective-permute-start.10 = (f32[32,80]{1,0:T(8,128)}, f32[32,80]{1,0:T(8,128)}, u32[]{:S(2)}, u32[]{:S(2)}) collective-permute-start(f32[32,80]{1,0:T(8,128)} %fusion.34), channel_id=1, source_target_pairs={{0,2},{2,0},{1,3},{3,1},{4,6},{6,4},{5,7},{7,5},{8,10},{10,8},{9,1... | collective-permute-start | bytes 30728 | tf_op jit(solution)/shard_map/ppermute | solution.py:649
  53.4 11.9 %copy-start.12 = (bf16[768,128]{1,0:T(8,128)(2,1)}, bf16[768,128]{1,0:T(8,128)(2,1)S(1)}, u32[]{:S(2)}) copy-start(bf16[768,128]{1,0:T(8,128)(2,1)S(1)} %get-tuple-element.46) | copy-start | bytes 589828
  54.1 16.4 %collective-permute-start.7 = (bf16[768,256]{1,0:T(8,128)(2,1)}, bf16[768,256]{1,0:T(8,128)(2,1)}, u32[]{:S(2)}, u32[]{:S(2)}) collective-permute-start(bf16[768,256]{1,0:T(8,128)(2,1)} %get-tuple-element.33), channel_id=1, source_target_pairs={{0,12},{1,13},{2,14},{3,15},{16,28},{17,29},{18,30},{19,31}} | collective-permute-start | bytes 1179656 | tf_op jit(solution)/shard_map/ppermute | solution.py:527
  56.2 32.0 %collective-permute-start.5 = (bf16[1152,256]{1,0:T(8,128)(2,1)}, bf16[1152,256]{1,0:T(8,128)(2,1)}, u32[]{:S(2)}, u32[]{:S(2)}) collective-permute-start(bf16[1152,256]{1,0:T(8,128)(2,1)} %get-tuple-element.32), channel_id=1, source_target_pairs={{8,12},{4,0},{9,13},{5,1},{10,14},{6,2},{11,15},{7,3},{24,28},{20,... | collective-permute-start | bytes 1769480 | tf_op jit(solution)/shard_map/ppermute | solution.py:527
  66.1 22.0 %collective-permute-start.6 = (bf16[768,256]{1,0:T(8,128)(2,1)}, bf16[768,256]{1,0:T(8,128)(2,1)S(1)}, u32[]{:S(2)}, u32[]{:S(2)}) collective-permute-start(bf16[768,256]{1,0:T(8,128)(2,1)} %get-tuple-element.33), channel_id=1, source_target_pairs={{4,12},{5,13},{6,14},{7,15},{20,28},{21,29},{22,30},{23,31}} | collective-permute-start | bytes 1179656 | tf_op jit(solution)/shard_map/ppermute | solution.py:527
  67.5 29.0 %collective-permute-start.12 = (bf16[1152,128]{1,0:T(8,128)(2,1)}, bf16[1152,128]{1,0:T(8,128)(2,1)S(1)}, u32[]{:S(2)}, u32[]{:S(2)}) collective-permute-start(bf16[1152,128]{1,0:T(8,128)(2,1)} %copy-done.11), channel_id=1, source_target_pairs={{4,0},{8,4},{12,8},{5,1},{9,5},{13,9},{6,2},{10,6},{14,10},{7,3},{... | collective-permute-start | bytes 884744 | tf_op jit(solution)/shard_map/ppermute | solution.py:527
  68.8 27.7 %collective-permute-start.13 = (bf16[1152,128]{1,0:T(8,128)(2,1)S(1)}, bf16[1152,128]{1,0:T(8,128)(2,1)S(1)}, u32[]{:S(2)}, u32[]{:S(2)}) collective-permute-start(bf16[1152,128]{1,0:T(8,128)(2,1)S(1)} %get-tuple-element.45), channel_id=1, source_target_pairs={{12,4},{13,5},{14,6},{15,7},{28,20},{29,21},{30,22},{31,23}} | collective-permute-start | bytes 884744 | tf_op jit(solution)/shard_map/ppermute | solution.py:527
  70.5 26.0 %collective-permute-start.14 = (bf16[768,128]{1,0:T(8,128)(2,1)}, bf16[768,128]{1,0:T(8,128)(2,1)S(1)}, u32[]{:S(2)}, u32[]{:S(2)}) collective-permute-start(bf16[768,128]{1,0:T(8,128)(2,1)} %copy-done.12), channel_id=1, source_target_pairs={{0,8},{1,9},{2,10},{3,11},{16,24},{17,25},{18,26},{19,27}} | collective-permute-start | bytes 589832 | tf_op jit(solution)/shard_map/ppermute | solution.py:527
  88.1 8.4 %copy-start.4 = (bf16[768,512]{1,0:T(8,128)(2,1)S(1)}, bf16[768,512]{1,0:T(8,128)(2,1)}, u32[]{:S(2)}) copy-start(bf16[768,512]{1,0:T(8,128)(2,1)} %copy-done.2) | copy-start | bytes 2359300
  100.8 15.5 %copy-start.5 = (bf16[320,512]{1,0:T(8,128)(2,1)S(1)}, bf16[320,512]{1,0:T(8,128)(2,1)}, u32[]{:S(2)}) copy-start(bf16[320,512]{1,0:T(8,128)(2,1)} %fusion.30.selector) | copy-start | bytes 983044
  100.8 15.5 %copy-start.8 = (f32[1,1,3,384]{3,1,2,0:T(1,128)S(1)}, f32[1,1,3,384]{3,1,2,0:T(1,128)}, u32[]{:S(2)}) copy-start(f32[1,1,3,384]{3,1,2,0:T(1,128)} %copy.37) | copy-start | bytes 13828
  100.9 1.5 %collective-permute-start.15 = (f32[3,40,384]{2,1,0:T(8,128)S(1)}, f32[3,40,384]{2,1,0:T(8,128)S(1)}, u32[]{:S(2)}, u32[]{:S(2)}) collective-permute-start(f32[3,40,384]{2,1,0:T(8,128)S(1)} %constant_dynamic-slice_fusion), channel_id=1, source_target_pairs={{0,1},{1,0},{2,3},{3,2},{4,5},{5,4},{6,7},{7,6},{8,9},{9,8},{10,11... | collective-permute-start | bytes 552968 | tf_op jit(solution)/shard_map/ppermute | solution.py:832
  102.4 5.5 %collective-permute-start.17 = (f32[40,256]{1,0:T(8,128)S(1)}, f32[40,256]{1,0:T(8,128)S(1)}, u32[]{:S(2)}, u32[]{:S(2)}) collective-permute-start(f32[40,256]{1,0:T(8,128)S(1)} %slice.50), channel_id=1, source_target_pairs={{0,8},{4,12},{1,9},{5,13},{2,10},{6,14},{3,11},{7,15},{16,24},{20,... | collective-permute-start | bytes 122888 | tf_op jit(solution)/shard_map/ppermute | solution.py:839
  103.7 4.2 %collective-permute-start.18 = (f32[40,384]{1,0:T(8,128)S(1)}, f32[40,384]{1,0:T(8,128)S(1)}, u32[]{:S(2)}, u32[]{:S(2)}) collective-permute-start(f32[40,384]{1,0:T(8,128)S(1)} %get-tuple-element.57), channel_id=1, source_target_pairs={{4,12},{12,8},{5,13},{13,9},{6,14},{14,10},{7,15},{15,11},{20,28},... | collective-permute-start | bytes 184328 | tf_op jit(solution)/shard_map/ppermute | solution.py:838
  104.4 5.7 %collective-permute-start.16 = (f32[40,640]{1,0:T(8,128)S(1)}, f32[40,640]{1,0:T(8,128)S(1)}, u32[]{:S(2)}, u32[]{:S(2)}) collective-permute-start(f32[40,640]{1,0:T(8,128)S(1)} %pad_maximum_fusion.1), channel_id=1, source_target_pairs={{0,4},{4,8},{8,12},{1,5},{5,9},{9,13},{2,6},{6,10},{10,14},{3,7},{... | collective-permute-start | bytes 307208 | tf_op jit(solution)/shard_map/ppermute | solution.py:835
  110.2 4.7 %collective-permute-start.19 = (f32[40,640]{1,0:T(8,128)S(1)}, f32[40,640]{1,0:T(8,128)S(1)}, u32[]{:S(2)}, u32[]{:S(2)}) collective-permute-start(f32[40,640]{1,0:T(8,128)S(1)} %fusion.32), channel_id=1, source_target_pairs={{0,2},{2,0},{1,3},{3,1},{4,6},{6,4},{5,7},{7,5},{8,10},{10,8},{9,1... | collective-permute-start | bytes 307208 | tf_op jit(solution)/shard_map/ppermute | solution.py:842
  114.9 1.4 %collective-permute-start.20 = (f32[40,640]{1,0:T(8,128)S(1)}, f32[40,640]{1,0:T(8,128)S(1)}, u32[]{:S(2)}, u32[]{:S(2)}) collective-permute-start(f32[40,640]{1,0:T(8,128)S(1)} %add.97.mine), channel_id=1, source_target_pairs={{0,1},{1,0},{2,3},{3,2},{4,5},{5,4},{6,7},{7,6},{8,9},{9,8},{10,11... | collective-permute-start | bytes 307208 | tf_op jit(solution)/shard_map/ppermute | solution.py:843
  (13 other events, 27.0 us)

commit v5 on v4

--- a/solution.py
+++ b/solution.py
@@ -1,5 +1,6 @@
 import functools
 import math
+import typing
 
 import jax
 import jax.numpy as jnp
@@ -216,8 +217,6 @@
 FAR_HEADS = 2
 MIDDLE = NEAR_HEADS
 FAR = NEAR_HEADS + MIDDLE_HEADS
-EARLY = 3
-LATE = NEAR_HEADS - EARLY
 STAT_ROWS = 8
 SLOTS = 3
 QUERY_ROWS = 192
@@ -225,7 +224,8 @@
 WINDOW = 32
 GRANT = 20 << 20
 
-OWN, OTHER, DOWN, UP, MAIN, PLACE, SLAB = range(7)
+OWN, OTHER, DOWN, UP, MAIN, LAST, LAST_COLUMN, PLACE, SLAB = range(9)
+STEPS = 9
 
 
 def plan_fits(heads_dev, span_count, slab_count, head_count):
@@ -238,16 +238,16 @@
 
 
 def scalar_operand(heads):
-    by_place = np.array(
-        [
-            [0, heads, MIDDLE, 0, MIDDLE, 0, 0, 0],
-            [0, heads, MIDDLE, MIDDLE, 0, 1, 0, 0],
-            [0, heads, 0, 0, MIDDLE, 2, 0, 0],
-            [0, heads, MIDDLE, 0, 0, 3, 0, 0],
-        ],
-        np.int32,
-    )
-    by_slab = np.array([heads, -heads, 0, 0, 0, 0, 1, 0], np.int32)
+    by_place = np.zeros((4, 12), np.int32)
+    by_place[:, OTHER] = heads
+    by_place[:, DOWN] = [MIDDLE, MIDDLE, 0, MIDDLE]
+    by_place[:, UP] = [0, MIDDLE, 0, 0]
+    by_place[:, MAIN] = [MIDDLE, 0, MIDDLE, 0]
+    by_place[:, LAST] = [0, 2, MIDDLE + 3, 0]
+    by_place[:, LAST_COLUMN] = [0, 2, 3, 0]
+    by_place[:, PLACE] = range(4)
+    by_slab = np.zeros(12, np.int32)
+    by_slab[[OWN, OTHER, SLAB]] = heads, -heads, 1
     row = lax.dynamic_slice_in_dim(jnp.array(by_place), lax.axis_index("span"), 1, 0)[0]
     return row + lax.axis_index("slab") * jnp.array(by_slab)
 
@@ -289,22 +289,24 @@
     )(scalars, *arrays)
 
 
-def pack_messages(scalars, messages, queries, keys, values, received, name):
-    rows = queries.shape[0]
-    half = rows // 2
+def message(scalars, pieces, arrays, name):
     copies, shapes = [], []
-    for target, (entry, shift, heads, whole) in enumerate(messages):
-        entries = () if entry is None else (entry,)
+    for target, parts in enumerate(pieces):
         at = 0
-        if whole:
-            copies.append((0, 0, rows, (OWN,) + entries, shift, target, 0, heads))
-            at = rows
-        for part, array in enumerate((1, 2)):
-            copies.append((array, 0, half, (OWN,) + entries, shift, target, at, heads))
-            copies.append((3, part * half, half, entries, shift, target, at + half, heads))
+        for source, row, rows, entries, shift, heads in parts:
+            copies.append((source, row, rows, entries, shift, target, at, heads))
             at += rows
-        shapes.append((at, heads * HD))
-    return pack(scalars, (queries, keys, values, received), shapes, copies, name)
+        shapes.append((at, parts[0][5] * HD))
+    return pack(scalars, arrays, shapes, copies, name)
+
+
+class Tokens(typing.NamedTuple):
+    query: int | None = None
+    pairs: tuple = ()
+    extra: int | None = None
+
+
+OWN_TOKENS = Tokens()
 
 
 def attend_kernel(variants, extra, span_count, scalars, mask, *refs):
@@ -315,6 +317,9 @@
     half = rows // 2
     step = pl.program_id(0)
     to_exp2 = math.log2(math.e) / math.sqrt(HD)
+    active = functools.reduce(
+        lambda a, b: a | b, [scalars[PLACE] == place for place in variants]
+    )
 
     @pl.when(step == 0)
     def _():
@@ -322,20 +327,23 @@
         squares[...] = jnp.zeros_like(squares)
 
     def query_of(source):
-        if source is None:
+        if source is OWN_TOKENS:
             return query_own[...]
-        if source[0] < 0:
-            return more[0][:, source[1] * HD : (source[1] + 1) * HD]
-        return payloads[source[0]][:rows]
+        if source.extra is not None:
+            return more[0][:, source.extra * HD : (source.extra + 1) * HD]
+        return payloads[source.query][:rows]
 
     def pair_of(source):
-        if source is None:
+        if source is OWN_TOKENS:
             parts = (key_own[...], received[:half], value_own[...], received[half:])
-        elif source[0] < 0:
-            lanes = slice(source[1] * HD, (source[1] + 1) * HD)
+        elif source.extra is not None:
+            lanes = slice(source.extra * HD, (source.extra + 1) * HD)
             parts = (more[1][:, lanes], more[3][:half, lanes], more[2][:, lanes], more[3][half:, lanes])
+        elif len(source.pairs) == 2:
+            one, two = (payloads[number] for number in source.pairs)
+            parts = (one[:half], two[:half], one[half:], two[half:])
         else:
-            payload = payloads[source[0]]
+            payload = payloads[source.pairs[0]]
             start = payload.shape[0] - 2 * rows
             return payload[start : start + rows], payload[start + rows :]
         return jnp.concatenate(parts[:2], axis=0), jnp.concatenate(parts[2:], axis=0)
@@ -392,9 +400,8 @@
             )
             pieces.append((both[:, :HD] / both[:, HD:]).astype(jnp.bfloat16))
         attended = jnp.concatenate(pieces, axis=0)
-        extra_head = source[1] if source is not None and source[0] < 0 else None
         folded[slot] += lax.dot_general(
-            projector(extra_head),
+            projector(source.extra),
             attended,
             (((1,), (1,)), ((), ())),
             preferred_element_type=jnp.float32,
@@ -402,14 +409,18 @@
         wide = attended.astype(jnp.float32)
         squares[slot] += wide * wide
 
-    for place, tasks in variants.items():
-
-        @pl.when(scalars[PLACE] == place)
+    for place, (steps, tasks) in variants.items():
+
+        @pl.when((scalars[PLACE] == place) & (step < steps))
         def _():
             for task in tasks:
                 one_query(*task)
 
-    @pl.when(step == pl.num_programs(0) - 1)
+    @pl.when((step == pl.num_programs(0) - 1) & jnp.logical_not(active))
+    def _():
+        sums_out[...] = sums_in[...]
+
+    @pl.when((step == pl.num_programs(0) - 1) & active)
     def _():
         ones_rows = jnp.ones((STAT_ROWS, HD), jnp.bfloat16)
         patch = weight.shape[0]
@@ -439,9 +450,15 @@
     half = rows // 2
     patch = weight.shape[0]
 
+    def moving(i, scalars):
+        used = functools.reduce(
+            lambda a, b: a | b, [scalars[PLACE] == place for place in variants]
+        )
+        return jnp.where(used, i, 0)
+
     def column(height, own_column):
         def index(i, scalars, mask):
-            head = first + i + (scalars[OWN] if own_column else 0)
+            head = first + moving(i, scalars) + (scalars[OWN] if own_column else 0)
             for entry in entries:
                 head = head + scalars[entry]
             return (0, head)
@@ -451,8 +468,20 @@
     def two_columns(height, own_column):
         return pl.BlockSpec(
             (height, 2 * HD),
-            lambda i, scalars, mask: (0, i + (scalars[OWN] // 2 if own_column else 0)),
-        )
+            lambda i, scalars, mask: (
+                0,
+                moving(i, scalars) + (scalars[OWN] // 2 if own_column else 0),
+            ),
+        )
+
+    def payload_column(payload, entry, shift):
+        last = payload.shape[1] // HD - 1
+
+        def index(i, scalars, mask):
+            at = shift + moving(i, scalars)
+            return (0, jnp.minimum(at if entry is None else at + scalars[entry], last))
+
+        return pl.BlockSpec((payload.shape[0], HD), index)
 
     sums_spec = pl.BlockSpec(sums.shape, lambda i, scalars, mask: (0, 0, 0))
     in_specs = [
@@ -477,14 +506,11 @@
             two_columns(1, True),
         ]
         arrays += [queries, keys, values, received, weight, gain]
-    in_specs += [
-        pl.BlockSpec(
-            (payload.shape[0], HD), lambda i, scalars, mask, start=start: (0, start + i)
-        )
-        for payload, start in payloads
-    ]
-    arrays += [payload for payload, _ in payloads]
-    pairs = steps * max(sum(len(task[3]) for task in tasks) for tasks in variants.values())
+    in_specs += [payload_column(*payload) for payload in payloads]
+    arrays += [payload[0] for payload in payloads]
+    pairs = max(
+        count * sum(len(task[3]) for task in tasks) for count, tasks in variants.values()
+    )
     span_count = math.isqrt(mask.shape[0])
     return pl.pallas_call(
         functools.partial(attend_kernel, variants, extra, span_count),
@@ -511,120 +537,194 @@
 
 def token_sums(scalars, queries, keys, values, span_mask, head_gain, patch_weight):
     rows = queries.shape[0]
+    half = rows // 2
     heads = NEAR_HEADS + MIDDLE_HEADS + FAR_HEADS
     queries, keys, values = (
         pltpu.with_memory_space_constraint(array, pltpu.HBM) for array in (queries, keys, values)
     )
-    half = rows // 2
-    (handed,) = pack(
+
+    def send(value, *pairs):
+        return lax.ppermute(value, "span", list(pairs))
+
+    def send_across(value, *pairs):
+        slabs = lax.axis_size("slab")
+        return lax.ppermute(
+            value,
+            ("span", "slab"),
+            [(a * slabs + s, b * slabs + 1 - s) for a, b in pairs for s in range(slabs)],
+        )
+
+    def tokens(entry, shift, count):
+        return [(0, 0, rows, (OWN, entry) if entry else (OWN,), shift, count)]
+
+    def own_half(slab_entry, entry, shift, count):
+        return [(part, 0, half, (slab_entry, entry), shift, count) for part in (1, 2)]
+
+    def pairs_of(entry, shift, count):
+        entries = (entry,) if entry else ()
+        return [
+            piece
+            for part in (1, 2)
+            for piece in (
+                (part, 0, half, (OWN,) + entries, shift, count),
+                (3, (part - 1) * half, half, entries, shift, count),
+            )
+        ]
+
+    handed, up_same, up_across, query_down, query_two = message(
         scalars,
-        (keys, values),
-        [(rows, heads * HD)],
-        [(0, 0, half, (OTHER,), 0, 0, 0, heads), (1, 0, half, (OTHER,), 0, 0, half, heads)],
-        "pack_handed",
-    )
+        [
+            [(part, 0, half, (OTHER,), 0, heads) for part in (1, 2)],
+            own_half(OWN, UP, 0, NEAR_HEADS),
+            own_half(OTHER, UP, 0, NEAR_HEADS),
+            tokens(DOWN, 0, MIDDLE_HEADS),
+            tokens(None, 0, NEAR_HEADS),
+        ],
+        (queries, keys, values),
+        "pack_first",
+    )
+    anchor = handed
     received = lax.ppermute(handed, "slab", SWAP)
-    send = lambda value, *pairs: lax.ppermute(value, "span", list(pairs))
-
-    def bring(messages, source, name):
-        return pack_messages(scalars, messages, queries, keys, values, source, name)
-
-    down, up, down_two, up_two = bring(
+    up_same = send(up_same, (0, 1), (1, 2))
+    up_across = send_across(up_across, (0, 1), (1, 2))
+    query_down = send(query_down, (1, 0), (2, 1), (3, 2))
+    query_two = send(query_two, (3, 1))
+
+    arrays = (queries, keys, values, received)
+    pair_down, pair_two, up_two = message(
+        scalars,
+        [pairs_of(DOWN, 0, MIDDLE_HEADS), pairs_of(None, 0, 2), pairs_of(None, MIDDLE, 3)],
+        arrays,
+        "pack_second",
+    )
+    pair_down = send(pair_down, (1, 0), (2, 1), (3, 2))
+    pair_two = send(pair_two, (3, 1))
+    up_two = send(up_two, (0, 2))
+
+    source, _ = lax.optimization_barrier((received, up_same))
+    far_all, far_pair, last_two, last_up = message(
+        scalars,
         [
-            (DOWN, 0, EARLY, True),
-            (UP, 0, NEAR_HEADS, False),
-            (None, 0, EARLY, True),
-            (None, MIDDLE, EARLY, False),
+            tokens(None, FAR, FAR_HEADS) + pairs_of(None, FAR, FAR_HEADS),
+            pairs_of(None, FAR, FAR_HEADS),
+            pairs_of(None, 2, 2),
+            pairs_of(None, MIDDLE + 3, 1),
         ],
-        received,
-        "pack_first",
-    )
-    down = send(down, (1, 0), (2, 1), (3, 2))
-    up = send(up, (0, 1), (1, 2))
-    down_two = send(down_two, (3, 1))
-    up_two = send(up_two, (0, 2))
-    source, _ = lax.optimization_barrier((received, up))
-    far_all, far_pair, late_down, late_down_two, late_up_two = bring(
-        [
-            (None, FAR, FAR_HEADS, True),
-            (None, FAR, FAR_HEADS, False),
-            (DOWN, EARLY, LATE, True),
-            (None, EARLY, LATE, True),
-            (None, MIDDLE + EARLY, LATE, False),
-        ],
-        source,
-        "pack_second",
+        (queries, keys, values, source),
+        "pack_third",
     )
     far_two = send(far_pair, (1, 3))
     far_three = send(far_pair, (0, 3))
     far_next = send(far_all, (2, 3), (1, 0))
-    late_down, late_down_two, late_up_two, _ = lax.optimization_barrier(
-        (late_down, late_down_two, late_up_two, down)
-    )
-    late_down = send(late_down, (1, 0), (2, 1), (3, 2))
-    late_down_two = send(late_down_two, (3, 1))
-    late_up_two = send(late_up_two, (0, 2))
+    last_two, last_up, _ = lax.optimization_barrier((last_two, last_up, pair_down))
+    last_two = send(last_two, (3, 1))
+    last_up = send(last_up, (0, 2))
 
     mask = span_mask.reshape(-1)
     weight = patch_weight.T
     own = (queries, keys, values, received, weight, head_gain[None, :])
     sums = jnp.zeros((SLOTS, weight.shape[0] + 2 * STAT_ROWS, rows), jnp.float32)
-    on_one, on_two, back_one, back_two = (0, 0), (1, 0), (2, 0), (3, 0)
-    main = {
-        0: [(None, 0, 0, [(None, 0)]), (on_one, 1, 1, [(None, 0), (on_one, 1)])],
-        1: [
-            (on_two, 2, 3, [(back_one, 0), (None, 1), (on_one, 2), (on_two, 3)]),
-            (on_one, 1, 2, [(back_one, 0), (None, 1), (on_one, 2)]),
-            (None, 0, 1, [(back_one, 0), (None, 1)]),
-        ],
-        2: [
-            (on_one, 1, 3, [(back_two, 0), (back_one, 1), (None, 2), (on_one, 3)]),
-            (None, 0, 2, [(back_two, 0), (back_one, 1), (None, 2)]),
-        ],
-    }
-    extra = [((-1, lane), 0, 0, [((-1, lane), 0)]) for lane in range(2)]
-    far = {
-        0: [(None, 0, 0, [(None, 0)]), ((0, 0), 1, 1, [(None, 0), ((0, 0), 1)])] + extra,
-        3: [
-            (None, 0, 3, [((2, 0), 0), ((1, 0), 1), ((0, 0), 2), (None, 3)]),
-            ((0, 0), 2, 2, [((2, 0), 0), ((1, 0), 1), ((0, 0), 2)]),
-        ],
-    }
     run = functools.partial(attend, own=own, scalars=scalars, mask=mask)
+
+    on_one, back_one, back_two = Tokens(0, (1,)), Tokens(None, (2, 3)), Tokens(None, (4,))
+    here = OWN_TOKENS
+    middle = [
+        (on_one, 1, 3, [(back_two, 0), (back_one, 1), (here, 2), (on_one, 3)]),
+        (here, 0, 2, [(back_two, 0), (back_one, 1), (here, 2)]),
+    ]
     sums = run(
-        EARLY,
+        MIDDLE_HEADS,
         (MAIN,),
         0,
         sums=sums,
-        payloads=[(down, 0), (down_two, 0), (up, 0), (up_two, 0)],
-        variants=main,
+        payloads=[
+            (query_down, None, 0),
+            (pair_down, None, 0),
+            (up_same, None, 0),
+            (up_across, None, 0),
+            (up_two, None, 0),
+        ],
+        variants={
+            0: (4, [(here, 0, 0, [(here, 0)]), (on_one, 1, 1, [(here, 0), (on_one, 1)])]),
+            1: (
+                4,
+                [
+                    (on_one, 1, 2, [(back_one, 0), (here, 1), (on_one, 2)]),
+                    (here, 0, 1, [(back_one, 0), (here, 1)]),
+                ],
+            ),
+            2: (3, middle),
+        },
         more=False,
-        name="early_heads",
-    )
+        name="main_heads",
+    )
+    on_two = Tokens(5, (6,))
+    last_span = [(on_two, 2, 3, [(back_one, 0), (here, 1), (on_one, 2), (on_two, 3)])]
+    sums = run(
+        2,
+        (MAIN,),
+        0,
+        sums=sums,
+        payloads=[
+            (query_down, None, 0),
+            (pair_down, None, 0),
+            (up_same, None, 0),
+            (up_across, None, 0),
+            (up_two, None, 0),
+            (query_two, None, 0),
+            (pair_two, None, 0),
+        ],
+        variants={1: (2, last_span)},
+        more=False,
+        name="near_heads",
+    )
+    beside, two_back, three_back = Tokens(0, (0,)), Tokens(None, (1,)), Tokens(None, (2,))
+    extras = [Tokens(None, (), lane) for lane in range(2)]
     sums = run(
         FAR_HEADS,
         (),
         FAR,
         sums=sums,
-        payloads=[(far_next, 0), (far_two, 0), (far_three, 0)],
-        variants=far,
+        payloads=[(far_next, None, 0), (far_two, None, 0), (far_three, None, 0)],
+        variants={
+            0: (
+                FAR_HEADS,
+                [(here, 0, 0, [(here, 0)]), (beside, 1, 1, [(here, 0), (beside, 1)])]
+                + [(head, 0, 0, [(head, 0)]) for head in extras],
+            ),
+            3: (
+                FAR_HEADS,
+                [
+                    (here, 0, 3, [(three_back, 0), (two_back, 1), (beside, 2), (here, 3)]),
+                    (beside, 2, 2, [(three_back, 0), (two_back, 1), (beside, 2)]),
+                ],
+            ),
+        },
         more=True,
         name="far_heads",
     )
 
     def last(sums):
         return run(
-            LATE,
-            (MAIN,),
-            EARLY,
+            2,
+            (LAST,),
+            0,
             sums=sums,
-            payloads=[(late_down, 0), (late_down_two, 0), (up, EARLY), (late_up_two, 0)],
-            variants=main,
+            payloads=[
+                (query_down, LAST_COLUMN, 0),
+                (pair_down, LAST_COLUMN, 0),
+                (up_same, LAST_COLUMN, 0),
+                (up_across, LAST_COLUMN, 0),
+                (last_up, None, 0),
+                (query_two, LAST_COLUMN, 0),
+                (last_two, None, 0),
+            ],
+            variants={1: (2, last_span), 2: (1, middle)},
             more=False,
-            name="late_heads",
-        )
-
-    return sums, last, up_two
+            name="last_heads",
+        )
+
+    return sums, last, anchor, pair_down
 
 
 def noise_window(noisy_latent):
@@ -800,7 +900,7 @@
     place = lax.axis_index("span")
     slab = lax.axis_index("slab")
     scalars = scalar_operand(heads_dev // lax.axis_size("slab"))
-    sums, last, anchor = token_sums(
+    sums, last, anchor, later = token_sums(
         scalars, queries, keys, values, span_mask, head_gain, patch_weight
     )
 

time: 120 us -> 122 us (1.017)
  waiting for transfers between devices: 31.7 us -> 10.3 us
  starting transfers between devices: 35.5 us -> 50.6 us
  other arithmetic: 5.91 us -> 9.83 us
  Pallas kernels: 29.7 us -> 33.6 us
    ppermute x1, waiting for transfers between devices: 12.5 us -> 1.82 us  [from_behind(): return lax.ppermute(value, axis, pairs)]
    ppermute x10 -> x12, starting transfers between devices: 24.5 us -> 34.3 us  [the longest x11 30.1 us: send(): return lax.ppermute(value, 'span', list(pairs))]
    ppermute x10 -> x12, waiting for transfers between devices: 8.08 us -> 0.03 us  [the longest x11 0.03 us: send(): return lax.ppermute(value, 'span', list(pairs))]
    pallas_call x3 -> x4, Pallas kernels: 19.1 us -> 21.9 us  [attend(): pl.pallas_call(functools.partial(attend_kernel, variants, extra, span_cou...]
    ppermute x1, starting transfers between devices: 1.29 us -> 3.48 us  [from_behind(): return lax.ppermute(value, axis, pairs)]
    ppermute x1, waiting for transfers between devices: 2.19 us -> 0.01 us  [per_device(): lax.ppermute(jnp.concatenate([own[:, skip:], after], axis=1), 'span', [(0...]
    ppermute x1, waiting for transfers between devices: 2.04 us -> 0.01 us  [token_sums(): received = lax.ppermute(handed, 'slab', SWAP)]
    ppermute x1, starting transfers between devices: 3.49 us -> 5.49 us  [per_device(): lax.ppermute(jnp.concatenate([own[:, skip:], after], axis=1), 'span', [(0...]
  transfers between devices with their start and end apart: 21 -> 23, of which waited for: 7 -> 6; matrix products, arithmetic and copies ran while one was open for 13% -> 16% of each run, Pallas kernels for 15% -> 21%
where the time goes in v5:
time: 122 us; the launch traced here: 120 us
  starting transfers between devices  50.6 us (41%)
  Pallas kernels  33.6 us (28%)
  local copies, waits for them, and re-layouts  15 us (12%)
  waiting for transfers between devices  10.3 us (8%)
  other arithmetic  9.83 us (8%)
  between operations  1.24 us (1%)
    ppermute x11, starting transfers between devices, send(): return lax.ppermute(value, 'span', list(pairs))  30.1 us
    pallas_call x4, Pallas kernels, attend(): pl.pallas_call(functools.partial(attend_kernel, variants, extra, span_cou...  21.9 us
    pallas_call x3, Pallas kernels, pack(): pl.pallas_call(functools.partial(pack_kernel, len(arrays), copies), name=...  9.26 us
    ppermute x1, starting transfers between devices, per_device(): lax.ppermute(jnp.concatenate([own[:, skip:], after], axis=1), 'span', [(0...  5.49 us
    reshape x1, local copies, waits for them, and re-layouts, banded_weight(): banded.transpose(1, 2, 0, 3, 4, 5)  5.27 us
    unnamed x52, local copies, waits for them, and re-layouts  4.37 us
    ppermute x1, starting transfers between devices, send_across(): lax.ppermute(value, ('span', 'slab'), [(a * slabs + s, b * slabs + 1 - s)...  4.17 us
    ppermute x1, waiting for transfers between devices, per_device(): total = total + lax.ppermute(total, 'head', SWAP)  4.13 us
  transfers between devices with their start and end apart: 23, of which 6 were waited for; matrix products, arithmetic and copies ran while one was open for 16% of the time, Pallas kernels for 21%

profile of v5, /device:TPU:0, one launch (start us, length us, event | category | flops | bytes accessed | tf_op | source)
XLA Modules:
  0.0 120.5 jit_solution(14244311065651675132)
XLA Ops:
  1.4 3.3 %pack_first.1 = (bf16[384,1280]{1,0:T(8,128)(2,1)S(1)}, bf16[384,512]{1,0:T(8,128)(2,1)}, bf16[384,512]{1,0:T(8,128)(2,1)S(1)}, bf16[384,512]{1,0:T(8,128)(2,1)}, bf16[384,512]{1,0:T(8,128)(2,1)}) custom-call(s32[12]{0:T(128)S(1)} %fusion.42.scalars, bf16[384,2560]{1,0:T(8,128)(2,1)} %refs_0_.13, bf16[192,2560]{1,0:T(8,128)(2,1)} %refs_1_.13, ...), custom_call_target="tpu_custom_call" | custom-call | bytes 5111808 | tf_op jit(solution)/shard_map/pack_first/pallas_call | solution.py:276
  5.9 4.5 %collective-permute-start.3 = (bf16[384,512]{1,0:T(8,128)(2,1)}, bf16[384,512]{1,0:T(8,128)(2,1)S(1)}, u32[]{:S(2)}, u32[]{:S(2)}) collective-permute-start(bf16[384,512]{1,0:T(8,128)(2,1)} %get-tuple-element.32), channel_id=1, source_target_pairs={{0,4},{4,8},{1,5},{5,9},{2,6},{6,10},{3,7},{7,11},{16,20},{20,24},... | collective-permute-start | bytes 1179656 | tf_op jit(solution)/shard_map/ppermute | solution.py:547
  11.4 1.5 %collective-permute-start.14 = (f32[64,2]{1,0:T(8,128)}, f32[64,2]{1,0:T(8,128)}, u32[]{:S(2)}, u32[]{:S(2)}) collective-permute-start(f32[64,2]{1,0:T(8,128)} %copy.33), channel_id=1, source_target_pairs={{0,2},{2,0},{1,3},{3,1},{4,6},{6,4},{5,7},{7,5},{8,10},{10,8},{9,1... | collective-permute-start | bytes 1544 | tf_op jit(solution)/shard_map/ppermute | solution.py:920
  13.3 3.5 %collective-permute-start.11 = (f32[8,16,32]{2,1,0:T(8,128)S(1)}, f32[8,16,32]{2,1,0:T(8,128)S(1)}, u32[]{:S(2)}, u32[]{:S(2)}) collective-permute-start(f32[8,16,32]{2,1,0:T(8,128)S(1)} %slice.44), channel_id=1, source_target_pairs={{0,4},{4,8},{8,12},{1,5},{5,9},{9,13},{2,6},{6,10},{10,14},{3,7},{... | collective-permute-start | bytes 49160 | tf_op jit(solution)/shard_map/ppermute | solution.py:46
  16.8 1.3 %collective-permute-start.1 = (bf16[384,512]{1,0:T(8,128)(2,1)}, bf16[384,512]{1,0:T(8,128)(2,1)S(1)}, u32[]{:S(2)}, u32[]{:S(2)}) collective-permute-start(bf16[384,512]{1,0:T(8,128)(2,1)} %get-tuple-element.30), channel_id=1, source_target_pairs={{4,0},{8,4},{12,8},{5,1},{9,5},{13,9},{6,2},{10,6},{14,10},{7,3},{... | collective-permute-start | bytes 1179656 | tf_op jit(solution)/shard_map/ppermute | solution.py:547
  19.2 1.8 %collective-permute-done.11 = f32[8,16,32]{2,1,0:T(8,128)S(1)} collective-permute-done((f32[8,16,32]{2,1,0:T(8,128)S(1)}, f32[8,16,32]{2,1,0:T(8,128)S(1)}, u32[]{:S(2)}, u32[]{:S(2)}) %collective-permute-start.11) | collective-permute-done | bytes 16416 | tf_op jit(solution)/shard_map/ppermute | solution.py:46
  23.0 4.2 %collective-permute-start.4 = (bf16[384,512]{1,0:T(8,128)(2,1)}, bf16[384,512]{1,0:T(8,128)(2,1)S(1)}, u32[]{:S(2)}, u32[]{:S(2)}) collective-permute-start(bf16[384,512]{1,0:T(8,128)(2,1)} %copy-done.5), channel_id=1, source_target_pairs={{0,5},{1,4},{4,9},{5,8},{2,7},{3,6},{6,11},{7,10},{16,21},{17,20},... | collective-permute-start | bytes 1179656 | tf_op jit(solution)/shard_map/ppermute | solution.py:551
  28.8 1.6 %collective-permute-start.13 = (f32[32,80]{1,0:T(8,128)S(1)}, f32[32,80]{1,0:T(8,128)S(1)}, u32[]{:S(2)}, u32[]{:S(2)}) collective-permute-start(f32[32,80]{1,0:T(8,128)S(1)} %fusion.34), channel_id=1, source_target_pairs={{0,2},{2,0},{1,3},{3,1},{4,6},{6,4},{5,7},{7,5},{8,10},{10,8},{9,1... | collective-permute-start | bytes 30728 | tf_op jit(solution)/shard_map/ppermute | solution.py:749
  30.3 3.2 %pack_second.1 = (bf16[768,512]{1,0:T(8,128)(2,1)}, bf16[768,256]{1,0:T(8,128)(2,1)}, bf16[768,384]{1,0:T(8,128)(2,1)}) custom-call(s32[12]{0:T(128)S(1)} %fusion.42.scalars, bf16[384,2560]{1,0:T(8,128)(2,1)} %refs_0_.13, bf16[192,2560]{1,0:T(8,128)(2,1)} %refs_1_.13, bf16[192,2560]{1,0:T(8,128)(2,1)} %refs_2_.13, ...), custom_call_target="tpu_custom_call" | custom-call | bytes 3538944 | tf_op jit(solution)/shard_map/pack_second/pallas_call | solution.py:276
  33.5 1.3 %collective-permute-start.2 = (bf16[768,512]{1,0:T(8,128)(2,1)}, bf16[768,512]{1,0:T(8,128)(2,1)S(1)}, u32[]{:S(2)}, u32[]{:S(2)}) collective-permute-start(bf16[768,512]{1,0:T(8,128)(2,1)} %get-tuple-element.31), channel_id=1, source_target_pairs={{4,0},{8,4},{12,8},{5,1},{9,5},{13,9},{6,2},{10,6},{14,10},{7,3},{... | collective-permute-start | bytes 2359304 | tf_op jit(solution)/shard_map/ppermute | solution.py:547
  34.9 1.4 %fusion.30.selector = bf16[320,512]{1,0:T(8,128)(2,1)} fusion(s32[320]{0:T(512)S(1)} %copy-done.18, s32[320]{0:T(512)S(1)} %copy-done.19, s32[]{:T(128)S(6)} %mul.56, s32[320]{0:T(512)S(1)} %copy-done.17, s32[320]{0:T(512)S(1)} %copy-done.20, s32[]{:T(128)S(6)} %mul.55, pred[320]{0:T(512)(128)(4,1)S(1)} %copy-done.24, pred[320]{0:T(512)(128)(4,1)S(1)} %copy-done.23), kind=kLoop, calls=%fused_computation.47 | loop fusion | flops 10158080 | bytes 333448 | tf_op jit(solution)/shard_map/convert_element_type | solution.py:764
  36.3 1.4 %collective-permute-start.6 = (bf16[384,512]{1,0:T(8,128)(2,1)}, bf16[384,512]{1,0:T(8,128)(2,1)}, u32[]{:S(2)}, u32[]{:S(2)}) collective-permute-start(bf16[384,512]{1,0:T(8,128)(2,1)} %get-tuple-element.35), channel_id=1, source_target_pairs={{12,4},{13,5},{14,6},{15,7},{28,20},{29,21},{30,22},{31,23}} | collective-permute-start | bytes 1179656 | tf_op jit(solution)/shard_map/ppermute | solution.py:547
  37.7 6.4 %collective-permute-start.5 = (bf16[768,384]{1,0:T(8,128)(2,1)}, bf16[768,384]{1,0:T(8,128)(2,1)}, u32[]{:S(2)}, u32[]{:S(2)}) collective-permute-start(bf16[768,384]{1,0:T(8,128)(2,1)} %get-tuple-element.34), channel_id=1, source_target_pairs={{0,8},{1,9},{2,10},{3,11},{16,24},{17,25},{18,26},{19,27}} | collective-permute-start | bytes 1769480 | tf_op jit(solution)/shard_map/ppermute | solution.py:547
  44.1 1.4 %collective-permute-start.7 = (bf16[768,256]{1,0:T(8,128)(2,1)}, bf16[768,256]{1,0:T(8,128)(2,1)}, u32[]{:S(2)}, u32[]{:S(2)}) collective-permute-start(bf16[768,256]{1,0:T(8,128)(2,1)} %get-tuple-element.36), channel_id=1, source_target_pairs={{12,4},{13,5},{14,6},{15,7},{28,20},{29,21},{30,22},{31,23}} | collective-permute-start | bytes 1179656 | tf_op jit(solution)/shard_map/ppermute | solution.py:547
  45.6 2.8 %pack_third.1 = (bf16[1152,256]{1,0:T(8,128)(2,1)}, bf16[768,256]{1,0:T(8,128)(2,1)S(1)}, bf16[768,256]{1,0:T(8,128)(2,1)S(1)}, bf16[768,128]{1,0:T(8,128)(2,1)S(1)}) custom-call(s32[12]{0:T(128)S(1)} %fusion.42.scalars, bf16[384,2560]{1,0:T(8,128)(2,1)} %refs_0_.13, bf16[192,2560]{1,0:T(8,128)(2,1)} %refs_1_.13, bf16[192,2560]{1,0:T(8,128)(2,1)} %refs_2_.13, ...), custom_call_target="tpu_custom_call" | custom-call | bytes 3145728 | tf_op jit(solution)/shard_map/pack_third/pallas_call | solution.py:276
  50.7 1.3 %collective-permute-start.8 = (bf16[1152,256]{1,0:T(8,128)(2,1)}, bf16[1152,256]{1,0:T(8,128)(2,1)}, u32[]{:S(2)}, u32[]{:S(2)}) collective-permute-start(bf16[1152,256]{1,0:T(8,128)(2,1)} %get-tuple-element.38), channel_id=1, source_target_pairs={{8,12},{4,0},{9,13},{5,1},{10,14},{6,2},{11,15},{7,3},{24,28},{20,... | collective-permute-start | bytes 1769480 | tf_op jit(solution)/shard_map/ppermute | solution.py:547
  52.0 1.4 %maximum_bitcast_fusion = bf16[3,3,5,16,3,384]{5,3,1,0,2,4:T(8,128)(2,1)} fusion(bf16[5,3,3,16,1,384]{5,3,2,1,0,4:T(8,128)(2,1)S(1)} %get-tuple-element.59, bf16[5,3,3,16,1,384]{5,3,2,1,0,4:T(8,128)(2,1)S(1)} %get-tuple-element.60, bf16[5,3,3,16,1,384]{5,3,2,1,0,4:T(8,128)(2,1)S(1)} %get-tuple-element.58), kind=kLoop, calls=%fused_computation | loop fusion | flops 1658880 | bytes 3317760 | tf_op jit(solution)/shard_map/transpose | solution.py:777
  53.5 4.0 %copy.34 = bf16[3,3,5,16,3,384]{5,4,3,2,1,0:T(4,128)(2,1)} copy(bf16[3,3,5,16,3,384]{5,3,1,0,2,4:T(8,128)(2,1)} %maximum_bitcast_fusion) | data formatting | bytes 3317760 | tf_op jit(solution)/shard_map/transpose | solution.py:777
  57.5 5.3 %reshape.34.band = bf16[3,240,1152]{2,1,0:T(8,128)(2,1)} reshape(bf16[3,3,5,16,3,384]{5,4,3,2,1,0:T(4,128)(2,1)} %copy.34) | data formatting | bytes 3317760 | tf_op jit(solution)/shard_map/reshape | solution.py:777
  63.5 3.9 %collective-permute-start.10 = (bf16[768,256]{1,0:T(8,128)(2,1)}, bf16[768,256]{1,0:T(8,128)(2,1)S(1)}, u32[]{:S(2)}, u32[]{:S(2)}) collective-permute-start(bf16[768,256]{1,0:T(8,128)(2,1)} %copy-done.7), channel_id=1, source_target_pairs={{0,12},{1,13},{2,14},{3,15},{16,28},{17,29},{18,30},{19,31}} | collective-permute-start | bytes 1179656 | tf_op jit(solution)/shard_map/ppermute | solution.py:547
  68.9 1.0 pad_maximum_fusion
  69.9 7.3 %collective-permute-start.15 = (bf16[768,128]{1,0:T(8,128)(2,1)}, bf16[768,128]{1,0:T(8,128)(2,1)S(1)}, u32[]{:S(2)}, u32[]{:S(2)}) collective-permute-start(bf16[768,128]{1,0:T(8,128)(2,1)} %copy-done.8), channel_id=1, source_target_pairs={{0,8},{1,9},{2,10},{3,11},{16,24},{17,25},{18,26},{19,27}} | collective-permute-start | bytes 589832 | tf_op jit(solution)/shard_map/ppermute | solution.py:547
  77.2 9.0 %main_heads.1.refs_6_ = f32[3,80,384]{2,1,0:T(8,128)S(1)} custom-call(s32[12]{0:T(128)S(1)} %fusion.42.scalars, s32[16]{0:T(128)S(1)} %reshape.30.mask, bf16[384,2560]{1,0:T(8,128)(2,1)} %refs_0_.13, bf16[192,2560]{1,0:T(8,128)(2,1)} %refs_1_.13, bf16[192,2560]{1,0:T(8,128)(2,1)} %refs_2_.13, bf16[384,1280]{1,0:T(8,128)(2,1)S(1)} %collective-permute-done.refs_3_.refs_10_, ...), custom_call_target="tpu_custom_call" | custom-call | flops 1585446912 | bytes 1179648 | tf_op jit(solution)/shard_map/main_heads/pallas_call | solution.py:515
  86.3 2.2 %near_heads.1.refs_6_ = f32[3,80,384]{2,1,0:T(8,128)S(1)} custom-call(s32[12]{0:T(128)S(1)} %fusion.42.scalars, s32[16]{0:T(128)S(1)} %reshape.30.mask, bf16[384,2560]{1,0:T(8,128)(2,1)} %refs_0_.13, bf16[192,2560]{1,0:T(8,128)(2,1)} %refs_1_.13, bf16[192,2560]{1,0:T(8,128)(2,1)} %refs_2_.13, bf16[384,1280]{1,0:T(8,128)(2,1)S(1)} %collective-permute-done.refs_3_.refs_10_, ...), custom_call_target="tpu_custom_call" | custom-call | flops 603979776 | bytes 589824 | tf_op jit(solution)/shard_map/near_heads/pallas_call | solution.py:515
  88.5 8.4 %far_heads.1.refs_6_ = f32[3,80,384]{2,1,0:T(8,128)S(1)} custom-call(s32[12]{0:T(128)S(1)} %fusion.42.scalars, s32[16]{0:T(128)S(1)} %reshape.30.mask, bf16[384,2560]{1,0:T(8,128)(2,1)} %refs_0_.13, bf16[192,2560]{1,0:T(8,128)(2,1)} %refs_1_.13, bf16[192,2560]{1,0:T(8,128)(2,1)} %refs_2_.13, bf16[384,1280]{1,0:T(8,128)(2,1)S(1)} %collective-permute-done.refs_3_.refs_10_, ...), custom_call_target="tpu_custom_call" | custom-call | flops 1056964608 | bytes 589824 | tf_op jit(solution)/shard_map/far_heads/pallas_call | solution.py:515
  96.9 2.3 %last_heads.1 = f32[3,80,384]{2,1,0:T(8,128)S(1)} custom-call(s32[12]{0:T(128)S(1)} %fusion.42.scalars, s32[16]{0:T(128)S(1)} %reshape.30.mask, bf16[384,2560]{1,0:T(8,128)(2,1)} %refs_0_.13, bf16[192,2560]{1,0:T(8,128)(2,1)} %refs_1_.13, bf16[192,2560]{1,0:T(8,128)(2,1)} %refs_2_.13, bf16[384,1280]{1,0:T(8,128)(2,1)S(1)} %collective-permute-done.refs_3_.refs_10_, ...), custom_call_target="tpu_custom_call" | custom-call | flops 603979776 | bytes 589824 | tf_op jit(solution)/shard_map/last_heads/pallas_call | solution.py:515
  100.1 1.4 %collective-permute-done.17 = f32[3,40,384]{2,1,0:T(8,128)S(1)} collective-permute-done((f32[3,40,384]{2,1,0:T(8,128)S(1)}, f32[3,40,384]{2,1,0:T(8,128)S(1)}, u32[]{:S(2)}, u32[]{:S(2)}) %collective-permute-start.17) | collective-permute-done | bytes 184352 | tf_op jit(solution)/shard_map/ppermute | solution.py:932
  102.5 5.5 %collective-permute-start.18 = (f32[40,640]{1,0:T(8,128)S(1)}, f32[40,640]{1,0:T(8,128)S(1)}, u32[]{:S(2)}, u32[]{:S(2)}) collective-permute-start(f32[40,640]{1,0:T(8,128)S(1)} %pad_maximum_fusion.1), channel_id=1, source_target_pairs={{0,4},{4,8},{8,12},{1,5},{5,9},{9,13},{2,6},{6,10},{10,14},{3,7},{... | collective-permute-start | bytes 307208 | tf_op jit(solution)/shard_map/ppermute | solution.py:935
  108.0 2.3 %collective-permute-start.19 = (f32[40,256]{1,0:T(8,128)S(1)}, f32[40,256]{1,0:T(8,128)S(1)}, u32[]{:S(2)}, u32[]{:S(2)}) collective-permute-start(f32[40,256]{1,0:T(8,128)S(1)} %slice.50), channel_id=1, source_target_pairs={{0,8},{4,12},{1,9},{5,13},{2,10},{6,14},{3,11},{7,15},{16,24},{20,... | collective-permute-start | bytes 122888 | tf_op jit(solution)/shard_map/ppermute | solution.py:939
  112.5 4.1 %collective-permute-done.21 = f32[40,640]{1,0:T(8,128)S(1)} collective-permute-done((f32[40,640]{1,0:T(8,128)S(1)}, f32[40,640]{1,0:T(8,128)S(1)}, u32[]{:S(2)}, u32[]{:S(2)}) %collective-permute-start.21) | collective-permute-done | bytes 102432 | tf_op jit(solution)/shard_map/ppermute | solution.py:942
  116.8 1.3 %collective-permute-done.22.other = f32[40,640]{1,0:T(8,128)S(1)} collective-permute-done((f32[40,640]{1,0:T(8,128)S(1)}, f32[40,640]{1,0:T(8,128)S(1)}, u32[]{:S(2)}, u32[]{:S(2)}) %collective-permute-start.22) | collective-permute-done | bytes 102432 | tf_op jit(solution)/shard_map/ppermute | solution.py:943
  118.1 2.4 %finish.1 = (f32[3,8,16,16]{3,2,1,0:T(8,128)}, bf16[3,8,16,384]{3,2,1,0:T(8,128)(2,1)}) custom-call(s32[12]{0:T(128)S(1)} %fusion.42.scalars, f32[40,640]{1,0:T(8,128)S(1)} %add.97.mine, f32[40,640]{1,0:T(8,128)S(1)} %collective-permute-done.22.other, f32[320,80]{1,0:T(8,128)S(1)} %bitcast.47, bf16[320,512]{1,0:T(8,128)(2,1)S(1)} %copy-done.4, ...), custom_call_target="tpu_custom_call" | custom-call | tf_op jit(solution)/shard_map/finish/pallas_call | solution.py:858
  (109 shorter events, 16.8 us)
Async XLA Ops:
  0.6 37.1 %copy-start = (f32[384]{0:T(512)S(1)}, f32[384]{0:T(512)}, u32[]{:S(2)}) copy-start(f32[384]{0:T(512)} %param.21) | copy-start | bytes 4612
  1.3 9.1 %copy-start.1 = (bf16[2560,64]{0,1:T(8,128)(2,1)S(1)}, bf16[2560,64]{0,1:T(8,128)(2,1)}, u32[]{:S(2)}) copy-start(bf16[2560,64]{0,1:T(8,128)(2,1)} %param.18) | copy-start | bytes 983044
  1.4 9.1 %copy-start.14 = (f32[2560]{0:T(1024)S(1)}, f32[2560]{0:T(1024)}, u32[]{:S(2)}) copy-start(f32[2560]{0:T(1024)} %param.16) | copy-start | bytes 30724
  1.4 9.1 %copy-start.16 = (f32[2560]{0:T(1024)S(1)}, f32[2560]{0:T(1024)}, u32[]{:S(2)}) copy-start(f32[2560]{0:T(1024)} %param.17) | copy-start | bytes 30724
  1.4 11.5 %copy-start.13 = (f32[3,8,16,16]{3,2,1,0:T(8,128)S(1)}, f32[3,8,16,16]{3,2,1,0:T(8,128)}, u32[]{:S(2)}) copy-start(f32[3,8,16,16]{3,2,1,0:T(8,128)} %param.19) | copy-start | bytes 73732
  5.4 23.3 %collective-permute-start = (bf16[384,1280]{1,0:T(8,128)(2,1)S(1)}, bf16[384,1280]{1,0:T(8,128)(2,1)S(1)}, u32[]{:S(2)}, u32[]{:S(2)}) collective-permute-start(bf16[384,1280]{1,0:T(8,128)(2,1)S(1)} %get-tuple-element.29), channel_id=1, source_target_pairs={{0,1},{1,0},{2,3},{3,2},{4,5},{5,4},{6,7},{7,6},{8,9},{9,8},{10,11... | collective-permute-start | bytes 2949128 | tf_op jit(solution)/shard_map/ppermute | solution.py:587
  5.9 31.8 %collective-permute-start.3 = (bf16[384,512]{1,0:T(8,128)(2,1)}, bf16[384,512]{1,0:T(8,128)(2,1)S(1)}, u32[]{:S(2)}, u32[]{:S(2)}) collective-permute-start(bf16[384,512]{1,0:T(8,128)(2,1)} %get-tuple-element.32), channel_id=1, source_target_pairs={{0,4},{4,8},{1,5},{5,9},{2,6},{6,10},{3,7},{7,11},{16,20},{20,24},... | collective-permute-start | bytes 1179656 | tf_op jit(solution)/shard_map/ppermute | solution.py:547
  11.4 22.1 %collective-permute-start.14 = (f32[64,2]{1,0:T(8,128)}, f32[64,2]{1,0:T(8,128)}, u32[]{:S(2)}, u32[]{:S(2)}) collective-permute-start(f32[64,2]{1,0:T(8,128)} %copy.33), channel_id=1, source_target_pairs={{0,2},{2,0},{1,3},{3,1},{4,6},{6,4},{5,7},{7,5},{8,10},{10,8},{9,1... | collective-permute-start | bytes 1544 | tf_op jit(solution)/shard_map/ppermute | solution.py:920
  13.2 20.3 %copy-start.9 = (f32[8,16,48]{2,1,0:T(8,128)}, f32[8,16,48]{2,1,0:T(8,128)S(1)}, u32[]{:S(2)}) copy-start(f32[8,16,48]{2,1,0:T(8,128)S(1)} %reshape.31) | copy-start | bytes 73732
  13.3 7.8 %collective-permute-start.11 = (f32[8,16,32]{2,1,0:T(8,128)S(1)}, f32[8,16,32]{2,1,0:T(8,128)S(1)}, u32[]{:S(2)}, u32[]{:S(2)}) collective-permute-start(f32[8,16,32]{2,1,0:T(8,128)S(1)} %slice.44), channel_id=1, source_target_pairs={{0,4},{4,8},{8,12},{1,5},{5,9},{9,13},{2,6},{6,10},{10,14},{3,7},{... | collective-permute-start | bytes 49160 | tf_op jit(solution)/shard_map/ppermute | solution.py:46
  16.8 27.3 %collective-permute-start.1 = (bf16[384,512]{1,0:T(8,128)(2,1)}, bf16[384,512]{1,0:T(8,128)(2,1)S(1)}, u32[]{:S(2)}, u32[]{:S(2)}) collective-permute-start(bf16[384,512]{1,0:T(8,128)(2,1)} %get-tuple-element.30), channel_id=1, source_target_pairs={{4,0},{8,4},{12,8},{5,1},{9,5},{13,9},{6,2},{10,6},{14,10},{7,3},{... | collective-permute-start | bytes 1179656 | tf_op jit(solution)/shard_map/ppermute | solution.py:547
  21.2 1.2 %collective-permute-start.12 = (f32[8,80]{1,0:T(8,128)S(1)}, f32[8,80]{1,0:T(8,128)S(1)}, u32[]{:S(2)}, u32[]{:S(2)}) collective-permute-start(f32[8,80]{1,0:T(8,128)S(1)} %select_bitcast_fusion.2), channel_id=1, source_target_pairs={{0,1},{1,0},{2,3},{3,2},{4,5},{5,4},{6,7},{7,6},{8,9},{9,8},{10,11... | collective-permute-start | bytes 7688 | tf_op jit(solution)/shard_map/ppermute | solution.py:737
  23.0 27.7 %collective-permute-start.4 = (bf16[384,512]{1,0:T(8,128)(2,1)}, bf16[384,512]{1,0:T(8,128)(2,1)S(1)}, u32[]{:S(2)}, u32[]{:S(2)}) collective-permute-start(bf16[384,512]{1,0:T(8,128)(2,1)} %copy-done.5), channel_id=1, source_target_pairs={{0,5},{1,4},{4,9},{5,8},{2,7},{3,6},{6,11},{7,10},{16,21},{17,20},... | collective-permute-start | bytes 1179656 | tf_op jit(solution)/shard_map/ppermute | solution.py:551
  28.7 16.8 %copy-start.12 = (bf16[432,384]{1,0:T(8,128)(2,1)S(1)}, bf16[432,384]{1,0:T(8,128)(2,1)}, u32[]{:S(2)}) copy-start(bf16[432,384]{1,0:T(8,128)(2,1)} %param.20) | copy-start | bytes 995332
  28.8 7.5 %collective-permute-start.13 = (f32[32,80]{1,0:T(8,128)S(1)}, f32[32,80]{1,0:T(8,128)S(1)}, u32[]{:S(2)}, u32[]{:S(2)}) collective-permute-start(f32[32,80]{1,0:T(8,128)S(1)} %fusion.34), channel_id=1, source_target_pairs={{0,2},{2,0},{1,3},{3,1},{4,6},{6,4},{5,7},{7,5},{8,10},{10,8},{9,1... | collective-permute-start | bytes 30728 | tf_op jit(solution)/shard_map/ppermute | solution.py:749
  33.5 33.9 %collective-permute-start.2 = (bf16[768,512]{1,0:T(8,128)(2,1)}, bf16[768,512]{1,0:T(8,128)(2,1)S(1)}, u32[]{:S(2)}, u32[]{:S(2)}) collective-permute-start(bf16[768,512]{1,0:T(8,128)(2,1)} %get-tuple-element.31), channel_id=1, source_target_pairs={{4,0},{8,4},{12,8},{5,1},{9,5},{13,9},{6,2},{10,6},{14,10},{7,3},{... | collective-permute-start | bytes 2359304 | tf_op jit(solution)/shard_map/ppermute | solution.py:547
  36.3 27.3 %collective-permute-start.6 = (bf16[384,512]{1,0:T(8,128)(2,1)}, bf16[384,512]{1,0:T(8,128)(2,1)}, u32[]{:S(2)}, u32[]{:S(2)}) collective-permute-start(bf16[384,512]{1,0:T(8,128)(2,1)} %get-tuple-element.35), channel_id=1, source_target_pairs={{12,4},{13,5},{14,6},{15,7},{28,20},{29,21},{30,22},{31,23}} | collective-permute-start | bytes 1179656 | tf_op jit(solution)/shard_map/ppermute | solution.py:547
  37.7 32.2 %collective-permute-start.5 = (bf16[768,384]{1,0:T(8,128)(2,1)}, bf16[768,384]{1,0:T(8,128)(2,1)}, u32[]{:S(2)}, u32[]{:S(2)}) collective-permute-start(bf16[768,384]{1,0:T(8,128)(2,1)} %get-tuple-element.34), channel_id=1, source_target_pairs={{0,8},{1,9},{2,10},{3,11},{16,24},{17,25},{18,26},{19,27}} | collective-permute-start | bytes 1769480 | tf_op jit(solution)/shard_map/ppermute | solution.py:547
  44.1 24.1 %collective-permute-start.7 = (bf16[768,256]{1,0:T(8,128)(2,1)}, bf16[768,256]{1,0:T(8,128)(2,1)}, u32[]{:S(2)}, u32[]{:S(2)}) collective-permute-start(bf16[768,256]{1,0:T(8,128)(2,1)} %get-tuple-element.36), channel_id=1, source_target_pairs={{12,4},{13,5},{14,6},{15,7},{28,20},{29,21},{30,22},{31,23}} | collective-permute-start | bytes 1179656 | tf_op jit(solution)/shard_map/ppermute | solution.py:547
  50.7 37.9 %collective-permute-start.8 = (bf16[1152,256]{1,0:T(8,128)(2,1)}, bf16[1152,256]{1,0:T(8,128)(2,1)}, u32[]{:S(2)}, u32[]{:S(2)}) collective-permute-start(bf16[1152,256]{1,0:T(8,128)(2,1)} %get-tuple-element.38), channel_id=1, source_target_pairs={{8,12},{4,0},{9,13},{5,1},{10,14},{6,2},{11,15},{7,3},{24,28},{20,... | collective-permute-start | bytes 1769480 | tf_op jit(solution)/shard_map/ppermute | solution.py:547
  63.5 25.0 %collective-permute-start.10 = (bf16[768,256]{1,0:T(8,128)(2,1)}, bf16[768,256]{1,0:T(8,128)(2,1)S(1)}, u32[]{:S(2)}, u32[]{:S(2)}) collective-permute-start(bf16[768,256]{1,0:T(8,128)(2,1)} %copy-done.7), channel_id=1, source_target_pairs={{0,12},{1,13},{2,14},{3,15},{16,28},{17,29},{18,30},{19,31}} | collective-permute-start | bytes 1179656 | tf_op jit(solution)/shard_map/ppermute | solution.py:547
  67.5 21.1 %collective-permute-start.9 = (bf16[768,256]{1,0:T(8,128)(2,1)}, bf16[768,256]{1,0:T(8,128)(2,1)S(1)}, u32[]{:S(2)}, u32[]{:S(2)}) collective-permute-start(bf16[768,256]{1,0:T(8,128)(2,1)} %copy-done.7), channel_id=1, source_target_pairs={{4,12},{5,13},{6,14},{7,15},{20,28},{21,29},{22,30},{23,31}} | collective-permute-start | bytes 1179656 | tf_op jit(solution)/shard_map/ppermute | solution.py:547
  68.2 28.7 %collective-permute-start.16 = (bf16[768,256]{1,0:T(8,128)(2,1)}, bf16[768,256]{1,0:T(8,128)(2,1)S(1)}, u32[]{:S(2)}, u32[]{:S(2)}) collective-permute-start(bf16[768,256]{1,0:T(8,128)(2,1)} %copy-done.6), channel_id=1, source_target_pairs={{12,4},{13,5},{14,6},{15,7},{28,20},{29,21},{30,22},{31,23}} | collective-permute-start | bytes 1179656 | tf_op jit(solution)/shard_map/ppermute | solution.py:547
  69.9 27.0 %collective-permute-start.15 = (bf16[768,128]{1,0:T(8,128)(2,1)}, bf16[768,128]{1,0:T(8,128)(2,1)S(1)}, u32[]{:S(2)}, u32[]{:S(2)}) collective-permute-start(bf16[768,128]{1,0:T(8,128)(2,1)} %copy-done.8), channel_id=1, source_target_pairs={{0,8},{1,9},{2,10},{3,11},{16,24},{17,25},{18,26},{19,27}} | collective-permute-start | bytes 589832 | tf_op jit(solution)/shard_map/ppermute | solution.py:547
  100.0 18.1 %copy-start.2 = (bf16[3,240,1152]{2,1,0:T(8,128)(2,1)S(1)}, bf16[3,240,1152]{2,1,0:T(8,128)(2,1)}, u32[]{:S(2)}) copy-start(bf16[3,240,1152]{2,1,0:T(8,128)(2,1)} %reshape.34.band) | copy-start | bytes 4976644
  100.0 18.1 %copy-start.4 = (bf16[320,512]{1,0:T(8,128)(2,1)S(1)}, bf16[320,512]{1,0:T(8,128)(2,1)}, u32[]{:S(2)}) copy-start(bf16[320,512]{1,0:T(8,128)(2,1)} %fusion.30.selector) | copy-start | bytes 983044
  100.0 1.5 %collective-permute-start.17 = (f32[3,40,384]{2,1,0:T(8,128)S(1)}, f32[3,40,384]{2,1,0:T(8,128)S(1)}, u32[]{:S(2)}, u32[]{:S(2)}) collective-permute-start(f32[3,40,384]{2,1,0:T(8,128)S(1)} %constant_dynamic-slice_fusion), channel_id=1, source_target_pairs={{0,1},{1,0},{2,3},{3,2},{4,5},{5,4},{6,7},{7,6},{8,9},{9,8},{10,11... | collective-permute-start | bytes 552968 | tf_op jit(solution)/shard_map/ppermute | solution.py:932
  102.5 9.4 %collective-permute-start.18 = (f32[40,640]{1,0:T(8,128)S(1)}, f32[40,640]{1,0:T(8,128)S(1)}, u32[]{:S(2)}, u32[]{:S(2)}) collective-permute-start(f32[40,640]{1,0:T(8,128)S(1)} %pad_maximum_fusion.1), channel_id=1, source_target_pairs={{0,4},{4,8},{8,12},{1,5},{5,9},{9,13},{2,6},{6,10},{10,14},{3,7},{... | collective-permute-start | bytes 307208 | tf_op jit(solution)/shard_map/ppermute | solution.py:935
  108.0 3.9 %collective-permute-start.19 = (f32[40,256]{1,0:T(8,128)S(1)}, f32[40,256]{1,0:T(8,128)S(1)}, u32[]{:S(2)}, u32[]{:S(2)}) collective-permute-start(f32[40,256]{1,0:T(8,128)S(1)} %slice.50), channel_id=1, source_target_pairs={{0,8},{4,12},{1,9},{5,13},{2,10},{6,14},{3,11},{7,15},{16,24},{20,... | collective-permute-start | bytes 122888 | tf_op jit(solution)/shard_map/ppermute | solution.py:939
  110.3 1.7 %collective-permute-start.20 = (f32[40,384]{1,0:T(8,128)S(1)}, f32[40,384]{1,0:T(8,128)S(1)}, u32[]{:S(2)}, u32[]{:S(2)}) collective-permute-start(f32[40,384]{1,0:T(8,128)S(1)} %get-tuple-element.61), channel_id=1, source_target_pairs={{4,12},{12,8},{5,13},{13,9},{6,14},{14,10},{7,15},{15,11},{20,28},... | collective-permute-start | bytes 184328 | tf_op jit(solution)/shard_map/ppermute | solution.py:938
  111.9 4.7 %collective-permute-start.21 = (f32[40,640]{1,0:T(8,128)S(1)}, f32[40,640]{1,0:T(8,128)S(1)}, u32[]{:S(2)}, u32[]{:S(2)}) collective-permute-start(f32[40,640]{1,0:T(8,128)S(1)} %fusion.32), channel_id=1, source_target_pairs={{0,2},{2,0},{1,3},{3,1},{4,6},{6,4},{5,7},{7,5},{8,10},{10,8},{9,1... | collective-permute-start | bytes 307208 | tf_op jit(solution)/shard_map/ppermute | solution.py:942
  116.7 1.4 %collective-permute-start.22 = (f32[40,640]{1,0:T(8,128)S(1)}, f32[40,640]{1,0:T(8,128)S(1)}, u32[]{:S(2)}, u32[]{:S(2)}) collective-permute-start(f32[40,640]{1,0:T(8,128)S(1)} %add.97.mine), channel_id=1, source_target_pairs={{0,1},{1,0},{2,3},{3,2},{4,5},{5,4},{6,7},{7,6},{8,9},{9,8},{10,11... | collective-permute-start | bytes 307208 | tf_op jit(solution)/shard_map/ppermute | solution.py:943
  (16 other events, 46.4 us)

commit v6 on v5

--- a/solution.py
+++ b/solution.py
@@ -252,7 +252,7 @@
     return row + lax.axis_index("slab") * jnp.array(by_slab)
 
 
-def pack_kernel(inputs, copies, scalars, *refs):
+def pack_kernel(inputs, copies, with_noise, scalars, *refs):
     ins, outs, semaphores = refs[:inputs], refs[inputs:-1], refs[-1]
     started = []
     for number, (source, row, rows, entries, shift, target, at, heads) in enumerate(copies):
@@ -267,21 +267,35 @@
         )
         copy.start()
         started.append(copy)
+    if with_noise:
+        noisy, out = ins[-1], outs[-1]
+        frames = noisy.shape[0]
+        out[...] = jnp.concatenate([noisy[frame] for frame in range(frames)], axis=-1)
     for copy in started:
         copy.wait()
 
 
-def pack(scalars, arrays, shapes, copies, name):
+def pack(scalars, arrays, shapes, copies, name, noisy=None):
     moved = sum(2 * 2 * rows * heads * HD for _, _, rows, _, _, _, _, heads in copies)
+    out_shape = [pltpu.HBM(shape, jnp.bfloat16) for shape in shapes]
+    in_specs = [pl.BlockSpec(memory_space=pl.ANY)] * len(arrays)
+    out_specs = [pl.BlockSpec(shape, lambda i, scalars: (0, 0)) for shape in shapes]
+    if noisy is not None:
+        frames, height, breadth, channels = noisy.shape
+        lanes = frames * channels
+        arrays = arrays + (noisy,)
+        in_specs.append(pl.BlockSpec(noisy.shape, lambda i, scalars: (0, 0, 0, 0)))
+        out_shape.append(jax.ShapeDtypeStruct((height, breadth, lanes), noisy.dtype))
+        out_specs.append(pl.BlockSpec((height, breadth, lanes), lambda i, scalars: (0, 0, 0)))
     return pl.pallas_call(
-        functools.partial(pack_kernel, len(arrays), copies),
+        functools.partial(pack_kernel, len(arrays), copies, noisy is not None),
         name=name,
-        out_shape=[jax.ShapeDtypeStruct(shape, jnp.bfloat16) for shape in shapes],
+        out_shape=out_shape,
         grid_spec=pltpu.PrefetchScalarGridSpec(
             num_scalar_prefetch=1,
             grid=(1,),
-            in_specs=[pl.BlockSpec(memory_space=pl.ANY)] * len(arrays),
-            out_specs=[pl.BlockSpec(shape, lambda i, scalars: (0, 0)) for shape in shapes],
+            in_specs=in_specs,
+            out_specs=out_specs,
             scratch_shapes=[pltpu.SemaphoreType.DMA((len(copies),))],
         ),
         compiler_params=pltpu.CompilerParams(vmem_limit_bytes=GRANT),
@@ -289,7 +303,7 @@
     )(scalars, *arrays)
 
 
-def message(scalars, pieces, arrays, name):
+def message(scalars, pieces, arrays, name, noisy=None):
     copies, shapes = [], []
     for target, parts in enumerate(pieces):
         at = 0
@@ -297,7 +311,7 @@
             copies.append((source, row, rows, entries, shift, target, at, heads))
             at += rows
         shapes.append((at, parts[0][5] * HD))
-    return pack(scalars, arrays, shapes, copies, name)
+    return pack(scalars, arrays, shapes, copies, name, noisy)
 
 
 class Tokens(typing.NamedTuple):
@@ -535,7 +549,7 @@
     )(scalars, mask, *arrays)
 
 
-def token_sums(scalars, queries, keys, values, span_mask, head_gain, patch_weight):
+def token_sums(scalars, queries, keys, values, span_mask, head_gain, patch_weight, noisy):
     rows = queries.shape[0]
     half = rows // 2
     heads = NEAR_HEADS + MIDDLE_HEADS + FAR_HEADS
@@ -571,7 +585,7 @@
             )
         ]
 
-    handed, up_same, up_across, query_down, query_two = message(
+    handed, up_same, up_across, query_down, query_two, noise = message(
         scalars,
         [
             [(part, 0, half, (OTHER,), 0, heads) for part in (1, 2)],
@@ -582,8 +596,10 @@
         ],
         (queries, keys, values),
         "pack_first",
-    )
-    anchor = handed
+        noisy,
+    )
+    lanes = 2 * noisy.shape[3]
+    noise = jnp.concatenate([from_behind(noise[:, :, -lanes:], "span", 1), noise], axis=2)
     received = lax.ppermute(handed, "slab", SWAP)
     up_same = send(up_same, (0, 1), (1, 2))
     up_across = send_across(up_across, (0, 1), (1, 2))
@@ -597,6 +613,7 @@
         arrays,
         "pack_second",
     )
+    anchor = pair_down
     pair_down = send(pair_down, (1, 0), (2, 1), (3, 2))
     pair_two = send(pair_two, (3, 1))
     up_two = send(up_two, (0, 2))
@@ -616,10 +633,9 @@
     far_two = send(far_pair, (1, 3))
     far_three = send(far_pair, (0, 3))
     far_next = send(far_all, (2, 3), (1, 0))
-    last_two, last_up, _ = lax.optimization_barrier((last_two, last_up, pair_down))
-    last_two = send(last_two, (3, 1))
-    last_up = send(last_up, (0, 2))
-
+    span_mask, head_gain, patch_weight, _ = lax.optimization_barrier(
+        (span_mask, head_gain, patch_weight, anchor)
+    )
     mask = span_mask.reshape(-1)
     weight = patch_weight.T
     own = (queries, keys, values, received, weight, head_gain[None, :])
@@ -658,6 +674,9 @@
         more=False,
         name="main_heads",
     )
+    last_two, last_up, sums = lax.optimization_barrier((last_two, last_up, sums))
+    last_two = send(last_two, (3, 1))
+    last_up = send(last_up, (0, 2))
     on_two = Tokens(5, (6,))
     last_span = [(on_two, 2, 3, [(back_one, 0), (here, 1), (on_one, 2), (on_two, 3)])]
     sums = run(
@@ -724,14 +743,11 @@
             name="last_heads",
         )
 
-    return sums, last, anchor, pair_down
-
-
-def noise_window(noisy_latent):
-    frames, height, breadth, channels = noisy_latent.shape
-    own = noisy_latent.transpose(1, 2, 0, 3).reshape(height, breadth, frames * channels)
-    earlier = from_behind(own[:, :, (frames - 2) * channels :], "span", 1)
-    grid = jnp.concatenate([earlier, own], axis=2)
+    return sums, last, anchor, noise
+
+
+def noise_window(grid):
+    height, breadth, _ = grid.shape
     slab = lax.axis_index("slab")
     edge = jnp.where(slab == 0, grid[:, breadth - 1], grid[:, 0])
     edge = lax.ppermute(edge, "slab", SWAP)[:, None]
@@ -900,15 +916,15 @@
     place = lax.axis_index("span")
     slab = lax.axis_index("slab")
     scalars = scalar_operand(heads_dev // lax.axis_size("slab"))
-    sums, last, anchor, later = token_sums(
-        scalars, queries, keys, values, span_mask, head_gain, patch_weight
-    )
-
-    noisy, weight, gain, shift, taps, bias, _ = lax.optimization_barrier(
-        (noisy_latent, patch_weight, head_gain, head_shift, conv_weight, conv_bias, anchor)
-    )
-    _, height, breadth, _ = noisy.shape
-    noise = noise_window(noisy)
+    sums, last, anchor, noise = token_sums(
+        scalars, queries, keys, values, span_mask, head_gain, patch_weight, noisy_latent
+    )
+
+    noise, weight, gain, shift, taps, bias, _ = lax.optimization_barrier(
+        (noise, patch_weight, head_gain, head_shift, conv_weight, conv_bias, anchor)
+    )
+    height, breadth, _ = noise.shape
+    noise = noise_window(noise)
     wide_weight = weight.T.astype(jnp.float32)
     constants = jnp.stack(
         [

time: 122 us -> 113 us (0.926)
  other arithmetic: 9.83 us -> 3.75 us
  starting transfers between devices: 50.6 us -> 54.6 us
  local copies, waits for them, and re-layouts: 15 us -> 11.3 us
  waiting for transfers between devices: 10.3 us -> 7.57 us
    ppermute x1, starting transfers between devices: 2.26 us -> 9.95 us  [per_device(): to_before = lax.ppermute(after[:, skip:], 'span', [(0, 2), (1, 3)])]
    ppermute x11, starting transfers between devices: 30.1 us -> 24.3 us  [send(): return lax.ppermute(value, 'span', list(pairs))]
    unnamed x52 -> x34, local copies, waits for them, and re-layouts: 4.37 us -> 1.73 us
    ppermute x1, starting transfers between devices: 5.49 us -> 7.58 us  [per_device(): lax.ppermute(jnp.concatenate([own[:, skip:], after], axis=1), 'span', [(0...]
    ppermute x1, waiting for transfers between devices: 1.82 us -> 0.01 us  [from_behind(): return lax.ppermute(value, axis, pairs)]
    transpose x1, local copies, waits for them, and re-layouts: 3.98 us -> 2.52 us  [banded_weight(): banded.transpose(1, 2, 0, 3, 4, 5)]
    another operation x1, local copies, waits for them, and re-layouts: 0.14 us -> 1.46 us  [banded_weight(): jnp.stack([jnp.pad(taps, ((n, FRAMES_SPAN - 1 - n), (0, 0), (0, 0), (0, 0...]
  transfers between devices with their start and end apart: 23 -> 23, of which waited for: 6 -> 4; matrix products, arithmetic and copies ran while one was open for 16% -> 10% of each run, Pallas kernels for 21% -> 23%
where the time goes in v6:
time: 113 us; the launch traced here: 112 us
  starting transfers between devices  54.6 us (48%)
  Pallas kernels  33.7 us (30%)
  local copies, waits for them, and re-layouts  11.3 us (10%)
  waiting for transfers between devices  7.57 us (7%)
  other arithmetic  3.75 us (3%)
  between operations  1.32 us (1%)
    ppermute x11, starting transfers between devices, send(): return lax.ppermute(value, 'span', list(pairs))  24.3 us
    pallas_call x4, Pallas kernels, attend(): pl.pallas_call(functools.partial(attend_kernel, variants, extra, span_cou...  21.2 us
    pallas_call x3, Pallas kernels, pack(): pl.pallas_call(functools.partial(pack_kernel, len(arrays), copies, noisy...  10 us
    ppermute x1, starting transfers between devices, per_device(): to_before = lax.ppermute(after[:, skip:], 'span', [(0, 2), (1, 3)])  9.95 us
    ppermute x1, starting transfers between devices, per_device(): lax.ppermute(jnp.concatenate([own[:, skip:], after], axis=1), 'span', [(0...  7.58 us
    reshape x1, local copies, waits for them, and re-layouts, banded_weight(): banded.transpose(1, 2, 0, 3, 4, 5)  5.27 us
    ppermute x1, starting transfers between devices, from_behind(): return lax.ppermute(value, axis, pairs)  4.48 us
    ppermute x1, waiting for transfers between devices, per_device(): total = total + lax.ppermute(total, 'head', SWAP)  3.85 us
  transfers between devices with their start and end apart: 23, of which 4 were waited for; matrix products, arithmetic and copies ran while one was open for 10% of the time, Pallas kernels for 23%

profile of v6, /device:TPU:0, one launch (start us, length us, event | category | flops | bytes accessed | tf_op | source)
XLA Modules:
  0.0 112.2 jit_solution(852229184462628388)
XLA Ops:
  1.4 0.9 copy-done.5
  2.3 3.8 %pack_first.1 = (bf16[384,1280]{1,0:T(8,128)(2,1)}, bf16[384,512]{1,0:T(8,128)(2,1)}, bf16[384,512]{1,0:T(8,128)(2,1)}, bf16[384,512]{1,0:T(8,128)(2,1)}, bf16[3...) custom-call(s32[12]{0:T(128)S(1)} %fusion.43.scalars, bf16[384,2560]{1,0:T(8,128)(2,1)} %refs_0_.13, ...), custom_call_target="tpu_custom_call" | custom-call | bytes 5111808 | tf_op jit(solution)/shard_map/pack_first/pallas_call | solution.py:290
  6.7 4.5 %collective-permute-start.11 = (f32[8,16,32]{2,1,0:T(8,128)S(1)}, f32[8,16,32]{2,1,0:T(8,128)S(1)}, u32[]{:S(2)}, u32[]{:S(2)}) collective-permute-start(f32[8,16,32]{2,1,0:T(8,128)S(1)} %slice.33), channel_id=1, source_target_pairs={{0,4},{4,8},{8,12},{1,5},{5,9},{9,13},{2,6},{6,10},{10,14},{3,7},{... | collective-permute-start | bytes 49160 | tf_op jit(solution)/shard_map/ppermute | solution.py:46
  11.2 3.4 %collective-permute-start.1 = (bf16[384,512]{1,0:T(8,128)(2,1)}, bf16[384,512]{1,0:T(8,128)(2,1)S(1)}, u32[]{:S(2)}, u32[]{:S(2)}) collective-permute-start(bf16[384,512]{1,0:T(8,128)(2,1)} %get-tuple-element.39), channel_id=1, source_target_pairs={{0,4},{4,8},{1,5},{5,9},{2,6},{6,10},{3,7},{7,11},{16,20},{20,24},... | collective-permute-start | bytes 1179656 | tf_op jit(solution)/shard_map/ppermute | solution.py:561
  14.7 1.3 %collective-permute-start.2 = (bf16[384,512]{1,0:T(8,128)(2,1)}, bf16[384,512]{1,0:T(8,128)(2,1)S(1)}, u32[]{:S(2)}, u32[]{:S(2)}) collective-permute-start(bf16[384,512]{1,0:T(8,128)(2,1)} %get-tuple-element.43), channel_id=1, source_target_pairs={{4,0},{8,4},{12,8},{5,1},{9,5},{13,9},{6,2},{10,6},{14,10},{7,3},{... | collective-permute-start | bytes 1179656 | tf_op jit(solution)/shard_map/ppermute | solution.py:561
  16.0 3.8 %collective-permute-start.4 = (bf16[384,512]{1,0:T(8,128)(2,1)}, bf16[384,512]{1,0:T(8,128)(2,1)S(1)}, u32[]{:S(2)}, u32[]{:S(2)}) collective-permute-start(bf16[384,512]{1,0:T(8,128)(2,1)} %get-tuple-element.44), channel_id=1, source_target_pairs={{0,5},{1,4},{4,9},{5,8},{2,7},{3,6},{6,11},{7,10},{16,21},{17,20},... | collective-permute-start | bytes 1179656 | tf_op jit(solution)/shard_map/ppermute | solution.py:565
  19.9 1.4 %fusion.30.selector = bf16[320,512]{1,0:T(8,128)(2,1)} fusion(s32[320]{0:T(512)S(1)} %get-tuple-element.79, s32[320]{0:T(512)S(1)} %get-tuple-element.80, s32[]{:T(128)S(6)} %mul.56, s32[320]{0:T(512)S(1)} %get-tuple-element.78, s32[320]{0:T(512)S(1)} %get-tuple-element.81, s32[]{:T(128)S(6)} %mul.55, pred[320]{0:T(512)(128)(4,1)S(1)} %get-tuple-element.83, ...), kind=kLoop, calls=%fused_computation.47 | loop fusion | flops 10158080 | bytes 333448 | tf_op jit(solution)/shard_map/convert_element_type | solution.py:780
  21.4 3.2 %pack_second.1 = (bf16[768,512]{1,0:T(8,128)(2,1)}, bf16[768,256]{1,0:T(8,128)(2,1)}, bf16[768,384]{1,0:T(8,128)(2,1)}) custom-call(s32[12]{0:T(128)S(1)} %fusion.43.scalars, bf16[384,2560]{1,0:T(8,128)(2,1)} %refs_0_.13, bf16[192,2560]{1,0:T(8,128)(2,1)} %refs_1_.13, bf16[192,2560]{1,0:T(8,128)(2,1)} %refs_2_.13, ...), custom_call_target="tpu_custom_call" | custom-call | bytes 3538944 | tf_op jit(solution)/shard_map/pack_second/pallas_call | solution.py:290
  24.6 1.3 %collective-permute-start.3 = (bf16[768,512]{1,0:T(8,128)(2,1)}, bf16[768,512]{1,0:T(8,128)(2,1)S(1)}, u32[]{:S(2)}, u32[]{:S(2)}) collective-permute-start(bf16[768,512]{1,0:T(8,128)(2,1)} %get-tuple-element.35), channel_id=1, source_target_pairs={{4,0},{8,4},{12,8},{5,1},{9,5},{13,9},{6,2},{10,6},{14,10},{7,3},{... | collective-permute-start | bytes 2359304 | tf_op jit(solution)/shard_map/ppermute | solution.py:561
  26.3 1.5 %collective-permute-start.14 = (f32[64,2]{1,0:T(8,128)S(1)}, f32[64,2]{1,0:T(8,128)S(1)}, u32[]{:S(2)}, u32[]{:S(2)}) collective-permute-start(f32[64,2]{1,0:T(8,128)S(1)} %copy.32), channel_id=1, source_target_pairs={{0,2},{2,0},{1,3},{3,1},{4,6},{6,4},{5,7},{7,5},{8,10},{10,8},{9,1... | collective-permute-start | bytes 1544 | tf_op jit(solution)/shard_map/ppermute | solution.py:936
  27.9 6.4 %collective-permute-start.5 = (bf16[768,384]{1,0:T(8,128)(2,1)}, bf16[768,384]{1,0:T(8,128)(2,1)}, u32[]{:S(2)}, u32[]{:S(2)}) collective-permute-start(bf16[768,384]{1,0:T(8,128)(2,1)} %get-tuple-element.45), channel_id=1, source_target_pairs={{0,8},{1,9},{2,10},{3,11},{16,24},{17,25},{18,26},{19,27}} | collective-permute-start | bytes 1769480 | tf_op jit(solution)/shard_map/ppermute | solution.py:561
  34.2 1.5 %pad_bitcast_fusion.2 = (bf16[5,3,3,16,1,384]{5,3,2,1,0,4:T(8,128)(2,1)S(1)}, bf16[5,3,3,16,1,384]{5,3,2,1,0,4:T(8,128)(2,1)S(1)}, bf16[5,3,3,16,1,384]{5,3,2,1,0,4:T(8,128)(2,1)S(1)}) fusion(bf16[3,3,3,16,384]{4,3,2,1,0:T(8,128)(2,1)} %bitcast.46), kind=kLoop, calls=%fused_computation.51 | loop fusion | bytes 1990656 | tf_op jit(solution)/shard_map/stack | solution.py:786
  36.0 2.5 %copy.33 = bf16[3,3,5,16,3,384]{5,4,3,2,1,0:T(4,128)(2,1)} copy(bf16[3,3,5,16,3,384]{5,3,1,0,2,4:T(8,128)(2,1)S(1)} %maximum_bitcast_fusion) | data formatting | bytes 3317760 | tf_op jit(solution)/shard_map/transpose | solution.py:793
  38.5 5.3 %reshape.30.band = bf16[3,240,1152]{2,1,0:T(8,128)(2,1)} reshape(bf16[3,3,5,16,3,384]{5,4,3,2,1,0:T(4,128)(2,1)} %copy.33) | data formatting | bytes 3317760 | tf_op jit(solution)/shard_map/reshape | solution.py:793
  43.9 3.1 %pack_third.1 = (bf16[1152,256]{1,0:T(8,128)(2,1)}, bf16[768,256]{1,0:T(8,128)(2,1)}, bf16[768,256]{1,0:T(8,128)(2,1)}, bf16[768,128]{1,0:T(8,128)(2,1)}) custom-call(s32[12]{0:T(128)S(1)} %fusion.43.scalars, bf16[384,2560]{1,0:T(8,128)(2,1)} %refs_0_.13, bf16[192,2560]{1,0:T(8,128)(2,1)} %refs_1_.13, bf16[192,2560]{1,0:T(8,128)(2,1)} %refs_2_.13, ...), custom_call_target="tpu_custom_call" | custom-call | bytes 3145728 | tf_op jit(solution)/shard_map/pack_third/pallas_call | solution.py:290
  48.5 1.3 %collective-permute-start.8 = (bf16[1152,256]{1,0:T(8,128)(2,1)}, bf16[1152,256]{1,0:T(8,128)(2,1)S(1)}, u32[]{:S(2)}, u32[]{:S(2)}) collective-permute-start(bf16[1152,256]{1,0:T(8,128)(2,1)} %get-tuple-element.49), channel_id=1, source_target_pairs={{8,12},{4,0},{9,13},{5,1},{10,14},{6,2},{11,15},{7,3},{24,28},{20,... | collective-permute-start | bytes 1769480 | tf_op jit(solution)/shard_map/ppermute | solution.py:561
  49.8 4.2 %collective-permute-start.10 = (bf16[768,256]{1,0:T(8,128)(2,1)}, bf16[768,256]{1,0:T(8,128)(2,1)S(1)}, u32[]{:S(2)}, u32[]{:S(2)}) collective-permute-start(bf16[768,256]{1,0:T(8,128)(2,1)} %get-tuple-element.50), channel_id=1, source_target_pairs={{0,12},{1,13},{2,14},{3,15},{16,28},{17,29},{18,30},{19,31}} | collective-permute-start | bytes 1179656 | tf_op jit(solution)/shard_map/ppermute | solution.py:561
  54.7 9.1 %main_heads.1.refs_6_ = f32[3,80,384]{2,1,0:T(8,128)S(1)} custom-call(s32[12]{0:T(128)S(1)} %fusion.43.scalars, s32[16]{0:T(128)S(1)} %reshape.27.mask, bf16[384,2560]{1,0:T(8,128)(2,1)} %refs_0_.13, bf16[192,2560]{1,0:T(8,128)(2,1)} %refs_1_.13, bf16[192,2560]{1,0:T(8,128)(2,1)} %refs_2_.13, bf16[384,1280]{1,0:T(8,128)(2,1)S(1)} %collective-permute-done.refs_3_.refs_10_, ...), custom_call_target="tpu_custom_call" | custom-call | flops 1585446912 | bytes 1179648 | tf_op jit(solution)/shard_map/main_heads/pallas_call | solution.py:529
  65.3 3.6 %collective-permute-start.15 = (bf16[768,128]{1,0:T(8,128)(2,1)S(1)}, bf16[768,128]{1,0:T(8,128)(2,1)S(1)}, u32[]{:S(2)}, u32[]{:S(2)}) collective-permute-start(bf16[768,128]{1,0:T(8,128)(2,1)S(1)} %copy-done.15), channel_id=1, source_target_pairs={{0,8},{1,9},{2,10},{3,11},{16,24},{17,25},{18,26},{19,27}} | collective-permute-start | bytes 589832 | tf_op jit(solution)/shard_map/ppermute | solution.py:561
  69.0 2.1 %near_heads.1.refs_6_ = f32[3,80,384]{2,1,0:T(8,128)S(1)} custom-call(s32[12]{0:T(128)S(1)} %fusion.43.scalars, s32[16]{0:T(128)S(1)} %reshape.27.mask, bf16[384,2560]{1,0:T(8,128)(2,1)} %refs_0_.13, bf16[192,2560]{1,0:T(8,128)(2,1)} %refs_1_.13, bf16[192,2560]{1,0:T(8,128)(2,1)} %refs_2_.13, bf16[384,1280]{1,0:T(8,128)(2,1)S(1)} %collective-permute-done.refs_3_.refs_10_, ...), custom_call_target="tpu_custom_call" | custom-call | flops 603979776 | bytes 589824 | tf_op jit(solution)/shard_map/near_heads/pallas_call | solution.py:529
  71.1 8.2 %far_heads.1.refs_6_ = f32[3,80,384]{2,1,0:T(8,128)S(1)} custom-call(s32[12]{0:T(128)S(1)} %fusion.43.scalars, s32[16]{0:T(128)S(1)} %reshape.27.mask, bf16[384,2560]{1,0:T(8,128)(2,1)} %refs_0_.13, bf16[192,2560]{1,0:T(8,128)(2,1)} %refs_1_.13, bf16[192,2560]{1,0:T(8,128)(2,1)} %refs_2_.13, bf16[384,1280]{1,0:T(8,128)(2,1)S(1)} %collective-permute-done.refs_3_.refs_10_, ...), custom_call_target="tpu_custom_call" | custom-call | flops 1056964608 | bytes 589824 | tf_op jit(solution)/shard_map/far_heads/pallas_call | solution.py:529
  79.3 1.9 %last_heads.1 = f32[3,80,384]{2,1,0:T(8,128)S(1)} custom-call(s32[12]{0:T(128)S(1)} %fusion.43.scalars, s32[16]{0:T(128)S(1)} %reshape.27.mask, bf16[384,2560]{1,0:T(8,128)(2,1)} %refs_0_.13, bf16[192,2560]{1,0:T(8,128)(2,1)} %refs_1_.13, bf16[192,2560]{1,0:T(8,128)(2,1)} %refs_2_.13, bf16[384,1280]{1,0:T(8,128)(2,1)S(1)} %collective-permute-done.refs_3_.refs_10_, ...), custom_call_target="tpu_custom_call" | custom-call | flops 603979776 | bytes 589824 | tf_op jit(solution)/shard_map/last_heads/pallas_call | solution.py:529
  81.2 0.7 copy-done.3
  82.0 1.4 %collective-permute-done.17 = f32[3,40,384]{2,1,0:T(8,128)S(1)} collective-permute-done((f32[3,40,384]{2,1,0:T(8,128)S(1)}, f32[3,40,384]{2,1,0:T(8,128)S(1)}, u32[]{:S(2)}, u32[]{:S(2)}) %collective-permute-start.17) | collective-permute-done | bytes 184352 | tf_op jit(solution)/shard_map/ppermute | solution.py:948
  83.4 1.0 dynamic-slice_add_fusion
  84.4 7.6 %collective-permute-start.18 = (f32[40,640]{1,0:T(8,128)S(1)}, f32[40,640]{1,0:T(8,128)S(1)}, u32[]{:S(2)}, u32[]{:S(2)}) collective-permute-start(f32[40,640]{1,0:T(8,128)S(1)} %pad_maximum_fusion.1), channel_id=1, source_target_pairs={{0,4},{4,8},{8,12},{1,5},{5,9},{9,13},{2,6},{6,10},{10,14},{3,7},{... | collective-permute-start | bytes 307208 | tf_op jit(solution)/shard_map/ppermute | solution.py:951
  92.0 9.9 %collective-permute-start.19 = (f32[40,256]{1,0:T(8,128)S(1)}, f32[40,256]{1,0:T(8,128)S(1)}, u32[]{:S(2)}, u32[]{:S(2)}) collective-permute-start(f32[40,256]{1,0:T(8,128)S(1)} %slice.51), channel_id=1, source_target_pairs={{0,8},{4,12},{1,9},{5,13},{2,10},{6,14},{3,11},{7,15},{16,24},{20,... | collective-permute-start | bytes 122888 | tf_op jit(solution)/shard_map/ppermute | solution.py:955
  102.7 1.0 collective-permute-done.19
  103.7 0.9 collective-permute-start.21
  104.5 3.9 %collective-permute-done.21 = f32[40,640]{1,0:T(8,128)S(1)} collective-permute-done((f32[40,640]{1,0:T(8,128)S(1)}, f32[40,640]{1,0:T(8,128)S(1)}, u32[]{:S(2)}, u32[]{:S(2)}) %collective-permute-start.21) | collective-permute-done | bytes 102432 | tf_op jit(solution)/shard_map/ppermute | solution.py:958
  108.5 1.3 %collective-permute-done.22.other = f32[40,640]{1,0:T(8,128)S(1)} collective-permute-done((f32[40,640]{1,0:T(8,128)S(1)}, f32[40,640]{1,0:T(8,128)S(1)}, u32[]{:S(2)}, u32[]{:S(2)}) %collective-permute-start.22) | collective-permute-done | bytes 102432 | tf_op jit(solution)/shard_map/ppermute | solution.py:959
  109.8 2.4 %finish.1 = (f32[3,8,16,16]{3,2,1,0:T(8,128)}, bf16[3,8,16,384]{3,2,1,0:T(8,128)(2,1)}) custom-call(s32[12]{0:T(128)S(1)} %fusion.43.scalars, f32[40,640]{1,0:T(8,128)S(1)} %add.97.mine, f32[40,640]{1,0:T(8,128)S(1)} %collective-permute-done.22.other, f32[320,80]{1,0:T(8,128)S(1)} %bitcast.44, bf16[320,512]{1,0:T(8,128)(2,1)S(1)} %copy-done.4, ...), custom_call_target="tpu_custom_call" | custom-call | tf_op jit(solution)/shard_map/finish/pallas_call | solution.py:874
  (90 shorter events, 6.7 us)
Async XLA Ops:
  0.6 27.2 %copy-start = (f32[384]{0:T(512)S(1)}, f32[384]{0:T(512)}, u32[]{:S(2)}) copy-start(f32[384]{0:T(512)} %param.21) | copy-start | bytes 4612
  6.1 15.3 %collective-permute-start = (bf16[384,1280]{1,0:T(8,128)(2,1)}, bf16[384,1280]{1,0:T(8,128)(2,1)S(1)}, u32[]{:S(2)}, u32[]{:S(2)}) collective-permute-start(bf16[384,1280]{1,0:T(8,128)(2,1)} %get-tuple-element.34), channel_id=1, source_target_pairs={{0,1},{1,0},{2,3},{3,2},{4,5},{5,4},{6,7},{7,6},{8,9},{9,8},{10,11... | collective-permute-start | bytes 2949128 | tf_op jit(solution)/shard_map/ppermute | solution.py:603
  6.7 14.5 %collective-permute-start.11 = (f32[8,16,32]{2,1,0:T(8,128)S(1)}, f32[8,16,32]{2,1,0:T(8,128)S(1)}, u32[]{:S(2)}, u32[]{:S(2)}) collective-permute-start(f32[8,16,32]{2,1,0:T(8,128)S(1)} %slice.33), channel_id=1, source_target_pairs={{0,4},{4,8},{8,12},{1,5},{5,9},{9,13},{2,6},{6,10},{10,14},{3,7},{... | collective-permute-start | bytes 49160 | tf_op jit(solution)/shard_map/ppermute | solution.py:46
  11.2 16.6 %collective-permute-start.1 = (bf16[384,512]{1,0:T(8,128)(2,1)}, bf16[384,512]{1,0:T(8,128)(2,1)S(1)}, u32[]{:S(2)}, u32[]{:S(2)}) collective-permute-start(bf16[384,512]{1,0:T(8,128)(2,1)} %get-tuple-element.39), channel_id=1, source_target_pairs={{0,4},{4,8},{1,5},{5,9},{2,6},{6,10},{3,7},{7,11},{16,20},{20,24},... | collective-permute-start | bytes 1179656 | tf_op jit(solution)/shard_map/ppermute | solution.py:561
  14.7 33.1 %collective-permute-start.2 = (bf16[384,512]{1,0:T(8,128)(2,1)}, bf16[384,512]{1,0:T(8,128)(2,1)S(1)}, u32[]{:S(2)}, u32[]{:S(2)}) collective-permute-start(bf16[384,512]{1,0:T(8,128)(2,1)} %get-tuple-element.43), channel_id=1, source_target_pairs={{4,0},{8,4},{12,8},{5,1},{9,5},{13,9},{6,2},{10,6},{14,10},{7,3},{... | collective-permute-start | bytes 1179656 | tf_op jit(solution)/shard_map/ppermute | solution.py:561
  16.0 32.5 %collective-permute-start.4 = (bf16[384,512]{1,0:T(8,128)(2,1)}, bf16[384,512]{1,0:T(8,128)(2,1)S(1)}, u32[]{:S(2)}, u32[]{:S(2)}) collective-permute-start(bf16[384,512]{1,0:T(8,128)(2,1)} %get-tuple-element.44), channel_id=1, source_target_pairs={{0,5},{1,4},{4,9},{5,8},{2,7},{3,6},{6,11},{7,10},{16,21},{17,20},... | collective-permute-start | bytes 1179656 | tf_op jit(solution)/shard_map/ppermute | solution.py:565
  21.4 28.4 %copy-start.6 = (f32[8,16,80]{2,1,0:T(8,128)}, f32[8,16,80]{2,1,0:T(8,128)S(1)}, u32[]{:S(2)}) copy-start(f32[8,16,80]{2,1,0:T(8,128)S(1)} %pad_maximum_fusion.2) | copy-start | bytes 122884
  24.6 29.4 %collective-permute-start.3 = (bf16[768,512]{1,0:T(8,128)(2,1)}, bf16[768,512]{1,0:T(8,128)(2,1)S(1)}, u32[]{:S(2)}, u32[]{:S(2)}) collective-permute-start(bf16[768,512]{1,0:T(8,128)(2,1)} %get-tuple-element.35), channel_id=1, source_target_pairs={{4,0},{8,4},{12,8},{5,1},{9,5},{13,9},{6,2},{10,6},{14,10},{7,3},{... | collective-permute-start | bytes 2359304 | tf_op jit(solution)/shard_map/ppermute | solution.py:561
  26.3 9.4 %collective-permute-start.14 = (f32[64,2]{1,0:T(8,128)S(1)}, f32[64,2]{1,0:T(8,128)S(1)}, u32[]{:S(2)}, u32[]{:S(2)}) collective-permute-start(f32[64,2]{1,0:T(8,128)S(1)} %copy.32), channel_id=1, source_target_pairs={{0,2},{2,0},{1,3},{3,1},{4,6},{6,4},{5,7},{7,5},{8,10},{10,8},{9,1... | collective-permute-start | bytes 1544 | tf_op jit(solution)/shard_map/ppermute | solution.py:936
  27.9 21.9 %collective-permute-start.5 = (bf16[768,384]{1,0:T(8,128)(2,1)}, bf16[768,384]{1,0:T(8,128)(2,1)}, u32[]{:S(2)}, u32[]{:S(2)}) collective-permute-start(bf16[768,384]{1,0:T(8,128)(2,1)} %get-tuple-element.45), channel_id=1, source_target_pairs={{0,8},{1,9},{2,10},{3,11},{16,24},{17,25},{18,26},{19,27}} | collective-permute-start | bytes 1769480 | tf_op jit(solution)/shard_map/ppermute | solution.py:561
  35.7 11.3 %collective-permute-start.12 = (f32[8,80]{1,0:T(8,128)S(1)}, f32[8,80]{1,0:T(8,128)S(1)}, u32[]{:S(2)}, u32[]{:S(2)}) collective-permute-start(f32[8,80]{1,0:T(8,128)S(1)} %fusion.35), channel_id=1, source_target_pairs={{0,1},{1,0},{2,3},{3,2},{4,5},{5,4},{6,7},{7,6},{8,9},{9,8},{10,11... | collective-permute-start | bytes 7688 | tf_op jit(solution)/shard_map/ppermute | solution.py:753
  38.5 5.3 %copy-start.10 = (s32[4,4]{1,0:T(4,128)S(1)}, s32[4,4]{1,0:T(4,128)}, u32[]{:S(2)}) copy-start(s32[4,4]{1,0:T(4,128)} %param.15) | copy-start | bytes 196
  47.0 16.8 %collective-permute-start.6 = (bf16[384,512]{1,0:T(8,128)(2,1)S(1)}, bf16[384,512]{1,0:T(8,128)(2,1)S(1)}, u32[]{:S(2)}, u32[]{:S(2)}) collective-permute-start(bf16[384,512]{1,0:T(8,128)(2,1)S(1)} %copy-done.11), channel_id=1, source_target_pairs={{12,4},{13,5},{14,6},{15,7},{28,20},{29,21},{30,22},{31,23}} | collective-permute-start | bytes 1179656 | tf_op jit(solution)/shard_map/ppermute | solution.py:561
  47.8 17.5 %collective-permute-start.7 = (bf16[768,256]{1,0:T(8,128)(2,1)S(1)}, bf16[768,256]{1,0:T(8,128)(2,1)S(1)}, u32[]{:S(2)}, u32[]{:S(2)}) collective-permute-start(bf16[768,256]{1,0:T(8,128)(2,1)S(1)} %copy-done.12), channel_id=1, source_target_pairs={{12,4},{13,5},{14,6},{15,7},{28,20},{29,21},{30,22},{31,23}} | collective-permute-start | bytes 1179656 | tf_op jit(solution)/shard_map/ppermute | solution.py:561
  48.5 22.6 %collective-permute-start.8 = (bf16[1152,256]{1,0:T(8,128)(2,1)}, bf16[1152,256]{1,0:T(8,128)(2,1)S(1)}, u32[]{:S(2)}, u32[]{:S(2)}) collective-permute-start(bf16[1152,256]{1,0:T(8,128)(2,1)} %get-tuple-element.49), channel_id=1, source_target_pairs={{8,12},{4,0},{9,13},{5,1},{10,14},{6,2},{11,15},{7,3},{24,28},{20,... | collective-permute-start | bytes 1769480 | tf_op jit(solution)/shard_map/ppermute | solution.py:561
  49.8 21.2 %collective-permute-start.10 = (bf16[768,256]{1,0:T(8,128)(2,1)}, bf16[768,256]{1,0:T(8,128)(2,1)S(1)}, u32[]{:S(2)}, u32[]{:S(2)}) collective-permute-start(bf16[768,256]{1,0:T(8,128)(2,1)} %get-tuple-element.50), channel_id=1, source_target_pairs={{0,12},{1,13},{2,14},{3,15},{16,28},{17,29},{18,30},{19,31}} | collective-permute-start | bytes 1179656 | tf_op jit(solution)/shard_map/ppermute | solution.py:561
  54.1 10.5 %collective-permute-start.13 = (f32[32,80]{1,0:T(8,128)S(1)}, f32[32,80]{1,0:T(8,128)S(1)}, u32[]{:S(2)}, u32[]{:S(2)}) collective-permute-start(f32[32,80]{1,0:T(8,128)S(1)} %fusion.34), channel_id=1, source_target_pairs={{0,2},{2,0},{1,3},{3,1},{4,6},{6,4},{5,7},{7,5},{8,10},{10,8},{9,1... | collective-permute-start | bytes 30728 | tf_op jit(solution)/shard_map/ppermute | solution.py:765
  54.7 9.1 %copy-start.14 = (bf16[768,256]{1,0:T(8,128)(2,1)S(1)}, bf16[768,256]{1,0:T(8,128)(2,1)}, u32[]{:S(2)}) copy-start(bf16[768,256]{1,0:T(8,128)(2,1)} %get-tuple-element.50) | copy-start | bytes 1179652
  54.7 9.8 %copy-start.13 = (bf16[768,256]{1,0:T(8,128)(2,1)S(1)}, bf16[768,256]{1,0:T(8,128)(2,1)}, u32[]{:S(2)}) copy-start(bf16[768,256]{1,0:T(8,128)(2,1)} %get-tuple-element.60) | copy-start | bytes 1179652
  54.7 10.5 %copy-start.15 = (bf16[768,128]{1,0:T(8,128)(2,1)S(1)}, bf16[768,128]{1,0:T(8,128)(2,1)}, u32[]{:S(2)}) copy-start(bf16[768,128]{1,0:T(8,128)(2,1)} %get-tuple-element.59) | copy-start | bytes 589828
  54.7 14.2 %copy-start.7 = (f32[8,16,80]{2,1,0:T(8,128)S(1)}, f32[8,16,80]{2,1,0:T(8,128)}, u32[]{:S(2)}) copy-start(f32[8,16,80]{2,1,0:T(8,128)} %copy-done.6) | copy-start | bytes 122884
  63.8 7.2 %collective-permute-start.9 = (bf16[768,256]{1,0:T(8,128)(2,1)S(1)}, bf16[768,256]{1,0:T(8,128)(2,1)S(1)}, u32[]{:S(2)}, u32[]{:S(2)}) collective-permute-start(bf16[768,256]{1,0:T(8,128)(2,1)S(1)} %copy-done.14), channel_id=1, source_target_pairs={{4,12},{5,13},{6,14},{7,15},{20,28},{21,29},{22,30},{23,31}} | collective-permute-start | bytes 1179656 | tf_op jit(solution)/shard_map/ppermute | solution.py:561
  64.5 14.8 %collective-permute-start.16 = (bf16[768,256]{1,0:T(8,128)(2,1)S(1)}, bf16[768,256]{1,0:T(8,128)(2,1)S(1)}, u32[]{:S(2)}, u32[]{:S(2)}) collective-permute-start(bf16[768,256]{1,0:T(8,128)(2,1)S(1)} %copy-done.13), channel_id=1, source_target_pairs={{12,4},{13,5},{14,6},{15,7},{28,20},{29,21},{30,22},{31,23}} | collective-permute-start | bytes 1179656 | tf_op jit(solution)/shard_map/ppermute | solution.py:561
  65.3 14.0 %collective-permute-start.15 = (bf16[768,128]{1,0:T(8,128)(2,1)S(1)}, bf16[768,128]{1,0:T(8,128)(2,1)S(1)}, u32[]{:S(2)}, u32[]{:S(2)}) collective-permute-start(bf16[768,128]{1,0:T(8,128)(2,1)S(1)} %copy-done.15), channel_id=1, source_target_pairs={{0,8},{1,9},{2,10},{3,11},{16,24},{17,25},{18,26},{19,27}} | collective-permute-start | bytes 589832 | tf_op jit(solution)/shard_map/ppermute | solution.py:561
  81.9 27.9 %copy-start.2 = (bf16[3,240,1152]{2,1,0:T(8,128)(2,1)S(1)}, bf16[3,240,1152]{2,1,0:T(8,128)(2,1)}, u32[]{:S(2)}) copy-start(bf16[3,240,1152]{2,1,0:T(8,128)(2,1)} %reshape.30.band) | copy-start | bytes 4976644
  81.9 27.9 %copy-start.4 = (bf16[320,512]{1,0:T(8,128)(2,1)S(1)}, bf16[320,512]{1,0:T(8,128)(2,1)}, u32[]{:S(2)}) copy-start(bf16[320,512]{1,0:T(8,128)(2,1)} %fusion.30.selector) | copy-start | bytes 983044
  81.9 1.5 %collective-permute-start.17 = (f32[3,40,384]{2,1,0:T(8,128)S(1)}, f32[3,40,384]{2,1,0:T(8,128)S(1)}, u32[]{:S(2)}, u32[]{:S(2)}) collective-permute-start(f32[3,40,384]{2,1,0:T(8,128)S(1)} %constant_dynamic-slice_fusion), channel_id=1, source_target_pairs={{0,1},{1,0},{2,3},{3,2},{4,5},{5,4},{6,7},{7,6},{8,9},{9,8},{10,11... | collective-permute-start | bytes 552968 | tf_op jit(solution)/shard_map/ppermute | solution.py:948
  84.4 19.2 %collective-permute-start.18 = (f32[40,640]{1,0:T(8,128)S(1)}, f32[40,640]{1,0:T(8,128)S(1)}, u32[]{:S(2)}, u32[]{:S(2)}) collective-permute-start(f32[40,640]{1,0:T(8,128)S(1)} %pad_maximum_fusion.1), channel_id=1, source_target_pairs={{0,4},{4,8},{8,12},{1,5},{5,9},{9,13},{2,6},{6,10},{10,14},{3,7},{... | collective-permute-start | bytes 307208 | tf_op jit(solution)/shard_map/ppermute | solution.py:951
  92.0 11.6 %collective-permute-start.19 = (f32[40,256]{1,0:T(8,128)S(1)}, f32[40,256]{1,0:T(8,128)S(1)}, u32[]{:S(2)}, u32[]{:S(2)}) collective-permute-start(f32[40,256]{1,0:T(8,128)S(1)} %slice.51), channel_id=1, source_target_pairs={{0,8},{4,12},{1,9},{5,13},{2,10},{6,14},{3,11},{7,15},{16,24},{20,... | collective-permute-start | bytes 122888 | tf_op jit(solution)/shard_map/ppermute | solution.py:955
  102.0 1.7 %collective-permute-start.20 = (f32[40,384]{1,0:T(8,128)S(1)}, f32[40,384]{1,0:T(8,128)S(1)}, u32[]{:S(2)}, u32[]{:S(2)}) collective-permute-start(f32[40,384]{1,0:T(8,128)S(1)} %get-tuple-element.71), channel_id=1, source_target_pairs={{4,12},{12,8},{5,13},{13,9},{6,14},{14,10},{7,15},{15,11},{20,28},... | collective-permute-start | bytes 184328 | tf_op jit(solution)/shard_map/ppermute | solution.py:954
  103.7 4.7 %collective-permute-start.21 = (f32[40,640]{1,0:T(8,128)S(1)}, f32[40,640]{1,0:T(8,128)S(1)}, u32[]{:S(2)}, u32[]{:S(2)}) collective-permute-start(f32[40,640]{1,0:T(8,128)S(1)} %fusion.32), channel_id=1, source_target_pairs={{0,2},{2,0},{1,3},{3,1},{4,6},{6,4},{5,7},{7,5},{8,10},{10,8},{9,1... | collective-permute-start | bytes 307208 | tf_op jit(solution)/shard_map/ppermute | solution.py:958
  108.4 1.4 %collective-permute-start.22 = (f32[40,640]{1,0:T(8,128)S(1)}, f32[40,640]{1,0:T(8,128)S(1)}, u32[]{:S(2)}, u32[]{:S(2)}) collective-permute-start(f32[40,640]{1,0:T(8,128)S(1)} %add.97.mine), channel_id=1, source_target_pairs={{0,1},{1,0},{2,3},{3,2},{4,5},{5,4},{6,7},{7,6},{8,9},{9,8},{10,11... | collective-permute-start | bytes 307208 | tf_op jit(solution)/shard_map/ppermute | solution.py:959
  (7 other events, 22.2 us)

commit v7 on v6

--- a/solution.py
+++ b/solution.py
@@ -252,9 +252,12 @@
     return row + lax.axis_index("slab") * jnp.array(by_slab)
 
 
-def pack_kernel(inputs, copies, with_noise, scalars, *refs):
-    ins, outs, semaphores = refs[:inputs], refs[inputs:-1], refs[-1]
-    started = []
+def pack_kernel(inputs, messages, copies, with_noise, scalars, *refs):
+    ins, rest = refs[:inputs], refs[inputs:]
+    outs = rest[: messages + with_noise]
+    staged = rest[messages + with_noise : -2]
+    arrive, leave = rest[-2:]
+    arriving = [[] for _ in range(messages)]
     for number, (source, row, rows, entries, shift, target, at, heads) in enumerate(copies):
         head = shift
         for entry in entries:
@@ -262,16 +265,23 @@
         column = pl.multiple_of(head * HD, HD)
         copy = pltpu.make_async_copy(
             ins[source].at[pl.ds(row, rows), pl.ds(column, heads * HD)],
-            outs[target].at[pl.ds(at, rows), :],
-            semaphores.at[number],
+            staged[target].at[pl.ds(at, rows), :],
+            arrive.at[number],
         )
         copy.start()
-        started.append(copy)
+        arriving[target].append(copy)
     if with_noise:
         noisy, out = ins[-1], outs[-1]
         frames = noisy.shape[0]
         out[...] = jnp.concatenate([noisy[frame] for frame in range(frames)], axis=-1)
-    for copy in started:
+    leaving = []
+    for target in range(messages):
+        for copy in arriving[target]:
+            copy.wait()
+        copy = pltpu.make_async_copy(staged[target], outs[target], leave.at[target])
+        copy.start()
+        leaving.append(copy)
+    for copy in leaving:
         copy.wait()
 
 
@@ -279,7 +289,7 @@
     moved = sum(2 * 2 * rows * heads * HD for _, _, rows, _, _, _, _, heads in copies)
     out_shape = [pltpu.HBM(shape, jnp.bfloat16) for shape in shapes]
     in_specs = [pl.BlockSpec(memory_space=pl.ANY)] * len(arrays)
-    out_specs = [pl.BlockSpec(shape, lambda i, scalars: (0, 0)) for shape in shapes]
+    out_specs = [pl.BlockSpec(memory_space=pl.ANY)] * len(shapes)
     if noisy is not None:
         frames, height, breadth, channels = noisy.shape
         lanes = frames * channels
@@ -288,7 +298,9 @@
         out_shape.append(jax.ShapeDtypeStruct((height, breadth, lanes), noisy.dtype))
         out_specs.append(pl.BlockSpec((height, breadth, lanes), lambda i, scalars: (0, 0, 0)))
     return pl.pallas_call(
-        functools.partial(pack_kernel, len(arrays), copies, noisy is not None),
+        functools.partial(
+            pack_kernel, len(arrays), len(shapes), copies, noisy is not None
+        ),
         name=name,
         out_shape=out_shape,
         grid_spec=pltpu.PrefetchScalarGridSpec(
@@ -296,7 +308,11 @@
             grid=(1,),
             in_specs=in_specs,
             out_specs=out_specs,
-            scratch_shapes=[pltpu.SemaphoreType.DMA((len(copies),))],
+            scratch_shapes=[pltpu.VMEM(shape, jnp.bfloat16) for shape in shapes]
+            + [
+                pltpu.SemaphoreType.DMA((len(copies),)),
+                pltpu.SemaphoreType.DMA((len(shapes),)),
+            ],
         ),
         compiler_params=pltpu.CompilerParams(vmem_limit_bytes=GRANT),
         cost_estimate=pl.CostEstimate(flops=0, bytes_accessed=moved, transcendentals=0),
@@ -323,10 +339,11 @@
 OWN_TOKENS = Tokens()
 
 
-def attend_kernel(variants, extra, span_count, scalars, mask, *refs):
-    query_own, key_own, value_own, received, weight, gain, sums_in = refs[:7]
-    more = refs[7 : 7 + extra]
-    payloads, (sums_out, folded, squares) = refs[7 + extra : -3], refs[-3:]
+def attend_kernel(variants, extra, span_count, fresh, scalars, mask, *refs):
+    query_own, key_own, value_own, received, weight, gain = refs[:6]
+    more = refs[6 : 6 + extra]
+    sums_out, folded, squares, carried, fetched, stored = refs[-6:]
+    payloads = refs[6 + extra : -6] if fresh else refs[6 + extra : -7]
     rows = query_own.shape[0]
     half = rows // 2
     step = pl.program_id(0)
@@ -335,10 +352,15 @@
         lambda a, b: a | b, [scalars[PLACE] == place for place in variants]
     )
 
-    @pl.when(step == 0)
+    last_step = step == pl.num_programs(0) - 1
+    fetch = None if fresh else pltpu.make_async_copy(refs[-7], carried, fetched)
+
+    @pl.when((step == 0) & active)
     def _():
         folded[...] = jnp.zeros_like(folded)
         squares[...] = jnp.zeros_like(squares)
+        if fetch is not None:
+            fetch.start()
 
     def query_of(source):
         if source is OWN_TOKENS:
@@ -430,15 +452,30 @@
             for task in tasks:
                 one_query(*task)
 
-    @pl.when((step == pl.num_programs(0) - 1) & jnp.logical_not(active))
-    def _():
-        sums_out[...] = sums_in[...]
-
-    @pl.when((step == pl.num_programs(0) - 1) & active)
+    def store():
+        copy = pltpu.make_async_copy(carried, sums_out, stored)
+        copy.start()
+        copy.wait()
+
+    if fresh:
+
+        @pl.when(last_step & jnp.logical_not(active))
+        def _():
+            carried[...] = jnp.zeros_like(carried)
+            store()
+
+    @pl.when(last_step & active)
     def _():
         ones_rows = jnp.ones((STAT_ROWS, HD), jnp.bfloat16)
         patch = weight.shape[0]
+        used = sorted({task[1] for _, tasks in variants.values() for task in tasks})
+        if fetch is not None:
+            fetch.wait()
         for slot in range(SLOTS):
+            if slot not in used:
+                if fresh:
+                    carried[slot] = jnp.zeros(carried.shape[1:], carried.dtype)
+                continue
             left = squares[slot]
             total = jnp.zeros((STAT_ROWS, rows), jnp.float32)
             for _ in range(3):
@@ -448,7 +485,7 @@
                     ones_rows, piece, (((1,), (1,)), ((), ())), preferred_element_type=jnp.float32
                 )
             done = folded[slot]
-            sums_out[slot] = sums_in[slot] + jnp.concatenate(
+            new = jnp.concatenate(
                 [
                     done[:patch] + done[patch : 2 * patch],
                     done[2 * patch : 2 * patch + STAT_ROWS],
@@ -456,9 +493,13 @@
                 ],
                 axis=0,
             )
-
-
-def attend(steps, entries, first, own, scalars, mask, sums, payloads, variants, more, name):
+            carried[slot] = new if fresh else carried[slot] + new
+        store()
+
+
+def attend(
+    steps, entries, first, own, scalars, mask, sums, payloads, variants, more, name, cost=1
+):
     queries, keys, values, received, weight, gain = own
     rows = queries.shape[0]
     half = rows // 2
@@ -497,7 +538,6 @@
 
         return pl.BlockSpec((payload.shape[0], HD), index)
 
-    sums_spec = pl.BlockSpec(sums.shape, lambda i, scalars, mask: (0, 0, 0))
     in_specs = [
         column(rows, True),
         column(half, True),
@@ -505,9 +545,8 @@
         column(rows, False),
         column(patch, True),
         column(1, True),
-        sums_spec,
     ]
-    arrays = [queries, keys, values, received, weight, gain, sums]
+    arrays = [queries, keys, values, received, weight, gain]
     extra = 0
     if more:
         extra = 6
@@ -522,34 +561,47 @@
         arrays += [queries, keys, values, received, weight, gain]
     in_specs += [payload_column(*payload) for payload in payloads]
     arrays += [payload[0] for payload in payloads]
+    fresh = sums is None
+    sums_shape = (SLOTS, patch + 2 * STAT_ROWS, rows)
+    aliases = {}
+    if not fresh:
+        aliases = {2 + len(arrays): 0}
+        in_specs.append(pl.BlockSpec(memory_space=pl.ANY))
+        arrays.append(sums)
     pairs = max(
         count * sum(len(task[3]) for task in tasks) for count, tasks in variants.values()
     )
     span_count = math.isqrt(mask.shape[0])
     return pl.pallas_call(
-        functools.partial(attend_kernel, variants, extra, span_count),
+        functools.partial(attend_kernel, variants, extra, span_count, fresh),
         name=name,
-        out_shape=jax.ShapeDtypeStruct(sums.shape, sums.dtype),
+        out_shape=pltpu.HBM(sums_shape, jnp.float32),
+        input_output_aliases=aliases,
         grid_spec=pltpu.PrefetchScalarGridSpec(
             num_scalar_prefetch=2,
             grid=(steps,),
             in_specs=in_specs,
-            out_specs=sums_spec,
+            out_specs=pl.BlockSpec(memory_space=pl.ANY),
             scratch_shapes=[
                 pltpu.VMEM((SLOTS, 2 * patch + 16, rows), jnp.float32),
                 pltpu.VMEM((SLOTS, rows, HD), jnp.float32),
+                pltpu.VMEM(sums_shape, jnp.float32),
+                pltpu.SemaphoreType.DMA,
+                pltpu.SemaphoreType.DMA,
             ],
         ),
         compiler_params=pltpu.CompilerParams(vmem_limit_bytes=GRANT),
         cost_estimate=pl.CostEstimate(
-            flops=pairs * 4 * rows * rows * HD,
+            flops=cost * pairs * 4 * rows * rows * HD,
             bytes_accessed=steps * HD * 2 * sum(spec.block_shape[0] for spec in in_specs[:4]),
-            transcendentals=pairs * rows * rows,
+            transcendentals=cost * pairs * rows * rows,
         ),
     )(scalars, mask, *arrays)
 
 
-def token_sums(scalars, queries, keys, values, span_mask, head_gain, patch_weight, noisy):
+def token_sums(
+    scalars, queries, keys, values, span_mask, head_gain, patch_weight, noisy, prepare
+):
     rows = queries.shape[0]
     half = rows // 2
     heads = NEAR_HEADS + MIDDLE_HEADS + FAR_HEADS
@@ -585,14 +637,13 @@
             )
         ]
 
-    handed, up_same, up_across, query_down, query_two, noise = message(
+    handed, up_same, up_across, query_down, noise = message(
         scalars,
         [
             [(part, 0, half, (OTHER,), 0, heads) for part in (1, 2)],
             own_half(OWN, UP, 0, NEAR_HEADS),
             own_half(OTHER, UP, 0, NEAR_HEADS),
             tokens(DOWN, 0, MIDDLE_HEADS),
-            tokens(None, 0, NEAR_HEADS),
         ],
         (queries, keys, values),
         "pack_first",
@@ -604,42 +655,42 @@
     up_same = send(up_same, (0, 1), (1, 2))
     up_across = send_across(up_across, (0, 1), (1, 2))
     query_down = send(query_down, (1, 0), (2, 1), (3, 2))
-    query_two = send(query_two, (3, 1))
 
     arrays = (queries, keys, values, received)
-    pair_down, pair_two, up_two = message(
+    pair_down, up_two = message(
         scalars,
-        [pairs_of(DOWN, 0, MIDDLE_HEADS), pairs_of(None, 0, 2), pairs_of(None, MIDDLE, 3)],
+        [pairs_of(DOWN, 0, MIDDLE_HEADS), pairs_of(None, MIDDLE, 3)],
         arrays,
         "pack_second",
     )
-    anchor = pair_down
-    pair_down = send(pair_down, (1, 0), (2, 1), (3, 2))
-    pair_two = send(pair_two, (3, 1))
-    up_two = send(up_two, (0, 2))
-
-    source, _ = lax.optimization_barrier((received, up_same))
-    far_all, far_pair, last_two, last_up = message(
+    source, _ = lax.optimization_barrier((received, pair_down))
+    two, far_all, far_pair, last_two, last_up = message(
         scalars,
         [
+            tokens(None, 0, 2) + pairs_of(None, 0, 2),
             tokens(None, FAR, FAR_HEADS) + pairs_of(None, FAR, FAR_HEADS),
             pairs_of(None, FAR, FAR_HEADS),
-            pairs_of(None, 2, 2),
+            tokens(None, 2, 2) + pairs_of(None, 2, 2),
             pairs_of(None, MIDDLE + 3, 1),
         ],
         (queries, keys, values, source),
         "pack_third",
     )
+    anchor = two
+    pair_down = send(pair_down, (1, 0), (2, 1), (3, 2))
+    up_two = send(up_two, (0, 2))
+    two = send(two, (3, 1))
+    far_next = send(far_all, (2, 3), (1, 0))
+    far_pair, prepared = lax.optimization_barrier((far_pair, prepare(noise, anchor)))
     far_two = send(far_pair, (1, 3))
     far_three = send(far_pair, (0, 3))
-    far_next = send(far_all, (2, 3), (1, 0))
+
     span_mask, head_gain, patch_weight, _ = lax.optimization_barrier(
         (span_mask, head_gain, patch_weight, anchor)
     )
     mask = span_mask.reshape(-1)
     weight = patch_weight.T
     own = (queries, keys, values, received, weight, head_gain[None, :])
-    sums = jnp.zeros((SLOTS, weight.shape[0] + 2 * STAT_ROWS, rows), jnp.float32)
     run = functools.partial(attend, own=own, scalars=scalars, mask=mask)
 
     on_one, back_one, back_two = Tokens(0, (1,)), Tokens(None, (2, 3)), Tokens(None, (4,))
@@ -652,7 +703,7 @@
         MIDDLE_HEADS,
         (MAIN,),
         0,
-        sums=sums,
+        sums=None,
         payloads=[
             (query_down, None, 0),
             (pair_down, None, 0),
@@ -677,7 +728,7 @@
     last_two, last_up, sums = lax.optimization_barrier((last_two, last_up, sums))
     last_two = send(last_two, (3, 1))
     last_up = send(last_up, (0, 2))
-    on_two = Tokens(5, (6,))
+    on_two = Tokens(5, (5,))
     last_span = [(on_two, 2, 3, [(back_one, 0), (here, 1), (on_one, 2), (on_two, 3)])]
     sums = run(
         2,
@@ -690,8 +741,7 @@
             (up_same, None, 0),
             (up_across, None, 0),
             (up_two, None, 0),
-            (query_two, None, 0),
-            (pair_two, None, 0),
+            (two, None, 0),
         ],
         variants={1: (2, last_span)},
         more=False,
@@ -721,6 +771,7 @@
         },
         more=True,
         name="far_heads",
+        cost=4,
     )
 
     def last(sums):
@@ -735,7 +786,6 @@
                 (up_same, LAST_COLUMN, 0),
                 (up_across, LAST_COLUMN, 0),
                 (last_up, None, 0),
-                (query_two, LAST_COLUMN, 0),
                 (last_two, None, 0),
             ],
             variants={1: (2, last_span), 2: (1, middle)},
@@ -743,7 +793,8 @@
             name="last_heads",
         )
 
-    return sums, last, anchor, noise
+    sums, prepared = lax.optimization_barrier((sums, prepared))
+    return last(sums), prepared
 
 
 def noise_window(grid):
@@ -780,19 +831,34 @@
     return (inside & (column == target)).astype(jnp.bfloat16)
 
 
+def band_kernel(weight, band):
+    outputs = weight.shape[1]
+    band[...] = jnp.zeros_like(band)
+    for row_tap in range(3):
+        for col_tap in range(3):
+            for frame_tap in range(3):
+                start = ((3 * frame_tap + row_tap) * 3 + col_tap) * LAT_CH
+                block = weight[start : start + LAT_CH]
+                for frame in range(FRAMES_SPAN):
+                    at = (col_tap * (FRAMES_SPAN + 2) + frame + frame_tap) * LAT_CH
+                    band[
+                        row_tap, at : at + LAT_CH, frame * outputs : (frame + 1) * outputs
+                    ] = block
+
+
 def banded_weight(conv_weight):
-    channels = conv_weight.shape[1]
-    taps = conv_weight.reshape(3, 3, 3, LAT_CH, channels)
-    banded = jnp.stack(
-        [
-            jnp.pad(taps, ((n, FRAMES_SPAN - 1 - n), (0, 0), (0, 0), (0, 0), (0, 0)))
-            for n in range(FRAMES_SPAN)
-        ],
-        axis=4,
-    )
-    return banded.transpose(1, 2, 0, 3, 4, 5).reshape(
-        3, 3 * (FRAMES_SPAN + 2) * LAT_CH, FRAMES_SPAN * channels
-    )
+    shape = (3, 3 * (FRAMES_SPAN + 2) * LAT_CH, FRAMES_SPAN * conv_weight.shape[1])
+    return pl.pallas_call(
+        band_kernel,
+        name="band",
+        out_shape=jax.ShapeDtypeStruct(shape, conv_weight.dtype),
+        in_specs=[pl.BlockSpec(memory_space=pltpu.VMEM)],
+        out_specs=pl.BlockSpec(memory_space=pltpu.VMEM),
+        compiler_params=pltpu.CompilerParams(vmem_limit_bytes=GRANT),
+        cost_estimate=pl.CostEstimate(
+            flops=0, bytes_accessed=2 * math.prod(shape), transcendentals=0
+        ),
+    )(conv_weight)
 
 
 def finish_kernel(
@@ -916,32 +982,38 @@
     place = lax.axis_index("span")
     slab = lax.axis_index("slab")
     scalars = scalar_operand(heads_dev // lax.axis_size("slab"))
-    sums, last, anchor, noise = token_sums(
-        scalars, queries, keys, values, span_mask, head_gain, patch_weight, noisy_latent
-    )
-
-    noise, weight, gain, shift, taps, bias, _ = lax.optimization_barrier(
-        (noise, patch_weight, head_gain, head_shift, conv_weight, conv_bias, anchor)
-    )
-    height, breadth, _ = noise.shape
-    noise = noise_window(noise)
-    wide_weight = weight.T.astype(jnp.float32)
-    constants = jnp.stack(
-        [
-            jnp.sum(wide_weight * gain[None, :], axis=1),
-            jnp.sum(wide_weight * shift[None, :], axis=1),
-        ],
-        axis=1,
-    )
-    constants = constants + lax.ppermute(constants, "head", SWAP)
-    selector = cell_selector(height, breadth)
-    band = banded_weight(taps)
-    bias = jnp.tile(bias, FRAMES_SPAN)[None, :]
-    sums, noise, constants, selector, band, bias = lax.optimization_barrier(
-        (sums, noise, constants, selector, band, bias)
-    )
-
-    sums = last(sums)
+    def prepare(noise, anchor):
+        noise, weight, gain, shift, taps, bias, _ = lax.optimization_barrier(
+            (noise, patch_weight, head_gain, head_shift, conv_weight, conv_bias, anchor)
+        )
+        height, breadth, _ = noise.shape
+        wide_weight = weight.T.astype(jnp.float32)
+        constants = jnp.stack(
+            [
+                jnp.sum(wide_weight * gain[None, :], axis=1),
+                jnp.sum(wide_weight * shift[None, :], axis=1),
+            ],
+            axis=1,
+        )
+        return (
+            noise_window(noise),
+            constants + lax.ppermute(constants, "head", SWAP),
+            cell_selector(height, breadth),
+            banded_weight(taps),
+            jnp.tile(bias, FRAMES_SPAN)[None, :],
+        )
+
+    sums, (noise, constants, selector, band, bias) = token_sums(
+        scalars,
+        queries,
+        keys,
+        values,
+        span_mask,
+        head_gain,
+        patch_weight,
+        noisy_latent,
+        prepare,
+    )
     half = sums.shape[1] // 2
     mine = lax.dynamic_slice_in_dim(sums, slab * half, half, 1)
     theirs = lax.dynamic_slice_in_dim(sums, (1 - slab) * half, half, 1)

time: 113 us -> 115 us (1.018)
  waiting for transfers between devices: 7.57 us -> 14.2 us
  starting transfers between devices: 54.6 us -> 48.4 us
    ppermute x1, starting transfers between devices: 9.95 us -> 1.29 us  [per_device(): to_before = lax.ppermute(after[:, skip:], 'span', [(0, 2), (1, 3)])]
    unnamed x34 -> x38, local copies, waits for them, and re-layouts: 1.73 us -> 9.95 us
    reshape x1 -> x0, local copies, waits for them, and re-layouts: 5.27 us -> none  [banded_weight(): banded.transpose(1, 2, 0, 3, 4, 5)]
    ppermute x1, waiting for transfers between devices: 0.01 us -> 4.86 us  [send_across(): lax.ppermute(value, ('span', 'slab'), [(a * slabs + s, b * slabs + 1 - s)...]
    ppermute x11 -> x10, starting transfers between devices: 24.3 us -> 27.7 us  [send(): return lax.ppermute(value, 'span', list(pairs))]
    ppermute x1, starting transfers between devices: 3.83 us -> 1.3 us  [send_across(): lax.ppermute(value, ('span', 'slab'), [(a * slabs + s, b * slabs + 1 - s)...]
    transpose x1 -> x0, local copies, waits for them, and re-layouts: 2.52 us -> none  [banded_weight(): banded.transpose(1, 2, 0, 3, 4, 5)]
    ppermute x1, waiting for transfers between devices: 0.01 us -> 2.39 us  [per_device(): lax.ppermute(jnp.concatenate([own[:, skip:], after], axis=1), 'span', [(0...]
  transfers between devices with their start and end apart: 23 -> 22, of which waited for: 4 -> 7; matrix products, arithmetic and copies ran while one was open for 10% -> 3% of each run, Pallas kernels for 23% -> 24%
where the time goes in v7:
time: 115 us; the launch traced here: 114 us
  starting transfers between devices  48.4 us (42%)
  Pallas kernels  34.2 us (30%)
  waiting for transfers between devices  14.2 us (12%)
  local copies, waits for them, and re-layouts  11.9 us (10%)
  other arithmetic  4.15 us (4%)
    ppermute x10, starting transfers between devices, send(): return lax.ppermute(value, 'span', list(pairs))  27.7 us
    pallas_call x4, Pallas kernels, attend(): pl.pallas_call(functools.partial(attend_kernel, variants, extra, span_cou...  22.5 us
    unnamed x38, local copies, waits for them, and re-layouts  9.95 us
    pallas_call x3, Pallas kernels, pack(): pl.pallas_call(functools.partial(pack_kernel, len(arrays), len(shapes), c...  9.15 us
    ppermute x1, starting transfers between devices, per_device(): lax.ppermute(jnp.concatenate([own[:, skip:], after], axis=1), 'span', [(0...  7.69 us
    ppermute x1, waiting for transfers between devices, send_across(): lax.ppermute(value, ('span', 'slab'), [(a * slabs + s, b * slabs + 1 - s)...  4.86 us
    ppermute x1, starting transfers between devices, from_behind(): return lax.ppermute(value, axis, pairs)  4.49 us
    ppermute x1, waiting for transfers between devices, per_device(): total = total + lax.ppermute(total, 'head', SWAP)  3.16 us
  transfers between devices with their start and end apart: 22, of which 7 were waited for; matrix products, arithmetic and copies ran while one was open for 3% of the time, Pallas kernels for 24%

profile of v7, /device:TPU:0, one launch (start us, length us, event | category | flops | bytes accessed | tf_op | source)
XLA Modules:
  0.0 114.0 jit_solution(144111318429600597)
XLA Ops:
  2.3 3.1 %pack_first.1 = (bf16[384,1280]{1,0:T(8,128)(2,1)}, bf16[384,512]{1,0:T(8,128)(2,1)}, bf16[384,512]{1,0:T(8,128)(2,1)}, bf16[384,512]{1,0:T(8,128)(2,1)}, f32[8,16,48]{2,1,0:T(8,128)S(1)}) custom-call(s32[12]{0:T(128)S(1)} %fusion.43.scalars, bf16[384,2560]{1,0:T(8,128)(2,1)} %refs_0_.13, bf16[192,2560]{1,0:T(8,128)(2,1)} %refs_1_.13, ...), custom_call_target="tpu_custom_call" | custom-call | bytes 4325376 | tf_op jit(solution)/shard_map/pack_first/pallas_call | solution.py:300
  6.0 4.5 %collective-permute-start.9 = (f32[8,16,32]{2,1,0:T(8,128)S(1)}, f32[8,16,32]{2,1,0:T(8,128)S(1)}, u32[]{:S(2)}, u32[]{:S(2)}) collective-permute-start(f32[8,16,32]{2,1,0:T(8,128)S(1)} %slice.33), channel_id=1, source_target_pairs={{0,4},{4,8},{8,12},{1,5},{5,9},{9,13},{2,6},{6,10},{10,14},{3,7},{... | collective-permute-start | bytes 49160 | tf_op jit(solution)/shard_map/ppermute | solution.py:46
  10.5 1.3 %collective-permute-start.1 = (bf16[384,512]{1,0:T(8,128)(2,1)}, bf16[384,512]{1,0:T(8,128)(2,1)S(1)}, u32[]{:S(2)}, u32[]{:S(2)}) collective-permute-start(bf16[384,512]{1,0:T(8,128)(2,1)} %get-tuple-element.46), channel_id=1, source_target_pairs={{4,0},{8,4},{12,8},{5,1},{9,5},{13,9},{6,2},{10,6},{14,10},{7,3},{... | collective-permute-start | bytes 1179656 | tf_op jit(solution)/shard_map/ppermute | solution.py:613
  11.8 5.3 %collective-permute-start.3 = (bf16[384,512]{1,0:T(8,128)(2,1)}, bf16[384,512]{1,0:T(8,128)(2,1)}, u32[]{:S(2)}, u32[]{:S(2)}) collective-permute-start(bf16[384,512]{1,0:T(8,128)(2,1)} %get-tuple-element.47), channel_id=1, source_target_pairs={{0,4},{4,8},{1,5},{5,9},{2,6},{6,10},{3,7},{7,11},{16,20},{20,24},... | collective-permute-start | bytes 1179656 | tf_op jit(solution)/shard_map/ppermute | solution.py:613
  17.2 1.4 %fusion.30.selector = bf16[320,512]{1,0:T(8,128)(2,1)} fusion(s32[320]{0:T(512)S(1)} %get-tuple-element.86, s32[320]{0:T(512)S(1)} %get-tuple-element.87, s32[]{:T(128)S(6)} %mul.56, s32[320]{0:T(512)S(1)} %get-tuple-element.85, s32[320]{0:T(512)S(1)} %get-tuple-element.88, s32[]{:T(128)S(6)} %mul.55, pred[320]{0:T(512)(128)(4,1)S(1)} %get-tuple-element.90, ...), kind=kLoop, calls=%fused_computation.46 | loop fusion | flops 10158080 | bytes 333448 | tf_op jit(solution)/shard_map/convert_element_type | solution.py:831
  18.6 2.8 %pack_second.1 = (bf16[768,512]{1,0:T(8,128)(2,1)}, bf16[768,384]{1,0:T(8,128)(2,1)}) custom-call(s32[12]{0:T(128)S(1)} %fusion.43.scalars, bf16[384,2560]{1,0:T(8,128)(2,1)} %refs_0_.13, bf16[192,2560]{1,0:T(8,128)(2,1)} %refs_1_.13, bf16[192,2560]{1,0:T(8,128)(2,1)} %refs_2_.13, bf16[384,1280]{1,0:T(8,128)(2,1)S(1)} %collective-permute-done.refs_3_.refs_9_), custom_call_target="tpu_custom_call" | custom-call | bytes 2752512 | tf_op jit(solution)/shard_map/pack_second/pallas_call | solution.py:300
  21.4 1.3 %collective-permute-start.2 = (bf16[768,512]{1,0:T(8,128)(2,1)}, bf16[768,512]{1,0:T(8,128)(2,1)S(1)}, u32[]{:S(2)}, u32[]{:S(2)}) collective-permute-start(bf16[768,512]{1,0:T(8,128)(2,1)} %get-tuple-element.40), channel_id=1, source_target_pairs={{4,0},{8,4},{12,8},{5,1},{9,5},{13,9},{6,2},{10,6},{14,10},{7,3},{... | collective-permute-start | bytes 2359304 | tf_op jit(solution)/shard_map/ppermute | solution.py:613
  22.8 5.8 %collective-permute-start.5 = (bf16[768,384]{1,0:T(8,128)(2,1)}, bf16[768,384]{1,0:T(8,128)(2,1)}, u32[]{:S(2)}, u32[]{:S(2)}) collective-permute-start(bf16[768,384]{1,0:T(8,128)(2,1)} %get-tuple-element.51), channel_id=1, source_target_pairs={{0,8},{1,9},{2,10},{3,11},{16,24},{17,25},{18,26},{19,27}} | collective-permute-start | bytes 1769480 | tf_op jit(solution)/shard_map/ppermute | solution.py:613
  28.5 3.2 %pack_third.1 = (bf16[1152,256]{1,0:T(8,128)(2,1)}, bf16[1152,256]{1,0:T(8,128)(2,1)}, bf16[768,256]{1,0:T(8,128)(2,1)}, bf16[1152,256]{1,0:T(8,128)(2,1)}, bf16[768,128]{1,0:T(8,128)(2,1)}) custom-call(s32[12]{0:T(128)S(1)} %fusion.43.scalars, bf16[384,2560]{1,0:T(8,128)(2,1)} %refs_0_.13, bf16[192,2560]{1,0:T(8,128)(2,1)} %refs_1_.13, ...), custom_call_target="tpu_custom_call" | custom-call | bytes 4718592 | tf_op jit(solution)/shard_map/pack_third/pallas_call | solution.py:300
  33.0 1.5 %collective-permute-start.12 = (f32[64,2]{1,0:T(8,128)S(1)}, f32[64,2]{1,0:T(8,128)S(1)}, u32[]{:S(2)}, u32[]{:S(2)}) collective-permute-start(f32[64,2]{1,0:T(8,128)S(1)} %copy.26), channel_id=1, source_target_pairs={{0,2},{2,0},{1,3},{3,1},{4,6},{6,4},{5,7},{7,5},{8,10},{10,8},{9,1... | collective-permute-start | bytes 1544 | tf_op jit(solution)/shard_map/ppermute | solution.py:1000
  35.3 1.3 %collective-permute-start.4 = (bf16[384,512]{1,0:T(8,128)(2,1)}, bf16[384,512]{1,0:T(8,128)(2,1)S(1)}, u32[]{:S(2)}, u32[]{:S(2)}) collective-permute-start(bf16[384,512]{1,0:T(8,128)(2,1)} %get-tuple-element.48), channel_id=1, source_target_pairs={{0,5},{1,4},{4,9},{5,8},{2,7},{3,6},{6,11},{7,10},{16,21},{17,20},... | collective-permute-start | bytes 1179656 | tf_op jit(solution)/shard_map/ppermute | solution.py:617
  37.0 1.5 %collective-permute-start.11 = (f32[32,80]{1,0:T(8,128)S(1)}, f32[32,80]{1,0:T(8,128)S(1)}, u32[]{:S(2)}, u32[]{:S(2)}) collective-permute-start(f32[32,80]{1,0:T(8,128)S(1)} %fusion.34), channel_id=1, source_target_pairs={{0,2},{2,0},{1,3},{3,1},{4,6},{6,4},{5,7},{7,5},{8,10},{10,8},{9,1... | collective-permute-start | bytes 30728 | tf_op jit(solution)/shard_map/ppermute | solution.py:816
  40.2 1.5 %collective-permute-start.15 = (bf16[1152,256]{1,0:T(8,128)(2,1)}, bf16[1152,256]{1,0:T(8,128)(2,1)}, u32[]{:S(2)}, u32[]{:S(2)}) collective-permute-start(bf16[1152,256]{1,0:T(8,128)(2,1)} %get-tuple-element.42), channel_id=1, source_target_pairs={{12,4},{13,5},{14,6},{15,7},{28,20},{29,21},{30,22},{31,23}} | collective-permute-start | bytes 1769480 | tf_op jit(solution)/shard_map/ppermute | solution.py:613
  41.7 1.3 %collective-permute-start.8 = (bf16[1152,256]{1,0:T(8,128)(2,1)}, bf16[1152,256]{1,0:T(8,128)(2,1)}, u32[]{:S(2)}, u32[]{:S(2)}) collective-permute-start(bf16[1152,256]{1,0:T(8,128)(2,1)} %get-tuple-element.54), channel_id=1, source_target_pairs={{8,12},{4,0},{9,13},{5,1},{10,14},{6,2},{11,15},{7,3},{24,28},{20,... | collective-permute-start | bytes 1769480 | tf_op jit(solution)/shard_map/ppermute | solution.py:613
  43.7 4.9 %collective-permute-done.4.refs_9_ = bf16[384,512]{1,0:T(8,128)(2,1)S(1)} collective-permute-done((bf16[384,512]{1,0:T(8,128)(2,1)}, bf16[384,512]{1,0:T(8,128)(2,1)S(1)}, u32[]{:S(2)}, u32[]{:S(2)}) %collective-permute-start.4) | collective-permute-done | bytes 393248 | tf_op jit(solution)/shard_map/ppermute | solution.py:617
  49.4 2.0 %collective-permute-start.14 = (bf16[768,256]{1,0:T(8,128)(2,1)}, bf16[768,256]{1,0:T(8,128)(2,1)}, u32[]{:S(2)}, u32[]{:S(2)}) collective-permute-start(bf16[768,256]{1,0:T(8,128)(2,1)} %get-tuple-element.63), channel_id=1, source_target_pairs={{0,12},{1,13},{2,14},{3,15},{16,28},{17,29},{18,30},{19,31}} | collective-permute-start | bytes 1179656 | tf_op jit(solution)/shard_map/ppermute | solution.py:613
  51.4 1.4 %collective-permute-start.13 = (bf16[768,256]{1,0:T(8,128)(2,1)}, bf16[768,256]{1,0:T(8,128)(2,1)}, u32[]{:S(2)}, u32[]{:S(2)}) collective-permute-start(bf16[768,256]{1,0:T(8,128)(2,1)} %get-tuple-element.63), channel_id=1, source_target_pairs={{4,12},{5,13},{6,14},{7,15},{20,28},{21,29},{22,30},{23,31}} | collective-permute-start | bytes 1179656 | tf_op jit(solution)/shard_map/ppermute | solution.py:613
  56.6 9.6 %main_heads.1.refs_12_ = f32[3,80,384]{2,1,0:T(8,128)} custom-call(s32[12]{0:T(128)S(1)} %fusion.43.scalars, s32[16]{0:T(128)S(1)} %reshape.21.mask, bf16[384,2560]{1,0:T(8,128)(2,1)} %refs_0_.13, bf16[192,2560]{1,0:T(8,128)(2,1)} %refs_1_.13, bf16[192,2560]{1,0:T(8,128)(2,1)} %refs_2_.13, bf16[384,1280]{1,0:T(8,128)(2,1)S(1)} %collective-permute-done.refs_3_.refs_9_, ...), custom_call_target="tpu_custom_call" | custom-call | flops 1585446912 | bytes 1179648 | tf_op jit(solution)/shard_map/main_heads/pallas_call | solution.py:575
  66.2 1.5 %collective-permute-start.7 = (bf16[1152,256]{1,0:T(8,128)(2,1)}, bf16[1152,256]{1,0:T(8,128)(2,1)}, u32[]{:S(2)}, u32[]{:S(2)}) collective-permute-start(bf16[1152,256]{1,0:T(8,128)(2,1)} %get-tuple-element.53), channel_id=1, source_target_pairs={{12,4},{13,5},{14,6},{15,7},{28,20},{29,21},{30,22},{31,23}} | collective-permute-start | bytes 1769480 | tf_op jit(solution)/shard_map/ppermute | solution.py:613
  67.7 6.2 %collective-permute-start.6 = (bf16[768,128]{1,0:T(8,128)(2,1)}, bf16[768,128]{1,0:T(8,128)(2,1)S(1)}, u32[]{:S(2)}, u32[]{:S(2)}) collective-permute-start(bf16[768,128]{1,0:T(8,128)(2,1)} %get-tuple-element.52), channel_id=1, source_target_pairs={{0,8},{1,9},{2,10},{3,11},{16,24},{17,25},{18,26},{19,27}} | collective-permute-start | bytes 589832 | tf_op jit(solution)/shard_map/ppermute | solution.py:613
  76.9 1.9 %near_heads.1.refs_15_ = f32[3,80,384]{2,1,0:T(8,128)} custom-call(s32[12]{0:T(128)S(1)} %fusion.43.scalars, s32[16]{0:T(128)S(1)} %reshape.21.mask, bf16[384,2560]{1,0:T(8,128)(2,1)} %refs_0_.13, bf16[192,2560]{1,0:T(8,128)(2,1)} %refs_1_.13, bf16[192,2560]{1,0:T(8,128)(2,1)} %refs_2_.13, ...), custom_call_target="tpu_custom_call", output_to_operand_aliasing={{}: (14, {})} | custom-call | flops 603979776 | bytes 589824 | tf_op jit(solution)/shard_map/near_heads/pallas_call | solution.py:575
  78.8 9.2 %far_heads.1.refs_12_ = f32[3,80,384]{2,1,0:T(8,128)} custom-call(s32[12]{0:T(128)S(1)} %fusion.43.scalars, s32[16]{0:T(128)S(1)} %reshape.21.mask, bf16[384,2560]{1,0:T(8,128)(2,1)} %refs_0_.13, bf16[192,2560]{1,0:T(8,128)(2,1)} %refs_1_.13, bf16[192,2560]{1,0:T(8,128)(2,1)} %refs_2_.13, ...), custom_call_target="tpu_custom_call", output_to_operand_aliasing={{}: (17, {})} | custom-call | flops 4227858432 | bytes 589824 | tf_op jit(solution)/shard_map/far_heads/pallas_call | solution.py:575
  88.0 1.8 %last_heads.1 = f32[3,80,384]{2,1,0:T(8,128)} custom-call(s32[12]{0:T(128)S(1)} %fusion.43.scalars, s32[16]{0:T(128)S(1)} %reshape.21.mask, bf16[384,2560]{1,0:T(8,128)(2,1)} %refs_0_.13, bf16[192,2560]{1,0:T(8,128)(2,1)} %refs_1_.13, bf16[192,2560]{1,0:T(8,128)(2,1)} %refs_2_.13, ...), custom_call_target="tpu_custom_call", output_to_operand_aliasing={{}: (14, {})} | custom-call | flops 603979776 | bytes 589824 | tf_op jit(solution)/shard_map/last_heads/pallas_call | solution.py:575
  89.8 1.0 constant_dynamic-slice_fusion
  90.9 1.4 %collective-permute-done.16 = f32[3,40,384]{2,1,0:T(8,128)S(1)} collective-permute-done((f32[3,40,384]{2,1,0:T(8,128)S(1)}, f32[3,40,384]{2,1,0:T(8,128)S(1)}, u32[]{:S(2)}, u32[]{:S(2)}) %collective-permute-start.16) | collective-permute-done | bytes 184352 | tf_op jit(solution)/shard_map/ppermute | solution.py:1020
  93.4 1.3 %collective-permute-start.18 = (f32[40,256]{1,0:T(8,128)S(1)}, f32[40,256]{1,0:T(8,128)S(1)}, u32[]{:S(2)}, u32[]{:S(2)}) collective-permute-start(f32[40,256]{1,0:T(8,128)S(1)} %slice.51), channel_id=1, source_target_pairs={{0,8},{4,12},{1,9},{5,13},{2,10},{6,14},{3,11},{7,15},{16,24},{20,... | collective-permute-start | bytes 122888 | tf_op jit(solution)/shard_map/ppermute | solution.py:1027
  95.3 7.7 %collective-permute-start.17 = (f32[40,640]{1,0:T(8,128)S(1)}, f32[40,640]{1,0:T(8,128)S(1)}, u32[]{:S(2)}, u32[]{:S(2)}) collective-permute-start(f32[40,640]{1,0:T(8,128)S(1)} %pad_maximum_fusion.1), channel_id=1, source_target_pairs={{0,4},{4,8},{8,12},{1,5},{5,9},{9,13},{2,6},{6,10},{10,14},{3,7},{... | collective-permute-start | bytes 307208 | tf_op jit(solution)/shard_map/ppermute | solution.py:1023
  103.1 2.4 %collective-permute-done.17 = f32[40,640]{1,0:T(8,128)S(1)} collective-permute-done((f32[40,640]{1,0:T(8,128)S(1)}, f32[40,640]{1,0:T(8,128)S(1)}, u32[]{:S(2)}, u32[]{:S(2)}) %collective-permute-start.17) | collective-permute-done | bytes 102432 | tf_op jit(solution)/shard_map/ppermute | solution.py:1023
  105.5 1.6 %collective-permute-start.20 = (f32[40,640]{1,0:T(8,128)S(1)}, f32[40,640]{1,0:T(8,128)S(1)}, u32[]{:S(2)}, u32[]{:S(2)}) collective-permute-start(f32[40,640]{1,0:T(8,128)S(1)} %fusion.32), channel_id=1, source_target_pairs={{0,2},{2,0},{1,3},{3,1},{4,6},{6,4},{5,7},{7,5},{8,10},{10,8},{9,1... | collective-permute-start | bytes 307208 | tf_op jit(solution)/shard_map/ppermute | solution.py:1030
  107.1 3.2 %collective-permute-done.20 = f32[40,640]{1,0:T(8,128)S(1)} collective-permute-done((f32[40,640]{1,0:T(8,128)S(1)}, f32[40,640]{1,0:T(8,128)S(1)}, u32[]{:S(2)}, u32[]{:S(2)}) %collective-permute-start.20) | collective-permute-done | bytes 102432 | tf_op jit(solution)/shard_map/ppermute | solution.py:1030
  110.3 1.3 %collective-permute-done.21.other = f32[40,640]{1,0:T(8,128)S(1)} collective-permute-done((f32[40,640]{1,0:T(8,128)S(1)}, f32[40,640]{1,0:T(8,128)S(1)}, u32[]{:S(2)}, u32[]{:S(2)}) %collective-permute-start.21) | collective-permute-done | bytes 102432 | tf_op jit(solution)/shard_map/ppermute | solution.py:1031
  111.6 2.4 %finish.1 = (f32[3,8,16,16]{3,2,1,0:T(8,128)}, bf16[3,8,16,384]{3,2,1,0:T(8,128)(2,1)}) custom-call(s32[12]{0:T(128)S(1)} %fusion.43.scalars, f32[40,640]{1,0:T(8,128)S(1)} %add.91.mine, f32[40,640]{1,0:T(8,128)S(1)} %collective-permute-done.21.other, f32[320,80]{1,0:T(8,128)S(1)} %bitcast.35, bf16[320,512]{1,0:T(8,128)(2,1)S(1)} %copy-done.10, ...), custom_call_target="tpu_custom_call" | custom-call | tf_op jit(solution)/shard_map/finish/pallas_call | solution.py:940
  (88 shorter events, 16.4 us)
Async XLA Ops:
  0.6 37.8 %copy-start = (f32[384]{0:T(512)S(1)}, f32[384]{0:T(512)}, u32[]{:S(2)}) copy-start(f32[384]{0:T(512)} %param.21) | copy-start | bytes 4612
  5.4 13.2 %collective-permute-start = (bf16[384,1280]{1,0:T(8,128)(2,1)}, bf16[384,1280]{1,0:T(8,128)(2,1)S(1)}, u32[]{:S(2)}, u32[]{:S(2)}) collective-permute-start(bf16[384,1280]{1,0:T(8,128)(2,1)} %get-tuple-element.39), channel_id=1, source_target_pairs={{0,1},{1,0},{2,3},{3,2},{4,5},{5,4},{6,7},{7,6},{8,9},{9,8},{10,11... | collective-permute-start | bytes 2949128 | tf_op jit(solution)/shard_map/ppermute | solution.py:654
  6.0 12.5 %collective-permute-start.9 = (f32[8,16,32]{2,1,0:T(8,128)S(1)}, f32[8,16,32]{2,1,0:T(8,128)S(1)}, u32[]{:S(2)}, u32[]{:S(2)}) collective-permute-start(f32[8,16,32]{2,1,0:T(8,128)S(1)} %slice.33), channel_id=1, source_target_pairs={{0,4},{4,8},{8,12},{1,5},{5,9},{9,13},{2,6},{6,10},{10,14},{3,7},{... | collective-permute-start | bytes 49160 | tf_op jit(solution)/shard_map/ppermute | solution.py:46
  10.5 24.0 %collective-permute-start.1 = (bf16[384,512]{1,0:T(8,128)(2,1)}, bf16[384,512]{1,0:T(8,128)(2,1)S(1)}, u32[]{:S(2)}, u32[]{:S(2)}) collective-permute-start(bf16[384,512]{1,0:T(8,128)(2,1)} %get-tuple-element.46), channel_id=1, source_target_pairs={{4,0},{8,4},{12,8},{5,1},{9,5},{13,9},{6,2},{10,6},{14,10},{7,3},{... | collective-permute-start | bytes 1179656 | tf_op jit(solution)/shard_map/ppermute | solution.py:613
  11.8 28.4 %collective-permute-start.3 = (bf16[384,512]{1,0:T(8,128)(2,1)}, bf16[384,512]{1,0:T(8,128)(2,1)}, u32[]{:S(2)}, u32[]{:S(2)}) collective-permute-start(bf16[384,512]{1,0:T(8,128)(2,1)} %get-tuple-element.47), channel_id=1, source_target_pairs={{0,4},{4,8},{1,5},{5,9},{2,6},{6,10},{3,7},{7,11},{16,20},{20,24},... | collective-permute-start | bytes 1179656 | tf_op jit(solution)/shard_map/ppermute | solution.py:613
  21.4 32.2 %collective-permute-start.2 = (bf16[768,512]{1,0:T(8,128)(2,1)}, bf16[768,512]{1,0:T(8,128)(2,1)S(1)}, u32[]{:S(2)}, u32[]{:S(2)}) collective-permute-start(bf16[768,512]{1,0:T(8,128)(2,1)} %get-tuple-element.40), channel_id=1, source_target_pairs={{4,0},{8,4},{12,8},{5,1},{9,5},{13,9},{6,2},{10,6},{14,10},{7,3},{... | collective-permute-start | bytes 2359304 | tf_op jit(solution)/shard_map/ppermute | solution.py:613
  22.7 9.2 %copy-start.1 = (bf16[2560,64]{0,1:T(8,128)(2,1)S(1)}, bf16[2560,64]{0,1:T(8,128)(2,1)}, u32[]{:S(2)}) copy-start(bf16[2560,64]{0,1:T(8,128)(2,1)} %param.18) | copy-start | bytes 983044
  22.7 9.2 %copy-start.16 = (f32[2560]{0:T(1024)S(1)}, f32[2560]{0:T(1024)}, u32[]{:S(2)}) copy-start(f32[2560]{0:T(1024)} %param.16) | copy-start | bytes 30724
  22.7 9.2 %copy-start.17 = (f32[2560]{0:T(1024)S(1)}, f32[2560]{0:T(1024)}, u32[]{:S(2)}) copy-start(f32[2560]{0:T(1024)} %param.17) | copy-start | bytes 30724
  22.8 28.6 %collective-permute-start.5 = (bf16[768,384]{1,0:T(8,128)(2,1)}, bf16[768,384]{1,0:T(8,128)(2,1)}, u32[]{:S(2)}, u32[]{:S(2)}) collective-permute-start(bf16[768,384]{1,0:T(8,128)(2,1)} %get-tuple-element.51), channel_id=1, source_target_pairs={{0,8},{1,9},{2,10},{3,11},{16,24},{17,25},{18,26},{19,27}} | collective-permute-start | bytes 1769480 | tf_op jit(solution)/shard_map/ppermute | solution.py:613
  31.8 1.2 %collective-permute-start.10 = (f32[8,80]{1,0:T(8,128)S(1)}, f32[8,80]{1,0:T(8,128)S(1)}, u32[]{:S(2)}, u32[]{:S(2)}) collective-permute-start(f32[8,80]{1,0:T(8,128)S(1)} %fusion.35), channel_id=1, source_target_pairs={{0,1},{1,0},{2,3},{3,2},{4,5},{5,4},{6,7},{7,6},{8,9},{9,8},{10,11... | collective-permute-start | bytes 7688 | tf_op jit(solution)/shard_map/ppermute | solution.py:804
  32.3 6.2 %copy-start.14 = (f32[64,2]{1,0:T(8,128)}, f32[64,2]{1,0:T(8,128)S(1)}, u32[]{:S(2)}) copy-start(f32[64,2]{1,0:T(8,128)S(1)} %copy.26) | copy-start | bytes 1540
  33.0 3.9 %collective-permute-start.12 = (f32[64,2]{1,0:T(8,128)S(1)}, f32[64,2]{1,0:T(8,128)S(1)}, u32[]{:S(2)}, u32[]{:S(2)}) collective-permute-start(f32[64,2]{1,0:T(8,128)S(1)} %copy.26), channel_id=1, source_target_pairs={{0,2},{2,0},{1,3},{3,1},{4,6},{6,4},{5,7},{7,5},{8,10},{10,8},{9,1... | collective-permute-start | bytes 1544 | tf_op jit(solution)/shard_map/ppermute | solution.py:1000
  35.3 13.3 %collective-permute-start.4 = (bf16[384,512]{1,0:T(8,128)(2,1)}, bf16[384,512]{1,0:T(8,128)(2,1)S(1)}, u32[]{:S(2)}, u32[]{:S(2)}) collective-permute-start(bf16[384,512]{1,0:T(8,128)(2,1)} %get-tuple-element.48), channel_id=1, source_target_pairs={{0,5},{1,4},{4,9},{5,8},{2,7},{3,6},{6,11},{7,10},{16,21},{17,20},... | collective-permute-start | bytes 1179656 | tf_op jit(solution)/shard_map/ppermute | solution.py:617
  37.0 4.8 %collective-permute-start.11 = (f32[32,80]{1,0:T(8,128)S(1)}, f32[32,80]{1,0:T(8,128)S(1)}, u32[]{:S(2)}, u32[]{:S(2)}) collective-permute-start(f32[32,80]{1,0:T(8,128)S(1)} %fusion.34), channel_id=1, source_target_pairs={{0,2},{2,0},{1,3},{3,1},{4,6},{6,4},{5,7},{7,5},{8,10},{10,8},{9,1... | collective-permute-start | bytes 30728 | tf_op jit(solution)/shard_map/ppermute | solution.py:816
  40.2 27.5 %collective-permute-start.15 = (bf16[1152,256]{1,0:T(8,128)(2,1)}, bf16[1152,256]{1,0:T(8,128)(2,1)}, u32[]{:S(2)}, u32[]{:S(2)}) collective-permute-start(bf16[1152,256]{1,0:T(8,128)(2,1)} %get-tuple-element.42), channel_id=1, source_target_pairs={{12,4},{13,5},{14,6},{15,7},{28,20},{29,21},{30,22},{31,23}} | collective-permute-start | bytes 1769480 | tf_op jit(solution)/shard_map/ppermute | solution.py:613
  41.7 37.1 %collective-permute-start.8 = (bf16[1152,256]{1,0:T(8,128)(2,1)}, bf16[1152,256]{1,0:T(8,128)(2,1)}, u32[]{:S(2)}, u32[]{:S(2)}) collective-permute-start(bf16[1152,256]{1,0:T(8,128)(2,1)} %get-tuple-element.54), channel_id=1, source_target_pairs={{8,12},{4,0},{9,13},{5,1},{10,14},{6,2},{11,15},{7,3},{24,28},{20,... | collective-permute-start | bytes 1769480 | tf_op jit(solution)/shard_map/ppermute | solution.py:613
  49.4 29.4 %collective-permute-start.14 = (bf16[768,256]{1,0:T(8,128)(2,1)}, bf16[768,256]{1,0:T(8,128)(2,1)}, u32[]{:S(2)}, u32[]{:S(2)}) collective-permute-start(bf16[768,256]{1,0:T(8,128)(2,1)} %get-tuple-element.63), channel_id=1, source_target_pairs={{0,12},{1,13},{2,14},{3,15},{16,28},{17,29},{18,30},{19,31}} | collective-permute-start | bytes 1179656 | tf_op jit(solution)/shard_map/ppermute | solution.py:613
  51.4 27.4 %collective-permute-start.13 = (bf16[768,256]{1,0:T(8,128)(2,1)}, bf16[768,256]{1,0:T(8,128)(2,1)}, u32[]{:S(2)}, u32[]{:S(2)}) collective-permute-start(bf16[768,256]{1,0:T(8,128)(2,1)} %get-tuple-element.63), channel_id=1, source_target_pairs={{4,12},{5,13},{6,14},{7,15},{20,28},{21,29},{22,30},{23,31}} | collective-permute-start | bytes 1179656 | tf_op jit(solution)/shard_map/ppermute | solution.py:613
  54.6 1.0 copy-start.5
  55.6 1.0 copy-start.8
  66.2 21.8 %collective-permute-start.7 = (bf16[1152,256]{1,0:T(8,128)(2,1)}, bf16[1152,256]{1,0:T(8,128)(2,1)}, u32[]{:S(2)}, u32[]{:S(2)}) collective-permute-start(bf16[1152,256]{1,0:T(8,128)(2,1)} %get-tuple-element.53), channel_id=1, source_target_pairs={{12,4},{13,5},{14,6},{15,7},{28,20},{29,21},{30,22},{31,23}} | collective-permute-start | bytes 1769480 | tf_op jit(solution)/shard_map/ppermute | solution.py:613
  67.7 20.3 %collective-permute-start.6 = (bf16[768,128]{1,0:T(8,128)(2,1)}, bf16[768,128]{1,0:T(8,128)(2,1)S(1)}, u32[]{:S(2)}, u32[]{:S(2)}) collective-permute-start(bf16[768,128]{1,0:T(8,128)(2,1)} %get-tuple-element.52), channel_id=1, source_target_pairs={{0,8},{1,9},{2,10},{3,11},{16,24},{17,25},{18,26},{19,27}} | collective-permute-start | bytes 589832 | tf_op jit(solution)/shard_map/ppermute | solution.py:613
  74.9 1.0 copy-start.6
  89.8 21.8 %copy-start.10 = (bf16[320,512]{1,0:T(8,128)(2,1)S(1)}, bf16[320,512]{1,0:T(8,128)(2,1)}, u32[]{:S(2)}) copy-start(bf16[320,512]{1,0:T(8,128)(2,1)} %fusion.30.selector) | copy-start | bytes 983044
  89.8 21.8 %copy-start.11 = (f32[10,32,80]{2,1,0:T(8,128)S(1)}, f32[10,32,80]{2,1,0:T(8,128)}, u32[]{:S(2)}) copy-start(f32[10,32,80]{2,1,0:T(8,128)} %pad_maximum_fusion) | copy-start | bytes 307204
  90.9 1.5 %collective-permute-start.16 = (f32[3,40,384]{2,1,0:T(8,128)S(1)}, f32[3,40,384]{2,1,0:T(8,128)S(1)}, u32[]{:S(2)}, u32[]{:S(2)}) collective-permute-start(f32[3,40,384]{2,1,0:T(8,128)S(1)} %constant_dynamic-slice_fusion), channel_id=1, source_target_pairs={{0,1},{1,0},{2,3},{3,2},{4,5},{5,4},{6,7},{7,6},{8,9},{9,8},{10,11... | collective-permute-start | bytes 552968 | tf_op jit(solution)/shard_map/ppermute | solution.py:1020
  93.4 9.7 %collective-permute-start.18 = (f32[40,256]{1,0:T(8,128)S(1)}, f32[40,256]{1,0:T(8,128)S(1)}, u32[]{:S(2)}, u32[]{:S(2)}) collective-permute-start(f32[40,256]{1,0:T(8,128)S(1)} %slice.51), channel_id=1, source_target_pairs={{0,8},{4,12},{1,9},{5,13},{2,10},{6,14},{3,11},{7,15},{16,24},{20,... | collective-permute-start | bytes 122888 | tf_op jit(solution)/shard_map/ppermute | solution.py:1027
  94.7 8.4 %collective-permute-start.19 = (f32[40,384]{1,0:T(8,128)S(1)}, f32[40,384]{1,0:T(8,128)S(1)}, u32[]{:S(2)}, u32[]{:S(2)}) collective-permute-start(f32[40,384]{1,0:T(8,128)S(1)} %get-tuple-element.78), channel_id=1, source_target_pairs={{4,12},{12,8},{5,13},{13,9},{6,14},{14,10},{7,15},{15,11},{20,28},... | collective-permute-start | bytes 184328 | tf_op jit(solution)/shard_map/ppermute | solution.py:1026
  95.3 10.1 %collective-permute-start.17 = (f32[40,640]{1,0:T(8,128)S(1)}, f32[40,640]{1,0:T(8,128)S(1)}, u32[]{:S(2)}, u32[]{:S(2)}) collective-permute-start(f32[40,640]{1,0:T(8,128)S(1)} %pad_maximum_fusion.1), channel_id=1, source_target_pairs={{0,4},{4,8},{8,12},{1,5},{5,9},{9,13},{2,6},{6,10},{10,14},{3,7},{... | collective-permute-start | bytes 307208 | tf_op jit(solution)/shard_map/ppermute | solution.py:1023
  105.5 4.7 %collective-permute-start.20 = (f32[40,640]{1,0:T(8,128)S(1)}, f32[40,640]{1,0:T(8,128)S(1)}, u32[]{:S(2)}, u32[]{:S(2)}) collective-permute-start(f32[40,640]{1,0:T(8,128)S(1)} %fusion.32), channel_id=1, source_target_pairs={{0,2},{2,0},{1,3},{3,1},{4,6},{6,4},{5,7},{7,5},{8,10},{10,8},{9,1... | collective-permute-start | bytes 307208 | tf_op jit(solution)/shard_map/ppermute | solution.py:1030
  110.2 1.4 %collective-permute-start.21 = (f32[40,640]{1,0:T(8,128)S(1)}, f32[40,640]{1,0:T(8,128)S(1)}, u32[]{:S(2)}, u32[]{:S(2)}) collective-permute-start(f32[40,640]{1,0:T(8,128)S(1)} %add.91.mine), channel_id=1, source_target_pairs={{0,1},{1,0},{2,3},{3,2},{4,5},{5,4},{6,7},{7,6},{8,9},{9,8},{10,11... | collective-permute-start | bytes 307208 | tf_op jit(solution)/shard_map/ppermute | solution.py:1031
  (8 other events, 7.1 us)

commit v8 on v7

--- a/solution.py
+++ b/solution.py
@@ -224,8 +224,7 @@
 WINDOW = 32
 GRANT = 20 << 20
 
-OWN, OTHER, DOWN, UP, MAIN, LAST, LAST_COLUMN, PLACE, SLAB = range(9)
-STEPS = 9
+OWN, OTHER, DOWN, UP, MAIN, PLACE, SLAB = range(7)
 
 
 def plan_fits(heads_dev, span_count, slab_count, head_count):
@@ -238,15 +237,13 @@
 
 
 def scalar_operand(heads):
-    by_place = np.zeros((4, 12), np.int32)
+    by_place = np.zeros((4, 8), np.int32)
     by_place[:, OTHER] = heads
     by_place[:, DOWN] = [MIDDLE, MIDDLE, 0, MIDDLE]
     by_place[:, UP] = [0, MIDDLE, 0, 0]
     by_place[:, MAIN] = [MIDDLE, 0, MIDDLE, 0]
-    by_place[:, LAST] = [0, 2, MIDDLE + 3, 0]
-    by_place[:, LAST_COLUMN] = [0, 2, 3, 0]
     by_place[:, PLACE] = range(4)
-    by_slab = np.zeros(12, np.int32)
+    by_slab = np.zeros(8, np.int32)
     by_slab[[OWN, OTHER, SLAB]] = heads, -heads, 1
     row = lax.dynamic_slice_in_dim(jnp.array(by_place), lax.axis_index("span"), 1, 0)[0]
     return row + lax.axis_index("slab") * jnp.array(by_slab)
@@ -342,8 +339,8 @@
 def attend_kernel(variants, extra, span_count, fresh, scalars, mask, *refs):
     query_own, key_own, value_own, received, weight, gain = refs[:6]
     more = refs[6 : 6 + extra]
-    sums_out, folded, squares, carried, fetched, stored = refs[-6:]
-    payloads = refs[6 + extra : -6] if fresh else refs[6 + extra : -7]
+    mine_out, theirs_out, folded, squares, carried, moved = refs[-6:]
+    payloads = refs[6 + extra : -6] if fresh else refs[6 + extra : -8]
     rows = query_own.shape[0]
     half = rows // 2
     step = pl.program_id(0)
@@ -353,13 +350,25 @@
     )
 
     last_step = step == pl.num_programs(0) - 1
-    fetch = None if fresh else pltpu.make_async_copy(refs[-7], carried, fetched)
+    part = carried.shape[1] // 2
+    halves = [
+        carried.at[:, pl.ds(pl.multiple_of(number * part, part), part)]
+        for number in (scalars[SLAB], 1 - scalars[SLAB])
+    ]
+    fetches = (
+        []
+        if fresh
+        else [
+            pltpu.make_async_copy(refs[number - 8], halves[number], moved.at[number])
+            for number in range(2)
+        ]
+    )
 
     @pl.when((step == 0) & active)
     def _():
         folded[...] = jnp.zeros_like(folded)
         squares[...] = jnp.zeros_like(squares)
-        if fetch is not None:
+        for fetch in fetches:
             fetch.start()
 
     def query_of(source):
@@ -445,17 +454,22 @@
         wide = attended.astype(jnp.float32)
         squares[slot] += wide * wide
 
-    for place, (steps, tasks) in variants.items():
-
-        @pl.when((scalars[PLACE] == place) & (step < steps))
+    for place, tasks in variants.items():
+
+        @pl.when(scalars[PLACE] == place)
         def _():
             for task in tasks:
                 one_query(*task)
 
     def store():
-        copy = pltpu.make_async_copy(carried, sums_out, stored)
-        copy.start()
-        copy.wait()
+        copies = [
+            pltpu.make_async_copy(halves[number], out, moved.at[2 + number])
+            for number, out in enumerate((mine_out, theirs_out))
+        ]
+        for copy in copies:
+            copy.start()
+        for copy in copies:
+            copy.wait()
 
     if fresh:
 
@@ -468,8 +482,8 @@
     def _():
         ones_rows = jnp.ones((STAT_ROWS, HD), jnp.bfloat16)
         patch = weight.shape[0]
-        used = sorted({task[1] for _, tasks in variants.values() for task in tasks})
-        if fetch is not None:
+        used = sorted({task[1] for tasks in variants.values() for task in tasks})
+        for fetch in fetches:
             fetch.wait()
         for slot in range(SLOTS):
             if slot not in used:
@@ -529,14 +543,10 @@
             ),
         )
 
-    def payload_column(payload, entry, shift):
-        last = payload.shape[1] // HD - 1
-
-        def index(i, scalars, mask):
-            at = shift + moving(i, scalars)
-            return (0, jnp.minimum(at if entry is None else at + scalars[entry], last))
-
-        return pl.BlockSpec((payload.shape[0], HD), index)
+    def payload_column(payload):
+        return pl.BlockSpec(
+            (payload.shape[0], HD), lambda i, scalars, mask: (0, moving(i, scalars))
+        )
 
     in_specs = [
         column(rows, True),
@@ -559,35 +569,32 @@
             two_columns(1, True),
         ]
         arrays += [queries, keys, values, received, weight, gain]
-    in_specs += [payload_column(*payload) for payload in payloads]
-    arrays += [payload[0] for payload in payloads]
+    in_specs += [payload_column(payload) for payload in payloads]
+    arrays += payloads
     fresh = sums is None
     sums_shape = (SLOTS, patch + 2 * STAT_ROWS, rows)
     aliases = {}
     if not fresh:
-        aliases = {2 + len(arrays): 0}
-        in_specs.append(pl.BlockSpec(memory_space=pl.ANY))
-        arrays.append(sums)
-    pairs = max(
-        count * sum(len(task[3]) for task in tasks) for count, tasks in variants.values()
-    )
+        aliases = {2 + len(arrays): 0, 3 + len(arrays): 1}
+        in_specs += [pl.BlockSpec(memory_space=pl.ANY)] * 2
+        arrays += sums
+    pairs = steps * max(sum(len(task[3]) for task in tasks) for tasks in variants.values())
     span_count = math.isqrt(mask.shape[0])
     return pl.pallas_call(
         functools.partial(attend_kernel, variants, extra, span_count, fresh),
         name=name,
-        out_shape=pltpu.HBM(sums_shape, jnp.float32),
+        out_shape=[pltpu.HBM((SLOTS, sums_shape[1] // 2, rows), jnp.float32)] * 2,
         input_output_aliases=aliases,
         grid_spec=pltpu.PrefetchScalarGridSpec(
             num_scalar_prefetch=2,
             grid=(steps,),
             in_specs=in_specs,
-            out_specs=pl.BlockSpec(memory_space=pl.ANY),
+            out_specs=[pl.BlockSpec(memory_space=pl.ANY)] * 2,
             scratch_shapes=[
                 pltpu.VMEM((SLOTS, 2 * patch + 16, rows), jnp.float32),
                 pltpu.VMEM((SLOTS, rows, HD), jnp.float32),
                 pltpu.VMEM(sums_shape, jnp.float32),
-                pltpu.SemaphoreType.DMA,
-                pltpu.SemaphoreType.DMA,
+                pltpu.SemaphoreType.DMA((4,)),
             ],
         ),
         compiler_params=pltpu.CompilerParams(vmem_limit_bytes=GRANT),
@@ -605,20 +612,16 @@
     rows = queries.shape[0]
     half = rows // 2
     heads = NEAR_HEADS + MIDDLE_HEADS + FAR_HEADS
-    queries, keys, values = (
-        pltpu.with_memory_space_constraint(array, pltpu.HBM) for array in (queries, keys, values)
-    )
+    in_place = lambda array: pltpu.with_memory_space_constraint(array, pltpu.HBM)
+    queries, keys, values = (in_place(array) for array in (queries, keys, values))
 
     def send(value, *pairs):
-        return lax.ppermute(value, "span", list(pairs))
+        return in_place(lax.ppermute(value, "span", list(pairs)))
 
     def send_across(value, *pairs):
         slabs = lax.axis_size("slab")
-        return lax.ppermute(
-            value,
-            ("span", "slab"),
-            [(a * slabs + s, b * slabs + 1 - s) for a, b in pairs for s in range(slabs)],
-        )
+        flipped = [(a * slabs + s, b * slabs + 1 - s) for a, b in pairs for s in range(slabs)]
+        return in_place(lax.ppermute(value, ("span", "slab"), flipped))
 
     def tokens(entry, shift, count):
         return [(0, 0, rows, (OWN, entry) if entry else (OWN,), shift, count)]
@@ -651,7 +654,7 @@
     )
     lanes = 2 * noisy.shape[3]
     noise = jnp.concatenate([from_behind(noise[:, :, -lanes:], "span", 1), noise], axis=2)
-    received = lax.ppermute(handed, "slab", SWAP)
+    received = in_place(lax.ppermute(handed, "slab", SWAP))
     up_same = send(up_same, (0, 1), (1, 2))
     up_across = send_across(up_across, (0, 1), (1, 2))
     query_down = send(query_down, (1, 0), (2, 1), (3, 2))
@@ -659,19 +662,17 @@
     arrays = (queries, keys, values, received)
     pair_down, up_two = message(
         scalars,
-        [pairs_of(DOWN, 0, MIDDLE_HEADS), pairs_of(None, MIDDLE, 3)],
+        [pairs_of(DOWN, 0, MIDDLE_HEADS), pairs_of(None, MIDDLE, MIDDLE_HEADS)],
         arrays,
         "pack_second",
     )
     source, _ = lax.optimization_barrier((received, pair_down))
-    two, far_all, far_pair, last_two, last_up = message(
+    two, far_all, far_pair = message(
         scalars,
         [
-            tokens(None, 0, 2) + pairs_of(None, 0, 2),
+            tokens(None, 0, NEAR_HEADS) + pairs_of(None, 0, NEAR_HEADS),
             tokens(None, FAR, FAR_HEADS) + pairs_of(None, FAR, FAR_HEADS),
             pairs_of(None, FAR, FAR_HEADS),
-            tokens(None, 2, 2) + pairs_of(None, 2, 2),
-            pairs_of(None, MIDDLE + 3, 1),
         ],
         (queries, keys, values, source),
         "pack_third",
@@ -695,57 +696,26 @@
 
     on_one, back_one, back_two = Tokens(0, (1,)), Tokens(None, (2, 3)), Tokens(None, (4,))
     here = OWN_TOKENS
-    middle = [
-        (on_one, 1, 3, [(back_two, 0), (back_one, 1), (here, 2), (on_one, 3)]),
-        (here, 0, 2, [(back_two, 0), (back_one, 1), (here, 2)]),
-    ]
+    payloads = [query_down, pair_down, up_same, up_across, up_two]
     sums = run(
         MIDDLE_HEADS,
         (MAIN,),
         0,
         sums=None,
-        payloads=[
-            (query_down, None, 0),
-            (pair_down, None, 0),
-            (up_same, None, 0),
-            (up_across, None, 0),
-            (up_two, None, 0),
-        ],
+        payloads=payloads,
         variants={
-            0: (4, [(here, 0, 0, [(here, 0)]), (on_one, 1, 1, [(here, 0), (on_one, 1)])]),
-            1: (
-                4,
-                [
-                    (on_one, 1, 2, [(back_one, 0), (here, 1), (on_one, 2)]),
-                    (here, 0, 1, [(back_one, 0), (here, 1)]),
-                ],
-            ),
-            2: (3, middle),
+            0: [(here, 0, 0, [(here, 0)]), (on_one, 1, 1, [(here, 0), (on_one, 1)])],
+            1: [
+                (on_one, 1, 2, [(back_one, 0), (here, 1), (on_one, 2)]),
+                (here, 0, 1, [(back_one, 0), (here, 1)]),
+            ],
+            2: [
+                (on_one, 1, 3, [(back_two, 0), (back_one, 1), (here, 2), (on_one, 3)]),
+                (here, 0, 2, [(back_two, 0), (back_one, 1), (here, 2)]),
+            ],
         },
         more=False,
         name="main_heads",
-    )
-    last_two, last_up, sums = lax.optimization_barrier((last_two, last_up, sums))
-    last_two = send(last_two, (3, 1))
-    last_up = send(last_up, (0, 2))
-    on_two = Tokens(5, (5,))
-    last_span = [(on_two, 2, 3, [(back_one, 0), (here, 1), (on_one, 2), (on_two, 3)])]
-    sums = run(
-        2,
-        (MAIN,),
-        0,
-        sums=sums,
-        payloads=[
-            (query_down, None, 0),
-            (pair_down, None, 0),
-            (up_same, None, 0),
-            (up_across, None, 0),
-            (up_two, None, 0),
-            (two, None, 0),
-        ],
-        variants={1: (2, last_span)},
-        more=False,
-        name="near_heads",
     )
     beside, two_back, three_back = Tokens(0, (0,)), Tokens(None, (1,)), Tokens(None, (2,))
     extras = [Tokens(None, (), lane) for lane in range(2)]
@@ -754,50 +724,35 @@
         (),
         FAR,
         sums=sums,
-        payloads=[(far_next, None, 0), (far_two, None, 0), (far_three, None, 0)],
+        payloads=[far_next, far_two, far_three],
         variants={
-            0: (
-                FAR_HEADS,
-                [(here, 0, 0, [(here, 0)]), (beside, 1, 1, [(here, 0), (beside, 1)])]
-                + [(head, 0, 0, [(head, 0)]) for head in extras],
-            ),
-            3: (
-                FAR_HEADS,
-                [
-                    (here, 0, 3, [(three_back, 0), (two_back, 1), (beside, 2), (here, 3)]),
-                    (beside, 2, 2, [(three_back, 0), (two_back, 1), (beside, 2)]),
-                ],
-            ),
+            0: [(here, 0, 0, [(here, 0)]), (beside, 1, 1, [(here, 0), (beside, 1)])]
+            + [(head, 0, 0, [(head, 0)]) for head in extras],
+            3: [
+                (here, 0, 3, [(three_back, 0), (two_back, 1), (beside, 2), (here, 3)]),
+                (beside, 2, 2, [(three_back, 0), (two_back, 1), (beside, 2)]),
+            ],
         },
         more=True,
         name="far_heads",
         cost=4,
     )
-
-    def last(sums):
-        return run(
-            2,
-            (LAST,),
-            0,
-            sums=sums,
-            payloads=[
-                (query_down, LAST_COLUMN, 0),
-                (pair_down, LAST_COLUMN, 0),
-                (up_same, LAST_COLUMN, 0),
-                (up_across, LAST_COLUMN, 0),
-                (last_up, None, 0),
-                (last_two, None, 0),
-            ],
-            variants={1: (2, last_span), 2: (1, middle)},
-            more=False,
-            name="last_heads",
-        )
-
+    on_two = Tokens(5, (5,))
     sums, prepared = lax.optimization_barrier((sums, prepared))
-    return last(sums), prepared
-
-
-def noise_window(grid):
+    sums = run(
+        NEAR_HEADS,
+        (MAIN,),
+        0,
+        sums=sums,
+        payloads=payloads + [two],
+        variants={1: [(on_two, 2, 3, [(back_one, 0), (here, 1), (on_one, 2), (on_two, 3)])]},
+        more=False,
+        name="near_heads",
+    )
+    return sums, prepared
+
+
+def noise_window(grid, constants):
     height, breadth, _ = grid.shape
     slab = lax.axis_index("slab")
     edge = jnp.where(slab == 0, grid[:, breadth - 1], grid[:, 0])
@@ -813,11 +768,15 @@
     )
     head = lax.axis_index("head")
     edge = jnp.where(head == 0, grid[height - 1], grid[0])
-    edge = lax.ppermute(edge, "head", SWAP)[None]
+    count = constants.shape[1]
+    extra = jnp.pad(constants, ((0, 8 - constants.shape[0]), (0, edge.shape[1] - count)))
+    sent = lax.ppermute(jnp.concatenate([edge, extra], axis=0), "head", SWAP)
+    edge = sent[None, :WINDOW]
+    constants = constants + sent[WINDOW : WINDOW + constants.shape[0], :count]
     grid = jnp.concatenate(
         [jnp.where(head == 1, edge, 0.0), grid, jnp.where(head == 0, edge, 0.0)], axis=0
     )
-    return grid.reshape((height + 2) * WINDOW, grid.shape[2])
+    return grid.reshape((height + 2) * WINDOW, grid.shape[2]), constants.T
 
 
 def cell_selector(height, breadth):
@@ -992,18 +951,18 @@
             [
                 jnp.sum(wide_weight * gain[None, :], axis=1),
                 jnp.sum(wide_weight * shift[None, :], axis=1),
-            ],
-            axis=1,
-        )
+            ]
+        )
+        window, constants = noise_window(noise, constants)
         return (
-            noise_window(noise),
-            constants + lax.ppermute(constants, "head", SWAP),
+            window,
+            constants,
             cell_selector(height, breadth),
             banded_weight(taps),
             jnp.tile(bias, FRAMES_SPAN)[None, :],
         )
 
-    sums, (noise, constants, selector, band, bias) = token_sums(
+    (mine, theirs), (noise, constants, selector, band, bias) = token_sums(
         scalars,
         queries,
         keys,
@@ -1014,9 +973,6 @@
         noisy_latent,
         prepare,
     )
-    half = sums.shape[1] // 2
-    mine = lax.dynamic_slice_in_dim(sums, slab * half, half, 1)
-    theirs = lax.dynamic_slice_in_dim(sums, (1 - slab) * half, half, 1)
     mine = mine + lax.ppermute(theirs, "slab", SWAP)
     own, after, third = mine[0], mine[1], mine[2]
     skip = TROWS * TCOLS

time: 115 us -> 120 us (1.043)
  waiting for transfers between devices: 14.2 us -> 25.8 us
  local copies, waits for them, and re-layouts: 11.9 us -> 4.69 us
  other arithmetic: 4.15 us -> 6.28 us
  starting transfers between devices: 48.4 us -> 47.1 us
    unnamed x38 -> x20, local copies, waits for them, and re-layouts: 9.95 us -> 1.92 us
    ppermute x1, starting transfers between devices: 1.29 us -> 7.15 us  [per_device(): to_before = lax.ppermute(after[:, skip:], 'span', [(0, 2), (1, 3)])]
    ppermute x14 -> x11, starting transfers between devices: 32.5 us -> 26.6 us  [the longest x8 22.4 us: send(): return in_place(lax.ppermute(value, 'span', list(pairs)))]
    ppermute x1, waiting for transfers between devices: 0.01 us -> 5.75 us  [from_behind(): return lax.ppermute(value, axis, pairs)]
    ppermute x14 -> x11, waiting for transfers between devices: 5.2 us -> 10.4 us  [the longest x1 10.4 us: send_across(): return in_place(lax.ppermute(value, ('span', 'slab'), flipped))]
    ppermute x1, waiting for transfers between devices: 2.39 us -> 0.01 us  [per_device(): lax.ppermute(jnp.concatenate([own[:, skip:], after], axis=1), 'span', [(0...]
    concatenate x0 -> x2, local copies, waits for them, and re-layouts: none -> 1.84 us  [noise_window(): jnp.concatenate([jnp.where(slab == 1, edge, 0.0), grid, jnp.where(slab ==...]
    concatenate x0 -> x2, other arithmetic: none -> 1.68 us  [the longest x1 0.98 us: noise_window(): jnp.concatenate([jnp.where(slab == 1, edge, 0.0), grid, jnp.where(slab ==...]
  transfers between devices with their start and end apart: 22 -> 19, of which waited for: 7 -> 7; matrix products, arithmetic and copies ran while one was open for 3% -> 6% of each run, Pallas kernels for 24% -> 22%
where the time goes in v8:
time: 120 us; the launch traced here: 118 us
  starting transfers between devices  47.1 us (39%)
  Pallas kernels  33.3 us (28%)
  waiting for transfers between devices  25.8 us (22%)
  other arithmetic  6.28 us (5%)
  local copies, waits for them, and re-layouts  4.69 us (4%)
    ppermute x8, starting transfers between devices, send(): return in_place(lax.ppermute(value, 'span', list(pairs)))  22.4 us
    pallas_call x3, Pallas kernels, attend(): pl.pallas_call(functools.partial(attend_kernel, variants, extra, span_cou...  21.2 us
    ppermute x1, waiting for transfers between devices, send_across(): return in_place(lax.ppermute(value, ('span', 'slab'), flipped))  10.4 us
    pallas_call x3, Pallas kernels, pack(): pl.pallas_call(functools.partial(pack_kernel, len(arrays), len(shapes), c...  9.54 us
    ppermute x1, starting transfers between devices, per_device(): lax.ppermute(jnp.concatenate([own[:, skip:], after], axis=1), 'span', [(0...  8.9 us
    ppermute x1, starting transfers between devices, per_device(): to_before = lax.ppermute(after[:, skip:], 'span', [(0, 2), (1, 3)])  7.15 us
    ppermute x1, waiting for transfers between devices, from_behind(): return lax.ppermute(value, axis, pairs)  5.75 us
    ppermute x1, waiting for transfers between devices, per_device(): total = total + lax.ppermute(total, 'head', SWAP)  4.28 us
  transfers between devices with their start and end apart: 19, of which 7 were waited for; matrix products, arithmetic and copies ran while one was open for 6% of the time, Pallas kernels for 22%

profile of v8, /device:TPU:0, one launch (start us, length us, event | category | flops | bytes accessed | tf_op | source)
XLA Modules:
  0.0 118.2 jit_solution(8763899858758680582)
XLA Ops:
  1.4 0.9 copy-done.3
  2.3 3.2 %pack_first.1 = (bf16[384,1280]{1,0:T(8,128)(2,1)}, bf16[384,512]{1,0:T(8,128)(2,1)}, bf16[384,512]{1,0:T(8,128)(2,1)}, bf16[384,512]{1,0:T(8,128)(2,1)}, f32[8,16,48]{2,1,0:T(8,128)S(1)}) custom-call(s32[8]{0:T(128)S(1)} %bitcast_add_fusion.scalars, bf16[384,2560]{1,0:T(8,128)(2,1)} %refs_0_.11, bf16[192,2560]{1,0:T(8,128)(2,1)} %refs_1_.11, ...), custom_call_target="tpu_custom_call" | custom-call | bytes 4325376 | tf_op jit(solution)/shard_map/pack_first/pallas_call | solution.py:297
  6.0 1.3 %collective-permute-start.1 = (bf16[384,512]{1,0:T(8,128)(2,1)}, bf16[384,512]{1,0:T(8,128)(2,1)}, u32[]{:S(2)}, u32[]{:S(2)}) collective-permute-start(bf16[384,512]{1,0:T(8,128)(2,1)} %get-tuple-element.48), channel_id=1, source_target_pairs={{4,0},{8,4},{12,8},{5,1},{9,5},{13,9},{6,2},{10,6},{14,10},{7,3},{... | collective-permute-start | bytes 1179656 | tf_op jit(solution)/shard_map/ppermute | solution.py:619
  7.3 5.9 %collective-permute-start.3 = (bf16[384,512]{1,0:T(8,128)(2,1)}, bf16[384,512]{1,0:T(8,128)(2,1)}, u32[]{:S(2)}, u32[]{:S(2)}) collective-permute-start(bf16[384,512]{1,0:T(8,128)(2,1)} %get-tuple-element.49), channel_id=1, source_target_pairs={{0,4},{4,8},{1,5},{5,9},{2,6},{6,10},{3,7},{7,11},{16,20},{20,24},... | collective-permute-start | bytes 1179656 | tf_op jit(solution)/shard_map/ppermute | solution.py:619
  13.3 3.2 %collective-permute-start.8 = (f32[8,16,32]{2,1,0:T(8,128)S(1)}, f32[8,16,32]{2,1,0:T(8,128)S(1)}, u32[]{:S(2)}, u32[]{:S(2)}) collective-permute-start(f32[8,16,32]{2,1,0:T(8,128)S(1)} %slice.39), channel_id=1, source_target_pairs={{0,4},{4,8},{8,12},{1,5},{5,9},{9,13},{2,6},{6,10},{10,14},{3,7},{... | collective-permute-start | bytes 49160 | tf_op jit(solution)/shard_map/ppermute | solution.py:46
  17.3 5.8 %collective-permute-done.8 = f32[8,16,32]{2,1,0:T(8,128)S(1)} collective-permute-done((f32[8,16,32]{2,1,0:T(8,128)S(1)}, f32[8,16,32]{2,1,0:T(8,128)S(1)}, u32[]{:S(2)}, u32[]{:S(2)}) %collective-permute-start.8) | collective-permute-done | bytes 16416 | tf_op jit(solution)/shard_map/ppermute | solution.py:46
  23.2 0.9 copy-done.4
  24.1 3.0 %pack_second.1 = (bf16[768,512]{1,0:T(8,128)(2,1)}, bf16[768,512]{1,0:T(8,128)(2,1)}) custom-call(s32[8]{0:T(128)S(1)} %bitcast_add_fusion.scalars, bf16[384,2560]{1,0:T(8,128)(2,1)} %refs_0_.11, bf16[192,2560]{1,0:T(8,128)(2,1)} %refs_1_.11, bf16[192,2560]{1,0:T(8,128)(2,1)} %refs_2_.11, bf16[384,1280]{1,0:T(8,128)(2,1)} %copy-done.4), custom_call_target="tpu_custom_call" | custom-call | bytes 3145728 | tf_op jit(solution)/shard_map/pack_second/pallas_call | solution.py:297
  27.2 1.4 %collective-permute-start.2 = (bf16[768,512]{1,0:T(8,128)(2,1)}, bf16[768,512]{1,0:T(8,128)(2,1)S(1)}, u32[]{:S(2)}, u32[]{:S(2)}) collective-permute-start(bf16[768,512]{1,0:T(8,128)(2,1)} %get-tuple-element.42), channel_id=1, source_target_pairs={{4,0},{8,4},{12,8},{5,1},{9,5},{13,9},{6,2},{10,6},{14,10},{7,3},{... | collective-permute-start | bytes 2359304 | tf_op jit(solution)/shard_map/ppermute | solution.py:619
  28.6 3.3 %pack_third.1 = (bf16[1152,512]{1,0:T(8,128)(2,1)}, bf16[1152,256]{1,0:T(8,128)(2,1)}, bf16[768,256]{1,0:T(8,128)(2,1)}) custom-call(s32[8]{0:T(128)S(1)} %bitcast_add_fusion.scalars, bf16[384,2560]{1,0:T(8,128)(2,1)} %refs_0_.11, bf16[192,2560]{1,0:T(8,128)(2,1)} %refs_1_.11, bf16[192,2560]{1,0:T(8,128)(2,1)} %refs_2_.11, bf16[384,1280]{1,0:T(8,128)(2,1)} %copy-done.4), custom_call_target="tpu_custom_call" | custom-call | bytes 4325376 | tf_op jit(solution)/shard_map/pack_third/pallas_call | solution.py:297
  32.1 7.4 %collective-permute-start.5 = (bf16[768,512]{1,0:T(8,128)(2,1)}, bf16[768,512]{1,0:T(8,128)(2,1)}, u32[]{:S(2)}, u32[]{:S(2)}) collective-permute-start(bf16[768,512]{1,0:T(8,128)(2,1)} %get-tuple-element.51), channel_id=1, source_target_pairs={{0,8},{1,9},{2,10},{3,11},{16,24},{17,25},{18,26},{19,27}} | collective-permute-start | bytes 2359304 | tf_op jit(solution)/shard_map/ppermute | solution.py:619
  41.0 1.0 maximum_maximum_fusion
  43.5 1.6 %collective-permute-start.10 = (f32[40,80]{0,1:T(8,128)}, f32[40,80]{0,1:T(8,128)S(1)}, u32[]{:S(2)}, u32[]{:S(2)}) collective-permute-start(f32[40,80]{0,1:T(8,128)} %select_maximum_fusion), channel_id=1, source_target_pairs={{0,2},{2,0},{1,3},{3,1},{4,6},{6,4},{5,7},{7,5},{8,10},{10,8},{9,1... | collective-permute-start | bytes 38408 | tf_op jit(solution)/shard_map/ppermute | solution.py:773
  45.4 1.8 %copy.61 = f32[8,32,80]{2,1,0:T(8,128)} copy(f32[8,32,80]{1,2,0:T(8,128)} %maximum_maximum_fusion) | data formatting | bytes 163840 | tf_op jit(solution)/shard_map/concatenate | solution.py:760
  47.1 2.1 %collective-permute-start.4 = (bf16[384,512]{1,0:T(8,128)(2,1)}, bf16[384,512]{1,0:T(8,128)(2,1)}, u32[]{:S(2)}, u32[]{:S(2)}) collective-permute-start(bf16[384,512]{1,0:T(8,128)(2,1)} %get-tuple-element.50), channel_id=1, source_target_pairs={{0,5},{1,4},{4,9},{5,8},{2,7},{3,6},{6,11},{7,10},{16,21},{17,20},... | collective-permute-start | bytes 1179656 | tf_op jit(solution)/shard_map/ppermute | solution.py:624
  49.2 1.7 %collective-permute-start.6 = (bf16[1152,512]{1,0:T(8,128)(2,1)}, bf16[1152,512]{1,0:T(8,128)(2,1)}, u32[]{:S(2)}, u32[]{:S(2)}) collective-permute-start(bf16[1152,512]{1,0:T(8,128)(2,1)} %get-tuple-element.44), channel_id=1, source_target_pairs={{12,4},{13,5},{14,6},{15,7},{28,20},{29,21},{30,22},{31,23}} | collective-permute-start | bytes 3538952 | tf_op jit(solution)/shard_map/ppermute | solution.py:619
  51.1 0.9 pad_maximum_fusion
  52.0 1.3 %collective-permute-start.7 = (bf16[1152,256]{1,0:T(8,128)(2,1)}, bf16[1152,256]{1,0:T(8,128)(2,1)}, u32[]{:S(2)}, u32[]{:S(2)}) collective-permute-start(bf16[1152,256]{1,0:T(8,128)(2,1)} %get-tuple-element.52), channel_id=1, source_target_pairs={{8,12},{4,0},{9,13},{5,1},{10,14},{6,2},{11,15},{7,3},{24,28},{20,... | collective-permute-start | bytes 1769480 | tf_op jit(solution)/shard_map/ppermute | solution.py:619
  53.4 10.4 %collective-permute-done.4.refs_9_ = bf16[384,512]{1,0:T(8,128)(2,1)} collective-permute-done((bf16[384,512]{1,0:T(8,128)(2,1)}, bf16[384,512]{1,0:T(8,128)(2,1)}, u32[]{:S(2)}, u32[]{:S(2)}) %collective-permute-start.4) | collective-permute-done | bytes 393248 | tf_op jit(solution)/shard_map/ppermute | solution.py:624
  63.8 1.4 %collective-permute-start.11 = (bf16[768,256]{1,0:T(8,128)(2,1)}, bf16[768,256]{1,0:T(8,128)(2,1)}, u32[]{:S(2)}, u32[]{:S(2)}) collective-permute-start(bf16[768,256]{1,0:T(8,128)(2,1)} %get-tuple-element.61), channel_id=1, source_target_pairs={{4,12},{5,13},{6,14},{7,15},{20,28},{21,29},{22,30},{23,31}} | collective-permute-start | bytes 1179656 | tf_op jit(solution)/shard_map/ppermute | solution.py:619
  65.2 2.0 %collective-permute-start.12 = (bf16[768,256]{1,0:T(8,128)(2,1)}, bf16[768,256]{1,0:T(8,128)(2,1)}, u32[]{:S(2)}, u32[]{:S(2)}) collective-permute-start(bf16[768,256]{1,0:T(8,128)(2,1)} %get-tuple-element.61), channel_id=1, source_target_pairs={{0,12},{1,13},{2,14},{3,15},{16,28},{17,29},{18,30},{19,31}} | collective-permute-start | bytes 1179656 | tf_op jit(solution)/shard_map/ppermute | solution.py:619
  67.3 9.6 %main_heads.1 = (f32[3,40,384]{2,1,0:T(8,128)}, f32[3,40,384]{2,1,0:T(8,128)}) custom-call(s32[8]{0:T(128)S(1)} %bitcast_add_fusion.scalars, s32[16]{0:T(128)S(1)} %reshape.21.mask, bf16[384,2560]{1,0:T(8,128)(2,1)} %refs_0_.11, bf16[192,2560]{1,0:T(8,128)(2,1)} %refs_1_.11, bf16[192,2560]{1,0:T(8,128)(2,1)} %refs_2_.11, bf16[384,1280]{1,0:T(8,128)(2,1)} %copy-done.4, ...), custom_call_target="tpu_custom_call" | custom-call | flops 2113929216 | bytes 1179648 | tf_op jit(solution)/shard_map/main_heads/pallas_call | solution.py:583
  77.0 9.3 %far_heads.1 = (f32[3,40,384]{2,1,0:T(8,128)}, f32[3,40,384]{2,1,0:T(8,128)}) custom-call(s32[8]{0:T(128)S(1)} %bitcast_add_fusion.scalars, s32[16]{0:T(128)S(1)} %reshape.21.mask, bf16[384,2560]{1,0:T(8,128)(2,1)} %refs_0_.11, bf16[192,2560]{1,0:T(8,128)(2,1)} %refs_1_.11, ...), custom_call_target="tpu_custom_call", output_to_operand_aliasing={{0}: (17, {}), {1}: (18, {})} | custom-call | flops 4227858432 | bytes 589824 | tf_op jit(solution)/shard_map/far_heads/pallas_call | solution.py:583
  86.4 2.2 %near_heads.1 = (f32[3,40,384]{2,1,0:T(8,128)}, f32[3,40,384]{2,1,0:T(8,128)}) custom-call(s32[8]{0:T(128)S(1)} %bitcast_add_fusion.scalars, s32[16]{0:T(128)S(1)} %reshape.21.mask, bf16[384,2560]{1,0:T(8,128)(2,1)} %refs_0_.11, bf16[192,2560]{1,0:T(8,128)(2,1)} %refs_1_.11, ...), custom_call_target="tpu_custom_call", output_to_operand_aliasing={{0}: (14, {}), {1}: (15, {})} | custom-call | flops 1207959552 | bytes 1179648 | tf_op jit(solution)/shard_map/near_heads/pallas_call | solution.py:583
  88.6 1.6 %collective-permute-done.13 = f32[3,40,384]{2,1,0:T(8,128)S(1)} collective-permute-done((f32[3,40,384]{2,1,0:T(8,128)}, f32[3,40,384]{2,1,0:T(8,128)S(1)}, u32[]{:S(2)}, u32[]{:S(2)}) %collective-permute-start.13) | collective-permute-done | bytes 184352 | tf_op jit(solution)/shard_map/ppermute | solution.py:976
  90.2 0.9 add.82
  91.3 8.9 %collective-permute-start.14 = (f32[40,640]{1,0:T(8,128)S(1)}, f32[40,640]{1,0:T(8,128)S(1)}, u32[]{:S(2)}, u32[]{:S(2)}) collective-permute-start(f32[40,640]{1,0:T(8,128)S(1)} %pad_maximum_fusion.1), channel_id=1, source_target_pairs={{0,4},{4,8},{8,12},{1,5},{5,9},{9,13},{2,6},{6,10},{10,14},{3,7},{... | collective-permute-start | bytes 307208 | tf_op jit(solution)/shard_map/ppermute | solution.py:979
  100.8 7.1 %collective-permute-start.15 = (f32[40,256]{1,0:T(8,128)S(1)}, f32[40,256]{1,0:T(8,128)S(1)}, u32[]{:S(2)}, u32[]{:S(2)}) collective-permute-start(f32[40,256]{1,0:T(8,128)S(1)} %slice.63), channel_id=1, source_target_pairs={{0,8},{4,12},{1,9},{5,13},{2,10},{6,14},{3,11},{7,15},{16,24},{20,... | collective-permute-start | bytes 122888 | tf_op jit(solution)/shard_map/ppermute | solution.py:983
  108.0 1.6 %collective-permute-done.15 = f32[40,256]{1,0:T(8,128)S(1)} collective-permute-done((f32[40,256]{1,0:T(8,128)S(1)}, f32[40,256]{1,0:T(8,128)S(1)}, u32[]{:S(2)}, u32[]{:S(2)}) %collective-permute-start.15) | collective-permute-done | bytes 40992 | tf_op jit(solution)/shard_map/ppermute | solution.py:983
  110.1 4.3 %collective-permute-done.17 = f32[40,640]{1,0:T(8,128)S(1)} collective-permute-done((f32[40,640]{1,0:T(8,128)S(1)}, f32[40,640]{1,0:T(8,128)S(1)}, u32[]{:S(2)}, u32[]{:S(2)}) %collective-permute-start.17) | collective-permute-done | bytes 102432 | tf_op jit(solution)/shard_map/ppermute | solution.py:986
  114.5 1.3 %collective-permute-done.18.other = f32[40,640]{1,0:T(8,128)S(1)} collective-permute-done((f32[40,640]{1,0:T(8,128)S(1)}, f32[40,640]{1,0:T(8,128)S(1)}, u32[]{:S(2)}, u32[]{:S(2)}) %collective-permute-start.18) | collective-permute-done | bytes 102432 | tf_op jit(solution)/shard_map/ppermute | solution.py:987
  115.8 2.4 %finish.1 = (f32[3,8,16,16]{3,2,1,0:T(8,128)}, bf16[3,8,16,384]{3,2,1,0:T(8,128)(2,1)}) custom-call(s32[8]{0:T(128)S(1)} %bitcast_add_fusion.scalars, f32[40,640]{1,0:T(8,128)S(1)} %add.85.mine, f32[40,640]{1,0:T(8,128)S(1)} %collective-permute-done.18.other, f32[320,80]{1,0:T(8,128)S(1)} %bitcast.34, bf16[320,512]{1,0:T(8,128)(2,1)S(1)} %fusion.30.selector, ...), custom_call_target="tpu_custom_call" | custom-call | tf_op jit(solution)/shard_map/finish/pallas_call | solution.py:899
  (71 shorter events, 7.3 us)
Async XLA Ops:
  0.6 44.5 %copy-start = (f32[384]{0:T(512)S(1)}, f32[384]{0:T(512)}, u32[]{:S(2)}) copy-start(f32[384]{0:T(512)} %param.21) | copy-start | bytes 4612
  1.4 0.9 copy-start.3
  5.5 17.7 %collective-permute-start = (bf16[384,1280]{1,0:T(8,128)(2,1)}, bf16[384,1280]{1,0:T(8,128)(2,1)S(1)}, u32[]{:S(2)}, u32[]{:S(2)}) collective-permute-start(bf16[384,1280]{1,0:T(8,128)(2,1)} %get-tuple-element.41), channel_id=1, source_target_pairs={{0,1},{1,0},{2,3},{3,2},{4,5},{5,4},{6,7},{7,6},{8,9},{9,8},{10,11... | collective-permute-start | bytes 2949128 | tf_op jit(solution)/shard_map/ppermute | solution.py:657
  6.0 41.1 %collective-permute-start.1 = (bf16[384,512]{1,0:T(8,128)(2,1)}, bf16[384,512]{1,0:T(8,128)(2,1)}, u32[]{:S(2)}, u32[]{:S(2)}) collective-permute-start(bf16[384,512]{1,0:T(8,128)(2,1)} %get-tuple-element.48), channel_id=1, source_target_pairs={{4,0},{8,4},{12,8},{5,1},{9,5},{13,9},{6,2},{10,6},{14,10},{7,3},{... | collective-permute-start | bytes 1179656 | tf_op jit(solution)/shard_map/ppermute | solution.py:619
  7.3 44.7 %collective-permute-start.3 = (bf16[384,512]{1,0:T(8,128)(2,1)}, bf16[384,512]{1,0:T(8,128)(2,1)}, u32[]{:S(2)}, u32[]{:S(2)}) collective-permute-start(bf16[384,512]{1,0:T(8,128)(2,1)} %get-tuple-element.49), channel_id=1, source_target_pairs={{0,4},{4,8},{1,5},{5,9},{2,6},{6,10},{3,7},{7,11},{16,20},{20,24},... | collective-permute-start | bytes 1179656 | tf_op jit(solution)/shard_map/ppermute | solution.py:619
  13.3 9.8 %collective-permute-start.8 = (f32[8,16,32]{2,1,0:T(8,128)S(1)}, f32[8,16,32]{2,1,0:T(8,128)S(1)}, u32[]{:S(2)}, u32[]{:S(2)}) collective-permute-start(f32[8,16,32]{2,1,0:T(8,128)S(1)} %slice.39), channel_id=1, source_target_pairs={{0,4},{4,8},{8,12},{1,5},{5,9},{9,13},{2,6},{6,10},{10,14},{3,7},{... | collective-permute-start | bytes 49160 | tf_op jit(solution)/shard_map/ppermute | solution.py:46
  23.1 0.9 copy-start.4
  27.1 12.4 %copy-start.1 = (bf16[2560,64]{0,1:T(8,128)(2,1)S(1)}, bf16[2560,64]{0,1:T(8,128)(2,1)}, u32[]{:S(2)}) copy-start(bf16[2560,64]{0,1:T(8,128)(2,1)} %param.18) | copy-start | bytes 983044
  27.1 12.4 %copy-start.6 = (f32[2560]{0:T(1024)S(1)}, f32[2560]{0:T(1024)}, u32[]{:S(2)}) copy-start(f32[2560]{0:T(1024)} %param.16) | copy-start | bytes 30724
  27.1 12.4 %copy-start.7 = (f32[2560]{0:T(1024)S(1)}, f32[2560]{0:T(1024)}, u32[]{:S(2)}) copy-start(f32[2560]{0:T(1024)} %param.17) | copy-start | bytes 30724
  27.2 38.0 %collective-permute-start.2 = (bf16[768,512]{1,0:T(8,128)(2,1)}, bf16[768,512]{1,0:T(8,128)(2,1)S(1)}, u32[]{:S(2)}, u32[]{:S(2)}) collective-permute-start(bf16[768,512]{1,0:T(8,128)(2,1)} %get-tuple-element.42), channel_id=1, source_target_pairs={{4,0},{8,4},{12,8},{5,1},{9,5},{13,9},{6,2},{10,6},{14,10},{7,3},{... | collective-permute-start | bytes 2359304 | tf_op jit(solution)/shard_map/ppermute | solution.py:619
  31.9 13.2 %copy-start.2 = (bf16[432,384]{1,0:T(8,128)(2,1)S(1)}, bf16[432,384]{1,0:T(8,128)(2,1)}, u32[]{:S(2)}) copy-start(bf16[432,384]{1,0:T(8,128)(2,1)} %weight) | copy-start | bytes 995332
  32.1 35.2 %collective-permute-start.5 = (bf16[768,512]{1,0:T(8,128)(2,1)}, bf16[768,512]{1,0:T(8,128)(2,1)}, u32[]{:S(2)}, u32[]{:S(2)}) collective-permute-start(bf16[768,512]{1,0:T(8,128)(2,1)} %get-tuple-element.51), channel_id=1, source_target_pairs={{0,8},{1,9},{2,10},{3,11},{16,24},{17,25},{18,26},{19,27}} | collective-permute-start | bytes 2359304 | tf_op jit(solution)/shard_map/ppermute | solution.py:619
  39.5 1.2 collective-permute-start.9
  42.8 24.4 %copy-start.8 = (s32[4,4]{1,0:T(4,128)S(1)}, s32[4,4]{1,0:T(4,128)}, u32[]{:S(2)}) copy-start(s32[4,4]{1,0:T(4,128)} %param.15) | copy-start | bytes 196
  43.5 5.7 %collective-permute-start.10 = (f32[40,80]{0,1:T(8,128)}, f32[40,80]{0,1:T(8,128)S(1)}, u32[]{:S(2)}, u32[]{:S(2)}) collective-permute-start(f32[40,80]{0,1:T(8,128)} %select_maximum_fusion), channel_id=1, source_target_pairs={{0,2},{2,0},{1,3},{3,1},{4,6},{6,4},{5,7},{7,5},{8,10},{10,8},{9,1... | collective-permute-start | bytes 38408 | tf_op jit(solution)/shard_map/ppermute | solution.py:773
  47.1 16.6 %collective-permute-start.4 = (bf16[384,512]{1,0:T(8,128)(2,1)}, bf16[384,512]{1,0:T(8,128)(2,1)}, u32[]{:S(2)}, u32[]{:S(2)}) collective-permute-start(bf16[384,512]{1,0:T(8,128)(2,1)} %get-tuple-element.50), channel_id=1, source_target_pairs={{0,5},{1,4},{4,9},{5,8},{2,7},{3,6},{6,11},{7,10},{16,21},{17,20},... | collective-permute-start | bytes 1179656 | tf_op jit(solution)/shard_map/ppermute | solution.py:624
  49.2 37.1 %collective-permute-start.6 = (bf16[1152,512]{1,0:T(8,128)(2,1)}, bf16[1152,512]{1,0:T(8,128)(2,1)}, u32[]{:S(2)}, u32[]{:S(2)}) collective-permute-start(bf16[1152,512]{1,0:T(8,128)(2,1)} %get-tuple-element.44), channel_id=1, source_target_pairs={{12,4},{13,5},{14,6},{15,7},{28,20},{29,21},{30,22},{31,23}} | collective-permute-start | bytes 3538952 | tf_op jit(solution)/shard_map/ppermute | solution.py:619
  52.0 25.0 %collective-permute-start.7 = (bf16[1152,256]{1,0:T(8,128)(2,1)}, bf16[1152,256]{1,0:T(8,128)(2,1)}, u32[]{:S(2)}, u32[]{:S(2)}) collective-permute-start(bf16[1152,256]{1,0:T(8,128)(2,1)} %get-tuple-element.52), channel_id=1, source_target_pairs={{8,12},{4,0},{9,13},{5,1},{10,14},{6,2},{11,15},{7,3},{24,28},{20,... | collective-permute-start | bytes 1769480 | tf_op jit(solution)/shard_map/ppermute | solution.py:619
  63.8 13.2 %collective-permute-start.11 = (bf16[768,256]{1,0:T(8,128)(2,1)}, bf16[768,256]{1,0:T(8,128)(2,1)}, u32[]{:S(2)}, u32[]{:S(2)}) collective-permute-start(bf16[768,256]{1,0:T(8,128)(2,1)} %get-tuple-element.61), channel_id=1, source_target_pairs={{4,12},{5,13},{6,14},{7,15},{20,28},{21,29},{22,30},{23,31}} | collective-permute-start | bytes 1179656 | tf_op jit(solution)/shard_map/ppermute | solution.py:619
  65.2 2.1 %copy-start.5 = (bf16[768,512]{1,0:T(8,128)(2,1)}, bf16[768,512]{1,0:T(8,128)(2,1)S(1)}, u32[]{:S(2)}) copy-start(bf16[768,512]{1,0:T(8,128)(2,1)S(1)} %collective-permute-done.2.refs_7_) | copy-start | bytes 2359300
  65.2 11.8 %collective-permute-start.12 = (bf16[768,256]{1,0:T(8,128)(2,1)}, bf16[768,256]{1,0:T(8,128)(2,1)}, u32[]{:S(2)}, u32[]{:S(2)}) collective-permute-start(bf16[768,256]{1,0:T(8,128)(2,1)} %get-tuple-element.61), channel_id=1, source_target_pairs={{0,12},{1,13},{2,14},{3,15},{16,28},{17,29},{18,30},{19,31}} | collective-permute-start | bytes 1179656 | tf_op jit(solution)/shard_map/ppermute | solution.py:619
  88.5 1.7 %collective-permute-start.13 = (f32[3,40,384]{2,1,0:T(8,128)}, f32[3,40,384]{2,1,0:T(8,128)S(1)}, u32[]{:S(2)}, u32[]{:S(2)}) collective-permute-start(f32[3,40,384]{2,1,0:T(8,128)} %get-tuple-element.74), channel_id=1, source_target_pairs={{0,1},{1,0},{2,3},{3,2},{4,5},{5,4},{6,7},{7,6},{8,9},{9,8},{10,11... | collective-permute-start | bytes 552968 | tf_op jit(solution)/shard_map/ppermute | solution.py:976
  91.3 18.4 %collective-permute-start.14 = (f32[40,640]{1,0:T(8,128)S(1)}, f32[40,640]{1,0:T(8,128)S(1)}, u32[]{:S(2)}, u32[]{:S(2)}) collective-permute-start(f32[40,640]{1,0:T(8,128)S(1)} %pad_maximum_fusion.1), channel_id=1, source_target_pairs={{0,4},{4,8},{8,12},{1,5},{5,9},{9,13},{2,6},{6,10},{10,14},{3,7},{... | collective-permute-start | bytes 307208 | tf_op jit(solution)/shard_map/ppermute | solution.py:979
  100.2 9.5 %collective-permute-start.16 = (f32[40,384]{1,0:T(8,128)S(1)}, f32[40,384]{1,0:T(8,128)S(1)}, u32[]{:S(2)}, u32[]{:S(2)}) collective-permute-start(f32[40,384]{1,0:T(8,128)S(1)} %get-tuple-element.82), channel_id=1, source_target_pairs={{4,12},{12,8},{5,13},{13,9},{6,14},{14,10},{7,15},{15,11},{20,28},... | collective-permute-start | bytes 184328 | tf_op jit(solution)/shard_map/ppermute | solution.py:982
  100.8 8.8 %collective-permute-start.15 = (f32[40,256]{1,0:T(8,128)S(1)}, f32[40,256]{1,0:T(8,128)S(1)}, u32[]{:S(2)}, u32[]{:S(2)}) collective-permute-start(f32[40,256]{1,0:T(8,128)S(1)} %slice.63), channel_id=1, source_target_pairs={{0,8},{4,12},{1,9},{5,13},{2,10},{6,14},{3,11},{7,15},{16,24},{20,... | collective-permute-start | bytes 122888 | tf_op jit(solution)/shard_map/ppermute | solution.py:983
  109.7 4.7 %collective-permute-start.17 = (f32[40,640]{1,0:T(8,128)S(1)}, f32[40,640]{1,0:T(8,128)S(1)}, u32[]{:S(2)}, u32[]{:S(2)}) collective-permute-start(f32[40,640]{1,0:T(8,128)S(1)} %fusion.32), channel_id=1, source_target_pairs={{0,2},{2,0},{1,3},{3,1},{4,6},{6,4},{5,7},{7,5},{8,10},{10,8},{9,1... | collective-permute-start | bytes 307208 | tf_op jit(solution)/shard_map/ppermute | solution.py:986
  114.4 1.4 %collective-permute-start.18 = (f32[40,640]{1,0:T(8,128)S(1)}, f32[40,640]{1,0:T(8,128)S(1)}, u32[]{:S(2)}, u32[]{:S(2)}) collective-permute-start(f32[40,640]{1,0:T(8,128)S(1)} %add.85.mine), channel_id=1, source_target_pairs={{0,1},{1,0},{2,3},{3,2},{4,5},{5,4},{6,7},{7,6},{8,9},{9,8},{10,11... | collective-permute-start | bytes 307208 | tf_op jit(solution)/shard_map/ppermute | solution.py:987

commit v9 on v8

--- a/solution.py
+++ b/solution.py
@@ -224,7 +224,7 @@
 WINDOW = 32
 GRANT = 20 << 20
 
-OWN, OTHER, DOWN, UP, MAIN, PLACE, SLAB = range(7)
+OWN, OTHER, DOWN, UP, MAIN, MAIN_CAP, FINAL, FINAL_CAP, PLACE, SLAB = range(10)
 
 
 def plan_fits(heads_dev, span_count, slab_count, head_count):
@@ -237,13 +237,16 @@
 
 
 def scalar_operand(heads):
-    by_place = np.zeros((4, 8), np.int32)
+    by_place = np.zeros((4, 12), np.int32)
     by_place[:, OTHER] = heads
     by_place[:, DOWN] = [MIDDLE, MIDDLE, 0, MIDDLE]
     by_place[:, UP] = [0, MIDDLE, 0, 0]
     by_place[:, MAIN] = [MIDDLE, 0, MIDDLE, 0]
+    by_place[:, MAIN_CAP] = [3, 3, 3, 0]
+    by_place[:, FINAL] = [FAR, 0, 0, FAR]
+    by_place[:, FINAL_CAP] = [1, 3, 0, 1]
     by_place[:, PLACE] = range(4)
-    by_slab = np.zeros(8, np.int32)
+    by_slab = np.zeros(12, np.int32)
     by_slab[[OWN, OTHER, SLAB]] = heads, -heads, 1
     row = lax.dynamic_slice_in_dim(jnp.array(by_place), lax.axis_index("span"), 1, 0)[0]
     return row + lax.axis_index("slab") * jnp.array(by_slab)
@@ -454,9 +457,9 @@
         wide = attended.astype(jnp.float32)
         squares[slot] += wide * wide
 
-    for place, tasks in variants.items():
-
-        @pl.when(scalars[PLACE] == place)
+    for place, (steps, tasks) in variants.items():
+
+        @pl.when((scalars[PLACE] == place) & (step < steps))
         def _():
             for task in tasks:
                 one_query(*task)
@@ -482,7 +485,7 @@
     def _():
         ones_rows = jnp.ones((STAT_ROWS, HD), jnp.bfloat16)
         patch = weight.shape[0]
-        used = sorted({task[1] for tasks in variants.values() for task in tasks})
+        used = sorted({task[1] for _, tasks in variants.values() for task in tasks})
         for fetch in fetches:
             fetch.wait()
         for slot in range(SLOTS):
@@ -511,42 +514,36 @@
         store()
 
 
-def attend(
-    steps, entries, first, own, scalars, mask, sums, payloads, variants, more, name, cost=1
-):
+def attend(steps, first, cap, own, scalars, mask, sums, payloads, variants, more, name, cost=1):
     queries, keys, values, received, weight, gain = own
     rows = queries.shape[0]
     half = rows // 2
     patch = weight.shape[0]
 
     def moving(i, scalars):
-        used = functools.reduce(
-            lambda a, b: a | b, [scalars[PLACE] == place for place in variants]
-        )
-        return jnp.where(used, i, 0)
+        return jnp.minimum(i, scalars[cap])
 
     def column(height, own_column):
         def index(i, scalars, mask):
-            head = first + moving(i, scalars) + (scalars[OWN] if own_column else 0)
-            for entry in entries:
-                head = head + scalars[entry]
-            return (0, head)
+            head = scalars[first] + moving(i, scalars)
+            return (0, head + scalars[OWN] if own_column else head)
 
         return pl.BlockSpec((height, HD), index)
 
     def two_columns(height, own_column):
-        return pl.BlockSpec(
-            (height, 2 * HD),
-            lambda i, scalars, mask: (
-                0,
-                moving(i, scalars) + (scalars[OWN] // 2 if own_column else 0),
-            ),
-        )
+        def index(i, scalars, mask):
+            pair = jnp.minimum(moving(i, scalars), 1)
+            return (0, pair + scalars[OWN] // 2 if own_column else pair)
+
+        return pl.BlockSpec((height, 2 * HD), index)
 
     def payload_column(payload):
-        return pl.BlockSpec(
-            (payload.shape[0], HD), lambda i, scalars, mask: (0, moving(i, scalars))
-        )
+        last = payload.shape[1] // HD - 1
+
+        def index(i, scalars, mask):
+            return (0, jnp.minimum(moving(i, scalars), last))
+
+        return pl.BlockSpec((payload.shape[0], HD), index)
 
     in_specs = [
         column(rows, True),
@@ -578,7 +575,9 @@
         aliases = {2 + len(arrays): 0, 3 + len(arrays): 1}
         in_specs += [pl.BlockSpec(memory_space=pl.ANY)] * 2
         arrays += sums
-    pairs = steps * max(sum(len(task[3]) for task in tasks) for tasks in variants.values())
+    pairs = max(
+        count * sum(len(task[3]) for task in tasks) for count, tasks in variants.values()
+    )
     span_count = math.isqrt(mask.shape[0])
     return pl.pallas_call(
         functools.partial(attend_kernel, variants, extra, span_count, fresh),
@@ -607,7 +606,7 @@
 
 
 def token_sums(
-    scalars, queries, keys, values, span_mask, head_gain, patch_weight, noisy, prepare
+    scalars, queries, keys, values, span_mask, head_gain, patch_weight, prepare
 ):
     rows = queries.shape[0]
     half = rows // 2
@@ -618,16 +617,8 @@
     def send(value, *pairs):
         return in_place(lax.ppermute(value, "span", list(pairs)))
 
-    def send_across(value, *pairs):
-        slabs = lax.axis_size("slab")
-        flipped = [(a * slabs + s, b * slabs + 1 - s) for a, b in pairs for s in range(slabs)]
-        return in_place(lax.ppermute(value, ("span", "slab"), flipped))
-
     def tokens(entry, shift, count):
         return [(0, 0, rows, (OWN, entry) if entry else (OWN,), shift, count)]
-
-    def own_half(slab_entry, entry, shift, count):
-        return [(part, 0, half, (slab_entry, entry), shift, count) for part in (1, 2)]
 
     def pairs_of(entry, shift, count):
         entries = (entry,) if entry else ()
@@ -640,49 +631,41 @@
             )
         ]
 
-    handed, up_same, up_across, query_down, noise = message(
+    (handed,) = message(
+        scalars,
+        [[(part, 0, half, (OTHER,), 0, heads) for part in (1, 2)]],
+        (queries, keys, values),
+        "pack_handed",
+    )
+    received = lax.ppermute(handed, "slab", SWAP)
+    down, up = message(
         scalars,
         [
-            [(part, 0, half, (OTHER,), 0, heads) for part in (1, 2)],
-            own_half(OWN, UP, 0, NEAR_HEADS),
-            own_half(OTHER, UP, 0, NEAR_HEADS),
-            tokens(DOWN, 0, MIDDLE_HEADS),
+            tokens(DOWN, 0, MIDDLE_HEADS) + pairs_of(DOWN, 0, MIDDLE_HEADS),
+            pairs_of(UP, 0, NEAR_HEADS),
         ],
-        (queries, keys, values),
+        (queries, keys, values, received),
         "pack_first",
-        noisy,
-    )
-    lanes = 2 * noisy.shape[3]
-    noise = jnp.concatenate([from_behind(noise[:, :, -lanes:], "span", 1), noise], axis=2)
-    received = in_place(lax.ppermute(handed, "slab", SWAP))
-    up_same = send(up_same, (0, 1), (1, 2))
-    up_across = send_across(up_across, (0, 1), (1, 2))
-    query_down = send(query_down, (1, 0), (2, 1), (3, 2))
-
-    arrays = (queries, keys, values, received)
-    pair_down, up_two = message(
-        scalars,
-        [pairs_of(DOWN, 0, MIDDLE_HEADS), pairs_of(None, MIDDLE, MIDDLE_HEADS)],
-        arrays,
-        "pack_second",
-    )
-    source, _ = lax.optimization_barrier((received, pair_down))
-    two, far_all, far_pair = message(
+    )
+    source, _ = lax.optimization_barrier((received, down))
+    down = send(down, (1, 0), (2, 1), (3, 2))
+    up = send(up, (0, 1), (1, 2))
+    up_two, two, far_all, far_pair = message(
         scalars,
         [
+            pairs_of(None, MIDDLE, MIDDLE_HEADS),
             tokens(None, 0, NEAR_HEADS) + pairs_of(None, 0, NEAR_HEADS),
             tokens(None, FAR, FAR_HEADS) + pairs_of(None, FAR, FAR_HEADS),
             pairs_of(None, FAR, FAR_HEADS),
         ],
         (queries, keys, values, source),
-        "pack_third",
+        "pack_second",
     )
     anchor = two
-    pair_down = send(pair_down, (1, 0), (2, 1), (3, 2))
     up_two = send(up_two, (0, 2))
     two = send(two, (3, 1))
     far_next = send(far_all, (2, 3), (1, 0))
-    far_pair, prepared = lax.optimization_barrier((far_pair, prepare(noise, anchor)))
+    far_pair, prepared = lax.optimization_barrier((far_pair, prepare(anchor)))
     far_two = send(far_pair, (1, 3))
     far_three = send(far_pair, (0, 3))
 
@@ -694,62 +677,71 @@
     own = (queries, keys, values, received, weight, head_gain[None, :])
     run = functools.partial(attend, own=own, scalars=scalars, mask=mask)
 
-    on_one, back_one, back_two = Tokens(0, (1,)), Tokens(None, (2, 3)), Tokens(None, (4,))
-    here = OWN_TOKENS
-    payloads = [query_down, pair_down, up_same, up_across, up_two]
+    here, on_one, back_one = OWN_TOKENS, Tokens(0, (0,)), Tokens(None, (1,))
+    back_two = Tokens(None, (2,))
     sums = run(
         MIDDLE_HEADS,
-        (MAIN,),
-        0,
+        MAIN,
+        MAIN_CAP,
         sums=None,
-        payloads=payloads,
+        payloads=[down, up, up_two],
         variants={
-            0: [(here, 0, 0, [(here, 0)]), (on_one, 1, 1, [(here, 0), (on_one, 1)])],
-            1: [
-                (on_one, 1, 2, [(back_one, 0), (here, 1), (on_one, 2)]),
-                (here, 0, 1, [(back_one, 0), (here, 1)]),
-            ],
-            2: [
-                (on_one, 1, 3, [(back_two, 0), (back_one, 1), (here, 2), (on_one, 3)]),
-                (here, 0, 2, [(back_two, 0), (back_one, 1), (here, 2)]),
-            ],
+            0: (4, [(here, 0, 0, [(here, 0)]), (on_one, 1, 1, [(here, 0), (on_one, 1)])]),
+            1: (
+                4,
+                [
+                    (on_one, 1, 2, [(back_one, 0), (here, 1), (on_one, 2)]),
+                    (here, 0, 1, [(back_one, 0), (here, 1)]),
+                ],
+            ),
+            2: (
+                4,
+                [
+                    (on_one, 1, 3, [(back_two, 0), (back_one, 1), (here, 2), (on_one, 3)]),
+                    (here, 0, 2, [(back_two, 0), (back_one, 1), (here, 2)]),
+                ],
+            ),
         },
         more=False,
         name="main_heads",
     )
-    beside, two_back, three_back = Tokens(0, (0,)), Tokens(None, (1,)), Tokens(None, (2,))
+    noise, *prepared = prepared
+    sums, noise = lax.optimization_barrier((sums, noise))
+    lanes = 2 * LAT_CH
+    before = from_behind(noise[:, -lanes:].reshape(-1, HD), "span", 1).reshape(-1, lanes)
+    on_two, beside = Tokens(2, (2,)), Tokens(3, (3,))
+    two_back, three_back = Tokens(None, (4,)), Tokens(None, (5,))
     extras = [Tokens(None, (), lane) for lane in range(2)]
+    sums, before, prepared = lax.optimization_barrier((sums, before, prepared))
     sums = run(
-        FAR_HEADS,
-        (),
-        FAR,
+        NEAR_HEADS,
+        FINAL,
+        FINAL_CAP,
         sums=sums,
-        payloads=[far_next, far_two, far_three],
+        payloads=[down, up, two, far_next, far_two, far_three],
         variants={
-            0: [(here, 0, 0, [(here, 0)]), (beside, 1, 1, [(here, 0), (beside, 1)])]
-            + [(head, 0, 0, [(head, 0)]) for head in extras],
-            3: [
-                (here, 0, 3, [(three_back, 0), (two_back, 1), (beside, 2), (here, 3)]),
-                (beside, 2, 2, [(three_back, 0), (two_back, 1), (beside, 2)]),
-            ],
+            0: (
+                FAR_HEADS,
+                [(here, 0, 0, [(here, 0)]), (beside, 1, 1, [(here, 0), (beside, 1)])]
+                + [(head, 0, 0, [(head, 0)]) for head in extras],
+            ),
+            1: (
+                NEAR_HEADS,
+                [(on_two, 2, 3, [(back_one, 0), (here, 1), (on_one, 2), (on_two, 3)])],
+            ),
+            3: (
+                FAR_HEADS,
+                [
+                    (here, 0, 3, [(three_back, 0), (two_back, 1), (beside, 2), (here, 3)]),
+                    (beside, 2, 2, [(three_back, 0), (two_back, 1), (beside, 2)]),
+                ],
+            ),
         },
         more=True,
-        name="far_heads",
+        name="final_heads",
         cost=4,
     )
-    on_two = Tokens(5, (5,))
-    sums, prepared = lax.optimization_barrier((sums, prepared))
-    sums = run(
-        NEAR_HEADS,
-        (MAIN,),
-        0,
-        sums=sums,
-        payloads=payloads + [two],
-        variants={1: [(on_two, 2, 3, [(back_one, 0), (here, 1), (on_one, 2), (on_two, 3)])]},
-        more=False,
-        name="near_heads",
-    )
-    return sums, prepared
+    return sums, (noise, before, *prepared)
 
 
 def noise_window(grid, constants):
@@ -769,9 +761,10 @@
     head = lax.axis_index("head")
     edge = jnp.where(head == 0, grid[height - 1], grid[0])
     count = constants.shape[1]
-    extra = jnp.pad(constants, ((0, 8 - constants.shape[0]), (0, edge.shape[1] - count)))
+    extra = jnp.pad(constants, ((0, 8 - constants.shape[0]), (0, HD - count)))
+    edge = jnp.pad(edge, ((0, 0), (0, HD - edge.shape[1])))
     sent = lax.ppermute(jnp.concatenate([edge, extra], axis=0), "head", SWAP)
-    edge = sent[None, :WINDOW]
+    edge = sent[None, :WINDOW, : grid.shape[2]]
     constants = constants + sent[WINDOW : WINDOW + constants.shape[0], :count]
     grid = jnp.concatenate(
         [jnp.where(head == 1, edge, 0.0), grid, jnp.where(head == 0, edge, 0.0)], axis=0
@@ -821,7 +814,7 @@
 
 
 def finish_kernel(
-    scalars, mine, other, noise, selector, band, bias, constants, clean, decoded, cells
+    scalars, mine, other, noise, before, selector, band, bias, constants, clean, decoded, cells
 ):
     frames, height, breadth, channels = clean.shape
     patch = constants.shape[0]
@@ -864,7 +857,9 @@
         for part in (high, low)
     )
     count = (height + 2) * WINDOW
-    cells[:count] = noise[...] - noise_level * chosen
+    cells[:count] = (
+        jnp.concatenate([before[...], noise[...]], axis=1) - noise_level * chosen
+    )
     cells[count:] = jnp.zeros_like(cells[count:])
     for frame in range(frames):
         lanes = slice((frame + 2) * channels, (frame + 3) * channels)
@@ -892,7 +887,9 @@
         )
 
 
-def finish(scalars, mine, other, noise, selector, band, bias, constants, shape, outputs):
+def finish(
+    scalars, mine, other, noise, before, selector, band, bias, constants, shape, outputs
+):
     whole = pl.BlockSpec(memory_space=pltpu.VMEM)
     frames, height, breadth, channels = shape
     rows = (height + 2) * WINDOW
@@ -903,11 +900,11 @@
             jax.ShapeDtypeStruct(shape, jnp.float32),
             jax.ShapeDtypeStruct((frames, height, breadth, outputs), jnp.bfloat16),
         ),
-        in_specs=[pl.BlockSpec(memory_space=pltpu.SMEM)] + [whole] * 7,
+        in_specs=[pl.BlockSpec(memory_space=pltpu.SMEM)] + [whole] * 8,
         out_specs=(whole, whole),
         scratch_shapes=[pltpu.VMEM((rows + 8, (frames + 2) * channels), jnp.float32)],
         compiler_params=pltpu.CompilerParams(vmem_limit_bytes=GRANT),
-    )(scalars, mine, other, noise, selector, band, bias, constants)
+    )(scalars, mine, other, noise, before, selector, band, bias, constants)
 
 
 def per_device(
@@ -941,11 +938,12 @@
     place = lax.axis_index("span")
     slab = lax.axis_index("slab")
     scalars = scalar_operand(heads_dev // lax.axis_size("slab"))
-    def prepare(noise, anchor):
+    def prepare(anchor):
         noise, weight, gain, shift, taps, bias, _ = lax.optimization_barrier(
-            (noise, patch_weight, head_gain, head_shift, conv_weight, conv_bias, anchor)
-        )
-        height, breadth, _ = noise.shape
+            (noisy_latent, patch_weight, head_gain, head_shift, conv_weight, conv_bias, anchor)
+        )
+        _, height, breadth, _ = noise.shape
+        noise = noise.transpose(1, 2, 0, 3).reshape(height, breadth, -1)
         wide_weight = weight.T.astype(jnp.float32)
         constants = jnp.stack(
             [
@@ -962,7 +960,7 @@
             jnp.tile(bias, FRAMES_SPAN)[None, :],
         )
 
-    (mine, theirs), (noise, constants, selector, band, bias) = token_sums(
+    (mine, theirs), (noise, before, constants, selector, band, bias) = token_sums(
         scalars,
         queries,
         keys,
@@ -970,7 +968,6 @@
         span_mask,
         head_gain,
         patch_weight,
-        noisy_latent,
         prepare,
     )
     mine = mine + lax.ppermute(theirs, "slab", SWAP)
@@ -990,6 +987,7 @@
         total,
         other,
         noise,
+        before,
         selector,
         band,
         bias,

time: 120 us -> 120 us (level)
  starting transfers between devices: 47.1 us -> 51.3 us
  local copies, waits for them, and re-layouts: 4.69 us -> 8.76 us
  waiting for transfers between devices: 25.8 us -> 22.1 us
  other arithmetic: 6.28 us -> 4.47 us
  Pallas kernels: 33.3 us -> 31.5 us
    ppermute x8 -> x7, waiting for transfers between devices: 0.02 us -> 9.77 us  [send(): return in_place(lax.ppermute(value, 'span', list(pairs)))]
    ppermute x2 -> x1, waiting for transfers between devices: 10.4 us -> 1.66 us  [token_sums(): received = lax.ppermute(handed, 'slab', SWAP)]
    ppermute x1, starting transfers between devices: 7.15 us -> 14.1 us  [per_device(): to_before = lax.ppermute(after[:, skip:], 'span', [(0, 2), (1, 3)])]
    ppermute x1, waiting for transfers between devices: 5.75 us -> 1.37 us  [from_behind(): return lax.ppermute(value, axis, pairs)]
    reshape x0 -> x3, local copies, waits for them, and re-layouts: none -> 3.31 us  [the longest x1 1.63 us: token_sums(): noise[:, -lanes:].reshape(-1, HD)]
    ppermute x1, waiting for transfers between devices: 0.01 us -> 2.19 us  [per_device(): lax.ppermute(jnp.concatenate([own[:, skip:], after], axis=1), 'span', [(0...]
    ppermute x2 -> x1, starting transfers between devices: 2.6 us -> 0.51 us  [token_sums(): received = lax.ppermute(handed, 'slab', SWAP)]
    concatenate x2 -> x1, local copies, waits for them, and re-layouts: 1.84 us -> 0.1 us  [noise_window(): sent = lax.ppermute(jnp.concatenate([edge, extra], axis=0), 'head', SWAP)]
  transfers between devices with their start and end apart: 19 -> 17, of which waited for: 7 -> 8; matrix products, arithmetic and copies ran while one was open for 6% -> 8% of each run, Pallas kernels for 22% -> 11%
where the time goes in v9:
time: 120 us; the launch traced here: 119 us
  starting transfers between devices  51.3 us (43%)
  Pallas kernels  31.5 us (26%)
  waiting for transfers between devices  22.1 us (18%)
  local copies, waits for them, and re-layouts  8.76 us (7%)
  other arithmetic  4.47 us (4%)
    ppermute x7, starting transfers between devices, send(): return in_place(lax.ppermute(value, 'span', list(pairs)))  21.4 us
    pallas_call x2, Pallas kernels, attend(): pl.pallas_call(functools.partial(attend_kernel, variants, extra, span_cou...  19.7 us
    ppermute x1, starting transfers between devices, per_device(): to_before = lax.ppermute(after[:, skip:], 'span', [(0, 2), (1, 3)])  14.1 us
    ppermute x7, waiting for transfers between devices, send(): return in_place(lax.ppermute(value, 'span', list(pairs)))  9.77 us
    ppermute x1, starting transfers between devices, per_device(): lax.ppermute(jnp.concatenate([own[:, skip:], after], axis=1), 'span', [(0...  9.5 us
    pallas_call x3, Pallas kernels, pack(): pl.pallas_call(functools.partial(pack_kernel, len(arrays), len(shapes), c...  9.19 us
    ppermute x1, waiting for transfers between devices, per_device(): total = total + lax.ppermute(total, 'head', SWAP)  3.27 us
    pallas_call x1, Pallas kernels, finish(): pl.pallas_call(finish_kernel, name='finish', out_shape=(jax.ShapeDtypeStr...  2.4 us
  transfers between devices with their start and end apart: 17, of which 8 were waited for; matrix products, arithmetic and copies ran while one was open for 8% of the time, Pallas kernels for 11%

profile of v9, /device:TPU:0, one launch (start us, length us, event | category | flops | bytes accessed | tf_op | source)
XLA Modules:
  0.0 119.1 jit_solution(8004520902822942798)
XLA Ops:
  1.4 2.7 %pack_handed.1 = bf16[384,1280]{1,0:T(8,128)(2,1)} custom-call(s32[12]{0:T(128)S(1)} %bitcast_add_fusion.scalars, bf16[384,2560]{1,0:T(8,128)(2,1)} %refs_6_.1, bf16[192,2560]{1,0:T(8,128)(2,1)} %refs_7_.1, bf16[192,2560]{1,0:T(8,128)(2,1)} %refs_8_.1), custom_call_target="tpu_custom_call" | custom-call | bytes 1966080 | tf_op jit(solution)/shard_map/pack_handed/pallas_call | solution.py:300
  5.3 1.7 %collective-permute-done.refs_3_.refs_9_ = bf16[384,1280]{1,0:T(8,128)(2,1)S(1)} collective-permute-done((bf16[384,1280]{1,0:T(8,128)(2,1)}, bf16[384,1280]{1,0:T(8,128)(2,1)S(1)}, u32[]{:S(2)}, u32[]{:S(2)}) %collective-permute-start) | collective-permute-done | bytes 983072 | tf_op jit(solution)/shard_map/ppermute | solution.py:640
  7.0 3.1 %pack_first.1 = (bf16[1152,512]{1,0:T(8,128)(2,1)}, bf16[768,512]{1,0:T(8,128)(2,1)}) custom-call(s32[12]{0:T(128)S(1)} %bitcast_add_fusion.scalars, bf16[384,2560]{1,0:T(8,128)(2,1)} %refs_6_.1, bf16[192,2560]{1,0:T(8,128)(2,1)} %refs_7_.1, bf16[192,2560]{1,0:T(8,128)(2,1)} %refs_8_.1, bf16[384,1280]{1,0:T(8,128)(2,1)S(1)} %collective-permute-done.refs_3_.refs_9_), custom_call_target="tpu_custom_call" | custom-call | bytes 3932160 | tf_op jit(solution)/shard_map/pack_first/pallas_call | solution.py:300
  10.1 1.3 %collective-permute-start.1 = (bf16[1152,512]{1,0:T(8,128)(2,1)}, bf16[1152,512]{1,0:T(8,128)(2,1)}, u32[]{:S(2)}, u32[]{:S(2)}) collective-permute-start(bf16[1152,512]{1,0:T(8,128)(2,1)} %get-tuple-element.38), channel_id=1, source_target_pairs={{4,0},{8,4},{12,8},{5,1},{9,5},{13,9},{6,2},{10,6},{14,10},{7,3},{... | collective-permute-start | bytes 3538952 | tf_op jit(solution)/shard_map/ppermute | solution.py:618
  11.4 6.5 %collective-permute-start.2 = (bf16[768,512]{1,0:T(8,128)(2,1)}, bf16[768,512]{1,0:T(8,128)(2,1)}, u32[]{:S(2)}, u32[]{:S(2)}) collective-permute-start(bf16[768,512]{1,0:T(8,128)(2,1)} %get-tuple-element.44), channel_id=1, source_target_pairs={{0,4},{4,8},{1,5},{5,9},{2,6},{6,10},{3,7},{7,11},{16,20},{20,24},... | collective-permute-start | bytes 2359304 | tf_op jit(solution)/shard_map/ppermute | solution.py:618
  17.9 3.4 %pack_second.1 = (bf16[768,512]{1,0:T(8,128)(2,1)}, bf16[1152,512]{1,0:T(8,128)(2,1)}, bf16[1152,256]{1,0:T(8,128)(2,1)}, bf16[768,256]{1,0:T(8,128)(2,1)}) custom-call(s32[12]{0:T(128)S(1)} %bitcast_add_fusion.scalars, bf16[384,2560]{1,0:T(8,128)(2,1)} %refs_6_.1, bf16[192,2560]{1,0:T(8,128)(2,1)} %refs_7_.1, bf16[192,2560]{1,0:T(8,128)(2,1)} %refs_8_.1, ...), custom_call_target="tpu_custom_call" | custom-call | bytes 5898240 | tf_op jit(solution)/shard_map/pack_second/pallas_call | solution.py:300
  21.4 1.7 %collective-permute-start.3 = (bf16[1152,512]{1,0:T(8,128)(2,1)}, bf16[1152,512]{1,0:T(8,128)(2,1)}, u32[]{:S(2)}, u32[]{:S(2)}) collective-permute-start(bf16[1152,512]{1,0:T(8,128)(2,1)} %get-tuple-element.40), channel_id=1, source_target_pairs={{12,4},{13,5},{14,6},{15,7},{28,20},{29,21},{30,22},{31,23}} | collective-permute-start | bytes 3538952 | tf_op jit(solution)/shard_map/ppermute | solution.py:618
  23.5 2.7 %collective-permute-start.9 = (bf16[768,512]{1,0:T(8,128)(2,1)}, bf16[768,512]{1,0:T(8,128)(2,1)}, u32[]{:S(2)}, u32[]{:S(2)}) collective-permute-start(bf16[768,512]{1,0:T(8,128)(2,1)} %get-tuple-element.54), channel_id=1, source_target_pairs={{0,8},{1,9},{2,10},{3,11},{16,24},{17,25},{18,26},{19,27}} | collective-permute-start | bytes 2359304 | tf_op jit(solution)/shard_map/ppermute | solution.py:618
  27.2 1.6 %collective-permute-start.6 = (f32[40,128]{0,1:T(8,128)S(1)}, f32[40,128]{0,1:T(8,128)S(1)}, u32[]{:S(2)}, u32[]{:S(2)}) collective-permute-start(f32[40,128]{0,1:T(8,128)S(1)} %copy.39), channel_id=1, source_target_pairs={{0,2},{2,0},{1,3},{3,1},{4,6},{6,4},{5,7},{7,5},{8,10},{10,8},{9,1... | collective-permute-start | bytes 61448 | tf_op jit(solution)/shard_map/ppermute | solution.py:766
  29.5 1.0 copy-done.3
  30.7 0.9 collective-permute-done.6
  31.5 1.3 %collective-permute-start.4 = (bf16[1152,256]{1,0:T(8,128)(2,1)}, bf16[1152,256]{1,0:T(8,128)(2,1)}, u32[]{:S(2)}, u32[]{:S(2)}) collective-permute-start(bf16[1152,256]{1,0:T(8,128)(2,1)} %get-tuple-element.45), channel_id=1, source_target_pairs={{8,12},{4,0},{9,13},{5,1},{10,14},{6,2},{11,15},{7,3},{24,28},{20,... | collective-permute-start | bytes 1769480 | tf_op jit(solution)/shard_map/ppermute | solution.py:618
  34.2 0.9 pad_maximum_fusion
  35.1 0.8 fusion.33.constants
  36.0 6.4 %collective-permute-start.8 = (bf16[768,256]{1,0:T(8,128)(2,1)}, bf16[768,256]{1,0:T(8,128)(2,1)}, u32[]{:S(2)}, u32[]{:S(2)}) collective-permute-start(bf16[768,256]{1,0:T(8,128)(2,1)} %get-tuple-element.53), channel_id=1, source_target_pairs={{0,12},{1,13},{2,14},{3,15},{16,28},{17,29},{18,30},{19,31}} | collective-permute-start | bytes 1179656 | tf_op jit(solution)/shard_map/ppermute | solution.py:618
  42.4 9.8 %collective-permute-done.9.refs_8_ = bf16[768,512]{1,0:T(8,128)(2,1)} collective-permute-done((bf16[768,512]{1,0:T(8,128)(2,1)}, bf16[768,512]{1,0:T(8,128)(2,1)}, u32[]{:S(2)}, u32[]{:S(2)}) %collective-permute-start.9) | collective-permute-done | bytes 786464 | tf_op jit(solution)/shard_map/ppermute | solution.py:618
  52.1 1.4 %collective-permute-start.7 = (bf16[768,256]{1,0:T(8,128)(2,1)}, bf16[768,256]{1,0:T(8,128)(2,1)}, u32[]{:S(2)}, u32[]{:S(2)}) collective-permute-start(bf16[768,256]{1,0:T(8,128)(2,1)} %get-tuple-element.53), channel_id=1, source_target_pairs={{4,12},{5,13},{6,14},{7,15},{20,28},{21,29},{22,30},{23,31}} | collective-permute-start | bytes 1179656 | tf_op jit(solution)/shard_map/ppermute | solution.py:618
  54.3 9.5 %main_heads.1 = (f32[3,40,384]{2,1,0:T(8,128)}, f32[3,40,384]{2,1,0:T(8,128)}) custom-call(s32[12]{0:T(128)S(1)} %bitcast_add_fusion.scalars, s32[16]{0:T(128)S(1)} %reshape.30.mask, bf16[384,2560]{1,0:T(8,128)(2,1)} %refs_6_.1, bf16[192,2560]{1,0:T(8,128)(2,1)} %refs_7_.1, bf16[192,2560]{1,0:T(8,128)(2,1)} %refs_8_.1, ...), custom_call_target="tpu_custom_call" | custom-call | flops 2113929216 | bytes 1179648 | tf_op jit(solution)/shard_map/main_heads/pallas_call | solution.py:582
  64.6 1.6 %reshape.33 = f32[80,128]{1,0:T(8,128)} reshape(f32[320,32]{1,0:T(8,128)} %slice.45) | data formatting | bytes 81920 | tf_op jit(solution)/shard_map/reshape | solution.py:711
  66.2 1.9 %collective-permute-start.10 = (f32[80,128]{1,0:T(8,128)}, f32[80,128]{1,0:T(8,128)}, u32[]{:S(2)}, u32[]{:S(2)}) collective-permute-start(f32[80,128]{1,0:T(8,128)} %reshape.33), channel_id=1, source_target_pairs={{0,4},{4,8},{8,12},{1,5},{5,9},{9,13},{2,6},{6,10},{10,14},{3,7},{... | collective-permute-start | bytes 122888 | tf_op jit(solution)/shard_map/ppermute | solution.py:46
  68.1 1.4 %collective-permute-done.10 = f32[80,128]{1,0:T(8,128)} collective-permute-done((f32[80,128]{1,0:T(8,128)}, f32[80,128]{1,0:T(8,128)}, u32[]{:S(2)}, u32[]{:S(2)}) %collective-permute-start.10) | collective-permute-done | bytes 40992 | tf_op jit(solution)/shard_map/ppermute | solution.py:46
  69.5 1.5 %reshape.34.before = f32[320,32]{1,0:T(8,128)} reshape(f32[80,128]{1,0:T(8,128)} %collective-permute-done.10) | data formatting | bytes 81920 | tf_op jit(solution)/shard_map/reshape | solution.py:711
  71.0 10.2 %final_heads.1 = (f32[3,40,384]{2,1,0:T(8,128)}, f32[3,40,384]{2,1,0:T(8,128)}) custom-call(s32[12]{0:T(128)S(1)} %bitcast_add_fusion.scalars, s32[16]{0:T(128)S(1)} %reshape.30.mask, bf16[384,2560]{1,0:T(8,128)(2,1)} %refs_6_.1, bf16[192,2560]{1,0:T(8,128)(2,1)} %refs_7_.1, ...), custom_call_target="tpu_custom_call", output_to_operand_aliasing={{0}: (20, {}), {1}: (21, {})} | custom-call | flops 4831838208 | bytes 1179648 | tf_op jit(solution)/shard_map/final_heads/pallas_call | solution.py:582
  81.4 1.6 %collective-permute-done.11 = f32[3,40,384]{2,1,0:T(8,128)S(1)} collective-permute-done((f32[3,40,384]{2,1,0:T(8,128)}, f32[3,40,384]{2,1,0:T(8,128)S(1)}, u32[]{:S(2)}, u32[]{:S(2)}) %collective-permute-start.11) | collective-permute-done | bytes 184352 | tf_op jit(solution)/shard_map/ppermute | solution.py:973
  83.0 0.9 add.84
  84.0 14.1 %collective-permute-start.13 = (f32[40,256]{1,0:T(8,128)S(1)}, f32[40,256]{1,0:T(8,128)S(1)}, u32[]{:S(2)}, u32[]{:S(2)}) collective-permute-start(f32[40,256]{1,0:T(8,128)S(1)} %slice.61), channel_id=1, source_target_pairs={{0,8},{4,12},{1,9},{5,13},{2,10},{6,14},{3,11},{7,15},{16,24},{20,... | collective-permute-start | bytes 122888 | tf_op jit(solution)/shard_map/ppermute | solution.py:980
  98.8 9.5 %collective-permute-start.12 = (f32[40,640]{1,0:T(8,128)S(1)}, f32[40,640]{1,0:T(8,128)S(1)}, u32[]{:S(2)}, u32[]{:S(2)}) collective-permute-start(f32[40,640]{1,0:T(8,128)S(1)} %pad_maximum_fusion.1), channel_id=1, source_target_pairs={{0,4},{4,8},{8,12},{1,5},{5,9},{9,13},{2,6},{6,10},{10,14},{3,7},{... | collective-permute-start | bytes 307208 | tf_op jit(solution)/shard_map/ppermute | solution.py:976
  108.3 2.2 %collective-permute-done.12 = f32[40,640]{1,0:T(8,128)S(1)} collective-permute-done((f32[40,640]{1,0:T(8,128)S(1)}, f32[40,640]{1,0:T(8,128)S(1)}, u32[]{:S(2)}, u32[]{:S(2)}) %collective-permute-start.12) | collective-permute-done | bytes 102432 | tf_op jit(solution)/shard_map/ppermute | solution.py:976
  110.5 1.5 %collective-permute-start.15 = (f32[40,640]{1,0:T(8,128)S(1)}, f32[40,640]{1,0:T(8,128)S(1)}, u32[]{:S(2)}, u32[]{:S(2)}) collective-permute-start(f32[40,640]{1,0:T(8,128)S(1)} %fusion.32), channel_id=1, source_target_pairs={{0,2},{2,0},{1,3},{3,1},{4,6},{6,4},{5,7},{7,5},{8,10},{10,8},{9,1... | collective-permute-start | bytes 307208 | tf_op jit(solution)/shard_map/ppermute | solution.py:983
  112.0 3.3 %collective-permute-done.15 = f32[40,640]{1,0:T(8,128)S(1)} collective-permute-done((f32[40,640]{1,0:T(8,128)S(1)}, f32[40,640]{1,0:T(8,128)S(1)}, u32[]{:S(2)}, u32[]{:S(2)}) %collective-permute-start.15) | collective-permute-done | bytes 102432 | tf_op jit(solution)/shard_map/ppermute | solution.py:983
  115.4 1.3 %collective-permute-done.16.other = f32[40,640]{1,0:T(8,128)S(1)} collective-permute-done((f32[40,640]{1,0:T(8,128)S(1)}, f32[40,640]{1,0:T(8,128)S(1)}, u32[]{:S(2)}, u32[]{:S(2)}) %collective-permute-start.16) | collective-permute-done | bytes 102432 | tf_op jit(solution)/shard_map/ppermute | solution.py:984
  116.7 2.4 %finish.1 = (f32[3,8,16,16]{3,2,1,0:T(8,128)}, bf16[3,8,16,384]{3,2,1,0:T(8,128)(2,1)}) custom-call(s32[12]{0:T(128)S(1)} %bitcast_add_fusion.scalars, f32[40,640]{1,0:T(8,128)S(1)} %add.87.mine, f32[40,640]{1,0:T(8,128)S(1)} %collective-permute-done.16.other, f32[320,48]{1,0:T(8,128)S(1)} %bitcast.33, f32[320,32]{1,0:T(8,128)S(1)} %copy-done.2, ...), custom_call_target="tpu_custom_call" | custom-call | tf_op jit(solution)/shard_map/finish/pallas_call | solution.py:896
  (67 shorter events, 8.0 us)
Async XLA Ops:
  0.6 28.2 %copy-start = (f32[384]{0:T(512)S(1)}, f32[384]{0:T(512)}, u32[]{:S(2)}) copy-start(f32[384]{0:T(512)} %param.21) | copy-start | bytes 4612
  4.1 2.9 %collective-permute-start = (bf16[384,1280]{1,0:T(8,128)(2,1)}, bf16[384,1280]{1,0:T(8,128)(2,1)S(1)}, u32[]{:S(2)}, u32[]{:S(2)}) collective-permute-start(bf16[384,1280]{1,0:T(8,128)(2,1)} %pack_handed.1), channel_id=1, source_target_pairs={{0,1},{1,0},{2,3},{3,2},{4,5},{5,4},{6,7},{7,6},{8,9},{9,8},{10,11... | collective-permute-start | bytes 2949128 | tf_op jit(solution)/shard_map/ppermute | solution.py:640
  10.1 44.3 %collective-permute-start.1 = (bf16[1152,512]{1,0:T(8,128)(2,1)}, bf16[1152,512]{1,0:T(8,128)(2,1)}, u32[]{:S(2)}, u32[]{:S(2)}) collective-permute-start(bf16[1152,512]{1,0:T(8,128)(2,1)} %get-tuple-element.38), channel_id=1, source_target_pairs={{4,0},{8,4},{12,8},{5,1},{9,5},{13,9},{6,2},{10,6},{14,10},{7,3},{... | collective-permute-start | bytes 3538952 | tf_op jit(solution)/shard_map/ppermute | solution.py:618
  11.4 11.7 %copy-start.5 = (f32[3,8,16,16]{3,2,1,0:T(8,128)S(1)}, f32[3,8,16,16]{3,2,1,0:T(8,128)}, u32[]{:S(2)}) copy-start(f32[3,8,16,16]{3,2,1,0:T(8,128)} %param.19) | copy-start | bytes 73732
  11.4 14.8 %copy-start.1 = (bf16[2560,64]{0,1:T(8,128)(2,1)S(1)}, bf16[2560,64]{0,1:T(8,128)(2,1)}, u32[]{:S(2)}) copy-start(bf16[2560,64]{0,1:T(8,128)(2,1)} %param.18) | copy-start | bytes 983044
  11.4 14.8 %copy-start.7 = (f32[2560]{0:T(1024)S(1)}, f32[2560]{0:T(1024)}, u32[]{:S(2)}) copy-start(f32[2560]{0:T(1024)} %param.16) | copy-start | bytes 30724
  11.4 14.8 %copy-start.10 = (f32[2560]{0:T(1024)S(1)}, f32[2560]{0:T(1024)}, u32[]{:S(2)}) copy-start(f32[2560]{0:T(1024)} %param.17) | copy-start | bytes 30724
  11.4 24.6 %collective-permute-start.2 = (bf16[768,512]{1,0:T(8,128)(2,1)}, bf16[768,512]{1,0:T(8,128)(2,1)}, u32[]{:S(2)}, u32[]{:S(2)}) collective-permute-start(bf16[768,512]{1,0:T(8,128)(2,1)} %get-tuple-element.44), channel_id=1, source_target_pairs={{0,4},{4,8},{1,5},{5,9},{2,6},{6,10},{3,7},{7,11},{16,20},{20,24},... | collective-permute-start | bytes 2359304 | tf_op jit(solution)/shard_map/ppermute | solution.py:618
  21.4 49.6 %collective-permute-start.3 = (bf16[1152,512]{1,0:T(8,128)(2,1)}, bf16[1152,512]{1,0:T(8,128)(2,1)}, u32[]{:S(2)}, u32[]{:S(2)}) collective-permute-start(bf16[1152,512]{1,0:T(8,128)(2,1)} %get-tuple-element.40), channel_id=1, source_target_pairs={{12,4},{13,5},{14,6},{15,7},{28,20},{29,21},{30,22},{31,23}} | collective-permute-start | bytes 3538952 | tf_op jit(solution)/shard_map/ppermute | solution.py:618
  23.4 3.1 %collective-permute-start.5 = (f32[8,48]{1,0:T(8,128)S(1)}, f32[8,48]{1,0:T(8,128)S(1)}, u32[]{:S(2)}, u32[]{:S(2)}) collective-permute-start(f32[8,48]{1,0:T(8,128)S(1)} %bitcast.43), channel_id=1, source_target_pairs={{0,1},{1,0},{2,3},{3,2},{4,5},{5,4},{6,7},{7,6},{8,9},{9,8},{10,11... | collective-permute-start | bytes 4616 | tf_op jit(solution)/shard_map/ppermute | solution.py:751
  23.5 28.6 %collective-permute-start.9 = (bf16[768,512]{1,0:T(8,128)(2,1)}, bf16[768,512]{1,0:T(8,128)(2,1)}, u32[]{:S(2)}, u32[]{:S(2)}) collective-permute-start(bf16[768,512]{1,0:T(8,128)(2,1)} %get-tuple-element.54), channel_id=1, source_target_pairs={{0,8},{1,9},{2,10},{3,11},{16,24},{17,25},{18,26},{19,27}} | collective-permute-start | bytes 2359304 | tf_op jit(solution)/shard_map/ppermute | solution.py:618
  26.5 0.6 copy-start.8
  26.5 0.6 copy-start.9
  27.1 1.7 %copy-start.4 = (f32[8,14,48]{2,1,0:T(8,128)}, f32[8,14,48]{2,1,0:T(8,128)S(1)}, u32[]{:S(2)}) copy-start(f32[8,14,48]{2,1,0:T(8,128)S(1)} %broadcast_in_dim.26) | copy-start | bytes 64516
  27.2 4.3 %collective-permute-start.6 = (f32[40,128]{0,1:T(8,128)S(1)}, f32[40,128]{0,1:T(8,128)S(1)}, u32[]{:S(2)}, u32[]{:S(2)}) collective-permute-start(f32[40,128]{0,1:T(8,128)S(1)} %copy.39), channel_id=1, source_target_pairs={{0,2},{2,0},{1,3},{3,1},{4,6},{6,4},{5,7},{7,5},{8,10},{10,8},{9,1... | collective-permute-start | bytes 61448 | tf_op jit(solution)/shard_map/ppermute | solution.py:766
  29.5 1.0 copy-start.3
  31.5 2.0 %copy-start.6 = (f32[40,128]{0,1:T(8,128)}, f32[40,128]{0,1:T(8,128)S(1)}, u32[]{:S(2)}) copy-start(f32[40,128]{0,1:T(8,128)S(1)} %collective-permute-done.6) | copy-start | bytes 61444
  31.5 39.5 %collective-permute-start.4 = (bf16[1152,256]{1,0:T(8,128)(2,1)}, bf16[1152,256]{1,0:T(8,128)(2,1)}, u32[]{:S(2)}, u32[]{:S(2)}) collective-permute-start(bf16[1152,256]{1,0:T(8,128)(2,1)} %get-tuple-element.45), channel_id=1, source_target_pairs={{8,12},{4,0},{9,13},{5,1},{10,14},{6,2},{11,15},{7,3},{24,28},{20,... | collective-permute-start | bytes 1769480 | tf_op jit(solution)/shard_map/ppermute | solution.py:618
  36.0 35.1 %collective-permute-start.8 = (bf16[768,256]{1,0:T(8,128)(2,1)}, bf16[768,256]{1,0:T(8,128)(2,1)}, u32[]{:S(2)}, u32[]{:S(2)}) collective-permute-start(bf16[768,256]{1,0:T(8,128)(2,1)} %get-tuple-element.53), channel_id=1, source_target_pairs={{0,12},{1,13},{2,14},{3,15},{16,28},{17,29},{18,30},{19,31}} | collective-permute-start | bytes 1179656 | tf_op jit(solution)/shard_map/ppermute | solution.py:618
  52.1 18.9 %collective-permute-start.7 = (bf16[768,256]{1,0:T(8,128)(2,1)}, bf16[768,256]{1,0:T(8,128)(2,1)}, u32[]{:S(2)}, u32[]{:S(2)}) collective-permute-start(bf16[768,256]{1,0:T(8,128)(2,1)} %get-tuple-element.53), channel_id=1, source_target_pairs={{4,12},{5,13},{6,14},{7,15},{20,28},{21,29},{22,30},{23,31}} | collective-permute-start | bytes 1179656 | tf_op jit(solution)/shard_map/ppermute | solution.py:618
  66.2 3.3 %collective-permute-start.10 = (f32[80,128]{1,0:T(8,128)}, f32[80,128]{1,0:T(8,128)}, u32[]{:S(2)}, u32[]{:S(2)}) collective-permute-start(f32[80,128]{1,0:T(8,128)} %reshape.33), channel_id=1, source_target_pairs={{0,4},{4,8},{8,12},{1,5},{5,9},{9,13},{2,6},{6,10},{10,14},{3,7},{... | collective-permute-start | bytes 122888 | tf_op jit(solution)/shard_map/ppermute | solution.py:46
  81.3 35.4 %copy-start.2 = (f32[320,32]{1,0:T(8,128)S(1)}, f32[320,32]{1,0:T(8,128)}, u32[]{:S(2)}) copy-start(f32[320,32]{1,0:T(8,128)} %reshape.34.before) | copy-start | bytes 122884
  81.3 1.7 %collective-permute-start.11 = (f32[3,40,384]{2,1,0:T(8,128)}, f32[3,40,384]{2,1,0:T(8,128)S(1)}, u32[]{:S(2)}, u32[]{:S(2)}) collective-permute-start(f32[3,40,384]{2,1,0:T(8,128)} %get-tuple-element.68), channel_id=1, source_target_pairs={{0,1},{1,0},{2,3},{3,2},{4,5},{5,4},{6,7},{7,6},{8,9},{9,8},{10,11... | collective-permute-start | bytes 552968 | tf_op jit(solution)/shard_map/ppermute | solution.py:973
  84.0 24.3 %collective-permute-start.13 = (f32[40,256]{1,0:T(8,128)S(1)}, f32[40,256]{1,0:T(8,128)S(1)}, u32[]{:S(2)}, u32[]{:S(2)}) collective-permute-start(f32[40,256]{1,0:T(8,128)S(1)} %slice.61), channel_id=1, source_target_pairs={{0,8},{4,12},{1,9},{5,13},{2,10},{6,14},{3,11},{7,15},{16,24},{20,... | collective-permute-start | bytes 122888 | tf_op jit(solution)/shard_map/ppermute | solution.py:980
  98.1 10.2 %collective-permute-start.14 = (f32[40,384]{1,0:T(8,128)S(1)}, f32[40,384]{1,0:T(8,128)S(1)}, u32[]{:S(2)}, u32[]{:S(2)}) collective-permute-start(f32[40,384]{1,0:T(8,128)S(1)} %get-tuple-element.76), channel_id=1, source_target_pairs={{4,12},{12,8},{5,13},{13,9},{6,14},{14,10},{7,15},{15,11},{20,28},... | collective-permute-start | bytes 184328 | tf_op jit(solution)/shard_map/ppermute | solution.py:979
  98.8 11.7 %collective-permute-start.12 = (f32[40,640]{1,0:T(8,128)S(1)}, f32[40,640]{1,0:T(8,128)S(1)}, u32[]{:S(2)}, u32[]{:S(2)}) collective-permute-start(f32[40,640]{1,0:T(8,128)S(1)} %pad_maximum_fusion.1), channel_id=1, source_target_pairs={{0,4},{4,8},{8,12},{1,5},{5,9},{9,13},{2,6},{6,10},{10,14},{3,7},{... | collective-permute-start | bytes 307208 | tf_op jit(solution)/shard_map/ppermute | solution.py:976
  110.5 4.7 %collective-permute-start.15 = (f32[40,640]{1,0:T(8,128)S(1)}, f32[40,640]{1,0:T(8,128)S(1)}, u32[]{:S(2)}, u32[]{:S(2)}) collective-permute-start(f32[40,640]{1,0:T(8,128)S(1)} %fusion.32), channel_id=1, source_target_pairs={{0,2},{2,0},{1,3},{3,1},{4,6},{6,4},{5,7},{7,5},{8,10},{10,8},{9,1... | collective-permute-start | bytes 307208 | tf_op jit(solution)/shard_map/ppermute | solution.py:983
  115.3 1.4 %collective-permute-start.16 = (f32[40,640]{1,0:T(8,128)S(1)}, f32[40,640]{1,0:T(8,128)S(1)}, u32[]{:S(2)}, u32[]{:S(2)}) collective-permute-start(f32[40,640]{1,0:T(8,128)S(1)} %add.87.mine), channel_id=1, source_target_pairs={{0,1},{1,0},{2,3},{3,2},{4,5},{5,4},{6,7},{7,6},{8,9},{9,8},{10,11... | collective-permute-start | bytes 307208 | tf_op jit(solution)/shard_map/ppermute | solution.py:984

commit v10 on v9

--- a/solution.py
+++ b/solution.py
@@ -252,55 +252,39 @@
     return row + lax.axis_index("slab") * jnp.array(by_slab)
 
 
-def pack_kernel(inputs, messages, copies, with_noise, scalars, *refs):
+def pack_kernel(inputs, messages, copies, scalars, *refs):
     ins, rest = refs[:inputs], refs[inputs:]
-    outs = rest[: messages + with_noise]
-    staged = rest[messages + with_noise : -2]
+    outs, staged = rest[:messages], rest[messages:-2]
     arrive, leave = rest[-2:]
-    arriving = [[] for _ in range(messages)]
+    arriving = []
     for number, (source, row, rows, entries, shift, target, at, heads) in enumerate(copies):
         head = shift
         for entry in entries:
             head = head + scalars[entry]
         column = pl.multiple_of(head * HD, HD)
+        place = staged[target].at[pl.ds(at, rows), :]
         copy = pltpu.make_async_copy(
-            ins[source].at[pl.ds(row, rows), pl.ds(column, heads * HD)],
-            staged[target].at[pl.ds(at, rows), :],
-            arrive.at[number],
+            ins[source].at[pl.ds(row, rows), pl.ds(column, heads * HD)], place, arrive.at[number]
         )
         copy.start()
-        arriving[target].append(copy)
-    if with_noise:
-        noisy, out = ins[-1], outs[-1]
-        frames = noisy.shape[0]
-        out[...] = jnp.concatenate([noisy[frame] for frame in range(frames)], axis=-1)
-    leaving = []
-    for target in range(messages):
-        for copy in arriving[target]:
-            copy.wait()
-        copy = pltpu.make_async_copy(staged[target], outs[target], leave.at[target])
-        copy.start()
-        leaving.append(copy)
-    for copy in leaving:
+        onward = pltpu.make_async_copy(
+            place, outs[target].at[pl.ds(at, rows), :], leave.at[number]
+        )
+        arriving.append((copy, onward))
+    for copy, onward in arriving:
         copy.wait()
-
-
-def pack(scalars, arrays, shapes, copies, name, noisy=None):
+        onward.start()
+    for _, onward in arriving:
+        onward.wait()
+
+
+def pack(scalars, arrays, shapes, copies, name):
     moved = sum(2 * 2 * rows * heads * HD for _, _, rows, _, _, _, _, heads in copies)
     out_shape = [pltpu.HBM(shape, jnp.bfloat16) for shape in shapes]
     in_specs = [pl.BlockSpec(memory_space=pl.ANY)] * len(arrays)
     out_specs = [pl.BlockSpec(memory_space=pl.ANY)] * len(shapes)
-    if noisy is not None:
-        frames, height, breadth, channels = noisy.shape
-        lanes = frames * channels
-        arrays = arrays + (noisy,)
-        in_specs.append(pl.BlockSpec(noisy.shape, lambda i, scalars: (0, 0, 0, 0)))
-        out_shape.append(jax.ShapeDtypeStruct((height, breadth, lanes), noisy.dtype))
-        out_specs.append(pl.BlockSpec((height, breadth, lanes), lambda i, scalars: (0, 0, 0)))
     return pl.pallas_call(
-        functools.partial(
-            pack_kernel, len(arrays), len(shapes), copies, noisy is not None
-        ),
+        functools.partial(pack_kernel, len(arrays), len(shapes), copies),
         name=name,
         out_shape=out_shape,
         grid_spec=pltpu.PrefetchScalarGridSpec(
@@ -311,7 +295,7 @@
             scratch_shapes=[pltpu.VMEM(shape, jnp.bfloat16) for shape in shapes]
             + [
                 pltpu.SemaphoreType.DMA((len(copies),)),
-                pltpu.SemaphoreType.DMA((len(shapes),)),
+                pltpu.SemaphoreType.DMA((len(copies),)),
             ],
         ),
         compiler_params=pltpu.CompilerParams(vmem_limit_bytes=GRANT),
@@ -319,7 +303,7 @@
     )(scalars, *arrays)
 
 
-def message(scalars, pieces, arrays, name, noisy=None):
+def message(scalars, pieces, arrays, name):
     copies, shapes = [], []
     for target, parts in enumerate(pieces):
         at = 0
@@ -327,7 +311,7 @@
             copies.append((source, row, rows, entries, shift, target, at, heads))
             at += rows
         shapes.append((at, parts[0][5] * HD))
-    return pack(scalars, arrays, shapes, copies, name, noisy)
+    return pack(scalars, arrays, shapes, copies, name)
 
 
 class Tokens(typing.NamedTuple):
@@ -633,7 +617,13 @@
 
     (handed,) = message(
         scalars,
-        [[(part, 0, half, (OTHER,), 0, heads) for part in (1, 2)]],
+        [
+            [
+                (part, row, half // 2, (OTHER,), 0, heads)
+                for part in (1, 2)
+                for row in (0, half // 2)
+            ]
+        ],
         (queries, keys, values),
         "pack_handed",
     )
@@ -705,14 +695,10 @@
         more=False,
         name="main_heads",
     )
-    noise, *prepared = prepared
-    sums, noise = lax.optimization_barrier((sums, noise))
-    lanes = 2 * LAT_CH
-    before = from_behind(noise[:, -lanes:].reshape(-1, HD), "span", 1).reshape(-1, lanes)
     on_two, beside = Tokens(2, (2,)), Tokens(3, (3,))
     two_back, three_back = Tokens(None, (4,)), Tokens(None, (5,))
     extras = [Tokens(None, (), lane) for lane in range(2)]
-    sums, before, prepared = lax.optimization_barrier((sums, before, prepared))
+    sums, prepared = lax.optimization_barrier((sums, prepared))
     sums = run(
         NEAR_HEADS,
         FINAL,
@@ -741,7 +727,7 @@
         name="final_heads",
         cost=4,
     )
-    return sums, (noise, before, *prepared)
+    return sums, prepared
 
 
 def noise_window(grid, constants):
@@ -954,13 +940,14 @@
         window, constants = noise_window(noise, constants)
         return (
             window,
+            window[:, -2 * LAT_CH :].reshape(16, -1),
             constants,
             cell_selector(height, breadth),
             banded_weight(taps),
             jnp.tile(bias, FRAMES_SPAN)[None, :],
         )
 
-    (mine, theirs), (noise, before, constants, selector, band, bias) = token_sums(
+    (mine, theirs), (noise, ahead, constants, selector, band, bias) = token_sums(
         scalars,
         queries,
         keys,
@@ -974,8 +961,12 @@
     own, after, third = mine[0], mine[1], mine[2]
     skip = TROWS * TCOLS
     from_one = lax.ppermute(
-        jnp.concatenate([own[:, skip:], after], axis=1), "span", [(0, 1), (1, 2), (2, 3)]
-    )
+        jnp.concatenate([jnp.concatenate([own[:, skip:], after], axis=1), ahead], axis=0),
+        "span",
+        [(0, 1), (1, 2), (2, 3)],
+    )
+    before = from_one[own.shape[0] :].reshape(-1, 2 * LAT_CH)
+    from_one = from_one[: own.shape[0]]
     to_current = lax.ppermute(third, "span", [(1, 3), (3, 2)])
     to_before = lax.ppermute(after[:, skip:], "span", [(0, 2), (1, 3)])
     kept = jnp.concatenate([jnp.where(place == 3, third[:, skip:], 0.0), own], axis=1)

time: 120 us -> 103 us (0.86)
  starting transfers between devices: 51.3 us -> 38.3 us
  local copies, waits for them, and re-layouts: 8.76 us -> 6.85 us
  waiting for transfers between devices: 22.1 us -> 20.3 us
    ppermute x2 -> x1, starting transfers between devices: 11.4 us -> 1.37 us  [per_device(): lax.ppermute(jnp.concatenate([jnp.concatenate([own[:, skip:], after], axi...]
    ppermute x1, starting transfers between devices: 14.1 us -> 11.2 us  [per_device(): to_before = lax.ppermute(after[:, skip:], 'span', [(0, 2), (1, 3)])]
    reshape x2, local copies, waits for them, and re-layouts: 3.16 us -> 1.11 us  [the longest x1 1.01 us: prepare(): window[:, -2 * LAT_CH:].reshape(16, -1)]
    ppermute x7, waiting for transfers between devices: 9.77 us -> 8.53 us  [send(): return in_place(lax.ppermute(value, 'span', list(pairs)))]
    ppermute x2 -> x1, waiting for transfers between devices: 3.56 us -> 3.19 us  [per_device(): lax.ppermute(jnp.concatenate([jnp.concatenate([own[:, skip:], after], axi...]
  transfers between devices with their start and end apart: 17 -> 16, of which waited for: 8 -> 7; matrix products, arithmetic and copies ran while one was open for 8% -> 8% of each run, Pallas kernels for 11% -> 13%
where the time goes in v10:
time: 103 us; the launch traced here: 102 us
  starting transfers between devices  38.3 us (37%)
  Pallas kernels  31.3 us (30%)
  waiting for transfers between devices  20.3 us (20%)
  local copies, waits for them, and re-layouts  6.85 us (7%)
  other arithmetic  4.49 us (4%)
    ppermute x7, starting transfers between devices, send(): return in_place(lax.ppermute(value, 'span', list(pairs)))  21.3 us
    pallas_call x2, Pallas kernels, attend(): pl.pallas_call(functools.partial(attend_kernel, variants, extra, span_cou...  19.7 us
    ppermute x1, starting transfers between devices, per_device(): to_before = lax.ppermute(after[:, skip:], 'span', [(0, 2), (1, 3)])  11.2 us
    pallas_call x3, Pallas kernels, pack(): pl.pallas_call(functools.partial(pack_kernel, len(arrays), len(shapes), c...  9.05 us
    ppermute x7, waiting for transfers between devices, send(): return in_place(lax.ppermute(value, 'span', list(pairs)))  8.53 us
    ppermute x1, waiting for transfers between devices, per_device(): total = total + lax.ppermute(total, 'head', SWAP)  3.27 us
    ppermute x1, waiting for transfers between devices, per_device(): lax.ppermute(jnp.concatenate([jnp.concatenate([own[:, skip:], after], axi...  3.19 us
    pallas_call x1, Pallas kernels, finish(): pl.pallas_call(finish_kernel, name='finish', out_shape=(jax.ShapeDtypeStr...  2.4 us
  transfers between devices with their start and end apart: 16, of which 7 were waited for; matrix products, arithmetic and copies ran while one was open for 8% of the time, Pallas kernels for 13%

profile of v10, /device:TPU:0, one launch (start us, length us, event | category | flops | bytes accessed | tf_op | source)
XLA Modules:
  0.0 102.3 jit_solution(6007388987938931419)
XLA Ops:
  1.4 2.6 %pack_handed.1 = bf16[384,1280]{1,0:T(8,128)(2,1)} custom-call(s32[12]{0:T(128)S(1)} %bitcast_add_fusion.scalars, bf16[384,2560]{1,0:T(8,128)(2,1)} %refs_6_.1, bf16[192,2560]{1,0:T(8,128)(2,1)} %refs_7_.1, bf16[192,2560]{1,0:T(8,128)(2,1)} %refs_8_.1), custom_call_target="tpu_custom_call" | custom-call | bytes 1966080 | tf_op jit(solution)/shard_map/pack_handed/pallas_call | solution.py:286
  4.5 0.7 fusion.30.selector
  5.3 1.7 %collective-permute-done.refs_3_.refs_9_ = bf16[384,1280]{1,0:T(8,128)(2,1)S(1)} collective-permute-done((bf16[384,1280]{1,0:T(8,128)(2,1)}, bf16[384,1280]{1,0:T(8,128)(2,1)S(1)}, u32[]{:S(2)}, u32[]{:S(2)}) %collective-permute-start) | collective-permute-done | bytes 983072 | tf_op jit(solution)/shard_map/ppermute | solution.py:630
  6.9 2.9 %pack_first.1 = (bf16[1152,512]{1,0:T(8,128)(2,1)}, bf16[768,512]{1,0:T(8,128)(2,1)}) custom-call(s32[12]{0:T(128)S(1)} %bitcast_add_fusion.scalars, bf16[384,2560]{1,0:T(8,128)(2,1)} %refs_6_.1, bf16[192,2560]{1,0:T(8,128)(2,1)} %refs_7_.1, bf16[192,2560]{1,0:T(8,128)(2,1)} %refs_8_.1, bf16[384,1280]{1,0:T(8,128)(2,1)S(1)} %collective-permute-done.refs_3_.refs_9_), custom_call_target="tpu_custom_call" | custom-call | bytes 3932160 | tf_op jit(solution)/shard_map/pack_first/pallas_call | solution.py:286
  9.9 1.3 %collective-permute-start.1 = (bf16[1152,512]{1,0:T(8,128)(2,1)}, bf16[1152,512]{1,0:T(8,128)(2,1)}, u32[]{:S(2)}, u32[]{:S(2)}) collective-permute-start(bf16[1152,512]{1,0:T(8,128)(2,1)} %get-tuple-element.37), channel_id=1, source_target_pairs={{4,0},{8,4},{12,8},{5,1},{9,5},{13,9},{6,2},{10,6},{14,10},{7,3},{... | collective-permute-start | bytes 3538952 | tf_op jit(solution)/shard_map/ppermute | solution.py:602
  11.2 6.5 %collective-permute-start.2 = (bf16[768,512]{1,0:T(8,128)(2,1)}, bf16[768,512]{1,0:T(8,128)(2,1)}, u32[]{:S(2)}, u32[]{:S(2)}) collective-permute-start(bf16[768,512]{1,0:T(8,128)(2,1)} %get-tuple-element.43), channel_id=1, source_target_pairs={{0,4},{4,8},{1,5},{5,9},{2,6},{6,10},{3,7},{7,11},{16,20},{20,24},... | collective-permute-start | bytes 2359304 | tf_op jit(solution)/shard_map/ppermute | solution.py:602
  17.8 3.5 %pack_second.1 = (bf16[768,512]{1,0:T(8,128)(2,1)}, bf16[1152,512]{1,0:T(8,128)(2,1)}, bf16[1152,256]{1,0:T(8,128)(2,1)}, bf16[768,256]{1,0:T(8,128)(2,1)}) custom-call(s32[12]{0:T(128)S(1)} %bitcast_add_fusion.scalars, bf16[384,2560]{1,0:T(8,128)(2,1)} %refs_6_.1, bf16[192,2560]{1,0:T(8,128)(2,1)} %refs_7_.1, bf16[192,2560]{1,0:T(8,128)(2,1)} %refs_8_.1, ...), custom_call_target="tpu_custom_call" | custom-call | bytes 5898240 | tf_op jit(solution)/shard_map/pack_second/pallas_call | solution.py:286
  21.2 1.7 %collective-permute-start.3 = (bf16[1152,512]{1,0:T(8,128)(2,1)}, bf16[1152,512]{1,0:T(8,128)(2,1)}, u32[]{:S(2)}, u32[]{:S(2)}) collective-permute-start(bf16[1152,512]{1,0:T(8,128)(2,1)} %get-tuple-element.39), channel_id=1, source_target_pairs={{12,4},{13,5},{14,6},{15,7},{28,20},{29,21},{30,22},{31,23}} | collective-permute-start | bytes 3538952 | tf_op jit(solution)/shard_map/ppermute | solution.py:602
  23.3 2.7 %collective-permute-start.9 = (bf16[768,512]{1,0:T(8,128)(2,1)}, bf16[768,512]{1,0:T(8,128)(2,1)}, u32[]{:S(2)}, u32[]{:S(2)}) collective-permute-start(bf16[768,512]{1,0:T(8,128)(2,1)} %get-tuple-element.53), channel_id=1, source_target_pairs={{0,8},{1,9},{2,10},{3,11},{16,24},{17,25},{18,26},{19,27}} | collective-permute-start | bytes 2359304 | tf_op jit(solution)/shard_map/ppermute | solution.py:602
  26.5 1.6 %collective-permute-start.6 = (f32[40,128]{0,1:T(8,128)S(1)}, f32[40,128]{0,1:T(8,128)S(1)}, u32[]{:S(2)}, u32[]{:S(2)}) collective-permute-start(f32[40,128]{0,1:T(8,128)S(1)} %copy.39), channel_id=1, source_target_pairs={{0,2},{2,0},{1,3},{3,1},{4,6},{6,4},{5,7},{7,5},{8,10},{10,8},{9,1... | collective-permute-start | bytes 61448 | tf_op jit(solution)/shard_map/ppermute | solution.py:752
  28.8 1.0 copy-done.2
  29.9 0.9 collective-permute-done.6
  30.8 1.3 %collective-permute-start.4 = (bf16[1152,256]{1,0:T(8,128)(2,1)}, bf16[1152,256]{1,0:T(8,128)(2,1)}, u32[]{:S(2)}, u32[]{:S(2)}) collective-permute-start(bf16[1152,256]{1,0:T(8,128)(2,1)} %get-tuple-element.44), channel_id=1, source_target_pairs={{8,12},{4,0},{9,13},{5,1},{10,14},{6,2},{11,15},{7,3},{24,28},{20,... | collective-permute-start | bytes 1769480 | tf_op jit(solution)/shard_map/ppermute | solution.py:602
  33.5 0.9 pad_maximum_fusion
  34.4 0.8 slice.63
  35.1 1.0 reshape.33
  36.2 0.8 fusion.33.constants
  37.0 6.4 %collective-permute-start.8 = (bf16[768,256]{1,0:T(8,128)(2,1)}, bf16[768,256]{1,0:T(8,128)(2,1)}, u32[]{:S(2)}, u32[]{:S(2)}) collective-permute-start(bf16[768,256]{1,0:T(8,128)(2,1)} %get-tuple-element.52), channel_id=1, source_target_pairs={{0,12},{1,13},{2,14},{3,15},{16,28},{17,29},{18,30},{19,31}} | collective-permute-start | bytes 1179656 | tf_op jit(solution)/shard_map/ppermute | solution.py:602
  43.4 8.5 %collective-permute-done.9.refs_8_ = bf16[768,512]{1,0:T(8,128)(2,1)} collective-permute-done((bf16[768,512]{1,0:T(8,128)(2,1)}, bf16[768,512]{1,0:T(8,128)(2,1)}, u32[]{:S(2)}, u32[]{:S(2)}) %collective-permute-start.9) | collective-permute-done | bytes 786464 | tf_op jit(solution)/shard_map/ppermute | solution.py:602
  51.9 1.4 %collective-permute-start.7 = (bf16[768,256]{1,0:T(8,128)(2,1)}, bf16[768,256]{1,0:T(8,128)(2,1)}, u32[]{:S(2)}, u32[]{:S(2)}) collective-permute-start(bf16[768,256]{1,0:T(8,128)(2,1)} %get-tuple-element.52), channel_id=1, source_target_pairs={{4,12},{5,13},{6,14},{7,15},{20,28},{21,29},{22,30},{23,31}} | collective-permute-start | bytes 1179656 | tf_op jit(solution)/shard_map/ppermute | solution.py:602
  53.3 0.8 reshape.30.mask
  54.8 9.5 %main_heads.1 = (f32[3,40,384]{2,1,0:T(8,128)}, f32[3,40,384]{2,1,0:T(8,128)}) custom-call(s32[12]{0:T(128)S(1)} %bitcast_add_fusion.scalars, s32[16]{0:T(128)S(1)} %reshape.30.mask, bf16[384,2560]{1,0:T(8,128)(2,1)} %refs_6_.1, bf16[192,2560]{1,0:T(8,128)(2,1)} %refs_7_.1, bf16[192,2560]{1,0:T(8,128)(2,1)} %refs_8_.1, ...), custom_call_target="tpu_custom_call" | custom-call | flops 2113929216 | bytes 1179648 | tf_op jit(solution)/shard_map/main_heads/pallas_call | solution.py:566
  64.4 10.2 %final_heads.1 = (f32[3,40,384]{2,1,0:T(8,128)}, f32[3,40,384]{2,1,0:T(8,128)}) custom-call(s32[12]{0:T(128)S(1)} %bitcast_add_fusion.scalars, s32[16]{0:T(128)S(1)} %reshape.30.mask, bf16[384,2560]{1,0:T(8,128)(2,1)} %refs_6_.1, bf16[192,2560]{1,0:T(8,128)(2,1)} %refs_7_.1, ...), custom_call_target="tpu_custom_call", output_to_operand_aliasing={{0}: (20, {}), {1}: (21, {})} | custom-call | flops 4831838208 | bytes 1179648 | tf_op jit(solution)/shard_map/final_heads/pallas_call | solution.py:566
  74.7 1.6 %collective-permute-done.10 = f32[3,40,384]{2,1,0:T(8,128)S(1)} collective-permute-done((f32[3,40,384]{2,1,0:T(8,128)}, f32[3,40,384]{2,1,0:T(8,128)S(1)}, u32[]{:S(2)}, u32[]{:S(2)}) %collective-permute-start.10) | collective-permute-done | bytes 184352 | tf_op jit(solution)/shard_map/ppermute | solution.py:960
  76.3 1.0 add.84
  77.3 11.2 %collective-permute-start.12 = (f32[40,256]{1,0:T(8,128)S(1)}, f32[40,256]{1,0:T(8,128)S(1)}, u32[]{:S(2)}, u32[]{:S(2)}) collective-permute-start(f32[40,256]{1,0:T(8,128)S(1)} %slice.71), channel_id=1, source_target_pairs={{0,8},{4,12},{1,9},{5,13},{2,10},{6,14},{3,11},{7,15},{16,24},{20,... | collective-permute-start | bytes 122888 | tf_op jit(solution)/shard_map/ppermute | solution.py:971
  89.2 1.4 %collective-permute-start.11 = (f32[56,640]{1,0:T(8,128)S(1)}, f32[56,640]{1,0:T(8,128)S(1)}, u32[]{:S(2)}, u32[]{:S(2)}) collective-permute-start(f32[56,640]{1,0:T(8,128)S(1)} %pad_maximum_fusion.1), channel_id=1, source_target_pairs={{0,4},{4,8},{8,12},{1,5},{5,9},{9,13},{2,6},{6,10},{10,14},{3,7},{... | collective-permute-start | bytes 430088 | tf_op jit(solution)/shard_map/ppermute | solution.py:963
  90.6 3.2 %collective-permute-done.11 = f32[56,640]{1,0:T(8,128)S(1)} collective-permute-done((f32[56,640]{1,0:T(8,128)S(1)}, f32[56,640]{1,0:T(8,128)S(1)}, u32[]{:S(2)}, u32[]{:S(2)}) %collective-permute-start.11) | collective-permute-done | bytes 143392 | tf_op jit(solution)/shard_map/ppermute | solution.py:963
  93.8 1.5 %collective-permute-start.14 = (f32[40,640]{1,0:T(8,128)S(1)}, f32[40,640]{1,0:T(8,128)S(1)}, u32[]{:S(2)}, u32[]{:S(2)}) collective-permute-start(f32[40,640]{1,0:T(8,128)S(1)} %fusion.32), channel_id=1, source_target_pairs={{0,2},{2,0},{1,3},{3,1},{4,6},{6,4},{5,7},{7,5},{8,10},{10,8},{9,1... | collective-permute-start | bytes 307208 | tf_op jit(solution)/shard_map/ppermute | solution.py:974
  95.2 3.3 %collective-permute-done.14 = f32[40,640]{1,0:T(8,128)S(1)} collective-permute-done((f32[40,640]{1,0:T(8,128)S(1)}, f32[40,640]{1,0:T(8,128)S(1)}, u32[]{:S(2)}, u32[]{:S(2)}) %collective-permute-start.14) | collective-permute-done | bytes 102432 | tf_op jit(solution)/shard_map/ppermute | solution.py:974
  98.7 1.2 %collective-permute-done.15.other = f32[40,640]{1,0:T(8,128)S(1)} collective-permute-done((f32[40,640]{1,0:T(8,128)S(1)}, f32[40,640]{1,0:T(8,128)S(1)}, u32[]{:S(2)}, u32[]{:S(2)}) %collective-permute-start.15) | collective-permute-done | bytes 102432 | tf_op jit(solution)/shard_map/ppermute | solution.py:975
  99.9 2.4 %finish.1 = (f32[3,8,16,16]{3,2,1,0:T(8,128)}, bf16[3,8,16,384]{3,2,1,0:T(8,128)(2,1)}) custom-call(s32[12]{0:T(128)S(1)} %bitcast_add_fusion.scalars, f32[40,640]{1,0:T(8,128)S(1)} %add.87.mine, f32[40,640]{1,0:T(8,128)S(1)} %collective-permute-done.15.other, f32[320,48]{1,0:T(8,128)S(1)} %bitcast.33, f32[320,32]{1,0:T(8,128)S(1)} %reshape.34.before, ...), custom_call_target="tpu_custom_call" | custom-call | tf_op jit(solution)/shard_map/finish/pallas_call | solution.py:882
  (60 shorter events, 6.0 us)
Async XLA Ops:
  0.6 27.4 %copy-start = (f32[384]{0:T(512)S(1)}, f32[384]{0:T(512)}, u32[]{:S(2)}) copy-start(f32[384]{0:T(512)} %param.21) | copy-start | bytes 4612
  4.0 2.9 %collective-permute-start = (bf16[384,1280]{1,0:T(8,128)(2,1)}, bf16[384,1280]{1,0:T(8,128)(2,1)S(1)}, u32[]{:S(2)}, u32[]{:S(2)}) collective-permute-start(bf16[384,1280]{1,0:T(8,128)(2,1)} %pack_handed.1), channel_id=1, source_target_pairs={{0,1},{1,0},{2,3},{3,2},{4,5},{5,4},{6,7},{7,6},{8,9},{9,8},{10,11... | collective-permute-start | bytes 2949128 | tf_op jit(solution)/shard_map/ppermute | solution.py:630
  9.9 44.9 %collective-permute-start.1 = (bf16[1152,512]{1,0:T(8,128)(2,1)}, bf16[1152,512]{1,0:T(8,128)(2,1)}, u32[]{:S(2)}, u32[]{:S(2)}) collective-permute-start(bf16[1152,512]{1,0:T(8,128)(2,1)} %get-tuple-element.37), channel_id=1, source_target_pairs={{4,0},{8,4},{12,8},{5,1},{9,5},{13,9},{6,2},{10,6},{14,10},{7,3},{... | collective-permute-start | bytes 3538952 | tf_op jit(solution)/shard_map/ppermute | solution.py:602
  11.2 11.8 %copy-start.4 = (f32[3,8,16,16]{3,2,1,0:T(8,128)S(1)}, f32[3,8,16,16]{3,2,1,0:T(8,128)}, u32[]{:S(2)}) copy-start(f32[3,8,16,16]{3,2,1,0:T(8,128)} %param.19) | copy-start | bytes 73732
  11.2 14.9 %copy-start.1 = (bf16[2560,64]{0,1:T(8,128)(2,1)S(1)}, bf16[2560,64]{0,1:T(8,128)(2,1)}, u32[]{:S(2)}) copy-start(bf16[2560,64]{0,1:T(8,128)(2,1)} %param.18) | copy-start | bytes 983044
  11.2 14.8 %copy-start.6 = (f32[2560]{0:T(1024)S(1)}, f32[2560]{0:T(1024)}, u32[]{:S(2)}) copy-start(f32[2560]{0:T(1024)} %param.16) | copy-start | bytes 30724
  11.2 14.8 %copy-start.7 = (f32[2560]{0:T(1024)S(1)}, f32[2560]{0:T(1024)}, u32[]{:S(2)}) copy-start(f32[2560]{0:T(1024)} %param.17) | copy-start | bytes 30724
  11.2 25.8 %collective-permute-start.2 = (bf16[768,512]{1,0:T(8,128)(2,1)}, bf16[768,512]{1,0:T(8,128)(2,1)}, u32[]{:S(2)}, u32[]{:S(2)}) collective-permute-start(bf16[768,512]{1,0:T(8,128)(2,1)} %get-tuple-element.43), channel_id=1, source_target_pairs={{0,4},{4,8},{1,5},{5,9},{2,6},{6,10},{3,7},{7,11},{16,20},{20,24},... | collective-permute-start | bytes 2359304 | tf_op jit(solution)/shard_map/ppermute | solution.py:602
  21.2 43.1 %collective-permute-start.3 = (bf16[1152,512]{1,0:T(8,128)(2,1)}, bf16[1152,512]{1,0:T(8,128)(2,1)}, u32[]{:S(2)}, u32[]{:S(2)}) collective-permute-start(bf16[1152,512]{1,0:T(8,128)(2,1)} %get-tuple-element.39), channel_id=1, source_target_pairs={{12,4},{13,5},{14,6},{15,7},{28,20},{29,21},{30,22},{31,23}} | collective-permute-start | bytes 3538952 | tf_op jit(solution)/shard_map/ppermute | solution.py:602
  23.2 3.1 %collective-permute-start.5 = (f32[8,48]{1,0:T(8,128)S(1)}, f32[8,48]{1,0:T(8,128)S(1)}, u32[]{:S(2)}, u32[]{:S(2)}) collective-permute-start(f32[8,48]{1,0:T(8,128)S(1)} %bitcast.43), channel_id=1, source_target_pairs={{0,1},{1,0},{2,3},{3,2},{4,5},{5,4},{6,7},{7,6},{8,9},{9,8},{10,11... | collective-permute-start | bytes 4616 | tf_op jit(solution)/shard_map/ppermute | solution.py:737
  23.3 28.6 %collective-permute-start.9 = (bf16[768,512]{1,0:T(8,128)(2,1)}, bf16[768,512]{1,0:T(8,128)(2,1)}, u32[]{:S(2)}, u32[]{:S(2)}) collective-permute-start(bf16[768,512]{1,0:T(8,128)(2,1)} %get-tuple-element.53), channel_id=1, source_target_pairs={{0,8},{1,9},{2,10},{3,11},{16,24},{17,25},{18,26},{19,27}} | collective-permute-start | bytes 2359304 | tf_op jit(solution)/shard_map/ppermute | solution.py:602
  26.3 1.7 %copy-start.3 = (f32[8,14,48]{2,1,0:T(8,128)}, f32[8,14,48]{2,1,0:T(8,128)S(1)}, u32[]{:S(2)}) copy-start(f32[8,14,48]{2,1,0:T(8,128)S(1)} %broadcast_in_dim.26) | copy-start | bytes 64516
  26.5 4.3 %collective-permute-start.6 = (f32[40,128]{0,1:T(8,128)S(1)}, f32[40,128]{0,1:T(8,128)S(1)}, u32[]{:S(2)}, u32[]{:S(2)}) collective-permute-start(f32[40,128]{0,1:T(8,128)S(1)} %copy.39), channel_id=1, source_target_pairs={{0,2},{2,0},{1,3},{3,1},{4,6},{6,4},{5,7},{7,5},{8,10},{10,8},{9,1... | collective-permute-start | bytes 61448 | tf_op jit(solution)/shard_map/ppermute | solution.py:752
  28.8 1.0 copy-start.2
  30.8 2.0 %copy-start.5 = (f32[40,128]{0,1:T(8,128)}, f32[40,128]{0,1:T(8,128)S(1)}, u32[]{:S(2)}) copy-start(f32[40,128]{0,1:T(8,128)S(1)} %collective-permute-done.6) | copy-start | bytes 61444
  30.8 33.5 %collective-permute-start.4 = (bf16[1152,256]{1,0:T(8,128)(2,1)}, bf16[1152,256]{1,0:T(8,128)(2,1)}, u32[]{:S(2)}, u32[]{:S(2)}) collective-permute-start(bf16[1152,256]{1,0:T(8,128)(2,1)} %get-tuple-element.44), channel_id=1, source_target_pairs={{8,12},{4,0},{9,13},{5,1},{10,14},{6,2},{11,15},{7,3},{24,28},{20,... | collective-permute-start | bytes 1769480 | tf_op jit(solution)/shard_map/ppermute | solution.py:602
  37.0 27.3 %collective-permute-start.8 = (bf16[768,256]{1,0:T(8,128)(2,1)}, bf16[768,256]{1,0:T(8,128)(2,1)}, u32[]{:S(2)}, u32[]{:S(2)}) collective-permute-start(bf16[768,256]{1,0:T(8,128)(2,1)} %get-tuple-element.52), channel_id=1, source_target_pairs={{0,12},{1,13},{2,14},{3,15},{16,28},{17,29},{18,30},{19,31}} | collective-permute-start | bytes 1179656 | tf_op jit(solution)/shard_map/ppermute | solution.py:602
  51.9 12.4 %collective-permute-start.7 = (bf16[768,256]{1,0:T(8,128)(2,1)}, bf16[768,256]{1,0:T(8,128)(2,1)}, u32[]{:S(2)}, u32[]{:S(2)}) collective-permute-start(bf16[768,256]{1,0:T(8,128)(2,1)} %get-tuple-element.52), channel_id=1, source_target_pairs={{4,12},{5,13},{6,14},{7,15},{20,28},{21,29},{22,30},{23,31}} | collective-permute-start | bytes 1179656 | tf_op jit(solution)/shard_map/ppermute | solution.py:602
  74.6 1.7 %collective-permute-start.10 = (f32[3,40,384]{2,1,0:T(8,128)}, f32[3,40,384]{2,1,0:T(8,128)S(1)}, u32[]{:S(2)}, u32[]{:S(2)}) collective-permute-start(f32[3,40,384]{2,1,0:T(8,128)} %get-tuple-element.65), channel_id=1, source_target_pairs={{0,1},{1,0},{2,3},{3,2},{4,5},{5,4},{6,7},{7,6},{8,9},{9,8},{10,11... | collective-permute-start | bytes 552968 | tf_op jit(solution)/shard_map/ppermute | solution.py:960
  77.3 13.3 %collective-permute-start.12 = (f32[40,256]{1,0:T(8,128)S(1)}, f32[40,256]{1,0:T(8,128)S(1)}, u32[]{:S(2)}, u32[]{:S(2)}) collective-permute-start(f32[40,256]{1,0:T(8,128)S(1)} %slice.71), channel_id=1, source_target_pairs={{0,8},{4,12},{1,9},{5,13},{2,10},{6,14},{3,11},{7,15},{16,24},{20,... | collective-permute-start | bytes 122888 | tf_op jit(solution)/shard_map/ppermute | solution.py:971
  88.5 2.1 %collective-permute-start.13 = (f32[40,384]{1,0:T(8,128)S(1)}, f32[40,384]{1,0:T(8,128)S(1)}, u32[]{:S(2)}, u32[]{:S(2)}) collective-permute-start(f32[40,384]{1,0:T(8,128)S(1)} %get-tuple-element.74), channel_id=1, source_target_pairs={{4,12},{12,8},{5,13},{13,9},{6,14},{14,10},{7,15},{15,11},{20,28},... | collective-permute-start | bytes 184328 | tf_op jit(solution)/shard_map/ppermute | solution.py:970
  89.2 4.6 %collective-permute-start.11 = (f32[56,640]{1,0:T(8,128)S(1)}, f32[56,640]{1,0:T(8,128)S(1)}, u32[]{:S(2)}, u32[]{:S(2)}) collective-permute-start(f32[56,640]{1,0:T(8,128)S(1)} %pad_maximum_fusion.1), channel_id=1, source_target_pairs={{0,4},{4,8},{8,12},{1,5},{5,9},{9,13},{2,6},{6,10},{10,14},{3,7},{... | collective-permute-start | bytes 430088 | tf_op jit(solution)/shard_map/ppermute | solution.py:963
  93.8 4.7 %collective-permute-start.14 = (f32[40,640]{1,0:T(8,128)S(1)}, f32[40,640]{1,0:T(8,128)S(1)}, u32[]{:S(2)}, u32[]{:S(2)}) collective-permute-start(f32[40,640]{1,0:T(8,128)S(1)} %fusion.32), channel_id=1, source_target_pairs={{0,2},{2,0},{1,3},{3,1},{4,6},{6,4},{5,7},{7,5},{8,10},{10,8},{9,1... | collective-permute-start | bytes 307208 | tf_op jit(solution)/shard_map/ppermute | solution.py:974
  98.5 1.4 %collective-permute-start.15 = (f32[40,640]{1,0:T(8,128)S(1)}, f32[40,640]{1,0:T(8,128)S(1)}, u32[]{:S(2)}, u32[]{:S(2)}) collective-permute-start(f32[40,640]{1,0:T(8,128)S(1)} %add.87.mine), channel_id=1, source_target_pairs={{0,1},{1,0},{2,3},{3,2},{4,5},{5,4},{6,7},{7,6},{8,9},{9,8},{10,11... | collective-permute-start | bytes 307208 | tf_op jit(solution)/shard_map/ppermute | solution.py:975

commit v11 on v10

--- a/solution.py
+++ b/solution.py
@@ -301,6 +301,38 @@
         compiler_params=pltpu.CompilerParams(vmem_limit_bytes=GRANT),
         cost_estimate=pl.CostEstimate(flops=0, bytes_accessed=moved, transcendentals=0),
     )(scalars, *arrays)
+
+
+def hand_kernel(heads, keys, values, out, arrive):
+    column = pl.multiple_of((1 - lax.axis_index("slab")) * heads * HD, heads * HD)
+    half = keys.shape[0]
+    copies = []
+    for number, source in enumerate((keys, values)):
+        copy = pltpu.make_async_copy(
+            source.at[:, pl.ds(column, heads * HD)],
+            out.at[pl.ds(number * half, half), :],
+            arrive.at[number],
+        )
+        copy.start()
+        copies.append(copy)
+    for copy in copies:
+        copy.wait()
+
+
+def pack_handed(keys, values, heads):
+    shape = (2 * keys.shape[0], heads * HD)
+    return pl.pallas_call(
+        functools.partial(hand_kernel, heads),
+        name="pack_handed",
+        out_shape=jax.ShapeDtypeStruct(shape, keys.dtype),
+        in_specs=[pl.BlockSpec(memory_space=pl.ANY)] * 2,
+        out_specs=pl.BlockSpec(memory_space=pltpu.VMEM),
+        scratch_shapes=[pltpu.SemaphoreType.DMA((2,))],
+        compiler_params=pltpu.CompilerParams(vmem_limit_bytes=GRANT),
+        cost_estimate=pl.CostEstimate(
+            flops=0, bytes_accessed=4 * math.prod(shape), transcendentals=0
+        ),
+    )(keys, values)
 
 
 def message(scalars, pieces, arrays, name):
@@ -469,14 +501,12 @@
     def _():
         ones_rows = jnp.ones((STAT_ROWS, HD), jnp.bfloat16)
         patch = weight.shape[0]
-        used = sorted({task[1] for _, tasks in variants.values() for task in tasks})
         for fetch in fetches:
             fetch.wait()
-        for slot in range(SLOTS):
-            if slot not in used:
-                if fresh:
-                    carried[slot] = jnp.zeros(carried.shape[1:], carried.dtype)
-                continue
+        if fresh:
+            carried[...] = jnp.zeros_like(carried)
+
+        def finish_slot(slot):
             left = squares[slot]
             total = jnp.zeros((STAT_ROWS, rows), jnp.float32)
             for _ in range(3):
@@ -486,7 +516,7 @@
                     ones_rows, piece, (((1,), (1,)), ((), ())), preferred_element_type=jnp.float32
                 )
             done = folded[slot]
-            new = jnp.concatenate(
+            carried[slot] += jnp.concatenate(
                 [
                     done[:patch] + done[patch : 2 * patch],
                     done[2 * patch : 2 * patch + STAT_ROWS],
@@ -494,7 +524,14 @@
                 ],
                 axis=0,
             )
-            carried[slot] = new if fresh else carried[slot] + new
+
+        for place, (_, tasks) in variants.items():
+
+            @pl.when(scalars[PLACE] == place)
+            def _():
+                for slot in sorted({task[1] for task in tasks}):
+                    finish_slot(slot)
+
         store()
 
 
@@ -615,31 +652,20 @@
             )
         ]
 
-    (handed,) = message(
+    handed = pack_handed(keys, values, heads)
+    received = lax.ppermute(handed, "slab", SWAP)
+    up, down = message(
         scalars,
         [
-            [
-                (part, row, half // 2, (OTHER,), 0, heads)
-                for part in (1, 2)
-                for row in (0, half // 2)
-            ]
-        ],
-        (queries, keys, values),
-        "pack_handed",
-    )
-    received = lax.ppermute(handed, "slab", SWAP)
-    down, up = message(
-        scalars,
-        [
+            pairs_of(UP, 0, NEAR_HEADS),
             tokens(DOWN, 0, MIDDLE_HEADS) + pairs_of(DOWN, 0, MIDDLE_HEADS),
-            pairs_of(UP, 0, NEAR_HEADS),
         ],
         (queries, keys, values, received),
         "pack_first",
     )
     source, _ = lax.optimization_barrier((received, down))
+    up = send(up, (0, 1), (1, 2))
     down = send(down, (1, 0), (2, 1), (3, 2))
-    up = send(up, (0, 1), (1, 2))
     up_two, two, far_all, far_pair = message(
         scalars,
         [
@@ -667,14 +693,14 @@
     own = (queries, keys, values, received, weight, head_gain[None, :])
     run = functools.partial(attend, own=own, scalars=scalars, mask=mask)
 
-    here, on_one, back_one = OWN_TOKENS, Tokens(0, (0,)), Tokens(None, (1,))
+    here, back_one, on_one = OWN_TOKENS, Tokens(None, (0,)), Tokens(1, (1,))
     back_two = Tokens(None, (2,))
     sums = run(
         MIDDLE_HEADS,
         MAIN,
         MAIN_CAP,
         sums=None,
-        payloads=[down, up, up_two],
+        payloads=[up, down, up_two],
         variants={
             0: (4, [(here, 0, 0, [(here, 0)]), (on_one, 1, 1, [(here, 0), (on_one, 1)])]),
             1: (
@@ -704,7 +730,7 @@
         FINAL,
         FINAL_CAP,
         sums=sums,
-        payloads=[down, up, two, far_next, far_two, far_three],
+        payloads=[up, down, two, far_next, far_two, far_three],
         variants={
             0: (
                 FAR_HEADS,

time: 103 us -> 101 us (0.981)
  Pallas kernels: 31.3 us -> 29.8 us
    pallas_call x3 -> x2, Pallas kernels: 9.05 us -> 6.42 us  [pack(): pl.pallas_call(functools.partial(pack_kernel, len(arrays), len(shapes), c...]
    pallas_call x0 -> x1, Pallas kernels: none -> 1.21 us  [pack_handed(): pl.pallas_call(functools.partial(hand_kernel, heads), name='pack_handed',...]
  transfers between devices with their start and end apart: 16 -> 16, of which waited for: 7 -> 7; matrix products, arithmetic and copies ran while one was open for 8% -> 9% of each run, Pallas kernels for 13% -> 13%
where the time goes in v11:
time: 101 us; the launch traced here: 100 us
  starting transfers between devices  38.4 us (38%)
  Pallas kernels  29.8 us (30%)
  waiting for transfers between devices  19.5 us (19%)
  local copies, waits for them, and re-layouts  6.84 us (7%)
  other arithmetic  4.44 us (4%)
  between operations  1.02 us (1%)
    ppermute x7, starting transfers between devices, send(): return in_place(lax.ppermute(value, 'span', list(pairs)))  21.3 us
    pallas_call x2, Pallas kernels, attend(): pl.pallas_call(functools.partial(attend_kernel, variants, extra, span_cou...  19.6 us
    ppermute x1, starting transfers between devices, per_device(): to_before = lax.ppermute(after[:, skip:], 'span', [(0, 2), (1, 3)])  11.3 us
    ppermute x7, waiting for transfers between devices, send(): return in_place(lax.ppermute(value, 'span', list(pairs)))  8.52 us
    pallas_call x2, Pallas kernels, pack(): pl.pallas_call(functools.partial(pack_kernel, len(arrays), len(shapes), c...  6.42 us
    ppermute x1, waiting for transfers between devices, per_device(): total = total + lax.ppermute(total, 'head', SWAP)  3.27 us
    ppermute x1, waiting for transfers between devices, per_device(): lax.ppermute(jnp.concatenate([jnp.concatenate([own[:, skip:], after], axi...  3.26 us
    pallas_call x1, Pallas kernels, finish(): pl.pallas_call(finish_kernel, name='finish', out_shape=(jax.ShapeDtypeStr...  2.4 us
  transfers between devices with their start and end apart: 16, of which 7 were waited for; matrix products, arithmetic and copies ran while one was open for 9% of the time, Pallas kernels for 13%

profile of v11, /device:TPU:0, one launch (start us, length us, event | category | flops | bytes accessed | tf_op | source)
XLA Modules:
  0.0 100.0 jit_solution(2318597517915156730)
XLA Ops:
  0.7 1.2 %pack_handed.1 = bf16[384,1280]{1,0:T(8,128)(2,1)S(1)} custom-call(bf16[192,2560]{1,0:T(8,128)(2,1)} %refs_7_.1, bf16[192,2560]{1,0:T(8,128)(2,1)} %refs_8_.1), custom_call_target="tpu_custom_call" | custom-call | bytes 1966080 | tf_op jit(solution)/shard_map/pack_handed/pallas_call | solution.py:324
  3.8 0.8 collective-permute-done.refs_3_.refs_9_
  4.6 2.9 %pack_first.1 = (bf16[768,512]{1,0:T(8,128)(2,1)}, bf16[1152,512]{1,0:T(8,128)(2,1)}) custom-call(s32[12]{0:T(128)S(1)} %bitcast_add_fusion.scalars, bf16[384,2560]{1,0:T(8,128)(2,1)} %refs_6_.1, bf16[192,2560]{1,0:T(8,128)(2,1)} %refs_7_.1, bf16[192,2560]{1,0:T(8,128)(2,1)} %refs_8_.1, bf16[384,1280]{1,0:T(8,128)(2,1)S(1)} %collective-permute-done.refs_3_.refs_9_), custom_call_target="tpu_custom_call" | custom-call | bytes 3932160 | tf_op jit(solution)/shard_map/pack_first/pallas_call | solution.py:286
  7.5 1.3 %collective-permute-start.2 = (bf16[1152,512]{1,0:T(8,128)(2,1)}, bf16[1152,512]{1,0:T(8,128)(2,1)}, u32[]{:S(2)}, u32[]{:S(2)}) collective-permute-start(bf16[1152,512]{1,0:T(8,128)(2,1)} %get-tuple-element.37), channel_id=1, source_target_pairs={{4,0},{8,4},{12,8},{5,1},{9,5},{13,9},{6,2},{10,6},{14,10},{7,3},{... | collective-permute-start | bytes 3538952 | tf_op jit(solution)/shard_map/ppermute | solution.py:639
  8.9 6.5 %collective-permute-start.1 = (bf16[768,512]{1,0:T(8,128)(2,1)}, bf16[768,512]{1,0:T(8,128)(2,1)}, u32[]{:S(2)}, u32[]{:S(2)}) collective-permute-start(bf16[768,512]{1,0:T(8,128)(2,1)} %get-tuple-element.43), channel_id=1, source_target_pairs={{0,4},{4,8},{1,5},{5,9},{2,6},{6,10},{3,7},{7,11},{16,20},{20,24},... | collective-permute-start | bytes 2359304 | tf_op jit(solution)/shard_map/ppermute | solution.py:639
  15.4 3.5 %pack_second.1 = (bf16[768,512]{1,0:T(8,128)(2,1)}, bf16[1152,512]{1,0:T(8,128)(2,1)}, bf16[1152,256]{1,0:T(8,128)(2,1)}, bf16[768,256]{1,0:T(8,128)(2,1)}) custom-call(s32[12]{0:T(128)S(1)} %bitcast_add_fusion.scalars, bf16[384,2560]{1,0:T(8,128)(2,1)} %refs_6_.1, bf16[192,2560]{1,0:T(8,128)(2,1)} %refs_7_.1, bf16[192,2560]{1,0:T(8,128)(2,1)} %refs_8_.1, ...), custom_call_target="tpu_custom_call" | custom-call | bytes 5898240 | tf_op jit(solution)/shard_map/pack_second/pallas_call | solution.py:286
  18.9 1.7 %collective-permute-start.3 = (bf16[1152,512]{1,0:T(8,128)(2,1)}, bf16[1152,512]{1,0:T(8,128)(2,1)}, u32[]{:S(2)}, u32[]{:S(2)}) collective-permute-start(bf16[1152,512]{1,0:T(8,128)(2,1)} %get-tuple-element.39), channel_id=1, source_target_pairs={{12,4},{13,5},{14,6},{15,7},{28,20},{29,21},{30,22},{31,23}} | collective-permute-start | bytes 3538952 | tf_op jit(solution)/shard_map/ppermute | solution.py:639
  21.0 2.7 %collective-permute-start.9 = (bf16[768,512]{1,0:T(8,128)(2,1)}, bf16[768,512]{1,0:T(8,128)(2,1)}, u32[]{:S(2)}, u32[]{:S(2)}) collective-permute-start(bf16[768,512]{1,0:T(8,128)(2,1)} %get-tuple-element.53), channel_id=1, source_target_pairs={{0,8},{1,9},{2,10},{3,11},{16,24},{17,25},{18,26},{19,27}} | collective-permute-start | bytes 2359304 | tf_op jit(solution)/shard_map/ppermute | solution.py:639
  24.1 1.6 %collective-permute-start.6 = (f32[40,128]{0,1:T(8,128)S(1)}, f32[40,128]{0,1:T(8,128)S(1)}, u32[]{:S(2)}, u32[]{:S(2)}) collective-permute-start(f32[40,128]{0,1:T(8,128)S(1)} %copy.39), channel_id=1, source_target_pairs={{0,2},{2,0},{1,3},{3,1},{4,6},{6,4},{5,7},{7,5},{8,10},{10,8},{9,1... | collective-permute-start | bytes 61448 | tf_op jit(solution)/shard_map/ppermute | solution.py:778
  26.4 1.0 copy-done.2
  27.6 0.9 collective-permute-done.6
  28.5 1.3 %collective-permute-start.4 = (bf16[1152,256]{1,0:T(8,128)(2,1)}, bf16[1152,256]{1,0:T(8,128)(2,1)}, u32[]{:S(2)}, u32[]{:S(2)}) collective-permute-start(bf16[1152,256]{1,0:T(8,128)(2,1)} %get-tuple-element.44), channel_id=1, source_target_pairs={{8,12},{4,0},{9,13},{5,1},{10,14},{6,2},{11,15},{7,3},{24,28},{20,... | collective-permute-start | bytes 1769480 | tf_op jit(solution)/shard_map/ppermute | solution.py:639
  31.1 0.9 pad_maximum_fusion
  32.0 0.8 slice.63
  32.8 1.0 %reshape.33 = f32[16,640]{1,0:T(8,128)S(1)} reshape(f32[320,32]{1,0:T(8,128)} %slice.63) | data formatting | bytes 81920 | tf_op jit(solution)/shard_map/reshape | solution.py:969
  33.8 0.8 fusion.33.constants
  34.7 6.4 %collective-permute-start.8 = (bf16[768,256]{1,0:T(8,128)(2,1)}, bf16[768,256]{1,0:T(8,128)(2,1)}, u32[]{:S(2)}, u32[]{:S(2)}) collective-permute-start(bf16[768,256]{1,0:T(8,128)(2,1)} %get-tuple-element.52), channel_id=1, source_target_pairs={{0,12},{1,13},{2,14},{3,15},{16,28},{17,29},{18,30},{19,31}} | collective-permute-start | bytes 1179656 | tf_op jit(solution)/shard_map/ppermute | solution.py:639
  41.1 8.5 %collective-permute-done.9.refs_8_ = bf16[768,512]{1,0:T(8,128)(2,1)} collective-permute-done((bf16[768,512]{1,0:T(8,128)(2,1)}, bf16[768,512]{1,0:T(8,128)(2,1)}, u32[]{:S(2)}, u32[]{:S(2)}) %collective-permute-start.9) | collective-permute-done | bytes 786464 | tf_op jit(solution)/shard_map/ppermute | solution.py:639
  49.6 1.4 %collective-permute-start.7 = (bf16[768,256]{1,0:T(8,128)(2,1)}, bf16[768,256]{1,0:T(8,128)(2,1)}, u32[]{:S(2)}, u32[]{:S(2)}) collective-permute-start(bf16[768,256]{1,0:T(8,128)(2,1)} %get-tuple-element.52), channel_id=1, source_target_pairs={{4,12},{5,13},{6,14},{7,15},{20,28},{21,29},{22,30},{23,31}} | collective-permute-start | bytes 1179656 | tf_op jit(solution)/shard_map/ppermute | solution.py:639
  51.0 0.8 reshape.30.mask
  51.7 0.7 broadcast_in_dim.24.refs_5_.refs_11_
  52.5 9.5 %main_heads.1 = (f32[3,40,384]{2,1,0:T(8,128)}, f32[3,40,384]{2,1,0:T(8,128)}) custom-call(s32[12]{0:T(128)S(1)} %bitcast_add_fusion.scalars, s32[16]{0:T(128)S(1)} %reshape.30.mask, bf16[384,2560]{1,0:T(8,128)(2,1)} %refs_6_.1, bf16[192,2560]{1,0:T(8,128)(2,1)} %refs_7_.1, bf16[192,2560]{1,0:T(8,128)(2,1)} %refs_8_.1, ...), custom_call_target="tpu_custom_call" | custom-call | flops 2113929216 | bytes 1179648 | tf_op jit(solution)/shard_map/main_heads/pallas_call | solution.py:603
  62.0 10.1 %final_heads.1 = (f32[3,40,384]{2,1,0:T(8,128)}, f32[3,40,384]{2,1,0:T(8,128)}) custom-call(s32[12]{0:T(128)S(1)} %bitcast_add_fusion.scalars, s32[16]{0:T(128)S(1)} %reshape.30.mask, bf16[384,2560]{1,0:T(8,128)(2,1)} %refs_6_.1, bf16[192,2560]{1,0:T(8,128)(2,1)} %refs_7_.1, ...), custom_call_target="tpu_custom_call", output_to_operand_aliasing={{0}: (20, {}), {1}: (21, {})} | custom-call | flops 4831838208 | bytes 1179648 | tf_op jit(solution)/shard_map/final_heads/pallas_call | solution.py:603
  72.2 1.6 %collective-permute-done.10 = f32[3,40,384]{2,1,0:T(8,128)S(1)} collective-permute-done((f32[3,40,384]{2,1,0:T(8,128)}, f32[3,40,384]{2,1,0:T(8,128)S(1)}, u32[]{:S(2)}, u32[]{:S(2)}) %collective-permute-start.10) | collective-permute-done | bytes 184352 | tf_op jit(solution)/shard_map/ppermute | solution.py:986
  73.9 1.0 add.84
  74.9 11.3 %collective-permute-start.12 = (f32[40,256]{1,0:T(8,128)S(1)}, f32[40,256]{1,0:T(8,128)S(1)}, u32[]{:S(2)}, u32[]{:S(2)}) collective-permute-start(f32[40,256]{1,0:T(8,128)S(1)} %slice.71), channel_id=1, source_target_pairs={{0,8},{4,12},{1,9},{5,13},{2,10},{6,14},{3,11},{7,15},{16,24},{20,... | collective-permute-start | bytes 122888 | tf_op jit(solution)/shard_map/ppermute | solution.py:997
  86.9 1.3 %collective-permute-start.11 = (f32[56,640]{1,0:T(8,128)S(1)}, f32[56,640]{1,0:T(8,128)S(1)}, u32[]{:S(2)}, u32[]{:S(2)}) collective-permute-start(f32[56,640]{1,0:T(8,128)S(1)} %pad_maximum_fusion.1), channel_id=1, source_target_pairs={{0,4},{4,8},{8,12},{1,5},{5,9},{9,13},{2,6},{6,10},{10,14},{3,7},{... | collective-permute-start | bytes 430088 | tf_op jit(solution)/shard_map/ppermute | solution.py:989
  88.2 3.3 %collective-permute-done.11 = f32[56,640]{1,0:T(8,128)S(1)} collective-permute-done((f32[56,640]{1,0:T(8,128)S(1)}, f32[56,640]{1,0:T(8,128)S(1)}, u32[]{:S(2)}, u32[]{:S(2)}) %collective-permute-start.11) | collective-permute-done | bytes 143392 | tf_op jit(solution)/shard_map/ppermute | solution.py:989
  91.5 1.5 %collective-permute-start.14 = (f32[40,640]{1,0:T(8,128)S(1)}, f32[40,640]{1,0:T(8,128)S(1)}, u32[]{:S(2)}, u32[]{:S(2)}) collective-permute-start(f32[40,640]{1,0:T(8,128)S(1)} %fusion.32), channel_id=1, source_target_pairs={{0,2},{2,0},{1,3},{3,1},{4,6},{6,4},{5,7},{7,5},{8,10},{10,8},{9,1... | collective-permute-start | bytes 307208 | tf_op jit(solution)/shard_map/ppermute | solution.py:1000
  92.9 3.3 %collective-permute-done.14 = f32[40,640]{1,0:T(8,128)S(1)} collective-permute-done((f32[40,640]{1,0:T(8,128)S(1)}, f32[40,640]{1,0:T(8,128)S(1)}, u32[]{:S(2)}, u32[]{:S(2)}) %collective-permute-start.14) | collective-permute-done | bytes 102432 | tf_op jit(solution)/shard_map/ppermute | solution.py:1000
  96.4 1.2 %collective-permute-done.15.other = f32[40,640]{1,0:T(8,128)S(1)} collective-permute-done((f32[40,640]{1,0:T(8,128)S(1)}, f32[40,640]{1,0:T(8,128)S(1)}, u32[]{:S(2)}, u32[]{:S(2)}) %collective-permute-start.15) | collective-permute-done | bytes 102432 | tf_op jit(solution)/shard_map/ppermute | solution.py:1001
  97.6 2.4 %finish.1 = (f32[3,8,16,16]{3,2,1,0:T(8,128)}, bf16[3,8,16,384]{3,2,1,0:T(8,128)(2,1)}) custom-call(s32[12]{0:T(128)S(1)} %bitcast_add_fusion.scalars, f32[40,640]{1,0:T(8,128)S(1)} %add.87.mine, f32[40,640]{1,0:T(8,128)S(1)} %collective-permute-done.15.other, f32[320,48]{1,0:T(8,128)S(1)} %bitcast.33, f32[320,32]{1,0:T(8,128)S(1)} %reshape.34.before, ...), custom_call_target="tpu_custom_call" | custom-call | tf_op jit(solution)/shard_map/finish/pallas_call | solution.py:908
  (62 shorter events, 5.9 us)
Async XLA Ops:
  0.6 25.1 %copy-start = (f32[384]{0:T(512)S(1)}, f32[384]{0:T(512)}, u32[]{:S(2)}) copy-start(f32[384]{0:T(512)} %param.21) | copy-start | bytes 4612
  0.6 1.8 %copy-start.8 = (s32[12]{0:T(128)S(1)}, s32[12]{0:T(128)}, u32[]{:S(2)}) copy-start(s32[12]{0:T(128)} %constant.107.clone) | copy-start | bytes 148
  1.9 2.7 %collective-permute-start = (bf16[384,1280]{1,0:T(8,128)(2,1)S(1)}, bf16[384,1280]{1,0:T(8,128)(2,1)S(1)}, u32[]{:S(2)}, u32[]{:S(2)}) collective-permute-start(bf16[384,1280]{1,0:T(8,128)(2,1)S(1)} %pack_handed.1), channel_id=1, source_target_pairs={{0,1},{1,0},{2,3},{3,2},{4,5},{5,4},{6,7},{7,6},{8,9},{9,8},{10,11... | collective-permute-start | bytes 2949128 | tf_op jit(solution)/shard_map/ppermute | solution.py:656
  7.5 45.0 %collective-permute-start.2 = (bf16[1152,512]{1,0:T(8,128)(2,1)}, bf16[1152,512]{1,0:T(8,128)(2,1)}, u32[]{:S(2)}, u32[]{:S(2)}) collective-permute-start(bf16[1152,512]{1,0:T(8,128)(2,1)} %get-tuple-element.37), channel_id=1, source_target_pairs={{4,0},{8,4},{12,8},{5,1},{9,5},{13,9},{6,2},{10,6},{14,10},{7,3},{... | collective-permute-start | bytes 3538952 | tf_op jit(solution)/shard_map/ppermute | solution.py:639
  8.8 11.8 %copy-start.4 = (f32[3,8,16,16]{3,2,1,0:T(8,128)S(1)}, f32[3,8,16,16]{3,2,1,0:T(8,128)}, u32[]{:S(2)}) copy-start(f32[3,8,16,16]{3,2,1,0:T(8,128)} %param.19) | copy-start | bytes 73732
  8.8 14.9 %copy-start.1 = (bf16[2560,64]{0,1:T(8,128)(2,1)S(1)}, bf16[2560,64]{0,1:T(8,128)(2,1)}, u32[]{:S(2)}) copy-start(bf16[2560,64]{0,1:T(8,128)(2,1)} %param.18) | copy-start | bytes 983044
  8.8 14.9 %copy-start.6 = (f32[2560]{0:T(1024)S(1)}, f32[2560]{0:T(1024)}, u32[]{:S(2)}) copy-start(f32[2560]{0:T(1024)} %param.16) | copy-start | bytes 30724
  8.8 14.8 %copy-start.7 = (f32[2560]{0:T(1024)S(1)}, f32[2560]{0:T(1024)}, u32[]{:S(2)}) copy-start(f32[2560]{0:T(1024)} %param.17) | copy-start | bytes 30724
  8.9 25.8 %collective-permute-start.1 = (bf16[768,512]{1,0:T(8,128)(2,1)}, bf16[768,512]{1,0:T(8,128)(2,1)}, u32[]{:S(2)}, u32[]{:S(2)}) collective-permute-start(bf16[768,512]{1,0:T(8,128)(2,1)} %get-tuple-element.43), channel_id=1, source_target_pairs={{0,4},{4,8},{1,5},{5,9},{2,6},{6,10},{3,7},{7,11},{16,20},{20,24},... | collective-permute-start | bytes 2359304 | tf_op jit(solution)/shard_map/ppermute | solution.py:639
  18.9 43.1 %collective-permute-start.3 = (bf16[1152,512]{1,0:T(8,128)(2,1)}, bf16[1152,512]{1,0:T(8,128)(2,1)}, u32[]{:S(2)}, u32[]{:S(2)}) collective-permute-start(bf16[1152,512]{1,0:T(8,128)(2,1)} %get-tuple-element.39), channel_id=1, source_target_pairs={{12,4},{13,5},{14,6},{15,7},{28,20},{29,21},{30,22},{31,23}} | collective-permute-start | bytes 3538952 | tf_op jit(solution)/shard_map/ppermute | solution.py:639
  20.9 3.1 %collective-permute-start.5 = (f32[8,48]{1,0:T(8,128)S(1)}, f32[8,48]{1,0:T(8,128)S(1)}, u32[]{:S(2)}, u32[]{:S(2)}) collective-permute-start(f32[8,48]{1,0:T(8,128)S(1)} %bitcast.43), channel_id=1, source_target_pairs={{0,1},{1,0},{2,3},{3,2},{4,5},{5,4},{6,7},{7,6},{8,9},{9,8},{10,11... | collective-permute-start | bytes 4616 | tf_op jit(solution)/shard_map/ppermute | solution.py:763
  21.0 28.6 %collective-permute-start.9 = (bf16[768,512]{1,0:T(8,128)(2,1)}, bf16[768,512]{1,0:T(8,128)(2,1)}, u32[]{:S(2)}, u32[]{:S(2)}) collective-permute-start(bf16[768,512]{1,0:T(8,128)(2,1)} %get-tuple-element.53), channel_id=1, source_target_pairs={{0,8},{1,9},{2,10},{3,11},{16,24},{17,25},{18,26},{19,27}} | collective-permute-start | bytes 2359304 | tf_op jit(solution)/shard_map/ppermute | solution.py:639
  24.0 1.7 %copy-start.3 = (f32[8,14,48]{2,1,0:T(8,128)}, f32[8,14,48]{2,1,0:T(8,128)S(1)}, u32[]{:S(2)}) copy-start(f32[8,14,48]{2,1,0:T(8,128)S(1)} %broadcast_in_dim.26) | copy-start | bytes 64516
  24.1 4.3 %collective-permute-start.6 = (f32[40,128]{0,1:T(8,128)S(1)}, f32[40,128]{0,1:T(8,128)S(1)}, u32[]{:S(2)}, u32[]{:S(2)}) collective-permute-start(f32[40,128]{0,1:T(8,128)S(1)} %copy.39), channel_id=1, source_target_pairs={{0,2},{2,0},{1,3},{3,1},{4,6},{6,4},{5,7},{7,5},{8,10},{10,8},{9,1... | collective-permute-start | bytes 61448 | tf_op jit(solution)/shard_map/ppermute | solution.py:778
  26.4 1.0 copy-start.2
  28.5 2.0 %copy-start.5 = (f32[40,128]{0,1:T(8,128)}, f32[40,128]{0,1:T(8,128)S(1)}, u32[]{:S(2)}) copy-start(f32[40,128]{0,1:T(8,128)S(1)} %collective-permute-done.6) | copy-start | bytes 61444
  28.5 33.6 %collective-permute-start.4 = (bf16[1152,256]{1,0:T(8,128)(2,1)}, bf16[1152,256]{1,0:T(8,128)(2,1)}, u32[]{:S(2)}, u32[]{:S(2)}) collective-permute-start(bf16[1152,256]{1,0:T(8,128)(2,1)} %get-tuple-element.44), channel_id=1, source_target_pairs={{8,12},{4,0},{9,13},{5,1},{10,14},{6,2},{11,15},{7,3},{24,28},{20,... | collective-permute-start | bytes 1769480 | tf_op jit(solution)/shard_map/ppermute | solution.py:639
  34.7 27.3 %collective-permute-start.8 = (bf16[768,256]{1,0:T(8,128)(2,1)}, bf16[768,256]{1,0:T(8,128)(2,1)}, u32[]{:S(2)}, u32[]{:S(2)}) collective-permute-start(bf16[768,256]{1,0:T(8,128)(2,1)} %get-tuple-element.52), channel_id=1, source_target_pairs={{0,12},{1,13},{2,14},{3,15},{16,28},{17,29},{18,30},{19,31}} | collective-permute-start | bytes 1179656 | tf_op jit(solution)/shard_map/ppermute | solution.py:639
  49.6 12.4 %collective-permute-start.7 = (bf16[768,256]{1,0:T(8,128)(2,1)}, bf16[768,256]{1,0:T(8,128)(2,1)}, u32[]{:S(2)}, u32[]{:S(2)}) collective-permute-start(bf16[768,256]{1,0:T(8,128)(2,1)} %get-tuple-element.52), channel_id=1, source_target_pairs={{4,12},{5,13},{6,14},{7,15},{20,28},{21,29},{22,30},{23,31}} | collective-permute-start | bytes 1179656 | tf_op jit(solution)/shard_map/ppermute | solution.py:639
  72.2 1.7 %collective-permute-start.10 = (f32[3,40,384]{2,1,0:T(8,128)}, f32[3,40,384]{2,1,0:T(8,128)S(1)}, u32[]{:S(2)}, u32[]{:S(2)}) collective-permute-start(f32[3,40,384]{2,1,0:T(8,128)} %get-tuple-element.65), channel_id=1, source_target_pairs={{0,1},{1,0},{2,3},{3,2},{4,5},{5,4},{6,7},{7,6},{8,9},{9,8},{10,11... | collective-permute-start | bytes 552968 | tf_op jit(solution)/shard_map/ppermute | solution.py:986
  74.9 13.3 %collective-permute-start.12 = (f32[40,256]{1,0:T(8,128)S(1)}, f32[40,256]{1,0:T(8,128)S(1)}, u32[]{:S(2)}, u32[]{:S(2)}) collective-permute-start(f32[40,256]{1,0:T(8,128)S(1)} %slice.71), channel_id=1, source_target_pairs={{0,8},{4,12},{1,9},{5,13},{2,10},{6,14},{3,11},{7,15},{16,24},{20,... | collective-permute-start | bytes 122888 | tf_op jit(solution)/shard_map/ppermute | solution.py:997
  86.2 2.0 %collective-permute-start.13 = (f32[40,384]{1,0:T(8,128)S(1)}, f32[40,384]{1,0:T(8,128)S(1)}, u32[]{:S(2)}, u32[]{:S(2)}) collective-permute-start(f32[40,384]{1,0:T(8,128)S(1)} %get-tuple-element.74), channel_id=1, source_target_pairs={{4,12},{12,8},{5,13},{13,9},{6,14},{14,10},{7,15},{15,11},{20,28},... | collective-permute-start | bytes 184328 | tf_op jit(solution)/shard_map/ppermute | solution.py:996
  86.9 4.6 %collective-permute-start.11 = (f32[56,640]{1,0:T(8,128)S(1)}, f32[56,640]{1,0:T(8,128)S(1)}, u32[]{:S(2)}, u32[]{:S(2)}) collective-permute-start(f32[56,640]{1,0:T(8,128)S(1)} %pad_maximum_fusion.1), channel_id=1, source_target_pairs={{0,4},{4,8},{8,12},{1,5},{5,9},{9,13},{2,6},{6,10},{10,14},{3,7},{... | collective-permute-start | bytes 430088 | tf_op jit(solution)/shard_map/ppermute | solution.py:989
  91.5 4.7 %collective-permute-start.14 = (f32[40,640]{1,0:T(8,128)S(1)}, f32[40,640]{1,0:T(8,128)S(1)}, u32[]{:S(2)}, u32[]{:S(2)}) collective-permute-start(f32[40,640]{1,0:T(8,128)S(1)} %fusion.32), channel_id=1, source_target_pairs={{0,2},{2,0},{1,3},{3,1},{4,6},{6,4},{5,7},{7,5},{8,10},{10,8},{9,1... | collective-permute-start | bytes 307208 | tf_op jit(solution)/shard_map/ppermute | solution.py:1000
  96.2 1.4 %collective-permute-start.15 = (f32[40,640]{1,0:T(8,128)S(1)}, f32[40,640]{1,0:T(8,128)S(1)}, u32[]{:S(2)}, u32[]{:S(2)}) collective-permute-start(f32[40,640]{1,0:T(8,128)S(1)} %add.87.mine), channel_id=1, source_target_pairs={{0,1},{1,0},{2,3},{3,2},{4,5},{5,4},{6,7},{7,6},{8,9},{9,8},{10,11... | collective-permute-start | bytes 307208 | tf_op jit(solution)/shard_map/ppermute | solution.py:1001

commit v12 on v11

--- a/solution.py
+++ b/solution.py
@@ -253,51 +253,34 @@
 
 
 def pack_kernel(inputs, messages, copies, scalars, *refs):
-    ins, rest = refs[:inputs], refs[inputs:]
-    outs, staged = rest[:messages], rest[messages:-2]
-    arrive, leave = rest[-2:]
+    ins, outs, arrive = refs[:inputs], refs[inputs:-1], refs[-1]
     arriving = []
     for number, (source, row, rows, entries, shift, target, at, heads) in enumerate(copies):
         head = shift
         for entry in entries:
             head = head + scalars[entry]
         column = pl.multiple_of(head * HD, HD)
-        place = staged[target].at[pl.ds(at, rows), :]
         copy = pltpu.make_async_copy(
-            ins[source].at[pl.ds(row, rows), pl.ds(column, heads * HD)], place, arrive.at[number]
+            ins[source].at[pl.ds(row, rows), pl.ds(column, heads * HD)],
+            outs[target].at[pl.ds(at, rows), :],
+            arrive.at[number],
         )
         copy.start()
-        onward = pltpu.make_async_copy(
-            place, outs[target].at[pl.ds(at, rows), :], leave.at[number]
-        )
-        arriving.append((copy, onward))
-    for copy, onward in arriving:
+        arriving.append(copy)
+    for copy in arriving:
         copy.wait()
-        onward.start()
-    for _, onward in arriving:
-        onward.wait()
 
 
 def pack(scalars, arrays, shapes, copies, name):
     moved = sum(2 * 2 * rows * heads * HD for _, _, rows, _, _, _, _, heads in copies)
-    out_shape = [pltpu.HBM(shape, jnp.bfloat16) for shape in shapes]
-    in_specs = [pl.BlockSpec(memory_space=pl.ANY)] * len(arrays)
-    out_specs = [pl.BlockSpec(memory_space=pl.ANY)] * len(shapes)
     return pl.pallas_call(
         functools.partial(pack_kernel, len(arrays), len(shapes), copies),
         name=name,
-        out_shape=out_shape,
-        grid_spec=pltpu.PrefetchScalarGridSpec(
-            num_scalar_prefetch=1,
-            grid=(1,),
-            in_specs=in_specs,
-            out_specs=out_specs,
-            scratch_shapes=[pltpu.VMEM(shape, jnp.bfloat16) for shape in shapes]
-            + [
-                pltpu.SemaphoreType.DMA((len(copies),)),
-                pltpu.SemaphoreType.DMA((len(copies),)),
-            ],
-        ),
+        out_shape=[jax.ShapeDtypeStruct(shape, jnp.bfloat16) for shape in shapes],
+        in_specs=[pl.BlockSpec(memory_space=pltpu.SMEM)]
+        + [pl.BlockSpec(memory_space=pl.ANY)] * len(arrays),
+        out_specs=[pl.BlockSpec(memory_space=pltpu.VMEM)] * len(shapes),
+        scratch_shapes=[pltpu.SemaphoreType.DMA((len(copies),))],
         compiler_params=pltpu.CompilerParams(vmem_limit_bytes=GRANT),
         cost_estimate=pl.CostEstimate(flops=0, bytes_accessed=moved, transcendentals=0),
     )(scalars, *arrays)
@@ -678,6 +661,7 @@
         "pack_second",
     )
     anchor = two
+    up, up_two = lax.optimization_barrier((up, up_two))
     up_two = send(up_two, (0, 2))
     two = send(two, (3, 1))
     far_next = send(far_all, (2, 3), (1, 0))

time: 101 us -> 105 us (1.040)
  waiting for transfers between devices: 19.5 us -> 21.5 us
    ppermute x1, starting transfers between devices: 1.3 us -> 12 us  [per_device(): lax.ppermute(jnp.concatenate([jnp.concatenate([own[:, skip:], after], axi...]
    ppermute x1, starting transfers between devices: 11.3 us -> 1.98 us  [per_device(): to_before = lax.ppermute(after[:, skip:], 'span', [(0, 2), (1, 3)])]
    ppermute x7, waiting for transfers between devices: 8.52 us -> 11.6 us  [send(): return in_place(lax.ppermute(value, 'span', list(pairs)))]
    ppermute x7, starting transfers between devices: 21.3 us -> 19.8 us  [send(): return in_place(lax.ppermute(value, 'span', list(pairs)))]
  transfers between devices with their start and end apart: 16 -> 16, of which waited for: 7 -> 8; matrix products, arithmetic and copies ran while one was open for 9% -> 10% of each run, Pallas kernels for 13% -> 13%
where the time goes in v12:
time: 105 us; the launch traced here: 104 us
  starting transfers between devices  38.8 us (37%)
  Pallas kernels  30 us (29%)
  waiting for transfers between devices  21.5 us (20%)
  local copies, waits for them, and re-layouts  7.62 us (7%)
  other arithmetic  5.14 us (5%)
    ppermute x7, starting transfers between devices, send(): return in_place(lax.ppermute(value, 'span', list(pairs)))  19.8 us
    pallas_call x2, Pallas kernels, attend(): pl.pallas_call(functools.partial(attend_kernel, variants, extra, span_cou...  19.6 us
    ppermute x1, starting transfers between devices, per_device(): lax.ppermute(jnp.concatenate([jnp.concatenate([own[:, skip:], after], axi...  12 us
    ppermute x7, waiting for transfers between devices, send(): return in_place(lax.ppermute(value, 'span', list(pairs)))  11.6 us
    pallas_call x2, Pallas kernels, pack(): pl.pallas_call(functools.partial(pack_kernel, len(arrays), len(shapes), c...  6.63 us
    ppermute x1, waiting for transfers between devices, per_device(): total = total + lax.ppermute(total, 'head', SWAP)  3.17 us
    ppermute x1, waiting for transfers between devices, per_device(): lax.ppermute(jnp.concatenate([jnp.concatenate([own[:, skip:], after], axi...  2.98 us
    pallas_call x1, Pallas kernels, finish(): pl.pallas_call(finish_kernel, name='finish', out_shape=(jax.ShapeDtypeStr...  2.4 us
  transfers between devices with their start and end apart: 16, of which 8 were waited for; matrix products, arithmetic and copies ran while one was open for 10% of the time, Pallas kernels for 13%

profile of v12, /device:TPU:0, one launch (start us, length us, event | category | flops | bytes accessed | tf_op | source)
XLA Modules:
  0.0 104.2 jit_solution(7895329801684244925)
XLA Ops:
  0.7 1.2 %pack_handed.1 = bf16[384,1280]{1,0:T(8,128)(2,1)S(1)} custom-call(bf16[192,2560]{1,0:T(8,128)(2,1)} %refs_7_.1, bf16[192,2560]{1,0:T(8,128)(2,1)} %refs_8_.1), custom_call_target="tpu_custom_call" | custom-call | bytes 1966080 | tf_op jit(solution)/shard_map/pack_handed/pallas_call | solution.py:307
  3.8 0.8 collective-permute-done.refs_3_.refs_9_
  4.6 3.0 %pack_first.1 = (bf16[768,512]{1,0:T(8,128)(2,1)S(1)}, bf16[1152,512]{1,0:T(8,128)(2,1)}) custom-call(s32[12]{0:T(128)S(1)} %bitcast_add_fusion.scalars, bf16[384,2560]{1,0:T(8,128)(2,1)} %refs_6_.1, bf16[192,2560]{1,0:T(8,128)(2,1)} %refs_7_.1, bf16[192,2560]{1,0:T(8,128)(2,1)} %refs_8_.1, bf16[384,1280]{1,0:T(8,128)(2,1)S(1)} %collective-permute-done.refs_3_.refs_9_), custom_call_target="tpu_custom_call" | custom-call | bytes 3932160 | tf_op jit(solution)/shard_map/pack_first/pallas_call | solution.py:276
  7.6 1.3 %collective-permute-start.2 = (bf16[1152,512]{1,0:T(8,128)(2,1)}, bf16[1152,512]{1,0:T(8,128)(2,1)}, u32[]{:S(2)}, u32[]{:S(2)}) collective-permute-start(bf16[1152,512]{1,0:T(8,128)(2,1)} %get-tuple-element.39), channel_id=1, source_target_pairs={{4,0},{8,4},{12,8},{5,1},{9,5},{13,9},{6,2},{10,6},{14,10},{7,3},{... | collective-permute-start | bytes 3538952 | tf_op jit(solution)/shard_map/ppermute | solution.py:622
  8.9 5.7 %collective-permute-start.1 = (bf16[768,512]{1,0:T(8,128)(2,1)S(1)}, bf16[768,512]{1,0:T(8,128)(2,1)S(1)}, u32[]{:S(2)}, u32[]{:S(2)}) collective-permute-start(bf16[768,512]{1,0:T(8,128)(2,1)S(1)} %get-tuple-element.45), channel_id=1, source_target_pairs={{0,4},{4,8},{1,5},{5,9},{2,6},{6,10},{3,7},{7,11},{16,20},{20,24},... | collective-permute-start | bytes 2359304 | tf_op jit(solution)/shard_map/ppermute | solution.py:622
  14.6 3.7 %pack_second.1 = (bf16[768,512]{1,0:T(8,128)(2,1)}, bf16[1152,512]{1,0:T(8,128)(2,1)}, bf16[1152,256]{1,0:T(8,128)(2,1)}, bf16[768,256]{1,0:T(8,128)(2,1)S(1)}) custom-call(s32[12]{0:T(128)S(1)} %bitcast_add_fusion.scalars, bf16[384,2560]{1,0:T(8,128)(2,1)} %refs_6_.1, bf16[192,2560]{1,0:T(8,128)(2,1)} %refs_7_.1, bf16[192,2560]{1,0:T(8,128)(2,1)} %refs_8_.1, ...), custom_call_target="tpu_custom_call" | custom-call | bytes 5898240 | tf_op jit(solution)/shard_map/pack_second/pallas_call | solution.py:276
  18.2 0.8 copy-done.3
  19.0 1.7 %collective-permute-start.3 = (bf16[1152,512]{1,0:T(8,128)(2,1)}, bf16[1152,512]{1,0:T(8,128)(2,1)}, u32[]{:S(2)}, u32[]{:S(2)}) collective-permute-start(bf16[1152,512]{1,0:T(8,128)(2,1)} %get-tuple-element.41), channel_id=1, source_target_pairs={{12,4},{13,5},{14,6},{15,7},{28,20},{29,21},{30,22},{31,23}} | collective-permute-start | bytes 3538952 | tf_op jit(solution)/shard_map/ppermute | solution.py:622
  21.1 0.9 fusion
  22.4 2.0 %collective-permute-start.6 = (f32[40,128]{0,1:T(8,128)S(1)}, f32[40,128]{0,1:T(8,128)S(1)}, u32[]{:S(2)}, u32[]{:S(2)}) collective-permute-start(f32[40,128]{0,1:T(8,128)S(1)} %copy.39), channel_id=1, source_target_pairs={{0,2},{2,0},{1,3},{3,1},{4,6},{6,4},{5,7},{7,5},{8,10},{10,8},{9,1... | collective-permute-start | bytes 61448 | tf_op jit(solution)/shard_map/ppermute | solution.py:762
  24.3 7.2 %collective-permute-done.1.refs_6_.refs_12_ = bf16[768,512]{1,0:T(8,128)(2,1)S(1)} collective-permute-done((bf16[768,512]{1,0:T(8,128)(2,1)S(1)}, bf16[768,512]{1,0:T(8,128)(2,1)S(1)}, u32[]{:S(2)}, u32[]{:S(2)}) %collective-permute-start.1) | collective-permute-done | bytes 786464 | tf_op jit(solution)/shard_map/ppermute | solution.py:622
  31.6 6.4 %collective-permute-start.9 = (bf16[768,512]{1,0:T(8,128)(2,1)}, bf16[768,512]{1,0:T(8,128)(2,1)}, u32[]{:S(2)}, u32[]{:S(2)}) collective-permute-start(bf16[768,512]{1,0:T(8,128)(2,1)} %get-tuple-element.57), channel_id=1, source_target_pairs={{0,8},{1,9},{2,10},{3,11},{16,24},{17,25},{18,26},{19,27}} | collective-permute-start | bytes 2359304 | tf_op jit(solution)/shard_map/ppermute | solution.py:622
  38.8 1.3 %collective-permute-start.4 = (bf16[1152,256]{1,0:T(8,128)(2,1)}, bf16[1152,256]{1,0:T(8,128)(2,1)}, u32[]{:S(2)}, u32[]{:S(2)}) collective-permute-start(bf16[1152,256]{1,0:T(8,128)(2,1)} %get-tuple-element.48), channel_id=1, source_target_pairs={{8,12},{4,0},{9,13},{5,1},{10,14},{6,2},{11,15},{7,3},{24,28},{20,... | collective-permute-start | bytes 1769480 | tf_op jit(solution)/shard_map/ppermute | solution.py:622
  40.1 1.0 copy-done.2
  42.6 0.9 pad_maximum_fusion
  43.5 0.8 slice.63
  44.3 1.0 reshape.33
  45.3 0.8 fusion.33.constants
  46.2 2.1 %collective-permute-start.8 = (bf16[768,256]{1,0:T(8,128)(2,1)}, bf16[768,256]{1,0:T(8,128)(2,1)}, u32[]{:S(2)}, u32[]{:S(2)}) collective-permute-start(bf16[768,256]{1,0:T(8,128)(2,1)} %copy-done.3), channel_id=1, source_target_pairs={{0,12},{1,13},{2,14},{3,15},{16,28},{17,29},{18,30},{19,31}} | collective-permute-start | bytes 1179656 | tf_op jit(solution)/shard_map/ppermute | solution.py:622
  48.2 1.4 %collective-permute-start.7 = (bf16[768,256]{1,0:T(8,128)(2,1)}, bf16[768,256]{1,0:T(8,128)(2,1)}, u32[]{:S(2)}, u32[]{:S(2)}) collective-permute-start(bf16[768,256]{1,0:T(8,128)(2,1)} %copy-done.3), channel_id=1, source_target_pairs={{4,12},{5,13},{6,14},{7,15},{20,28},{21,29},{22,30},{23,31}} | collective-permute-start | bytes 1179656 | tf_op jit(solution)/shard_map/ppermute | solution.py:622
  51.1 4.4 %collective-permute-done.9.refs_8_ = bf16[768,512]{1,0:T(8,128)(2,1)} collective-permute-done((bf16[768,512]{1,0:T(8,128)(2,1)}, bf16[768,512]{1,0:T(8,128)(2,1)}, u32[]{:S(2)}, u32[]{:S(2)}) %collective-permute-start.9) | collective-permute-done | bytes 786464 | tf_op jit(solution)/shard_map/ppermute | solution.py:622
  55.5 9.5 %main_heads.1 = (f32[3,40,384]{2,1,0:T(8,128)}, f32[3,40,384]{2,1,0:T(8,128)}) custom-call(s32[12]{0:T(128)S(1)} %bitcast_add_fusion.scalars, s32[16]{0:T(128)S(1)} %reshape.30.mask, bf16[384,2560]{1,0:T(8,128)(2,1)} %refs_6_.1, bf16[192,2560]{1,0:T(8,128)(2,1)} %refs_7_.1, bf16[192,2560]{1,0:T(8,128)(2,1)} %refs_8_.1, ...), custom_call_target="tpu_custom_call" | custom-call | flops 2113929216 | bytes 1179648 | tf_op jit(solution)/shard_map/main_heads/pallas_call | solution.py:586
  65.0 10.1 %final_heads.1 = (f32[3,40,384]{2,1,0:T(8,128)}, f32[3,40,384]{2,1,0:T(8,128)}) custom-call(s32[12]{0:T(128)S(1)} %bitcast_add_fusion.scalars, s32[16]{0:T(128)S(1)} %reshape.30.mask, bf16[384,2560]{1,0:T(8,128)(2,1)} %refs_6_.1, bf16[192,2560]{1,0:T(8,128)(2,1)} %refs_7_.1, ...), custom_call_target="tpu_custom_call", output_to_operand_aliasing={{0}: (20, {}), {1}: (21, {})} | custom-call | flops 4831838208 | bytes 1179648 | tf_op jit(solution)/shard_map/final_heads/pallas_call | solution.py:586
  75.3 1.6 %collective-permute-done.10 = f32[3,40,384]{2,1,0:T(8,128)S(1)} collective-permute-done((f32[3,40,384]{2,1,0:T(8,128)}, f32[3,40,384]{2,1,0:T(8,128)S(1)}, u32[]{:S(2)}, u32[]{:S(2)}) %collective-permute-start.10) | collective-permute-done | bytes 184352 | tf_op jit(solution)/shard_map/ppermute | solution.py:970
  76.9 1.0 add.84
  77.9 2.0 %collective-permute-start.12 = (f32[40,256]{1,0:T(8,128)S(1)}, f32[40,256]{1,0:T(8,128)S(1)}, u32[]{:S(2)}, u32[]{:S(2)}) collective-permute-start(f32[40,256]{1,0:T(8,128)S(1)} %slice.71), channel_id=1, source_target_pairs={{0,8},{4,12},{1,9},{5,13},{2,10},{6,14},{3,11},{7,15},{16,24},{20,... | collective-permute-start | bytes 122888 | tf_op jit(solution)/shard_map/ppermute | solution.py:981
  80.6 12.0 %collective-permute-start.11 = (f32[56,640]{1,0:T(8,128)S(1)}, f32[56,640]{1,0:T(8,128)S(1)}, u32[]{:S(2)}, u32[]{:S(2)}) collective-permute-start(f32[56,640]{1,0:T(8,128)S(1)} %pad_maximum_fusion.1), channel_id=1, source_target_pairs={{0,4},{4,8},{8,12},{1,5},{5,9},{9,13},{2,6},{6,10},{10,14},{3,7},{... | collective-permute-start | bytes 430088 | tf_op jit(solution)/shard_map/ppermute | solution.py:973
  92.6 3.0 %collective-permute-done.11 = f32[56,640]{1,0:T(8,128)S(1)} collective-permute-done((f32[56,640]{1,0:T(8,128)S(1)}, f32[56,640]{1,0:T(8,128)S(1)}, u32[]{:S(2)}, u32[]{:S(2)}) %collective-permute-start.11) | collective-permute-done | bytes 143392 | tf_op jit(solution)/shard_map/ppermute | solution.py:973
  95.6 1.6 %collective-permute-start.14 = (f32[40,640]{1,0:T(8,128)S(1)}, f32[40,640]{1,0:T(8,128)S(1)}, u32[]{:S(2)}, u32[]{:S(2)}) collective-permute-start(f32[40,640]{1,0:T(8,128)S(1)} %fusion.32), channel_id=1, source_target_pairs={{0,2},{2,0},{1,3},{3,1},{4,6},{6,4},{5,7},{7,5},{8,10},{10,8},{9,1... | collective-permute-start | bytes 307208 | tf_op jit(solution)/shard_map/ppermute | solution.py:984
  97.2 3.2 %collective-permute-done.14 = f32[40,640]{1,0:T(8,128)S(1)} collective-permute-done((f32[40,640]{1,0:T(8,128)S(1)}, f32[40,640]{1,0:T(8,128)S(1)}, u32[]{:S(2)}, u32[]{:S(2)}) %collective-permute-start.14) | collective-permute-done | bytes 102432 | tf_op jit(solution)/shard_map/ppermute | solution.py:984
  100.6 1.2 %collective-permute-done.15.other = f32[40,640]{1,0:T(8,128)S(1)} collective-permute-done((f32[40,640]{1,0:T(8,128)S(1)}, f32[40,640]{1,0:T(8,128)S(1)}, u32[]{:S(2)}, u32[]{:S(2)}) %collective-permute-start.15) | collective-permute-done | bytes 102432 | tf_op jit(solution)/shard_map/ppermute | solution.py:985
  101.8 2.4 %finish.1 = (f32[3,8,16,16]{3,2,1,0:T(8,128)}, bf16[3,8,16,384]{3,2,1,0:T(8,128)(2,1)}) custom-call(s32[12]{0:T(128)S(1)} %bitcast_add_fusion.scalars, f32[40,640]{1,0:T(8,128)S(1)} %add.87.mine, f32[40,640]{1,0:T(8,128)S(1)} %collective-permute-done.15.other, f32[320,48]{1,0:T(8,128)S(1)} %bitcast.33, f32[320,32]{1,0:T(8,128)S(1)} %reshape.34.before, ...), custom_call_target="tpu_custom_call" | custom-call | tf_op jit(solution)/shard_map/finish/pallas_call | solution.py:892
  (62 shorter events, 7.4 us)
Async XLA Ops:
  0.6 37.4 %copy-start = (f32[384]{0:T(512)S(1)}, f32[384]{0:T(512)}, u32[]{:S(2)}) copy-start(f32[384]{0:T(512)} %param.21) | copy-start | bytes 4612
  0.6 1.8 %copy-start.8 = (s32[12]{0:T(128)S(1)}, s32[12]{0:T(128)}, u32[]{:S(2)}) copy-start(s32[12]{0:T(128)} %constant.107.clone) | copy-start | bytes 148
  1.9 2.7 %collective-permute-start = (bf16[384,1280]{1,0:T(8,128)(2,1)S(1)}, bf16[384,1280]{1,0:T(8,128)(2,1)S(1)}, u32[]{:S(2)}, u32[]{:S(2)}) collective-permute-start(bf16[384,1280]{1,0:T(8,128)(2,1)S(1)} %pack_handed.1), channel_id=1, source_target_pairs={{0,1},{1,0},{2,3},{3,2},{4,5},{5,4},{6,7},{7,6},{8,9},{9,8},{10,11... | collective-permute-start | bytes 2949128 | tf_op jit(solution)/shard_map/ppermute | solution.py:639
  7.6 40.7 %collective-permute-start.2 = (bf16[1152,512]{1,0:T(8,128)(2,1)}, bf16[1152,512]{1,0:T(8,128)(2,1)}, u32[]{:S(2)}, u32[]{:S(2)}) collective-permute-start(bf16[1152,512]{1,0:T(8,128)(2,1)} %get-tuple-element.39), channel_id=1, source_target_pairs={{4,0},{8,4},{12,8},{5,1},{9,5},{13,9},{6,2},{10,6},{14,10},{7,3},{... | collective-permute-start | bytes 3538952 | tf_op jit(solution)/shard_map/ppermute | solution.py:622
  8.9 11.8 %copy-start.6 = (f32[3,8,16,16]{3,2,1,0:T(8,128)S(1)}, f32[3,8,16,16]{3,2,1,0:T(8,128)}, u32[]{:S(2)}) copy-start(f32[3,8,16,16]{3,2,1,0:T(8,128)} %param.19) | copy-start | bytes 73732
  8.9 12.2 %copy-start.1 = (bf16[2560,64]{0,1:T(8,128)(2,1)S(1)}, bf16[2560,64]{0,1:T(8,128)(2,1)}, u32[]{:S(2)}) copy-start(bf16[2560,64]{0,1:T(8,128)(2,1)} %param.18) | copy-start | bytes 983044
  8.9 22.7 %collective-permute-start.1 = (bf16[768,512]{1,0:T(8,128)(2,1)S(1)}, bf16[768,512]{1,0:T(8,128)(2,1)S(1)}, u32[]{:S(2)}, u32[]{:S(2)}) collective-permute-start(bf16[768,512]{1,0:T(8,128)(2,1)S(1)} %get-tuple-element.45), channel_id=1, source_target_pairs={{0,4},{4,8},{1,5},{5,9},{2,6},{6,10},{3,7},{7,11},{16,20},{20,24},... | collective-permute-start | bytes 2359304 | tf_op jit(solution)/shard_map/ppermute | solution.py:622
  18.2 0.8 copy-start.3
  19.0 46.0 %collective-permute-start.3 = (bf16[1152,512]{1,0:T(8,128)(2,1)}, bf16[1152,512]{1,0:T(8,128)(2,1)}, u32[]{:S(2)}, u32[]{:S(2)}) collective-permute-start(bf16[1152,512]{1,0:T(8,128)(2,1)} %get-tuple-element.41), channel_id=1, source_target_pairs={{12,4},{13,5},{14,6},{15,7},{28,20},{29,21},{30,22},{31,23}} | collective-permute-start | bytes 3538952 | tf_op jit(solution)/shard_map/ppermute | solution.py:622
  21.0 1.2 %collective-permute-start.5 = (f32[8,48]{1,0:T(8,128)S(1)}, f32[8,48]{1,0:T(8,128)S(1)}, u32[]{:S(2)}, u32[]{:S(2)}) collective-permute-start(f32[8,48]{1,0:T(8,128)S(1)} %bitcast.43), channel_id=1, source_target_pairs={{0,1},{1,0},{2,3},{3,2},{4,5},{5,4},{6,7},{7,6},{8,9},{9,8},{10,11... | collective-permute-start | bytes 4616 | tf_op jit(solution)/shard_map/ppermute | solution.py:747
  22.2 16.6 %copy-start.5 = (f32[8,14,48]{2,1,0:T(8,128)}, f32[8,14,48]{2,1,0:T(8,128)S(1)}, u32[]{:S(2)}) copy-start(f32[8,14,48]{2,1,0:T(8,128)S(1)} %broadcast_in_dim.26) | copy-start | bytes 64516
  22.4 18.9 %collective-permute-start.6 = (f32[40,128]{0,1:T(8,128)S(1)}, f32[40,128]{0,1:T(8,128)S(1)}, u32[]{:S(2)}, u32[]{:S(2)}) collective-permute-start(f32[40,128]{0,1:T(8,128)S(1)} %copy.39), channel_id=1, source_target_pairs={{0,2},{2,0},{1,3},{3,1},{4,6},{6,4},{5,7},{7,5},{8,10},{10,8},{9,1... | collective-permute-start | bytes 61448 | tf_op jit(solution)/shard_map/ppermute | solution.py:762
  31.6 7.2 %copy-start.4 = (bf16[768,512]{1,0:T(8,128)(2,1)}, bf16[768,512]{1,0:T(8,128)(2,1)S(1)}, u32[]{:S(2)}) copy-start(bf16[768,512]{1,0:T(8,128)(2,1)S(1)} %collective-permute-done.1.refs_6_.refs_12_) | copy-start | bytes 2359300
  31.6 23.9 %collective-permute-start.9 = (bf16[768,512]{1,0:T(8,128)(2,1)}, bf16[768,512]{1,0:T(8,128)(2,1)}, u32[]{:S(2)}, u32[]{:S(2)}) collective-permute-start(bf16[768,512]{1,0:T(8,128)(2,1)} %get-tuple-element.57), channel_id=1, source_target_pairs={{0,8},{1,9},{2,10},{3,11},{16,24},{17,25},{18,26},{19,27}} | collective-permute-start | bytes 2359304 | tf_op jit(solution)/shard_map/ppermute | solution.py:622
  38.8 26.2 %collective-permute-start.4 = (bf16[1152,256]{1,0:T(8,128)(2,1)}, bf16[1152,256]{1,0:T(8,128)(2,1)}, u32[]{:S(2)}, u32[]{:S(2)}) collective-permute-start(bf16[1152,256]{1,0:T(8,128)(2,1)} %get-tuple-element.48), channel_id=1, source_target_pairs={{8,12},{4,0},{9,13},{5,1},{10,14},{6,2},{11,15},{7,3},{24,28},{20,... | collective-permute-start | bytes 1769480 | tf_op jit(solution)/shard_map/ppermute | solution.py:622
  40.1 1.0 copy-start.2
  41.2 0.7 copy-start.7
  46.2 18.8 %collective-permute-start.8 = (bf16[768,256]{1,0:T(8,128)(2,1)}, bf16[768,256]{1,0:T(8,128)(2,1)}, u32[]{:S(2)}, u32[]{:S(2)}) collective-permute-start(bf16[768,256]{1,0:T(8,128)(2,1)} %copy-done.3), channel_id=1, source_target_pairs={{0,12},{1,13},{2,14},{3,15},{16,28},{17,29},{18,30},{19,31}} | collective-permute-start | bytes 1179656 | tf_op jit(solution)/shard_map/ppermute | solution.py:622
  48.2 16.8 %collective-permute-start.7 = (bf16[768,256]{1,0:T(8,128)(2,1)}, bf16[768,256]{1,0:T(8,128)(2,1)}, u32[]{:S(2)}, u32[]{:S(2)}) collective-permute-start(bf16[768,256]{1,0:T(8,128)(2,1)} %copy-done.3), channel_id=1, source_target_pairs={{4,12},{5,13},{6,14},{7,15},{20,28},{21,29},{22,30},{23,31}} | collective-permute-start | bytes 1179656 | tf_op jit(solution)/shard_map/ppermute | solution.py:622
  75.2 1.7 %collective-permute-start.10 = (f32[3,40,384]{2,1,0:T(8,128)}, f32[3,40,384]{2,1,0:T(8,128)S(1)}, u32[]{:S(2)}, u32[]{:S(2)}) collective-permute-start(f32[3,40,384]{2,1,0:T(8,128)} %get-tuple-element.69), channel_id=1, source_target_pairs={{0,1},{1,0},{2,3},{3,2},{4,5},{5,4},{6,7},{7,6},{8,9},{9,8},{10,11... | collective-permute-start | bytes 552968 | tf_op jit(solution)/shard_map/ppermute | solution.py:970
  77.9 14.8 %collective-permute-start.12 = (f32[40,256]{1,0:T(8,128)S(1)}, f32[40,256]{1,0:T(8,128)S(1)}, u32[]{:S(2)}, u32[]{:S(2)}) collective-permute-start(f32[40,256]{1,0:T(8,128)S(1)} %slice.71), channel_id=1, source_target_pairs={{0,8},{4,12},{1,9},{5,13},{2,10},{6,14},{3,11},{7,15},{16,24},{20,... | collective-permute-start | bytes 122888 | tf_op jit(solution)/shard_map/ppermute | solution.py:981
  79.9 12.8 %collective-permute-start.13 = (f32[40,384]{1,0:T(8,128)S(1)}, f32[40,384]{1,0:T(8,128)S(1)}, u32[]{:S(2)}, u32[]{:S(2)}) collective-permute-start(f32[40,384]{1,0:T(8,128)S(1)} %get-tuple-element.78), channel_id=1, source_target_pairs={{4,12},{12,8},{5,13},{13,9},{6,14},{14,10},{7,15},{15,11},{20,28},... | collective-permute-start | bytes 184328 | tf_op jit(solution)/shard_map/ppermute | solution.py:980
  80.6 15.1 %collective-permute-start.11 = (f32[56,640]{1,0:T(8,128)S(1)}, f32[56,640]{1,0:T(8,128)S(1)}, u32[]{:S(2)}, u32[]{:S(2)}) collective-permute-start(f32[56,640]{1,0:T(8,128)S(1)} %pad_maximum_fusion.1), channel_id=1, source_target_pairs={{0,4},{4,8},{8,12},{1,5},{5,9},{9,13},{2,6},{6,10},{10,14},{3,7},{... | collective-permute-start | bytes 430088 | tf_op jit(solution)/shard_map/ppermute | solution.py:973
  95.6 4.7 %collective-permute-start.14 = (f32[40,640]{1,0:T(8,128)S(1)}, f32[40,640]{1,0:T(8,128)S(1)}, u32[]{:S(2)}, u32[]{:S(2)}) collective-permute-start(f32[40,640]{1,0:T(8,128)S(1)} %fusion.32), channel_id=1, source_target_pairs={{0,2},{2,0},{1,3},{3,1},{4,6},{6,4},{5,7},{7,5},{8,10},{10,8},{9,1... | collective-permute-start | bytes 307208 | tf_op jit(solution)/shard_map/ppermute | solution.py:984
  100.4 1.4 %collective-permute-start.15 = (f32[40,640]{1,0:T(8,128)S(1)}, f32[40,640]{1,0:T(8,128)S(1)}, u32[]{:S(2)}, u32[]{:S(2)}) collective-permute-start(f32[40,640]{1,0:T(8,128)S(1)} %add.87.mine), channel_id=1, source_target_pairs={{0,1},{1,0},{2,3},{3,2},{4,5},{5,4},{6,7},{7,6},{8,9},{9,8},{10,11... | collective-permute-start | bytes 307208 | tf_op jit(solution)/shard_map/ppermute | solution.py:985

commit v13 on v11

--- a/solution.py
+++ b/solution.py
@@ -242,9 +242,9 @@
     by_place[:, DOWN] = [MIDDLE, MIDDLE, 0, MIDDLE]
     by_place[:, UP] = [0, MIDDLE, 0, 0]
     by_place[:, MAIN] = [MIDDLE, 0, MIDDLE, 0]
-    by_place[:, MAIN_CAP] = [3, 3, 3, 0]
+    by_place[:, MAIN_CAP] = [1, 1, 1, 0]
     by_place[:, FINAL] = [FAR, 0, 0, FAR]
-    by_place[:, FINAL_CAP] = [1, 3, 0, 1]
+    by_place[:, FINAL_CAP] = [0, 1, 0, 0]
     by_place[:, PLACE] = range(4)
     by_slab = np.zeros(12, np.int32)
     by_slab[[OWN, OTHER, SLAB]] = heads, -heads, 1
@@ -355,7 +355,7 @@
 OWN_TOKENS = Tokens()
 
 
-def attend_kernel(variants, extra, span_count, fresh, scalars, mask, *refs):
+def attend_kernel(variants, extra, span_count, fresh, wide, scalars, mask, *refs):
     query_own, key_own, value_own, received, weight, gain = refs[:6]
     more = refs[6 : 6 + extra]
     mine_out, theirs_out, folded, squares, carried, moved = refs[-6:]
@@ -390,41 +390,47 @@
         for fetch in fetches:
             fetch.start()
 
-    def query_of(source):
+    def lanes_of(head):
+        return slice(head * HD, (head + 1) * HD)
+
+    def query_of(source, lanes):
         if source is OWN_TOKENS:
-            return query_own[...]
+            return query_own[:, lanes]
         if source.extra is not None:
-            return more[0][:, source.extra * HD : (source.extra + 1) * HD]
-        return payloads[source.query][:rows]
-
-    def pair_of(source):
+            return more[0][:, lanes_of(source.extra)]
+        return payloads[source.query][:rows, lanes]
+
+    def pair_of(source, lanes):
         if source is OWN_TOKENS:
-            parts = (key_own[...], received[:half], value_own[...], received[half:])
+            parts = (
+                key_own[:, lanes],
+                received[:half, lanes],
+                value_own[:, lanes],
+                received[half:, lanes],
+            )
         elif source.extra is not None:
-            lanes = slice(source.extra * HD, (source.extra + 1) * HD)
-            parts = (more[1][:, lanes], more[3][:half, lanes], more[2][:, lanes], more[3][half:, lanes])
-        elif len(source.pairs) == 2:
-            one, two = (payloads[number] for number in source.pairs)
-            parts = (one[:half], two[:half], one[half:], two[half:])
+            own = lanes_of(source.extra)
+            parts = (more[1][:, own], more[3][:half, own], more[2][:, own], more[3][half:, own])
         else:
             payload = payloads[source.pairs[0]]
             start = payload.shape[0] - 2 * rows
-            return payload[start : start + rows], payload[start + rows :]
+            return payload[start : start + rows, lanes], payload[start + rows :, lanes]
         return jnp.concatenate(parts[:2], axis=0), jnp.concatenate(parts[2:], axis=0)
 
-    def projector(extra_head):
+    def projector(extra_head, lanes):
         if extra_head is None:
-            scaled = weight[...].astype(jnp.float32) * gain[...]
+            scaled = weight[:, lanes].astype(jnp.float32) * gain[:, lanes]
         else:
-            lanes = slice(extra_head * HD, (extra_head + 1) * HD)
-            scaled = more[4][:, lanes].astype(jnp.float32) * more[5][:, lanes]
+            own = lanes_of(extra_head)
+            scaled = more[4][:, own].astype(jnp.float32) * more[5][:, own]
         high = scaled.astype(jnp.bfloat16)
         low = (scaled - high.astype(jnp.float32)).astype(jnp.bfloat16)
         return jnp.concatenate([high, low, jnp.ones((16, HD), jnp.bfloat16)], axis=0)
 
-    def one_query(source, slot, query_span, key_sources):
-        query = query_of(source)
-        pairs = [pair_of(key_source) for key_source, _ in key_sources]
+    def one_query(head, source, slot, query_span, key_sources):
+        lanes = lanes_of(head)
+        query = query_of(source, lanes)
+        pairs = [pair_of(key_source, lanes) for key_source, _ in key_sources]
         open_to = [
             None if key_span == query_span else mask[query_span * span_count + key_span] > 0
             for _, key_span in key_sources
@@ -465,7 +471,7 @@
             pieces.append((both[:, :HD] / both[:, HD:]).astype(jnp.bfloat16))
         attended = jnp.concatenate(pieces, axis=0)
         folded[slot] += lax.dot_general(
-            projector(source.extra),
+            projector(source.extra, lanes),
             attended,
             (((1,), (1,)), ((), ())),
             preferred_element_type=jnp.float32,
@@ -473,12 +479,15 @@
         wide = attended.astype(jnp.float32)
         squares[slot] += wide * wide
 
-    for place, (steps, tasks) in variants.items():
-
-        @pl.when((scalars[PLACE] == place) & (step < steps))
-        def _():
-            for task in tasks:
-                one_query(*task)
+    for place, groups in variants.items():
+        for steps, tasks in groups:
+
+            @pl.when((scalars[PLACE] == place) & (step < steps))
+            def _():
+                for head in range(wide):
+                    for task in tasks:
+                        if head == 0 or task[0].extra is None:
+                            one_query(head, *task)
 
     def store():
         copies = [
@@ -525,17 +534,19 @@
                 axis=0,
             )
 
-        for place, (_, tasks) in variants.items():
+        for place, groups in variants.items():
 
             @pl.when(scalars[PLACE] == place)
             def _():
-                for slot in sorted({task[1] for task in tasks}):
+                for slot in sorted({task[1] for _, tasks in groups for task in tasks}):
                     finish_slot(slot)
 
         store()
 
 
-def attend(steps, first, cap, own, scalars, mask, sums, payloads, variants, more, name, cost=1):
+def attend(
+    steps, wide, first, cap, own, scalars, mask, sums, payloads, variants, more, name, cost=1
+):
     queries, keys, values, received, weight, gain = own
     rows = queries.shape[0]
     half = rows // 2
@@ -546,25 +557,24 @@
 
     def column(height, own_column):
         def index(i, scalars, mask):
-            head = scalars[first] + moving(i, scalars)
-            return (0, head + scalars[OWN] if own_column else head)
-
-        return pl.BlockSpec((height, HD), index)
+            head = scalars[first] + scalars[OWN] if own_column else scalars[first]
+            return (0, head // wide + moving(i, scalars))
+
+        return pl.BlockSpec((height, wide * HD), index)
 
     def two_columns(height, own_column):
         def index(i, scalars, mask):
-            pair = jnp.minimum(moving(i, scalars), 1)
-            return (0, pair + scalars[OWN] // 2 if own_column else pair)
+            return (0, i + scalars[OWN] // 2 if own_column else i)
 
         return pl.BlockSpec((height, 2 * HD), index)
 
     def payload_column(payload):
-        last = payload.shape[1] // HD - 1
+        last = payload.shape[1] // (wide * HD) - 1
 
         def index(i, scalars, mask):
             return (0, jnp.minimum(moving(i, scalars), last))
 
-        return pl.BlockSpec((payload.shape[0], HD), index)
+        return pl.BlockSpec((payload.shape[0], wide * HD), index)
 
     in_specs = [
         column(rows, True),
@@ -597,11 +607,12 @@
         in_specs += [pl.BlockSpec(memory_space=pl.ANY)] * 2
         arrays += sums
     pairs = max(
-        count * sum(len(task[3]) for task in tasks) for count, tasks in variants.values()
+        sum(count * wide * sum(len(task[3]) for task in tasks) for count, tasks in groups)
+        for groups in variants.values()
     )
     span_count = math.isqrt(mask.shape[0])
     return pl.pallas_call(
-        functools.partial(attend_kernel, variants, extra, span_count, fresh),
+        functools.partial(attend_kernel, variants, extra, span_count, fresh, wide),
         name=name,
         out_shape=[pltpu.HBM((SLOTS, sums_shape[1] // 2, rows), jnp.float32)] * 2,
         input_output_aliases=aliases,
@@ -620,7 +631,7 @@
         compiler_params=pltpu.CompilerParams(vmem_limit_bytes=GRANT),
         cost_estimate=pl.CostEstimate(
             flops=cost * pairs * 4 * rows * rows * HD,
-            bytes_accessed=steps * HD * 2 * sum(spec.block_shape[0] for spec in in_specs[:4]),
+            bytes_accessed=steps * wide * HD * 2 * sum(spec.block_shape[0] for spec in in_specs[:4]),
             transcendentals=cost * pairs * rows * rows,
         ),
     )(scalars, mask, *arrays)
@@ -696,27 +707,32 @@
     here, back_one, on_one = OWN_TOKENS, Tokens(None, (0,)), Tokens(1, (1,))
     back_two = Tokens(None, (2,))
     sums = run(
-        MIDDLE_HEADS,
+        MIDDLE_HEADS // 2,
+        2,
         MAIN,
         MAIN_CAP,
         sums=None,
         payloads=[up, down, up_two],
         variants={
-            0: (4, [(here, 0, 0, [(here, 0)]), (on_one, 1, 1, [(here, 0), (on_one, 1)])]),
-            1: (
-                4,
-                [
-                    (on_one, 1, 2, [(back_one, 0), (here, 1), (on_one, 2)]),
-                    (here, 0, 1, [(back_one, 0), (here, 1)]),
-                ],
-            ),
-            2: (
-                4,
-                [
-                    (on_one, 1, 3, [(back_two, 0), (back_one, 1), (here, 2), (on_one, 3)]),
-                    (here, 0, 2, [(back_two, 0), (back_one, 1), (here, 2)]),
-                ],
-            ),
+            0: [(2, [(here, 0, 0, [(here, 0)]), (on_one, 1, 1, [(here, 0), (on_one, 1)])])],
+            1: [
+                (
+                    2,
+                    [
+                        (on_one, 1, 2, [(back_one, 0), (here, 1), (on_one, 2)]),
+                        (here, 0, 1, [(back_one, 0), (here, 1)]),
+                    ],
+                )
+            ],
+            2: [
+                (
+                    2,
+                    [
+                        (on_one, 1, 3, [(back_two, 0), (back_one, 1), (here, 2), (on_one, 3)]),
+                        (here, 0, 2, [(back_two, 0), (back_one, 1), (here, 2)]),
+                    ],
+                )
+            ],
         },
         more=False,
         name="main_heads",
@@ -726,28 +742,27 @@
     extras = [Tokens(None, (), lane) for lane in range(2)]
     sums, prepared = lax.optimization_barrier((sums, prepared))
     sums = run(
-        NEAR_HEADS,
+        NEAR_HEADS // 2,
+        2,
         FINAL,
         FINAL_CAP,
         sums=sums,
         payloads=[up, down, two, far_next, far_two, far_three],
         variants={
-            0: (
-                FAR_HEADS,
-                [(here, 0, 0, [(here, 0)]), (beside, 1, 1, [(here, 0), (beside, 1)])]
-                + [(head, 0, 0, [(head, 0)]) for head in extras],
-            ),
-            1: (
-                NEAR_HEADS,
-                [(on_two, 2, 3, [(back_one, 0), (here, 1), (on_one, 2), (on_two, 3)])],
-            ),
-            3: (
-                FAR_HEADS,
-                [
-                    (here, 0, 3, [(three_back, 0), (two_back, 1), (beside, 2), (here, 3)]),
-                    (beside, 2, 2, [(three_back, 0), (two_back, 1), (beside, 2)]),
-                ],
-            ),
+            0: [
+                (1, [(here, 0, 0, [(here, 0)]), (beside, 1, 1, [(here, 0), (beside, 1)])]),
+                (2, [(head, 0, 0, [(head, 0)]) for head in extras]),
+            ],
+            1: [(2, [(on_two, 2, 3, [(back_one, 0), (here, 1), (on_one, 2), (on_two, 3)])])],
+            3: [
+                (
+                    1,
+                    [
+                        (here, 0, 3, [(three_back, 0), (two_back, 1), (beside, 2), (here, 3)]),
+                        (beside, 2, 2, [(three_back, 0), (two_back, 1), (beside, 2)]),
+                    ],
+                )
+            ],
         },
         more=True,
         name="final_heads",

time: 101 us -> 101 us (level)
  no operation moved by 1% of the time
where the time goes in v13:
time: 101 us; the launch traced here: 99.8 us
  starting transfers between devices  38.3 us (38%)
  Pallas kernels  29.7 us (29%)
  waiting for transfers between devices  19.5 us (19%)
  local copies, waits for them, and re-layouts  6.84 us (7%)
  other arithmetic  4.44 us (4%)
  between operations  1.02 us (1%)
    ppermute x7, starting transfers between devices, send(): return in_place(lax.ppermute(value, 'span', list(pairs)))  21.3 us
    pallas_call x2, Pallas kernels, attend(): pl.pallas_call(functools.partial(attend_kernel, variants, extra, span_cou...  19.5 us
    ppermute x1, starting transfers between devices, per_device(): to_before = lax.ppermute(after[:, skip:], 'span', [(0, 2), (1, 3)])  11.2 us
    ppermute x7, waiting for transfers between devices, send(): return in_place(lax.ppermute(value, 'span', list(pairs)))  8.52 us
    pallas_call x2, Pallas kernels, pack(): pl.pallas_call(functools.partial(pack_kernel, len(arrays), len(shapes), c...  6.42 us
    ppermute x1, waiting for transfers between devices, per_device(): total = total + lax.ppermute(total, 'head', SWAP)  3.27 us
    ppermute x1, waiting for transfers between devices, per_device(): lax.ppermute(jnp.concatenate([jnp.concatenate([own[:, skip:], after], axi...  3.26 us
    pallas_call x1, Pallas kernels, finish(): pl.pallas_call(finish_kernel, name='finish', out_shape=(jax.ShapeDtypeStr...  2.4 us
  transfers between devices with their start and end apart: 16, of which 7 were waited for; matrix products, arithmetic and copies ran while one was open for 9% of the time, Pallas kernels for 13%

profile of v13, /device:TPU:0, one launch (start us, length us, event | category | flops | bytes accessed | tf_op | source)
XLA Modules:
  0.0 99.8 jit_solution(10881754711281880530)
XLA Ops:
  0.7 1.2 %pack_handed.1 = bf16[384,1280]{1,0:T(8,128)(2,1)S(1)} custom-call(bf16[192,2560]{1,0:T(8,128)(2,1)} %refs_7_.1, bf16[192,2560]{1,0:T(8,128)(2,1)} %refs_8_.1), custom_call_target="tpu_custom_call" | custom-call | bytes 1966080 | tf_op jit(solution)/shard_map/pack_handed/pallas_call | solution.py:324
  3.8 0.8 collective-permute-done.refs_3_.refs_9_
  4.6 2.9 %pack_first.1 = (bf16[768,512]{1,0:T(8,128)(2,1)}, bf16[1152,512]{1,0:T(8,128)(2,1)}) custom-call(s32[12]{0:T(128)S(1)} %bitcast_add_fusion.scalars, bf16[384,2560]{1,0:T(8,128)(2,1)} %refs_6_.1, bf16[192,2560]{1,0:T(8,128)(2,1)} %refs_7_.1, bf16[192,2560]{1,0:T(8,128)(2,1)} %refs_8_.1, bf16[384,1280]{1,0:T(8,128)(2,1)S(1)} %collective-permute-done.refs_3_.refs_9_), custom_call_target="tpu_custom_call" | custom-call | bytes 3932160 | tf_op jit(solution)/shard_map/pack_first/pallas_call | solution.py:286
  7.5 1.3 %collective-permute-start.2 = (bf16[1152,512]{1,0:T(8,128)(2,1)}, bf16[1152,512]{1,0:T(8,128)(2,1)}, u32[]{:S(2)}, u32[]{:S(2)}) collective-permute-start(bf16[1152,512]{1,0:T(8,128)(2,1)} %get-tuple-element.37), channel_id=1, source_target_pairs={{4,0},{8,4},{12,8},{5,1},{9,5},{13,9},{6,2},{10,6},{14,10},{7,3},{... | collective-permute-start | bytes 3538952 | tf_op jit(solution)/shard_map/ppermute | solution.py:650
  8.9 6.5 %collective-permute-start.1 = (bf16[768,512]{1,0:T(8,128)(2,1)}, bf16[768,512]{1,0:T(8,128)(2,1)}, u32[]{:S(2)}, u32[]{:S(2)}) collective-permute-start(bf16[768,512]{1,0:T(8,128)(2,1)} %get-tuple-element.43), channel_id=1, source_target_pairs={{0,4},{4,8},{1,5},{5,9},{2,6},{6,10},{3,7},{7,11},{16,20},{20,24},... | collective-permute-start | bytes 2359304 | tf_op jit(solution)/shard_map/ppermute | solution.py:650
  15.4 3.5 %pack_second.1 = (bf16[768,512]{1,0:T(8,128)(2,1)}, bf16[1152,512]{1,0:T(8,128)(2,1)}, bf16[1152,256]{1,0:T(8,128)(2,1)}, bf16[768,256]{1,0:T(8,128)(2,1)}) custom-call(s32[12]{0:T(128)S(1)} %bitcast_add_fusion.scalars, bf16[384,2560]{1,0:T(8,128)(2,1)} %refs_6_.1, bf16[192,2560]{1,0:T(8,128)(2,1)} %refs_7_.1, bf16[192,2560]{1,0:T(8,128)(2,1)} %refs_8_.1, ...), custom_call_target="tpu_custom_call" | custom-call | bytes 5898240 | tf_op jit(solution)/shard_map/pack_second/pallas_call | solution.py:286
  18.9 1.7 %collective-permute-start.3 = (bf16[1152,512]{1,0:T(8,128)(2,1)}, bf16[1152,512]{1,0:T(8,128)(2,1)}, u32[]{:S(2)}, u32[]{:S(2)}) collective-permute-start(bf16[1152,512]{1,0:T(8,128)(2,1)} %get-tuple-element.39), channel_id=1, source_target_pairs={{12,4},{13,5},{14,6},{15,7},{28,20},{29,21},{30,22},{31,23}} | collective-permute-start | bytes 3538952 | tf_op jit(solution)/shard_map/ppermute | solution.py:650
  21.0 2.7 %collective-permute-start.9 = (bf16[768,512]{1,0:T(8,128)(2,1)}, bf16[768,512]{1,0:T(8,128)(2,1)}, u32[]{:S(2)}, u32[]{:S(2)}) collective-permute-start(bf16[768,512]{1,0:T(8,128)(2,1)} %get-tuple-element.53), channel_id=1, source_target_pairs={{0,8},{1,9},{2,10},{3,11},{16,24},{17,25},{18,26},{19,27}} | collective-permute-start | bytes 2359304 | tf_op jit(solution)/shard_map/ppermute | solution.py:650
  24.1 1.6 %collective-permute-start.6 = (f32[40,128]{0,1:T(8,128)S(1)}, f32[40,128]{0,1:T(8,128)S(1)}, u32[]{:S(2)}, u32[]{:S(2)}) collective-permute-start(f32[40,128]{0,1:T(8,128)S(1)} %copy.39), channel_id=1, source_target_pairs={{0,2},{2,0},{1,3},{3,1},{4,6},{6,4},{5,7},{7,5},{8,10},{10,8},{9,1... | collective-permute-start | bytes 61448 | tf_op jit(solution)/shard_map/ppermute | solution.py:793
  26.4 1.0 copy-done.2
  27.6 0.9 collective-permute-done.6
  28.5 1.3 %collective-permute-start.4 = (bf16[1152,256]{1,0:T(8,128)(2,1)}, bf16[1152,256]{1,0:T(8,128)(2,1)}, u32[]{:S(2)}, u32[]{:S(2)}) collective-permute-start(bf16[1152,256]{1,0:T(8,128)(2,1)} %get-tuple-element.44), channel_id=1, source_target_pairs={{8,12},{4,0},{9,13},{5,1},{10,14},{6,2},{11,15},{7,3},{24,28},{20,... | collective-permute-start | bytes 1769480 | tf_op jit(solution)/shard_map/ppermute | solution.py:650
  31.1 0.9 pad_maximum_fusion
  32.0 0.8 slice.63
  32.8 1.0 %reshape.33 = f32[16,640]{1,0:T(8,128)S(1)} reshape(f32[320,32]{1,0:T(8,128)} %slice.63) | data formatting | bytes 81920 | tf_op jit(solution)/shard_map/reshape | solution.py:984
  33.8 0.8 fusion.33.constants
  34.7 6.4 %collective-permute-start.8 = (bf16[768,256]{1,0:T(8,128)(2,1)}, bf16[768,256]{1,0:T(8,128)(2,1)}, u32[]{:S(2)}, u32[]{:S(2)}) collective-permute-start(bf16[768,256]{1,0:T(8,128)(2,1)} %get-tuple-element.52), channel_id=1, source_target_pairs={{0,12},{1,13},{2,14},{3,15},{16,28},{17,29},{18,30},{19,31}} | collective-permute-start | bytes 1179656 | tf_op jit(solution)/shard_map/ppermute | solution.py:650
  41.1 8.5 %collective-permute-done.9.refs_8_ = bf16[768,512]{1,0:T(8,128)(2,1)} collective-permute-done((bf16[768,512]{1,0:T(8,128)(2,1)}, bf16[768,512]{1,0:T(8,128)(2,1)}, u32[]{:S(2)}, u32[]{:S(2)}) %collective-permute-start.9) | collective-permute-done | bytes 786464 | tf_op jit(solution)/shard_map/ppermute | solution.py:650
  49.6 1.4 %collective-permute-start.7 = (bf16[768,256]{1,0:T(8,128)(2,1)}, bf16[768,256]{1,0:T(8,128)(2,1)}, u32[]{:S(2)}, u32[]{:S(2)}) collective-permute-start(bf16[768,256]{1,0:T(8,128)(2,1)} %get-tuple-element.52), channel_id=1, source_target_pairs={{4,12},{5,13},{6,14},{7,15},{20,28},{21,29},{22,30},{23,31}} | collective-permute-start | bytes 1179656 | tf_op jit(solution)/shard_map/ppermute | solution.py:650
  51.0 0.8 reshape.30.mask
  51.7 0.7 broadcast_in_dim.24.refs_5_.refs_11_
  52.5 9.4 %main_heads.1 = (f32[3,40,384]{2,1,0:T(8,128)}, f32[3,40,384]{2,1,0:T(8,128)}) custom-call(s32[12]{0:T(128)S(1)} %bitcast_add_fusion.scalars, s32[16]{0:T(128)S(1)} %reshape.30.mask, bf16[384,2560]{1,0:T(8,128)(2,1)} %refs_6_.1, bf16[192,2560]{1,0:T(8,128)(2,1)} %refs_7_.1, bf16[192,2560]{1,0:T(8,128)(2,1)} %refs_8_.1, ...), custom_call_target="tpu_custom_call" | custom-call | flops 2113929216 | bytes 1179648 | tf_op jit(solution)/shard_map/main_heads/pallas_call | solution.py:614
  61.9 10.1 %final_heads.1 = (f32[3,40,384]{2,1,0:T(8,128)}, f32[3,40,384]{2,1,0:T(8,128)}) custom-call(s32[12]{0:T(128)S(1)} %bitcast_add_fusion.scalars, s32[16]{0:T(128)S(1)} %reshape.30.mask, bf16[384,2560]{1,0:T(8,128)(2,1)} %refs_6_.1, bf16[192,2560]{1,0:T(8,128)(2,1)} %refs_7_.1, ...), custom_call_target="tpu_custom_call", output_to_operand_aliasing={{0}: (20, {}), {1}: (21, {})} | custom-call | flops 4831838208 | bytes 1179648 | tf_op jit(solution)/shard_map/final_heads/pallas_call | solution.py:614
  72.1 1.6 %collective-permute-done.10 = f32[3,40,384]{2,1,0:T(8,128)S(1)} collective-permute-done((f32[3,40,384]{2,1,0:T(8,128)}, f32[3,40,384]{2,1,0:T(8,128)S(1)}, u32[]{:S(2)}, u32[]{:S(2)}) %collective-permute-start.10) | collective-permute-done | bytes 184352 | tf_op jit(solution)/shard_map/ppermute | solution.py:1001
  73.7 1.0 add.84
  74.7 11.2 %collective-permute-start.12 = (f32[40,256]{1,0:T(8,128)S(1)}, f32[40,256]{1,0:T(8,128)S(1)}, u32[]{:S(2)}, u32[]{:S(2)}) collective-permute-start(f32[40,256]{1,0:T(8,128)S(1)} %slice.71), channel_id=1, source_target_pairs={{0,8},{4,12},{1,9},{5,13},{2,10},{6,14},{3,11},{7,15},{16,24},{20,... | collective-permute-start | bytes 122888 | tf_op jit(solution)/shard_map/ppermute | solution.py:1012
  86.7 1.3 %collective-permute-start.11 = (f32[56,640]{1,0:T(8,128)S(1)}, f32[56,640]{1,0:T(8,128)S(1)}, u32[]{:S(2)}, u32[]{:S(2)}) collective-permute-start(f32[56,640]{1,0:T(8,128)S(1)} %pad_maximum_fusion.1), channel_id=1, source_target_pairs={{0,4},{4,8},{8,12},{1,5},{5,9},{9,13},{2,6},{6,10},{10,14},{3,7},{... | collective-permute-start | bytes 430088 | tf_op jit(solution)/shard_map/ppermute | solution.py:1004
  88.0 3.3 %collective-permute-done.11 = f32[56,640]{1,0:T(8,128)S(1)} collective-permute-done((f32[56,640]{1,0:T(8,128)S(1)}, f32[56,640]{1,0:T(8,128)S(1)}, u32[]{:S(2)}, u32[]{:S(2)}) %collective-permute-start.11) | collective-permute-done | bytes 143392 | tf_op jit(solution)/shard_map/ppermute | solution.py:1004
  91.3 1.5 %collective-permute-start.14 = (f32[40,640]{1,0:T(8,128)S(1)}, f32[40,640]{1,0:T(8,128)S(1)}, u32[]{:S(2)}, u32[]{:S(2)}) collective-permute-start(f32[40,640]{1,0:T(8,128)S(1)} %fusion.32), channel_id=1, source_target_pairs={{0,2},{2,0},{1,3},{3,1},{4,6},{6,4},{5,7},{7,5},{8,10},{10,8},{9,1... | collective-permute-start | bytes 307208 | tf_op jit(solution)/shard_map/ppermute | solution.py:1015
  92.8 3.3 %collective-permute-done.14 = f32[40,640]{1,0:T(8,128)S(1)} collective-permute-done((f32[40,640]{1,0:T(8,128)S(1)}, f32[40,640]{1,0:T(8,128)S(1)}, u32[]{:S(2)}, u32[]{:S(2)}) %collective-permute-start.14) | collective-permute-done | bytes 102432 | tf_op jit(solution)/shard_map/ppermute | solution.py:1015
  96.2 1.2 %collective-permute-done.15.other = f32[40,640]{1,0:T(8,128)S(1)} collective-permute-done((f32[40,640]{1,0:T(8,128)S(1)}, f32[40,640]{1,0:T(8,128)S(1)}, u32[]{:S(2)}, u32[]{:S(2)}) %collective-permute-start.15) | collective-permute-done | bytes 102432 | tf_op jit(solution)/shard_map/ppermute | solution.py:1016
  97.4 2.4 %finish.1 = (f32[3,8,16,16]{3,2,1,0:T(8,128)}, bf16[3,8,16,384]{3,2,1,0:T(8,128)(2,1)}) custom-call(s32[12]{0:T(128)S(1)} %bitcast_add_fusion.scalars, f32[40,640]{1,0:T(8,128)S(1)} %add.87.mine, f32[40,640]{1,0:T(8,128)S(1)} %collective-permute-done.15.other, f32[320,48]{1,0:T(8,128)S(1)} %bitcast.33, f32[320,32]{1,0:T(8,128)S(1)} %reshape.34.before, ...), custom_call_target="tpu_custom_call" | custom-call | tf_op jit(solution)/shard_map/finish/pallas_call | solution.py:923
  (62 shorter events, 5.9 us)
Async XLA Ops:
  0.6 25.1 %copy-start = (f32[384]{0:T(512)S(1)}, f32[384]{0:T(512)}, u32[]{:S(2)}) copy-start(f32[384]{0:T(512)} %param.21) | copy-start | bytes 4612
  0.6 1.8 %copy-start.8 = (s32[12]{0:T(128)S(1)}, s32[12]{0:T(128)}, u32[]{:S(2)}) copy-start(s32[12]{0:T(128)} %constant.107.clone) | copy-start | bytes 148
  1.9 2.7 %collective-permute-start = (bf16[384,1280]{1,0:T(8,128)(2,1)S(1)}, bf16[384,1280]{1,0:T(8,128)(2,1)S(1)}, u32[]{:S(2)}, u32[]{:S(2)}) collective-permute-start(bf16[384,1280]{1,0:T(8,128)(2,1)S(1)} %pack_handed.1), channel_id=1, source_target_pairs={{0,1},{1,0},{2,3},{3,2},{4,5},{5,4},{6,7},{7,6},{8,9},{9,8},{10,11... | collective-permute-start | bytes 2949128 | tf_op jit(solution)/shard_map/ppermute | solution.py:667
  7.5 45.0 %collective-permute-start.2 = (bf16[1152,512]{1,0:T(8,128)(2,1)}, bf16[1152,512]{1,0:T(8,128)(2,1)}, u32[]{:S(2)}, u32[]{:S(2)}) collective-permute-start(bf16[1152,512]{1,0:T(8,128)(2,1)} %get-tuple-element.37), channel_id=1, source_target_pairs={{4,0},{8,4},{12,8},{5,1},{9,5},{13,9},{6,2},{10,6},{14,10},{7,3},{... | collective-permute-start | bytes 3538952 | tf_op jit(solution)/shard_map/ppermute | solution.py:650
  8.8 11.8 %copy-start.4 = (f32[3,8,16,16]{3,2,1,0:T(8,128)S(1)}, f32[3,8,16,16]{3,2,1,0:T(8,128)}, u32[]{:S(2)}) copy-start(f32[3,8,16,16]{3,2,1,0:T(8,128)} %param.19) | copy-start | bytes 73732
  8.8 14.9 %copy-start.1 = (bf16[2560,64]{0,1:T(8,128)(2,1)S(1)}, bf16[2560,64]{0,1:T(8,128)(2,1)}, u32[]{:S(2)}) copy-start(bf16[2560,64]{0,1:T(8,128)(2,1)} %param.18) | copy-start | bytes 983044
  8.8 14.9 %copy-start.6 = (f32[2560]{0:T(1024)S(1)}, f32[2560]{0:T(1024)}, u32[]{:S(2)}) copy-start(f32[2560]{0:T(1024)} %param.16) | copy-start | bytes 30724
  8.8 14.8 %copy-start.7 = (f32[2560]{0:T(1024)S(1)}, f32[2560]{0:T(1024)}, u32[]{:S(2)}) copy-start(f32[2560]{0:T(1024)} %param.17) | copy-start | bytes 30724
  8.9 25.8 %collective-permute-start.1 = (bf16[768,512]{1,0:T(8,128)(2,1)}, bf16[768,512]{1,0:T(8,128)(2,1)}, u32[]{:S(2)}, u32[]{:S(2)}) collective-permute-start(bf16[768,512]{1,0:T(8,128)(2,1)} %get-tuple-element.43), channel_id=1, source_target_pairs={{0,4},{4,8},{1,5},{5,9},{2,6},{6,10},{3,7},{7,11},{16,20},{20,24},... | collective-permute-start | bytes 2359304 | tf_op jit(solution)/shard_map/ppermute | solution.py:650
  18.9 43.0 %collective-permute-start.3 = (bf16[1152,512]{1,0:T(8,128)(2,1)}, bf16[1152,512]{1,0:T(8,128)(2,1)}, u32[]{:S(2)}, u32[]{:S(2)}) collective-permute-start(bf16[1152,512]{1,0:T(8,128)(2,1)} %get-tuple-element.39), channel_id=1, source_target_pairs={{12,4},{13,5},{14,6},{15,7},{28,20},{29,21},{30,22},{31,23}} | collective-permute-start | bytes 3538952 | tf_op jit(solution)/shard_map/ppermute | solution.py:650
  20.9 3.1 %collective-permute-start.5 = (f32[8,48]{1,0:T(8,128)S(1)}, f32[8,48]{1,0:T(8,128)S(1)}, u32[]{:S(2)}, u32[]{:S(2)}) collective-permute-start(f32[8,48]{1,0:T(8,128)S(1)} %bitcast.43), channel_id=1, source_target_pairs={{0,1},{1,0},{2,3},{3,2},{4,5},{5,4},{6,7},{7,6},{8,9},{9,8},{10,11... | collective-permute-start | bytes 4616 | tf_op jit(solution)/shard_map/ppermute | solution.py:778
  21.0 28.6 %collective-permute-start.9 = (bf16[768,512]{1,0:T(8,128)(2,1)}, bf16[768,512]{1,0:T(8,128)(2,1)}, u32[]{:S(2)}, u32[]{:S(2)}) collective-permute-start(bf16[768,512]{1,0:T(8,128)(2,1)} %get-tuple-element.53), channel_id=1, source_target_pairs={{0,8},{1,9},{2,10},{3,11},{16,24},{17,25},{18,26},{19,27}} | collective-permute-start | bytes 2359304 | tf_op jit(solution)/shard_map/ppermute | solution.py:650
  24.0 1.7 %copy-start.3 = (f32[8,14,48]{2,1,0:T(8,128)}, f32[8,14,48]{2,1,0:T(8,128)S(1)}, u32[]{:S(2)}) copy-start(f32[8,14,48]{2,1,0:T(8,128)S(1)} %broadcast_in_dim.26) | copy-start | bytes 64516
  24.1 4.3 %collective-permute-start.6 = (f32[40,128]{0,1:T(8,128)S(1)}, f32[40,128]{0,1:T(8,128)S(1)}, u32[]{:S(2)}, u32[]{:S(2)}) collective-permute-start(f32[40,128]{0,1:T(8,128)S(1)} %copy.39), channel_id=1, source_target_pairs={{0,2},{2,0},{1,3},{3,1},{4,6},{6,4},{5,7},{7,5},{8,10},{10,8},{9,1... | collective-permute-start | bytes 61448 | tf_op jit(solution)/shard_map/ppermute | solution.py:793
  26.4 1.0 copy-start.2
  28.5 2.0 %copy-start.5 = (f32[40,128]{0,1:T(8,128)}, f32[40,128]{0,1:T(8,128)S(1)}, u32[]{:S(2)}) copy-start(f32[40,128]{0,1:T(8,128)S(1)} %collective-permute-done.6) | copy-start | bytes 61444
  28.5 33.5 %collective-permute-start.4 = (bf16[1152,256]{1,0:T(8,128)(2,1)}, bf16[1152,256]{1,0:T(8,128)(2,1)}, u32[]{:S(2)}, u32[]{:S(2)}) collective-permute-start(bf16[1152,256]{1,0:T(8,128)(2,1)} %get-tuple-element.44), channel_id=1, source_target_pairs={{8,12},{4,0},{9,13},{5,1},{10,14},{6,2},{11,15},{7,3},{24,28},{20,... | collective-permute-start | bytes 1769480 | tf_op jit(solution)/shard_map/ppermute | solution.py:650
  34.7 27.2 %collective-permute-start.8 = (bf16[768,256]{1,0:T(8,128)(2,1)}, bf16[768,256]{1,0:T(8,128)(2,1)}, u32[]{:S(2)}, u32[]{:S(2)}) collective-permute-start(bf16[768,256]{1,0:T(8,128)(2,1)} %get-tuple-element.52), channel_id=1, source_target_pairs={{0,12},{1,13},{2,14},{3,15},{16,28},{17,29},{18,30},{19,31}} | collective-permute-start | bytes 1179656 | tf_op jit(solution)/shard_map/ppermute | solution.py:650
  49.6 12.3 %collective-permute-start.7 = (bf16[768,256]{1,0:T(8,128)(2,1)}, bf16[768,256]{1,0:T(8,128)(2,1)}, u32[]{:S(2)}, u32[]{:S(2)}) collective-permute-start(bf16[768,256]{1,0:T(8,128)(2,1)} %get-tuple-element.52), channel_id=1, source_target_pairs={{4,12},{5,13},{6,14},{7,15},{20,28},{21,29},{22,30},{23,31}} | collective-permute-start | bytes 1179656 | tf_op jit(solution)/shard_map/ppermute | solution.py:650
  72.0 1.7 %collective-permute-start.10 = (f32[3,40,384]{2,1,0:T(8,128)}, f32[3,40,384]{2,1,0:T(8,128)S(1)}, u32[]{:S(2)}, u32[]{:S(2)}) collective-permute-start(f32[3,40,384]{2,1,0:T(8,128)} %get-tuple-element.65), channel_id=1, source_target_pairs={{0,1},{1,0},{2,3},{3,2},{4,5},{5,4},{6,7},{7,6},{8,9},{9,8},{10,11... | collective-permute-start | bytes 552968 | tf_op jit(solution)/shard_map/ppermute | solution.py:1001
  74.7 13.3 %collective-permute-start.12 = (f32[40,256]{1,0:T(8,128)S(1)}, f32[40,256]{1,0:T(8,128)S(1)}, u32[]{:S(2)}, u32[]{:S(2)}) collective-permute-start(f32[40,256]{1,0:T(8,128)S(1)} %slice.71), channel_id=1, source_target_pairs={{0,8},{4,12},{1,9},{5,13},{2,10},{6,14},{3,11},{7,15},{16,24},{20,... | collective-permute-start | bytes 122888 | tf_op jit(solution)/shard_map/ppermute | solution.py:1012
  86.0 2.0 %collective-permute-start.13 = (f32[40,384]{1,0:T(8,128)S(1)}, f32[40,384]{1,0:T(8,128)S(1)}, u32[]{:S(2)}, u32[]{:S(2)}) collective-permute-start(f32[40,384]{1,0:T(8,128)S(1)} %get-tuple-element.74), channel_id=1, source_target_pairs={{4,12},{12,8},{5,13},{13,9},{6,14},{14,10},{7,15},{15,11},{20,28},... | collective-permute-start | bytes 184328 | tf_op jit(solution)/shard_map/ppermute | solution.py:1011
  86.7 4.6 %collective-permute-start.11 = (f32[56,640]{1,0:T(8,128)S(1)}, f32[56,640]{1,0:T(8,128)S(1)}, u32[]{:S(2)}, u32[]{:S(2)}) collective-permute-start(f32[56,640]{1,0:T(8,128)S(1)} %pad_maximum_fusion.1), channel_id=1, source_target_pairs={{0,4},{4,8},{8,12},{1,5},{5,9},{9,13},{2,6},{6,10},{10,14},{3,7},{... | collective-permute-start | bytes 430088 | tf_op jit(solution)/shard_map/ppermute | solution.py:1004
  91.3 4.7 %collective-permute-start.14 = (f32[40,640]{1,0:T(8,128)S(1)}, f32[40,640]{1,0:T(8,128)S(1)}, u32[]{:S(2)}, u32[]{:S(2)}) collective-permute-start(f32[40,640]{1,0:T(8,128)S(1)} %fusion.32), channel_id=1, source_target_pairs={{0,2},{2,0},{1,3},{3,1},{4,6},{6,4},{5,7},{7,5},{8,10},{10,8},{9,1... | collective-permute-start | bytes 307208 | tf_op jit(solution)/shard_map/ppermute | solution.py:1015
  96.0 1.4 %collective-permute-start.15 = (f32[40,640]{1,0:T(8,128)S(1)}, f32[40,640]{1,0:T(8,128)S(1)}, u32[]{:S(2)}, u32[]{:S(2)}) collective-permute-start(f32[40,640]{1,0:T(8,128)S(1)} %add.87.mine), channel_id=1, source_target_pairs={{0,1},{1,0},{2,3},{3,2},{4,5},{5,4},{6,7},{7,6},{8,9},{9,8},{10,11... | collective-permute-start | bytes 307208 | tf_op jit(solution)/shard_map/ppermute | solution.py:1016

commit v14 on v13

--- a/solution.py
+++ b/solution.py
@@ -355,11 +355,17 @@
 OWN_TOKENS = Tokens()
 
 
-def attend_kernel(variants, extra, span_count, fresh, wide, scalars, mask, *refs):
-    query_own, key_own, value_own, received, weight, gain = refs[:6]
-    more = refs[6 : 6 + extra]
-    mine_out, theirs_out, folded, squares, carried, moved = refs[-6:]
-    payloads = refs[6 + extra : -6] if fresh else refs[6 + extra : -8]
+def attend_kernel(variants, extra, span_count, fresh, wide, final, scalars, mask, *refs):
+    if final:
+        sources, (weight, gain), brought = refs[:4], refs[4:6], refs[6 : 6 + final]
+        sums_in, (mine_out, theirs_out) = refs[6 + final : 8 + final], refs[8 + final : 10 + final]
+        folded, squares, carried, moved, *own_refs = refs[10 + final : 18 + final]
+        query_own, key_own, value_own, received = own_refs
+        more, payloads, landed = refs[18 + final : 22 + final], refs[22 + final : -1], refs[-1]
+    else:
+        query_own, key_own, value_own, received, weight, gain = refs[:6]
+        mine_out, theirs_out, folded, squares, carried, moved = refs[-6:]
+        payloads, sums_in = refs[6:-6], None
     rows = query_own.shape[0]
     half = rows // 2
     step = pl.program_id(0)
@@ -378,7 +384,7 @@
         []
         if fresh
         else [
-            pltpu.make_async_copy(refs[number - 8], halves[number], moved.at[number])
+            pltpu.make_async_copy(sums_in[number], halves[number], moved.at[number])
             for number in range(2)
         ]
     )
@@ -418,11 +424,12 @@
         return jnp.concatenate(parts[:2], axis=0), jnp.concatenate(parts[2:], axis=0)
 
     def projector(extra_head, lanes):
-        if extra_head is None:
-            scaled = weight[:, lanes].astype(jnp.float32) * gain[:, lanes]
-        else:
-            own = lanes_of(extra_head)
-            scaled = more[4][:, own].astype(jnp.float32) * more[5][:, own]
+        if final:
+            head = scalars[OWN] + (
+                scalars[FINAL] + lanes.start // HD if extra_head is None else extra_head
+            )
+            lanes = pl.ds(pl.multiple_of(head * HD, HD), HD)
+        scaled = weight[:, lanes].astype(jnp.float32) * gain[:, lanes]
         high = scaled.astype(jnp.bfloat16)
         low = (scaled - high.astype(jnp.float32)).astype(jnp.bfloat16)
         return jnp.concatenate([high, low, jnp.ones((16, HD), jnp.bfloat16)], axis=0)
@@ -479,15 +486,56 @@
         wide = attended.astype(jnp.float32)
         squares[slot] += wide * wide
 
+    def fetch_head(number, head, used):
+        copies = []
+        place = pl.ds(number * HD, HD)
+        for index, (source, target) in enumerate(zip(sources, own_refs if used else more)):
+            column = head if index == 3 else scalars[OWN] + head
+            column = pl.ds(pl.multiple_of(column * HD, HD), HD)
+            copies.append((source.at[:, column], target.at[:, place]))
+        copies += [(brought[index].at[:, place], payloads[index].at[:, place]) for index in used]
+        started = []
+        for index, (source, target) in enumerate(copies):
+            slot = number if used else 4 + number
+            copy = pltpu.make_async_copy(source, target, landed.at[slot, index])
+            copy.start()
+            started.append(copy)
+        return started
+
     for place, groups in variants.items():
+        if final:
+            count, tasks, extra_tasks = groups
+            used = set()
+            for source, _, _, key_sources in tasks:
+                for tokens in [source] + [key_source for key_source, _ in key_sources]:
+                    used |= set(tokens.pairs) | ({tokens.query} if tokens.query is not None else set())
+
+            @pl.when(scalars[PLACE] == place)
+            def _():
+                waits = [
+                    fetch_head(head, scalars[FINAL] + head, sorted(used)) for head in range(count)
+                ]
+                extra_waits = [
+                    fetch_head(number, number, ()) for number in range(len(extra_tasks))
+                ]
+                for head in range(count):
+                    for copy in waits[head]:
+                        copy.wait()
+                    for task in tasks:
+                        one_query(head, *task)
+                for copies, task in zip(extra_waits, extra_tasks):
+                    for copy in copies:
+                        copy.wait()
+                    one_query(0, *task)
+
+            continue
         for steps, tasks in groups:
 
             @pl.when((scalars[PLACE] == place) & (step < steps))
             def _():
                 for head in range(wide):
                     for task in tasks:
-                        if head == 0 or task[0].extra is None:
-                            one_query(head, *task)
+                        one_query(head, *task)
 
     def store():
         copies = [
@@ -538,15 +586,14 @@
 
             @pl.when(scalars[PLACE] == place)
             def _():
-                for slot in sorted({task[1] for _, tasks in groups for task in tasks}):
+                tasks = groups[1] if final else [task for _, some in groups for task in some]
+                for slot in sorted({task[1] for task in tasks}):
                     finish_slot(slot)
 
         store()
 
 
-def attend(
-    steps, wide, first, cap, own, scalars, mask, sums, payloads, variants, more, name, cost=1
-):
+def attend(steps, wide, first, cap, own, scalars, mask, sums, payloads, variants, name, cost=1):
     queries, keys, values, received, weight, gain = own
     rows = queries.shape[0]
     half = rows // 2
@@ -561,12 +608,6 @@
             return (0, head // wide + moving(i, scalars))
 
         return pl.BlockSpec((height, wide * HD), index)
-
-    def two_columns(height, own_column):
-        def index(i, scalars, mask):
-            return (0, i + scalars[OWN] // 2 if own_column else i)
-
-        return pl.BlockSpec((height, 2 * HD), index)
 
     def payload_column(payload):
         last = payload.shape[1] // (wide * HD) - 1
@@ -585,34 +626,34 @@
         column(1, True),
     ]
     arrays = [queries, keys, values, received, weight, gain]
-    extra = 0
-    if more:
-        extra = 6
-        in_specs += [
-            two_columns(rows, True),
-            two_columns(half, True),
-            two_columns(half, True),
-            two_columns(rows, False),
-            two_columns(patch, True),
-            two_columns(1, True),
-        ]
-        arrays += [queries, keys, values, received, weight, gain]
     in_specs += [payload_column(payload) for payload in payloads]
     arrays += payloads
     fresh = sums is None
     sums_shape = (SLOTS, patch + 2 * STAT_ROWS, rows)
+    scratch = [
+        pltpu.VMEM((SLOTS, 2 * patch + 16, rows), jnp.float32),
+        pltpu.VMEM((SLOTS, rows, HD), jnp.float32),
+        pltpu.VMEM(sums_shape, jnp.float32),
+        pltpu.SemaphoreType.DMA((4,)),
+    ]
     aliases = {}
     if not fresh:
+        anywhere = pl.BlockSpec(memory_space=pl.ANY)
+        whole = lambda array: pl.BlockSpec(array.shape, lambda i, scalars, mask: (0, 0))
+        in_specs = [anywhere] * 4 + [whole(weight), whole(gain)] + [anywhere] * len(payloads)
+        scratch += 2 * [
+            pltpu.VMEM((height, 4 * HD), jnp.bfloat16) for height in (rows, half, half, rows)
+        ]
+        scratch += [pltpu.VMEM(payload.shape, payload.dtype) for payload in payloads]
+        scratch.append(pltpu.SemaphoreType.DMA((8, 4 + len(payloads))))
         aliases = {2 + len(arrays): 0, 3 + len(arrays): 1}
-        in_specs += [pl.BlockSpec(memory_space=pl.ANY)] * 2
+        in_specs += [anywhere] * 2
         arrays += sums
-    pairs = max(
-        sum(count * wide * sum(len(task[3]) for task in tasks) for count, tasks in groups)
-        for groups in variants.values()
-    )
+    flops = 4 * rows * rows * HD * cost * 16
     span_count = math.isqrt(mask.shape[0])
+    final = 0 if fresh else len(payloads)
     return pl.pallas_call(
-        functools.partial(attend_kernel, variants, extra, span_count, fresh, wide),
+        functools.partial(attend_kernel, variants, 0, span_count, fresh, wide, final),
         name=name,
         out_shape=[pltpu.HBM((SLOTS, sums_shape[1] // 2, rows), jnp.float32)] * 2,
         input_output_aliases=aliases,
@@ -621,18 +662,13 @@
             grid=(steps,),
             in_specs=in_specs,
             out_specs=[pl.BlockSpec(memory_space=pl.ANY)] * 2,
-            scratch_shapes=[
-                pltpu.VMEM((SLOTS, 2 * patch + 16, rows), jnp.float32),
-                pltpu.VMEM((SLOTS, rows, HD), jnp.float32),
-                pltpu.VMEM(sums_shape, jnp.float32),
-                pltpu.SemaphoreType.DMA((4,)),
-            ],
+            scratch_shapes=scratch,
         ),
         compiler_params=pltpu.CompilerParams(vmem_limit_bytes=GRANT),
         cost_estimate=pl.CostEstimate(
-            flops=cost * pairs * 4 * rows * rows * HD,
-            bytes_accessed=steps * wide * HD * 2 * sum(spec.block_shape[0] for spec in in_specs[:4]),
-            transcendentals=cost * pairs * rows * rows,
+            flops=flops,
+            bytes_accessed=4 * HD * 2 * 3 * rows,
+            transcendentals=flops // (4 * HD),
         ),
     )(scalars, mask, *arrays)
 
@@ -734,37 +770,39 @@
                 )
             ],
         },
-        more=False,
         name="main_heads",
     )
     on_two, beside = Tokens(2, (2,)), Tokens(3, (3,))
     two_back, three_back = Tokens(None, (4,)), Tokens(None, (5,))
-    extras = [Tokens(None, (), lane) for lane in range(2)]
+    extras = [Tokens(None, (), lane) for lane in range(NEAR_HEADS)]
     sums, prepared = lax.optimization_barrier((sums, prepared))
     sums = run(
-        NEAR_HEADS // 2,
-        2,
+        1,
+        1,
         FINAL,
         FINAL_CAP,
         sums=sums,
         payloads=[up, down, two, far_next, far_two, far_three],
         variants={
-            0: [
-                (1, [(here, 0, 0, [(here, 0)]), (beside, 1, 1, [(here, 0), (beside, 1)])]),
-                (2, [(head, 0, 0, [(head, 0)]) for head in extras]),
-            ],
-            1: [(2, [(on_two, 2, 3, [(back_one, 0), (here, 1), (on_one, 2), (on_two, 3)])])],
-            3: [
-                (
-                    1,
-                    [
-                        (here, 0, 3, [(three_back, 0), (two_back, 1), (beside, 2), (here, 3)]),
-                        (beside, 2, 2, [(three_back, 0), (two_back, 1), (beside, 2)]),
-                    ],
-                )
-            ],
+            0: (
+                FAR_HEADS,
+                [(here, 0, 0, [(here, 0)]), (beside, 1, 1, [(here, 0), (beside, 1)])],
+                [(head, 0, 0, [(head, 0)]) for head in extras],
+            ),
+            1: (
+                NEAR_HEADS,
+                [(on_two, 2, 3, [(back_one, 0), (here, 1), (on_one, 2), (on_two, 3)])],
+                [],
+            ),
+            3: (
+                FAR_HEADS,
+                [
+                    (here, 0, 3, [(three_back, 0), (two_back, 1), (beside, 2), (here, 3)]),
+                    (beside, 2, 2, [(three_back, 0), (two_back, 1), (beside, 2)]),
+                ],
+                [],
+            ),
         },
-        more=True,
         name="final_heads",
         cost=4,
     )

time: 101 us -> 99.8 us (0.988)
    ppermute x1, starting transfers between devices: 11.2 us -> 9.81 us  [per_device(): to_before = lax.ppermute(after[:, skip:], 'span', [(0, 2), (1, 3)])]
where the time goes in v14:
time: 99.8 us; the launch traced here: 99.1 us
  starting transfers between devices  37.9 us (38%)
  Pallas kernels  29.7 us (30%)
  waiting for transfers between devices  19.2 us (19%)
  local copies, waits for them, and re-layouts  6.84 us (7%)
  other arithmetic  4.44 us (4%)
  between operations  1.02 us (1%)
    ppermute x7, starting transfers between devices, send(): return in_place(lax.ppermute(value, 'span', list(pairs)))  21.3 us
    pallas_call x2, Pallas kernels, attend(): pl.pallas_call(functools.partial(attend_kernel, variants, 0, span_count,...  19.5 us
    ppermute x1, starting transfers between devices, per_device(): to_before = lax.ppermute(after[:, skip:], 'span', [(0, 2), (1, 3)])  9.81 us
    ppermute x7, waiting for transfers between devices, send(): return in_place(lax.ppermute(value, 'span', list(pairs)))  8.52 us
    pallas_call x2, Pallas kernels, pack(): pl.pallas_call(functools.partial(pack_kernel, len(arrays), len(shapes), c...  6.42 us
    ppermute x1, waiting for transfers between devices, per_device(): total = total + lax.ppermute(total, 'head', SWAP)  3.23 us
    ppermute x1, waiting for transfers between devices, per_device(): lax.ppermute(jnp.concatenate([jnp.concatenate([own[:, skip:], after], axi...  2.98 us
    pallas_call x1, Pallas kernels, finish(): pl.pallas_call(finish_kernel, name='finish', out_shape=(jax.ShapeDtypeStr...  2.4 us
  transfers between devices with their start and end apart: 16, of which 7 were waited for; matrix products, arithmetic and copies ran while one was open for 9% of the time, Pallas kernels for 13%

profile of v14, /device:TPU:0, one launch (start us, length us, event | category | flops | bytes accessed | tf_op | source)
XLA Modules:
  0.0 99.1 jit_solution(12513685736244543311)
XLA Ops:
  0.7 1.2 %pack_handed.1 = bf16[384,1280]{1,0:T(8,128)(2,1)S(1)} custom-call(bf16[192,2560]{1,0:T(8,128)(2,1)} %refs_1_.7, bf16[192,2560]{1,0:T(8,128)(2,1)} %refs_2_.7), custom_call_target="tpu_custom_call" | custom-call | bytes 1966080 | tf_op jit(solution)/shard_map/pack_handed/pallas_call | solution.py:324
  3.8 0.8 collective-permute-done.refs_3_
  4.6 2.9 %pack_first.1 = (bf16[768,512]{1,0:T(8,128)(2,1)}, bf16[1152,512]{1,0:T(8,128)(2,1)}) custom-call(s32[12]{0:T(128)S(1)} %bitcast_add_fusion.scalars, bf16[384,2560]{1,0:T(8,128)(2,1)} %refs_0_.7, bf16[192,2560]{1,0:T(8,128)(2,1)} %refs_1_.7, bf16[192,2560]{1,0:T(8,128)(2,1)} %refs_2_.7, bf16[384,1280]{1,0:T(8,128)(2,1)S(1)} %collective-permute-done.refs_3_), custom_call_target="tpu_custom_call" | custom-call | bytes 3932160 | tf_op jit(solution)/shard_map/pack_first/pallas_call | solution.py:286
  7.5 1.3 %collective-permute-start.2 = (bf16[1152,512]{1,0:T(8,128)(2,1)}, bf16[1152,512]{1,0:T(8,128)(2,1)}, u32[]{:S(2)}, u32[]{:S(2)}) collective-permute-start(bf16[1152,512]{1,0:T(8,128)(2,1)} %get-tuple-element.37), channel_id=1, source_target_pairs={{4,0},{8,4},{12,8},{5,1},{9,5},{13,9},{6,2},{10,6},{14,10},{7,3},{... | collective-permute-start | bytes 3538952 | tf_op jit(solution)/shard_map/ppermute | solution.py:686
  8.9 6.5 %collective-permute-start.1 = (bf16[768,512]{1,0:T(8,128)(2,1)}, bf16[768,512]{1,0:T(8,128)(2,1)}, u32[]{:S(2)}, u32[]{:S(2)}) collective-permute-start(bf16[768,512]{1,0:T(8,128)(2,1)} %get-tuple-element.43), channel_id=1, source_target_pairs={{0,4},{4,8},{1,5},{5,9},{2,6},{6,10},{3,7},{7,11},{16,20},{20,24},... | collective-permute-start | bytes 2359304 | tf_op jit(solution)/shard_map/ppermute | solution.py:686
  15.4 3.5 %pack_second.1 = (bf16[768,512]{1,0:T(8,128)(2,1)}, bf16[1152,512]{1,0:T(8,128)(2,1)}, bf16[1152,256]{1,0:T(8,128)(2,1)}, bf16[768,256]{1,0:T(8,128)(2,1)}) custom-call(s32[12]{0:T(128)S(1)} %bitcast_add_fusion.scalars, bf16[384,2560]{1,0:T(8,128)(2,1)} %refs_0_.7, bf16[192,2560]{1,0:T(8,128)(2,1)} %refs_1_.7, bf16[192,2560]{1,0:T(8,128)(2,1)} %refs_2_.7, ...), custom_call_target="tpu_custom_call" | custom-call | bytes 5898240 | tf_op jit(solution)/shard_map/pack_second/pallas_call | solution.py:286
  18.9 1.7 %collective-permute-start.3 = (bf16[1152,512]{1,0:T(8,128)(2,1)}, bf16[1152,512]{1,0:T(8,128)(2,1)}, u32[]{:S(2)}, u32[]{:S(2)}) collective-permute-start(bf16[1152,512]{1,0:T(8,128)(2,1)} %get-tuple-element.39), channel_id=1, source_target_pairs={{12,4},{13,5},{14,6},{15,7},{28,20},{29,21},{30,22},{31,23}} | collective-permute-start | bytes 3538952 | tf_op jit(solution)/shard_map/ppermute | solution.py:686
  21.0 2.7 %collective-permute-start.9 = (bf16[768,512]{1,0:T(8,128)(2,1)}, bf16[768,512]{1,0:T(8,128)(2,1)}, u32[]{:S(2)}, u32[]{:S(2)}) collective-permute-start(bf16[768,512]{1,0:T(8,128)(2,1)} %get-tuple-element.53), channel_id=1, source_target_pairs={{0,8},{1,9},{2,10},{3,11},{16,24},{17,25},{18,26},{19,27}} | collective-permute-start | bytes 2359304 | tf_op jit(solution)/shard_map/ppermute | solution.py:686
  24.1 1.6 %collective-permute-start.6 = (f32[40,128]{0,1:T(8,128)S(1)}, f32[40,128]{0,1:T(8,128)S(1)}, u32[]{:S(2)}, u32[]{:S(2)}) collective-permute-start(f32[40,128]{0,1:T(8,128)S(1)} %copy.39), channel_id=1, source_target_pairs={{0,2},{2,0},{1,3},{3,1},{4,6},{6,4},{5,7},{7,5},{8,10},{10,8},{9,1... | collective-permute-start | bytes 61448 | tf_op jit(solution)/shard_map/ppermute | solution.py:831
  26.4 1.0 copy-done.2
  27.6 0.9 collective-permute-done.6
  28.5 1.3 %collective-permute-start.4 = (bf16[1152,256]{1,0:T(8,128)(2,1)}, bf16[1152,256]{1,0:T(8,128)(2,1)}, u32[]{:S(2)}, u32[]{:S(2)}) collective-permute-start(bf16[1152,256]{1,0:T(8,128)(2,1)} %get-tuple-element.44), channel_id=1, source_target_pairs={{8,12},{4,0},{9,13},{5,1},{10,14},{6,2},{11,15},{7,3},{24,28},{20,... | collective-permute-start | bytes 1769480 | tf_op jit(solution)/shard_map/ppermute | solution.py:686
  31.1 0.9 pad_maximum_fusion
  32.0 0.8 slice.63
  32.8 1.0 %reshape.33 = f32[16,640]{1,0:T(8,128)S(1)} reshape(f32[320,32]{1,0:T(8,128)} %slice.63) | data formatting | bytes 81920 | tf_op jit(solution)/shard_map/reshape | solution.py:1022
  33.8 0.8 fusion.33.constants
  34.7 6.4 %collective-permute-start.8 = (bf16[768,256]{1,0:T(8,128)(2,1)}, bf16[768,256]{1,0:T(8,128)(2,1)}, u32[]{:S(2)}, u32[]{:S(2)}) collective-permute-start(bf16[768,256]{1,0:T(8,128)(2,1)} %get-tuple-element.52), channel_id=1, source_target_pairs={{0,12},{1,13},{2,14},{3,15},{16,28},{17,29},{18,30},{19,31}} | collective-permute-start | bytes 1179656 | tf_op jit(solution)/shard_map/ppermute | solution.py:686
  41.1 8.5 %collective-permute-done.9.refs_8_ = bf16[768,512]{1,0:T(8,128)(2,1)} collective-permute-done((bf16[768,512]{1,0:T(8,128)(2,1)}, bf16[768,512]{1,0:T(8,128)(2,1)}, u32[]{:S(2)}, u32[]{:S(2)}) %collective-permute-start.9) | collective-permute-done | bytes 786464 | tf_op jit(solution)/shard_map/ppermute | solution.py:686
  49.6 1.4 %collective-permute-start.7 = (bf16[768,256]{1,0:T(8,128)(2,1)}, bf16[768,256]{1,0:T(8,128)(2,1)}, u32[]{:S(2)}, u32[]{:S(2)}) collective-permute-start(bf16[768,256]{1,0:T(8,128)(2,1)} %get-tuple-element.52), channel_id=1, source_target_pairs={{4,12},{5,13},{6,14},{7,15},{20,28},{21,29},{22,30},{23,31}} | collective-permute-start | bytes 1179656 | tf_op jit(solution)/shard_map/ppermute | solution.py:686
  51.0 0.8 reshape.30.mask
  51.7 0.7 broadcast_in_dim.24.refs_5_
  52.5 9.4 %main_heads.1 = (f32[3,40,384]{2,1,0:T(8,128)}, f32[3,40,384]{2,1,0:T(8,128)}) custom-call(s32[12]{0:T(128)S(1)} %bitcast_add_fusion.scalars, s32[16]{0:T(128)S(1)} %reshape.30.mask, bf16[384,2560]{1,0:T(8,128)(2,1)} %refs_0_.7, bf16[192,2560]{1,0:T(8,128)(2,1)} %refs_1_.7, bf16[192,2560]{1,0:T(8,128)(2,1)} %refs_2_.7, ...), custom_call_target="tpu_custom_call" | custom-call | flops 1207959552 | bytes 1179648 | tf_op jit(solution)/shard_map/main_heads/pallas_call | solution.py:655
  61.9 10.1 %final_heads.1 = (f32[3,40,384]{2,1,0:T(8,128)}, f32[3,40,384]{2,1,0:T(8,128)}) custom-call(s32[12]{0:T(128)S(1)} %bitcast_add_fusion.scalars, s32[16]{0:T(128)S(1)} %reshape.30.mask, bf16[384,2560]{1,0:T(8,128)(2,1)} %refs_0_.7, bf16[192,2560]{1,0:T(8,128)(2,1)} %refs_1_.7, ...), custom_call_target="tpu_custom_call", output_to_operand_aliasing={{0}: (14, {}), {1}: (15, {})} | custom-call | flops 4831838208 | bytes 1179648 | tf_op jit(solution)/shard_map/final_heads/pallas_call | solution.py:655
  72.1 1.6 %collective-permute-done.10 = f32[3,40,384]{2,1,0:T(8,128)S(1)} collective-permute-done((f32[3,40,384]{2,1,0:T(8,128)}, f32[3,40,384]{2,1,0:T(8,128)S(1)}, u32[]{:S(2)}, u32[]{:S(2)}) %collective-permute-start.10) | collective-permute-done | bytes 184352 | tf_op jit(solution)/shard_map/ppermute | solution.py:1039
  73.7 1.0 add.84
  74.7 9.8 %collective-permute-start.12 = (f32[40,256]{1,0:T(8,128)S(1)}, f32[40,256]{1,0:T(8,128)S(1)}, u32[]{:S(2)}, u32[]{:S(2)}) collective-permute-start(f32[40,256]{1,0:T(8,128)S(1)} %slice.71), channel_id=1, source_target_pairs={{0,8},{4,12},{1,9},{5,13},{2,10},{6,14},{3,11},{7,15},{16,24},{20,... | collective-permute-start | bytes 122888 | tf_op jit(solution)/shard_map/ppermute | solution.py:1050
  85.2 2.3 %collective-permute-start.11 = (f32[56,640]{1,0:T(8,128)S(1)}, f32[56,640]{1,0:T(8,128)S(1)}, u32[]{:S(2)}, u32[]{:S(2)}) collective-permute-start(f32[56,640]{1,0:T(8,128)S(1)} %pad_maximum_fusion.1), channel_id=1, source_target_pairs={{0,4},{4,8},{8,12},{1,5},{5,9},{9,13},{2,6},{6,10},{10,14},{3,7},{... | collective-permute-start | bytes 430088 | tf_op jit(solution)/shard_map/ppermute | solution.py:1042
  87.6 3.0 %collective-permute-done.11 = f32[56,640]{1,0:T(8,128)S(1)} collective-permute-done((f32[56,640]{1,0:T(8,128)S(1)}, f32[56,640]{1,0:T(8,128)S(1)}, u32[]{:S(2)}, u32[]{:S(2)}) %collective-permute-start.11) | collective-permute-done | bytes 143392 | tf_op jit(solution)/shard_map/ppermute | solution.py:1042
  90.6 1.5 %collective-permute-start.14 = (f32[40,640]{1,0:T(8,128)S(1)}, f32[40,640]{1,0:T(8,128)S(1)}, u32[]{:S(2)}, u32[]{:S(2)}) collective-permute-start(f32[40,640]{1,0:T(8,128)S(1)} %fusion.32), channel_id=1, source_target_pairs={{0,2},{2,0},{1,3},{3,1},{4,6},{6,4},{5,7},{7,5},{8,10},{10,8},{9,1... | collective-permute-start | bytes 307208 | tf_op jit(solution)/shard_map/ppermute | solution.py:1053
  92.0 3.2 %collective-permute-done.14 = f32[40,640]{1,0:T(8,128)S(1)} collective-permute-done((f32[40,640]{1,0:T(8,128)S(1)}, f32[40,640]{1,0:T(8,128)S(1)}, u32[]{:S(2)}, u32[]{:S(2)}) %collective-permute-start.14) | collective-permute-done | bytes 102432 | tf_op jit(solution)/shard_map/ppermute | solution.py:1053
  95.5 1.2 %collective-permute-done.15.other = f32[40,640]{1,0:T(8,128)S(1)} collective-permute-done((f32[40,640]{1,0:T(8,128)S(1)}, f32[40,640]{1,0:T(8,128)S(1)}, u32[]{:S(2)}, u32[]{:S(2)}) %collective-permute-start.15) | collective-permute-done | bytes 102432 | tf_op jit(solution)/shard_map/ppermute | solution.py:1054
  96.7 2.4 %finish.1 = (f32[3,8,16,16]{3,2,1,0:T(8,128)}, bf16[3,8,16,384]{3,2,1,0:T(8,128)(2,1)}) custom-call(s32[12]{0:T(128)S(1)} %bitcast_add_fusion.scalars, f32[40,640]{1,0:T(8,128)S(1)} %add.87.mine, f32[40,640]{1,0:T(8,128)S(1)} %collective-permute-done.15.other, f32[320,48]{1,0:T(8,128)S(1)} %bitcast.33, f32[320,32]{1,0:T(8,128)S(1)} %reshape.34.before, ...), custom_call_target="tpu_custom_call" | custom-call | tf_op jit(solution)/shard_map/finish/pallas_call | solution.py:961
  (62 shorter events, 5.9 us)
Async XLA Ops:
  0.6 25.1 %copy-start = (f32[384]{0:T(512)S(1)}, f32[384]{0:T(512)}, u32[]{:S(2)}) copy-start(f32[384]{0:T(512)} %param.21) | copy-start | bytes 4612
  0.6 1.8 %copy-start.8 = (s32[12]{0:T(128)S(1)}, s32[12]{0:T(128)}, u32[]{:S(2)}) copy-start(s32[12]{0:T(128)} %constant.107.clone) | copy-start | bytes 148
  1.9 2.7 %collective-permute-start = (bf16[384,1280]{1,0:T(8,128)(2,1)S(1)}, bf16[384,1280]{1,0:T(8,128)(2,1)S(1)}, u32[]{:S(2)}, u32[]{:S(2)}) collective-permute-start(bf16[384,1280]{1,0:T(8,128)(2,1)S(1)} %pack_handed.1), channel_id=1, source_target_pairs={{0,1},{1,0},{2,3},{3,2},{4,5},{5,4},{6,7},{7,6},{8,9},{9,8},{10,11... | collective-permute-start | bytes 2949128 | tf_op jit(solution)/shard_map/ppermute | solution.py:703
  7.5 45.0 %collective-permute-start.2 = (bf16[1152,512]{1,0:T(8,128)(2,1)}, bf16[1152,512]{1,0:T(8,128)(2,1)}, u32[]{:S(2)}, u32[]{:S(2)}) collective-permute-start(bf16[1152,512]{1,0:T(8,128)(2,1)} %get-tuple-element.37), channel_id=1, source_target_pairs={{4,0},{8,4},{12,8},{5,1},{9,5},{13,9},{6,2},{10,6},{14,10},{7,3},{... | collective-permute-start | bytes 3538952 | tf_op jit(solution)/shard_map/ppermute | solution.py:686
  8.8 11.8 %copy-start.4 = (f32[3,8,16,16]{3,2,1,0:T(8,128)S(1)}, f32[3,8,16,16]{3,2,1,0:T(8,128)}, u32[]{:S(2)}) copy-start(f32[3,8,16,16]{3,2,1,0:T(8,128)} %param.19) | copy-start | bytes 73732
  8.8 14.9 %copy-start.1 = (bf16[2560,64]{0,1:T(8,128)(2,1)S(1)}, bf16[2560,64]{0,1:T(8,128)(2,1)}, u32[]{:S(2)}) copy-start(bf16[2560,64]{0,1:T(8,128)(2,1)} %param.18) | copy-start | bytes 983044
  8.8 14.9 %copy-start.6 = (f32[2560]{0:T(1024)S(1)}, f32[2560]{0:T(1024)}, u32[]{:S(2)}) copy-start(f32[2560]{0:T(1024)} %param.16) | copy-start | bytes 30724
  8.8 14.8 %copy-start.7 = (f32[2560]{0:T(1024)S(1)}, f32[2560]{0:T(1024)}, u32[]{:S(2)}) copy-start(f32[2560]{0:T(1024)} %param.17) | copy-start | bytes 30724
  8.9 25.8 %collective-permute-start.1 = (bf16[768,512]{1,0:T(8,128)(2,1)}, bf16[768,512]{1,0:T(8,128)(2,1)}, u32[]{:S(2)}, u32[]{:S(2)}) collective-permute-start(bf16[768,512]{1,0:T(8,128)(2,1)} %get-tuple-element.43), channel_id=1, source_target_pairs={{0,4},{4,8},{1,5},{5,9},{2,6},{6,10},{3,7},{7,11},{16,20},{20,24},... | collective-permute-start | bytes 2359304 | tf_op jit(solution)/shard_map/ppermute | solution.py:686
  18.9 43.0 %collective-permute-start.3 = (bf16[1152,512]{1,0:T(8,128)(2,1)}, bf16[1152,512]{1,0:T(8,128)(2,1)}, u32[]{:S(2)}, u32[]{:S(2)}) collective-permute-start(bf16[1152,512]{1,0:T(8,128)(2,1)} %get-tuple-element.39), channel_id=1, source_target_pairs={{12,4},{13,5},{14,6},{15,7},{28,20},{29,21},{30,22},{31,23}} | collective-permute-start | bytes 3538952 | tf_op jit(solution)/shard_map/ppermute | solution.py:686
  20.9 3.1 %collective-permute-start.5 = (f32[8,48]{1,0:T(8,128)S(1)}, f32[8,48]{1,0:T(8,128)S(1)}, u32[]{:S(2)}, u32[]{:S(2)}) collective-permute-start(f32[8,48]{1,0:T(8,128)S(1)} %bitcast.42), channel_id=1, source_target_pairs={{0,1},{1,0},{2,3},{3,2},{4,5},{5,4},{6,7},{7,6},{8,9},{9,8},{10,11... | collective-permute-start | bytes 4616 | tf_op jit(solution)/shard_map/ppermute | solution.py:816
  21.0 28.6 %collective-permute-start.9 = (bf16[768,512]{1,0:T(8,128)(2,1)}, bf16[768,512]{1,0:T(8,128)(2,1)}, u32[]{:S(2)}, u32[]{:S(2)}) collective-permute-start(bf16[768,512]{1,0:T(8,128)(2,1)} %get-tuple-element.53), channel_id=1, source_target_pairs={{0,8},{1,9},{2,10},{3,11},{16,24},{17,25},{18,26},{19,27}} | collective-permute-start | bytes 2359304 | tf_op jit(solution)/shard_map/ppermute | solution.py:686
  24.0 1.7 %copy-start.3 = (f32[8,14,48]{2,1,0:T(8,128)}, f32[8,14,48]{2,1,0:T(8,128)S(1)}, u32[]{:S(2)}) copy-start(f32[8,14,48]{2,1,0:T(8,128)S(1)} %broadcast_in_dim.26) | copy-start | bytes 64516
  24.1 4.3 %collective-permute-start.6 = (f32[40,128]{0,1:T(8,128)S(1)}, f32[40,128]{0,1:T(8,128)S(1)}, u32[]{:S(2)}, u32[]{:S(2)}) collective-permute-start(f32[40,128]{0,1:T(8,128)S(1)} %copy.39), channel_id=1, source_target_pairs={{0,2},{2,0},{1,3},{3,1},{4,6},{6,4},{5,7},{7,5},{8,10},{10,8},{9,1... | collective-permute-start | bytes 61448 | tf_op jit(solution)/shard_map/ppermute | solution.py:831
  26.4 1.0 copy-start.2
  28.5 2.0 %copy-start.5 = (f32[40,128]{0,1:T(8,128)}, f32[40,128]{0,1:T(8,128)S(1)}, u32[]{:S(2)}) copy-start(f32[40,128]{0,1:T(8,128)S(1)} %collective-permute-done.6) | copy-start | bytes 61444
  28.5 33.5 %collective-permute-start.4 = (bf16[1152,256]{1,0:T(8,128)(2,1)}, bf16[1152,256]{1,0:T(8,128)(2,1)}, u32[]{:S(2)}, u32[]{:S(2)}) collective-permute-start(bf16[1152,256]{1,0:T(8,128)(2,1)} %get-tuple-element.44), channel_id=1, source_target_pairs={{8,12},{4,0},{9,13},{5,1},{10,14},{6,2},{11,15},{7,3},{24,28},{20,... | collective-permute-start | bytes 1769480 | tf_op jit(solution)/shard_map/ppermute | solution.py:686
  34.7 27.2 %collective-permute-start.8 = (bf16[768,256]{1,0:T(8,128)(2,1)}, bf16[768,256]{1,0:T(8,128)(2,1)}, u32[]{:S(2)}, u32[]{:S(2)}) collective-permute-start(bf16[768,256]{1,0:T(8,128)(2,1)} %get-tuple-element.52), channel_id=1, source_target_pairs={{0,12},{1,13},{2,14},{3,15},{16,28},{17,29},{18,30},{19,31}} | collective-permute-start | bytes 1179656 | tf_op jit(solution)/shard_map/ppermute | solution.py:686
  49.6 12.3 %collective-permute-start.7 = (bf16[768,256]{1,0:T(8,128)(2,1)}, bf16[768,256]{1,0:T(8,128)(2,1)}, u32[]{:S(2)}, u32[]{:S(2)}) collective-permute-start(bf16[768,256]{1,0:T(8,128)(2,1)} %get-tuple-element.52), channel_id=1, source_target_pairs={{4,12},{5,13},{6,14},{7,15},{20,28},{21,29},{22,30},{23,31}} | collective-permute-start | bytes 1179656 | tf_op jit(solution)/shard_map/ppermute | solution.py:686
  72.0 1.7 %collective-permute-start.10 = (f32[3,40,384]{2,1,0:T(8,128)}, f32[3,40,384]{2,1,0:T(8,128)S(1)}, u32[]{:S(2)}, u32[]{:S(2)}) collective-permute-start(f32[3,40,384]{2,1,0:T(8,128)} %get-tuple-element.65), channel_id=1, source_target_pairs={{0,1},{1,0},{2,3},{3,2},{4,5},{5,4},{6,7},{7,6},{8,9},{9,8},{10,11... | collective-permute-start | bytes 552968 | tf_op jit(solution)/shard_map/ppermute | solution.py:1039
  74.7 12.8 %collective-permute-start.12 = (f32[40,256]{1,0:T(8,128)S(1)}, f32[40,256]{1,0:T(8,128)S(1)}, u32[]{:S(2)}, u32[]{:S(2)}) collective-permute-start(f32[40,256]{1,0:T(8,128)S(1)} %slice.71), channel_id=1, source_target_pairs={{0,8},{4,12},{1,9},{5,13},{2,10},{6,14},{3,11},{7,15},{16,24},{20,... | collective-permute-start | bytes 122888 | tf_op jit(solution)/shard_map/ppermute | solution.py:1050
  84.5 3.0 %collective-permute-start.13 = (f32[40,384]{1,0:T(8,128)S(1)}, f32[40,384]{1,0:T(8,128)S(1)}, u32[]{:S(2)}, u32[]{:S(2)}) collective-permute-start(f32[40,384]{1,0:T(8,128)S(1)} %get-tuple-element.74), channel_id=1, source_target_pairs={{4,12},{12,8},{5,13},{13,9},{6,14},{14,10},{7,15},{15,11},{20,28},... | collective-permute-start | bytes 184328 | tf_op jit(solution)/shard_map/ppermute | solution.py:1049
  85.2 5.3 %collective-permute-start.11 = (f32[56,640]{1,0:T(8,128)S(1)}, f32[56,640]{1,0:T(8,128)S(1)}, u32[]{:S(2)}, u32[]{:S(2)}) collective-permute-start(f32[56,640]{1,0:T(8,128)S(1)} %pad_maximum_fusion.1), channel_id=1, source_target_pairs={{0,4},{4,8},{8,12},{1,5},{5,9},{9,13},{2,6},{6,10},{10,14},{3,7},{... | collective-permute-start | bytes 430088 | tf_op jit(solution)/shard_map/ppermute | solution.py:1042
  90.6 4.7 %collective-permute-start.14 = (f32[40,640]{1,0:T(8,128)S(1)}, f32[40,640]{1,0:T(8,128)S(1)}, u32[]{:S(2)}, u32[]{:S(2)}) collective-permute-start(f32[40,640]{1,0:T(8,128)S(1)} %fusion.32), channel_id=1, source_target_pairs={{0,2},{2,0},{1,3},{3,1},{4,6},{6,4},{5,7},{7,5},{8,10},{10,8},{9,1... | collective-permute-start | bytes 307208 | tf_op jit(solution)/shard_map/ppermute | solution.py:1053
  95.3 1.4 %collective-permute-start.15 = (f32[40,640]{1,0:T(8,128)S(1)}, f32[40,640]{1,0:T(8,128)S(1)}, u32[]{:S(2)}, u32[]{:S(2)}) collective-permute-start(f32[40,640]{1,0:T(8,128)S(1)} %add.87.mine), channel_id=1, source_target_pairs={{0,1},{1,0},{2,3},{3,2},{4,5},{5,4},{6,7},{7,6},{8,9},{9,8},{10,11... | collective-permute-start | bytes 307208 | tf_op jit(solution)/shard_map/ppermute | solution.py:1054

commit v15 on v14

--- a/solution.py
+++ b/solution.py
@@ -1039,15 +1039,13 @@
     mine = mine + lax.ppermute(theirs, "slab", SWAP)
     own, after, third = mine[0], mine[1], mine[2]
     skip = TROWS * TCOLS
-    from_one = lax.ppermute(
-        jnp.concatenate([jnp.concatenate([own[:, skip:], after], axis=1), ahead], axis=0),
-        "span",
-        [(0, 1), (1, 2), (2, 3)],
-    )
+    ahead = jnp.concatenate([jnp.concatenate([own[:, skip:], after], axis=1), ahead], axis=0)
+    from_one = lax.ppermute(ahead, "span", [(0, 1), (1, 2), (2, 3)])
+    sent_current, sent_before, _ = lax.optimization_barrier((third, after[:, skip:], ahead))
     before = from_one[own.shape[0] :].reshape(-1, 2 * LAT_CH)
     from_one = from_one[: own.shape[0]]
-    to_current = lax.ppermute(third, "span", [(1, 3), (3, 2)])
-    to_before = lax.ppermute(after[:, skip:], "span", [(0, 2), (1, 3)])
+    to_current = lax.ppermute(sent_current, "span", [(1, 3), (3, 2)])
+    to_before = lax.ppermute(sent_before, "span", [(0, 2), (1, 3)])
     kept = jnp.concatenate([jnp.where(place == 3, third[:, skip:], 0.0), own], axis=1)
     total = kept + from_one + jnp.concatenate([to_before, to_current], axis=1)
     total = total + lax.ppermute(total, "head", SWAP)

time: 99.8 us -> 98.8 us (0.990)
  the two profiles are of different devices: /device:TPU:0 before, /device:TPU:25 now
where the time goes in v15:
time: 98.8 us; the launch traced here: 98.1 us
  waiting for transfers between devices  35.2 us (36%)
  starting transfers between devices  28.6 us (29%)
  Pallas kernels  22.1 us (22%)
  local copies, waits for them, and re-layouts  6.84 us (7%)
  other arithmetic  4.44 us (4%)
    ppermute x7, waiting for transfers between devices, send(): return in_place(lax.ppermute(value, 'span', list(pairs)))  24.8 us
    ppermute x7, starting transfers between devices, send(): return in_place(lax.ppermute(value, 'span', list(pairs)))  14 us
    pallas_call x2, Pallas kernels, attend(): pl.pallas_call(functools.partial(attend_kernel, variants, 0, span_count,...  11.9 us
    pallas_call x2, Pallas kernels, pack(): pl.pallas_call(functools.partial(pack_kernel, len(arrays), len(shapes), c...  6.42 us
    ppermute x1, starting transfers between devices, per_device(): to_current = lax.ppermute(sent_current, 'span', [(1, 3), (3, 2)])  4.55 us
    ppermute x1, waiting for transfers between devices, per_device(): to_before = lax.ppermute(sent_before, 'span', [(0, 2), (1, 3)])  2.44 us
    ppermute x1, starting transfers between devices, per_device(): other = lax.ppermute(total, 'slab', SWAP)  2.42 us
    pallas_call x1, Pallas kernels, finish(): pl.pallas_call(finish_kernel, name='finish', out_shape=(jax.ShapeDtypeStr...  2.41 us
  transfers between devices with their start and end apart: 16, of which 9 were waited for; matrix products, arithmetic and copies ran while one was open for 9% of the time, Pallas kernels for 7%

profile of v15, /device:TPU:25, one launch (start us, length us, event | category | flops | bytes accessed | tf_op | source)
XLA Modules:
  0.0 98.1 jit_solution(12453566400412011157)
XLA Ops:
  0.7 1.2 %pack_handed.1 = bf16[384,1280]{1,0:T(8,128)(2,1)S(1)} custom-call(bf16[192,2560]{1,0:T(8,128)(2,1)} %refs_1_.7, bf16[192,2560]{1,0:T(8,128)(2,1)} %refs_2_.7), custom_call_target="tpu_custom_call" | custom-call | bytes 1966080 | tf_op jit(solution)/shard_map/pack_handed/pallas_call | solution.py:324
  4.8 2.9 %pack_first.1 = (bf16[768,512]{1,0:T(8,128)(2,1)}, bf16[1152,512]{1,0:T(8,128)(2,1)}) custom-call(s32[12]{0:T(128)S(1)} %bitcast_add_fusion.scalars, bf16[384,2560]{1,0:T(8,128)(2,1)} %refs_0_.7, bf16[192,2560]{1,0:T(8,128)(2,1)} %refs_1_.7, bf16[192,2560]{1,0:T(8,128)(2,1)} %refs_2_.7, bf16[384,1280]{1,0:T(8,128)(2,1)S(1)} %collective-permute-done.refs_3_), custom_call_target="tpu_custom_call" | custom-call | bytes 3932160 | tf_op jit(solution)/shard_map/pack_first/pallas_call | solution.py:286
  7.7 3.1 %collective-permute-start.2 = (bf16[1152,512]{1,0:T(8,128)(2,1)}, bf16[1152,512]{1,0:T(8,128)(2,1)}, u32[]{:S(2)}, u32[]{:S(2)}) collective-permute-start(bf16[1152,512]{1,0:T(8,128)(2,1)} %get-tuple-element.39), channel_id=1, source_target_pairs={{4,0},{8,4},{12,8},{5,1},{9,5},{13,9},{6,2},{10,6},{14,10},{7,3},{... | collective-permute-start | bytes 3538952 | tf_op jit(solution)/shard_map/ppermute | solution.py:686
  10.9 1.7 %collective-permute-start.1 = (bf16[768,512]{1,0:T(8,128)(2,1)}, bf16[768,512]{1,0:T(8,128)(2,1)}, u32[]{:S(2)}, u32[]{:S(2)}) collective-permute-start(bf16[768,512]{1,0:T(8,128)(2,1)} %get-tuple-element.45), channel_id=1, source_target_pairs={{0,4},{4,8},{1,5},{5,9},{2,6},{6,10},{3,7},{7,11},{16,20},{20,24},... | collective-permute-start | bytes 2359304 | tf_op jit(solution)/shard_map/ppermute | solution.py:686
  12.6 3.5 %pack_second.1 = (bf16[768,512]{1,0:T(8,128)(2,1)}, bf16[1152,512]{1,0:T(8,128)(2,1)}, bf16[1152,256]{1,0:T(8,128)(2,1)}, bf16[768,256]{1,0:T(8,128)(2,1)}) custom-call(s32[12]{0:T(128)S(1)} %bitcast_add_fusion.scalars, bf16[384,2560]{1,0:T(8,128)(2,1)} %refs_0_.7, bf16[192,2560]{1,0:T(8,128)(2,1)} %refs_1_.7, bf16[192,2560]{1,0:T(8,128)(2,1)} %refs_2_.7, ...), custom_call_target="tpu_custom_call" | custom-call | bytes 5898240 | tf_op jit(solution)/shard_map/pack_second/pallas_call | solution.py:286
  16.1 3.6 %collective-permute-start.3 = (bf16[1152,512]{1,0:T(8,128)(2,1)}, bf16[1152,512]{1,0:T(8,128)(2,1)}, u32[]{:S(2)}, u32[]{:S(2)}) collective-permute-start(bf16[1152,512]{1,0:T(8,128)(2,1)} %get-tuple-element.41), channel_id=1, source_target_pairs={{12,4},{13,5},{14,6},{15,7},{28,20},{29,21},{30,22},{31,23}} | collective-permute-start | bytes 3538952 | tf_op jit(solution)/shard_map/ppermute | solution.py:686
  20.0 1.3 %collective-permute-start.5 = (f32[8,48]{1,0:T(8,128)S(1)}, f32[8,48]{1,0:T(8,128)S(1)}, u32[]{:S(2)}, u32[]{:S(2)}) collective-permute-start(f32[8,48]{1,0:T(8,128)S(1)} %bitcast.42), channel_id=1, source_target_pairs={{0,1},{1,0},{2,3},{3,2},{4,5},{5,4},{6,7},{7,6},{8,9},{9,8},{10,11... | collective-permute-start | bytes 4616 | tf_op jit(solution)/shard_map/ppermute | solution.py:816
  21.3 1.6 %collective-permute-start.9 = (bf16[768,512]{1,0:T(8,128)(2,1)}, bf16[768,512]{1,0:T(8,128)(2,1)}, u32[]{:S(2)}, u32[]{:S(2)}) collective-permute-start(bf16[768,512]{1,0:T(8,128)(2,1)} %get-tuple-element.55), channel_id=1, source_target_pairs={{0,8},{1,9},{2,10},{3,11},{16,24},{17,25},{18,26},{19,27}} | collective-permute-start | bytes 2359304 | tf_op jit(solution)/shard_map/ppermute | solution.py:686
  23.3 1.3 %collective-permute-start.6 = (f32[40,128]{0,1:T(8,128)S(1)}, f32[40,128]{0,1:T(8,128)S(1)}, u32[]{:S(2)}, u32[]{:S(2)}) collective-permute-start(f32[40,128]{0,1:T(8,128)S(1)} %copy.39), channel_id=1, source_target_pairs={{0,2},{2,0},{1,3},{3,1},{4,6},{6,4},{5,7},{7,5},{8,10},{10,8},{9,1... | collective-permute-start | bytes 61448 | tf_op jit(solution)/shard_map/ppermute | solution.py:831
  25.3 1.0 copy-done.2
  27.0 1.3 %collective-permute-start.4 = (bf16[1152,256]{1,0:T(8,128)(2,1)}, bf16[1152,256]{1,0:T(8,128)(2,1)}, u32[]{:S(2)}, u32[]{:S(2)}) collective-permute-start(bf16[1152,256]{1,0:T(8,128)(2,1)} %get-tuple-element.46), channel_id=1, source_target_pairs={{8,12},{4,0},{9,13},{5,1},{10,14},{6,2},{11,15},{7,3},{24,28},{20,... | collective-permute-start | bytes 1769480 | tf_op jit(solution)/shard_map/ppermute | solution.py:686
  29.7 0.9 pad_maximum_fusion
  31.4 1.0 %reshape.33 = f32[16,640]{1,0:T(8,128)S(1)} reshape(f32[320,32]{1,0:T(8,128)} %slice.63) | data formatting | bytes 81920 | tf_op jit(solution)/shard_map/reshape | solution.py:1022
  32.4 0.8 fusion.33.constants
  33.2 1.3 %collective-permute-start.8 = (bf16[768,256]{1,0:T(8,128)(2,1)}, bf16[768,256]{1,0:T(8,128)(2,1)}, u32[]{:S(2)}, u32[]{:S(2)}) collective-permute-start(bf16[768,256]{1,0:T(8,128)(2,1)} %get-tuple-element.54), channel_id=1, source_target_pairs={{0,12},{1,13},{2,14},{3,15},{16,28},{17,29},{18,30},{19,31}} | collective-permute-start | bytes 1179656 | tf_op jit(solution)/shard_map/ppermute | solution.py:686
  34.5 1.5 %collective-permute-start.7 = (bf16[768,256]{1,0:T(8,128)(2,1)}, bf16[768,256]{1,0:T(8,128)(2,1)}, u32[]{:S(2)}, u32[]{:S(2)}) collective-permute-start(bf16[768,256]{1,0:T(8,128)(2,1)} %get-tuple-element.54), channel_id=1, source_target_pairs={{4,12},{5,13},{6,14},{7,15},{20,28},{21,29},{22,30},{23,31}} | collective-permute-start | bytes 1179656 | tf_op jit(solution)/shard_map/ppermute | solution.py:686
  37.5 2.9 %main_heads.1 = (f32[3,40,384]{2,1,0:T(8,128)}, f32[3,40,384]{2,1,0:T(8,128)}) custom-call(s32[12]{0:T(128)S(1)} %bitcast_add_fusion.scalars, s32[16]{0:T(128)S(1)} %reshape.30.mask, bf16[384,2560]{1,0:T(8,128)(2,1)} %refs_0_.7, bf16[192,2560]{1,0:T(8,128)(2,1)} %refs_1_.7, bf16[192,2560]{1,0:T(8,128)(2,1)} %refs_2_.7, ...), custom_call_target="tpu_custom_call" | custom-call | flops 1207959552 | bytes 1179648 | tf_op jit(solution)/shard_map/main_heads/pallas_call | solution.py:655
  40.4 15.5 %collective-permute-done.8.refs_11_ = bf16[768,256]{1,0:T(8,128)(2,1)} collective-permute-done((bf16[768,256]{1,0:T(8,128)(2,1)}, bf16[768,256]{1,0:T(8,128)(2,1)}, u32[]{:S(2)}, u32[]{:S(2)}) %collective-permute-start.8) | collective-permute-done | bytes 393248 | tf_op jit(solution)/shard_map/ppermute | solution.py:686
  55.9 9.3 %collective-permute-done.7.refs_10_ = bf16[768,256]{1,0:T(8,128)(2,1)} collective-permute-done((bf16[768,256]{1,0:T(8,128)(2,1)}, bf16[768,256]{1,0:T(8,128)(2,1)}, u32[]{:S(2)}, u32[]{:S(2)}) %collective-permute-start.7) | collective-permute-done | bytes 393248 | tf_op jit(solution)/shard_map/ppermute | solution.py:686
  65.3 8.9 %final_heads.1 = (f32[3,40,384]{2,1,0:T(8,128)}, f32[3,40,384]{2,1,0:T(8,128)}) custom-call(s32[12]{0:T(128)S(1)} %bitcast_add_fusion.scalars, s32[16]{0:T(128)S(1)} %reshape.30.mask, bf16[384,2560]{1,0:T(8,128)(2,1)} %refs_0_.7, bf16[192,2560]{1,0:T(8,128)(2,1)} %refs_1_.7, ...), custom_call_target="tpu_custom_call", output_to_operand_aliasing={{0}: (14, {}), {1}: (15, {})} | custom-call | flops 4831838208 | bytes 1179648 | tf_op jit(solution)/shard_map/final_heads/pallas_call | solution.py:655
  74.8 1.3 %collective-permute-done.10 = f32[3,40,384]{2,1,0:T(8,128)S(1)} collective-permute-done((f32[3,40,384]{2,1,0:T(8,128)}, f32[3,40,384]{2,1,0:T(8,128)S(1)}, u32[]{:S(2)}, u32[]{:S(2)}) %collective-permute-start.10) | collective-permute-done | bytes 184352 | tf_op jit(solution)/shard_map/ppermute | solution.py:1039
  76.0 1.0 add.84
  77.1 1.3 %collective-permute-start.11 = (f32[56,640]{1,0:T(8,128)S(1)}, f32[56,640]{1,0:T(8,128)S(1)}, u32[]{:S(2)}, u32[]{:S(2)}) collective-permute-start(f32[56,640]{1,0:T(8,128)S(1)} %pad_maximum_fusion.1), channel_id=1, source_target_pairs={{0,4},{4,8},{8,12},{1,5},{5,9},{9,13},{2,6},{6,10},{10,14},{3,7},{... | collective-permute-start | bytes 430088 | tf_op jit(solution)/shard_map/ppermute | solution.py:1043
  78.4 1.3 %collective-permute-start.12 = (f32[40,256]{1,0:T(8,128)S(1)}, f32[40,256]{1,0:T(8,128)S(1)}, u32[]{:S(2)}, u32[]{:S(2)}) collective-permute-start(f32[40,256]{1,0:T(8,128)S(1)} %slice.71), channel_id=1, source_target_pairs={{0,8},{4,12},{1,9},{5,13},{2,10},{6,14},{3,11},{7,15},{16,24},{20,... | collective-permute-start | bytes 122888 | tf_op jit(solution)/shard_map/ppermute | solution.py:1048
  79.7 4.5 %collective-permute-start.13 = (f32[40,384]{1,0:T(8,128)S(1)}, f32[40,384]{1,0:T(8,128)S(1)}, u32[]{:S(2)}, u32[]{:S(2)}) collective-permute-start(f32[40,384]{1,0:T(8,128)S(1)} %get-tuple-element.70), channel_id=1, source_target_pairs={{4,12},{12,8},{5,13},{13,9},{6,14},{14,10},{7,15},{15,11},{20,28},... | collective-permute-start | bytes 184328 | tf_op jit(solution)/shard_map/ppermute | solution.py:1047
  84.2 2.4 %collective-permute-done.12 = f32[40,256]{1,0:T(8,128)S(1)} collective-permute-done((f32[40,256]{1,0:T(8,128)S(1)}, f32[40,256]{1,0:T(8,128)S(1)}, u32[]{:S(2)}, u32[]{:S(2)}) %collective-permute-start.12) | collective-permute-done | bytes 40992 | tf_op jit(solution)/shard_map/ppermute | solution.py:1048
  86.7 2.0 %collective-permute-done.13 = f32[40,384]{1,0:T(8,128)S(1)} collective-permute-done((f32[40,384]{1,0:T(8,128)S(1)}, f32[40,384]{1,0:T(8,128)S(1)}, u32[]{:S(2)}, u32[]{:S(2)}) %collective-permute-start.13) | collective-permute-done | bytes 61472 | tf_op jit(solution)/shard_map/ppermute | solution.py:1047
  88.8 1.2 %collective-permute-start.14 = (f32[40,640]{1,0:T(8,128)S(1)}, f32[40,640]{1,0:T(8,128)S(1)}, u32[]{:S(2)}, u32[]{:S(2)}) collective-permute-start(f32[40,640]{1,0:T(8,128)S(1)} %fusion.32), channel_id=1, source_target_pairs={{0,2},{2,0},{1,3},{3,1},{4,6},{6,4},{5,7},{7,5},{8,10},{10,8},{9,1... | collective-permute-start | bytes 307208 | tf_op jit(solution)/shard_map/ppermute | solution.py:1051
  89.9 2.4 %collective-permute-done.14 = f32[40,640]{1,0:T(8,128)S(1)} collective-permute-done((f32[40,640]{1,0:T(8,128)S(1)}, f32[40,640]{1,0:T(8,128)S(1)}, u32[]{:S(2)}, u32[]{:S(2)}) %collective-permute-start.14) | collective-permute-done | bytes 102432 | tf_op jit(solution)/shard_map/ppermute | solution.py:1051
  92.4 2.4 %collective-permute-start.15 = (f32[40,640]{1,0:T(8,128)S(1)}, f32[40,640]{1,0:T(8,128)S(1)}, u32[]{:S(2)}, u32[]{:S(2)}) collective-permute-start(f32[40,640]{1,0:T(8,128)S(1)} %add.87.mine), channel_id=1, source_target_pairs={{0,1},{1,0},{2,3},{3,2},{4,5},{5,4},{6,7},{7,6},{8,9},{9,8},{10,11... | collective-permute-start | bytes 307208 | tf_op jit(solution)/shard_map/ppermute | solution.py:1052
  94.9 0.8 collective-permute-done.15.other
  95.7 2.4 %finish.1 = (f32[3,8,16,16]{3,2,1,0:T(8,128)}, bf16[3,8,16,384]{3,2,1,0:T(8,128)(2,1)}) custom-call(s32[12]{0:T(128)S(1)} %bitcast_add_fusion.scalars, f32[40,640]{1,0:T(8,128)S(1)} %add.87.mine, f32[40,640]{1,0:T(8,128)S(1)} %collective-permute-done.15.other, f32[320,48]{1,0:T(8,128)S(1)} %bitcast.33, f32[320,32]{1,0:T(8,128)S(1)} %reshape.34.before, ...), custom_call_target="tpu_custom_call" | custom-call | tf_op jit(solution)/shard_map/finish/pallas_call | solution.py:961
  (62 shorter events, 9.5 us)
Async XLA Ops:
  0.6 23.9 %copy-start = (f32[384]{0:T(512)S(1)}, f32[384]{0:T(512)}, u32[]{:S(2)}) copy-start(f32[384]{0:T(512)} %param.21) | copy-start | bytes 4612
  0.6 2.0 %copy-start.8 = (s32[12]{0:T(128)S(1)}, s32[12]{0:T(128)}, u32[]{:S(2)}) copy-start(s32[12]{0:T(128)} %constant.107.clone) | copy-start | bytes 148
  1.9 2.9 %collective-permute-start = (bf16[384,1280]{1,0:T(8,128)(2,1)S(1)}, bf16[384,1280]{1,0:T(8,128)(2,1)S(1)}, u32[]{:S(2)}, u32[]{:S(2)}) collective-permute-start(bf16[384,1280]{1,0:T(8,128)(2,1)S(1)} %pack_handed.1), channel_id=1, source_target_pairs={{0,1},{1,0},{2,3},{3,2},{4,5},{5,4},{6,7},{7,6},{8,9},{9,8},{10,11... | collective-permute-start | bytes 2949128 | tf_op jit(solution)/shard_map/ppermute | solution.py:703
  7.7 29.8 %collective-permute-start.2 = (bf16[1152,512]{1,0:T(8,128)(2,1)}, bf16[1152,512]{1,0:T(8,128)(2,1)}, u32[]{:S(2)}, u32[]{:S(2)}) collective-permute-start(bf16[1152,512]{1,0:T(8,128)(2,1)} %get-tuple-element.39), channel_id=1, source_target_pairs={{4,0},{8,4},{12,8},{5,1},{9,5},{13,9},{6,2},{10,6},{14,10},{7,3},{... | collective-permute-start | bytes 3538952 | tf_op jit(solution)/shard_map/ppermute | solution.py:686
  10.8 8.9 %copy-start.4 = (f32[3,8,16,16]{3,2,1,0:T(8,128)S(1)}, f32[3,8,16,16]{3,2,1,0:T(8,128)}, u32[]{:S(2)}) copy-start(f32[3,8,16,16]{3,2,1,0:T(8,128)} %param.19) | copy-start | bytes 73732
  10.8 12.0 %copy-start.1 = (bf16[2560,64]{0,1:T(8,128)(2,1)S(1)}, bf16[2560,64]{0,1:T(8,128)(2,1)}, u32[]{:S(2)}) copy-start(bf16[2560,64]{0,1:T(8,128)(2,1)} %param.18) | copy-start | bytes 983044
  10.8 12.0 %copy-start.6 = (f32[2560]{0:T(1024)S(1)}, f32[2560]{0:T(1024)}, u32[]{:S(2)}) copy-start(f32[2560]{0:T(1024)} %param.16) | copy-start | bytes 30724
  10.8 12.0 %copy-start.7 = (f32[2560]{0:T(1024)S(1)}, f32[2560]{0:T(1024)}, u32[]{:S(2)}) copy-start(f32[2560]{0:T(1024)} %param.17) | copy-start | bytes 30724
  10.9 22.4 %collective-permute-start.1 = (bf16[768,512]{1,0:T(8,128)(2,1)}, bf16[768,512]{1,0:T(8,128)(2,1)}, u32[]{:S(2)}, u32[]{:S(2)}) collective-permute-start(bf16[768,512]{1,0:T(8,128)(2,1)} %get-tuple-element.45), channel_id=1, source_target_pairs={{0,4},{4,8},{1,5},{5,9},{2,6},{6,10},{3,7},{7,11},{16,20},{20,24},... | collective-permute-start | bytes 2359304 | tf_op jit(solution)/shard_map/ppermute | solution.py:686
  16.1 49.2 %collective-permute-start.3 = (bf16[1152,512]{1,0:T(8,128)(2,1)}, bf16[1152,512]{1,0:T(8,128)(2,1)}, u32[]{:S(2)}, u32[]{:S(2)}) collective-permute-start(bf16[1152,512]{1,0:T(8,128)(2,1)} %get-tuple-element.41), channel_id=1, source_target_pairs={{12,4},{13,5},{14,6},{15,7},{28,20},{29,21},{30,22},{31,23}} | collective-permute-start | bytes 3538952 | tf_op jit(solution)/shard_map/ppermute | solution.py:686
  20.0 3.1 %collective-permute-start.5 = (f32[8,48]{1,0:T(8,128)S(1)}, f32[8,48]{1,0:T(8,128)S(1)}, u32[]{:S(2)}, u32[]{:S(2)}) collective-permute-start(f32[8,48]{1,0:T(8,128)S(1)} %bitcast.42), channel_id=1, source_target_pairs={{0,1},{1,0},{2,3},{3,2},{4,5},{5,4},{6,7},{7,6},{8,9},{9,8},{10,11... | collective-permute-start | bytes 4616 | tf_op jit(solution)/shard_map/ppermute | solution.py:816
  21.3 13.3 %collective-permute-start.9 = (bf16[768,512]{1,0:T(8,128)(2,1)}, bf16[768,512]{1,0:T(8,128)(2,1)}, u32[]{:S(2)}, u32[]{:S(2)}) collective-permute-start(bf16[768,512]{1,0:T(8,128)(2,1)} %get-tuple-element.55), channel_id=1, source_target_pairs={{0,8},{1,9},{2,10},{3,11},{16,24},{17,25},{18,26},{19,27}} | collective-permute-start | bytes 2359304 | tf_op jit(solution)/shard_map/ppermute | solution.py:686
  23.1 1.4 %copy-start.3 = (f32[8,14,48]{2,1,0:T(8,128)}, f32[8,14,48]{2,1,0:T(8,128)S(1)}, u32[]{:S(2)}) copy-start(f32[8,14,48]{2,1,0:T(8,128)S(1)} %broadcast_in_dim.26) | copy-start | bytes 64516
  23.3 3.8 %collective-permute-start.6 = (f32[40,128]{0,1:T(8,128)S(1)}, f32[40,128]{0,1:T(8,128)S(1)}, u32[]{:S(2)}, u32[]{:S(2)}) collective-permute-start(f32[40,128]{0,1:T(8,128)S(1)} %copy.39), channel_id=1, source_target_pairs={{0,2},{2,0},{1,3},{3,1},{4,6},{6,4},{5,7},{7,5},{8,10},{10,8},{9,1... | collective-permute-start | bytes 61448 | tf_op jit(solution)/shard_map/ppermute | solution.py:831
  25.2 1.0 copy-start.2
  27.0 2.0 %copy-start.5 = (f32[40,128]{0,1:T(8,128)}, f32[40,128]{0,1:T(8,128)S(1)}, u32[]{:S(2)}) copy-start(f32[40,128]{0,1:T(8,128)S(1)} %collective-permute-done.6) | copy-start | bytes 61444
  27.0 38.2 %collective-permute-start.4 = (bf16[1152,256]{1,0:T(8,128)(2,1)}, bf16[1152,256]{1,0:T(8,128)(2,1)}, u32[]{:S(2)}, u32[]{:S(2)}) collective-permute-start(bf16[1152,256]{1,0:T(8,128)(2,1)} %get-tuple-element.46), channel_id=1, source_target_pairs={{8,12},{4,0},{9,13},{5,1},{10,14},{6,2},{11,15},{7,3},{24,28},{20,... | collective-permute-start | bytes 1769480 | tf_op jit(solution)/shard_map/ppermute | solution.py:686
  33.2 22.7 %collective-permute-start.8 = (bf16[768,256]{1,0:T(8,128)(2,1)}, bf16[768,256]{1,0:T(8,128)(2,1)}, u32[]{:S(2)}, u32[]{:S(2)}) collective-permute-start(bf16[768,256]{1,0:T(8,128)(2,1)} %get-tuple-element.54), channel_id=1, source_target_pairs={{0,12},{1,13},{2,14},{3,15},{16,28},{17,29},{18,30},{19,31}} | collective-permute-start | bytes 1179656 | tf_op jit(solution)/shard_map/ppermute | solution.py:686
  34.5 30.7 %collective-permute-start.7 = (bf16[768,256]{1,0:T(8,128)(2,1)}, bf16[768,256]{1,0:T(8,128)(2,1)}, u32[]{:S(2)}, u32[]{:S(2)}) collective-permute-start(bf16[768,256]{1,0:T(8,128)(2,1)} %get-tuple-element.54), channel_id=1, source_target_pairs={{4,12},{5,13},{6,14},{7,15},{20,28},{21,29},{22,30},{23,31}} | collective-permute-start | bytes 1179656 | tf_op jit(solution)/shard_map/ppermute | solution.py:686
  74.2 1.8 %collective-permute-start.10 = (f32[3,40,384]{2,1,0:T(8,128)}, f32[3,40,384]{2,1,0:T(8,128)S(1)}, u32[]{:S(2)}, u32[]{:S(2)}) collective-permute-start(f32[3,40,384]{2,1,0:T(8,128)} %get-tuple-element.67), channel_id=1, source_target_pairs={{0,1},{1,0},{2,3},{3,2},{4,5},{5,4},{6,7},{7,6},{8,9},{9,8},{10,11... | collective-permute-start | bytes 552968 | tf_op jit(solution)/shard_map/ppermute | solution.py:1039
  77.1 11.7 %collective-permute-start.11 = (f32[56,640]{1,0:T(8,128)S(1)}, f32[56,640]{1,0:T(8,128)S(1)}, u32[]{:S(2)}, u32[]{:S(2)}) collective-permute-start(f32[56,640]{1,0:T(8,128)S(1)} %pad_maximum_fusion.1), channel_id=1, source_target_pairs={{0,4},{4,8},{8,12},{1,5},{5,9},{9,13},{2,6},{6,10},{10,14},{3,7},{... | collective-permute-start | bytes 430088 | tf_op jit(solution)/shard_map/ppermute | solution.py:1043
  78.4 8.3 %collective-permute-start.12 = (f32[40,256]{1,0:T(8,128)S(1)}, f32[40,256]{1,0:T(8,128)S(1)}, u32[]{:S(2)}, u32[]{:S(2)}) collective-permute-start(f32[40,256]{1,0:T(8,128)S(1)} %slice.71), channel_id=1, source_target_pairs={{0,8},{4,12},{1,9},{5,13},{2,10},{6,14},{3,11},{7,15},{16,24},{20,... | collective-permute-start | bytes 122888 | tf_op jit(solution)/shard_map/ppermute | solution.py:1048
  79.7 9.1 %collective-permute-start.13 = (f32[40,384]{1,0:T(8,128)S(1)}, f32[40,384]{1,0:T(8,128)S(1)}, u32[]{:S(2)}, u32[]{:S(2)}) collective-permute-start(f32[40,384]{1,0:T(8,128)S(1)} %get-tuple-element.70), channel_id=1, source_target_pairs={{4,12},{12,8},{5,13},{13,9},{6,14},{14,10},{7,15},{15,11},{20,28},... | collective-permute-start | bytes 184328 | tf_op jit(solution)/shard_map/ppermute | solution.py:1047
  88.8 3.6 %collective-permute-start.14 = (f32[40,640]{1,0:T(8,128)S(1)}, f32[40,640]{1,0:T(8,128)S(1)}, u32[]{:S(2)}, u32[]{:S(2)}) collective-permute-start(f32[40,640]{1,0:T(8,128)S(1)} %fusion.32), channel_id=1, source_target_pairs={{0,2},{2,0},{1,3},{3,1},{4,6},{6,4},{5,7},{7,5},{8,10},{10,8},{9,1... | collective-permute-start | bytes 307208 | tf_op jit(solution)/shard_map/ppermute | solution.py:1051
  92.4 3.4 %collective-permute-start.15 = (f32[40,640]{1,0:T(8,128)S(1)}, f32[40,640]{1,0:T(8,128)S(1)}, u32[]{:S(2)}, u32[]{:S(2)}) collective-permute-start(f32[40,640]{1,0:T(8,128)S(1)} %add.87.mine), channel_id=1, source_target_pairs={{0,1},{1,0},{2,3},{3,2},{4,5},{5,4},{6,7},{7,6},{8,9},{9,8},{10,11... | collective-permute-start | bytes 307208 | tf_op jit(solution)/shard_map/ppermute | solution.py:1052

commit v16 on v15

--- a/solution.py
+++ b/solution.py
@@ -728,7 +728,7 @@
     up_two = send(up_two, (0, 2))
     two = send(two, (3, 1))
     far_next = send(far_all, (2, 3), (1, 0))
-    far_pair, prepared = lax.optimization_barrier((far_pair, prepare(anchor)))
+    prepared = prepare(anchor)
     far_two = send(far_pair, (1, 3))
     far_three = send(far_pair, (0, 3))
 

time: 98.8 us -> 102 us (1.032)
  starting transfers between devices: 28.6 us -> 31.3 us
  local copies, waits for them, and re-layouts: 6.84 us -> 5.49 us
  waiting for transfers between devices: 35.2 us -> 36.5 us
    ppermute x1, starting transfers between devices: 4.55 us -> 7.23 us  [per_device(): to_current = lax.ppermute(sent_current, 'span', [(1, 3), (3, 2)])]
    ppermute x7, waiting for transfers between devices: 24.8 us -> 26.2 us  [send(): return in_place(lax.ppermute(value, 'span', list(pairs)))]
  transfers between devices with their start and end apart: 16 -> 16, of which waited for: 9 -> 9; matrix products, arithmetic and copies ran while one was open for 9% -> 7% of each run, Pallas kernels for 7% -> 7%
where the time goes in v16:
time: 102 us
  waiting for transfers between devices  36.5 us (36%)
  starting transfers between devices  31.3 us (31%)
  Pallas kernels  22.1 us (22%)
  local copies, waits for them, and re-layouts  5.49 us (5%)
  other arithmetic  5.25 us (5%)
    ppermute x7, waiting for transfers between devices, send(): return in_place(lax.ppermute(value, 'span', list(pairs)))  26.2 us
    ppermute x7, starting transfers between devices, send(): return in_place(lax.ppermute(value, 'span', list(pairs)))  14.1 us
    pallas_call x2, Pallas kernels, attend(): pl.pallas_call(functools.partial(attend_kernel, variants, 0, span_count,...  11.9 us
    ppermute x1, starting transfers between devices, per_device(): to_current = lax.ppermute(sent_current, 'span', [(1, 3), (3, 2)])  7.23 us
    pallas_call x2, Pallas kernels, pack(): pl.pallas_call(functools.partial(pack_kernel, len(arrays), len(shapes), c...  6.45 us
    ppermute x1, waiting for transfers between devices, per_device(): to_before = lax.ppermute(sent_before, 'span', [(0, 2), (1, 3)])  2.44 us
    ppermute x1, starting transfers between devices, per_device(): other = lax.ppermute(total, 'slab', SWAP)  2.42 us
    ppermute x1, waiting for transfers between devices, per_device(): total = total + lax.ppermute(total, 'head', SWAP)  2.4 us
  transfers between devices with their start and end apart: 16, of which 9 were waited for; matrix products, arithmetic and copies ran while one was open for 7% of the time, Pallas kernels for 7%

profile of v16, /device:TPU:25, one launch (start us, length us, event | category | flops | bytes accessed | tf_op | source)
XLA Modules:
  0.0 101.6 jit_solution(8786267453299183733)
XLA Ops:
  0.7 1.2 %pack_handed.1 = bf16[384,1280]{1,0:T(8,128)(2,1)S(1)} custom-call(bf16[192,2560]{1,0:T(8,128)(2,1)} %refs_1_.7, bf16[192,2560]{1,0:T(8,128)(2,1)} %refs_2_.7), custom_call_target="tpu_custom_call" | custom-call | bytes 1966080 | tf_op jit(solution)/shard_map/pack_handed/pallas_call | solution.py:324
  4.8 2.9 %pack_first.1 = (bf16[768,512]{1,0:T(8,128)(2,1)}, bf16[1152,512]{1,0:T(8,128)(2,1)}) custom-call(s32[12]{0:T(128)S(1)} %bitcast_add_fusion.scalars, bf16[384,2560]{1,0:T(8,128)(2,1)} %refs_0_.7, bf16[192,2560]{1,0:T(8,128)(2,1)} %refs_1_.7, bf16[192,2560]{1,0:T(8,128)(2,1)} %refs_2_.7, bf16[384,1280]{1,0:T(8,128)(2,1)S(1)} %collective-permute-done.refs_3_), custom_call_target="tpu_custom_call" | custom-call | bytes 3932160 | tf_op jit(solution)/shard_map/pack_first/pallas_call | solution.py:286
  7.8 3.1 %collective-permute-start.2 = (bf16[1152,512]{1,0:T(8,128)(2,1)}, bf16[1152,512]{1,0:T(8,128)(2,1)}, u32[]{:S(2)}, u32[]{:S(2)}) collective-permute-start(bf16[1152,512]{1,0:T(8,128)(2,1)} %get-tuple-element.32), channel_id=1, source_target_pairs={{4,0},{8,4},{12,8},{5,1},{9,5},{13,9},{6,2},{10,6},{14,10},{7,3},{... | collective-permute-start | bytes 3538952 | tf_op jit(solution)/shard_map/ppermute | solution.py:686
  10.9 1.7 %collective-permute-start.1 = (bf16[768,512]{1,0:T(8,128)(2,1)}, bf16[768,512]{1,0:T(8,128)(2,1)}, u32[]{:S(2)}, u32[]{:S(2)}) collective-permute-start(bf16[768,512]{1,0:T(8,128)(2,1)} %get-tuple-element.38), channel_id=1, source_target_pairs={{0,4},{4,8},{1,5},{5,9},{2,6},{6,10},{3,7},{7,11},{16,20},{20,24},... | collective-permute-start | bytes 2359304 | tf_op jit(solution)/shard_map/ppermute | solution.py:686
  12.6 3.5 %pack_second.1 = (bf16[768,512]{1,0:T(8,128)(2,1)}, bf16[1152,512]{1,0:T(8,128)(2,1)}, bf16[1152,256]{1,0:T(8,128)(2,1)}, bf16[768,256]{1,0:T(8,128)(2,1)}) custom-call(s32[12]{0:T(128)S(1)} %bitcast_add_fusion.scalars, bf16[384,2560]{1,0:T(8,128)(2,1)} %refs_0_.7, bf16[192,2560]{1,0:T(8,128)(2,1)} %refs_1_.7, bf16[192,2560]{1,0:T(8,128)(2,1)} %refs_2_.7, ...), custom_call_target="tpu_custom_call" | custom-call | bytes 5898240 | tf_op jit(solution)/shard_map/pack_second/pallas_call | solution.py:286
  16.1 3.7 %collective-permute-start.3 = (bf16[1152,512]{1,0:T(8,128)(2,1)}, bf16[1152,512]{1,0:T(8,128)(2,1)}, u32[]{:S(2)}, u32[]{:S(2)}) collective-permute-start(bf16[1152,512]{1,0:T(8,128)(2,1)} %get-tuple-element.34), channel_id=1, source_target_pairs={{12,4},{13,5},{14,6},{15,7},{28,20},{29,21},{30,22},{31,23}} | collective-permute-start | bytes 3538952 | tf_op jit(solution)/shard_map/ppermute | solution.py:686
  20.1 1.3 %collective-permute-start.8 = (f32[8,48]{1,0:T(8,128)S(1)}, f32[8,48]{1,0:T(8,128)S(1)}, u32[]{:S(2)}, u32[]{:S(2)}) collective-permute-start(f32[8,48]{1,0:T(8,128)S(1)} %bitcast.42), channel_id=1, source_target_pairs={{0,1},{1,0},{2,3},{3,2},{4,5},{5,4},{6,7},{7,6},{8,9},{9,8},{10,11... | collective-permute-start | bytes 4616 | tf_op jit(solution)/shard_map/ppermute | solution.py:816
  21.4 1.6 %collective-permute-start.7 = (bf16[768,512]{1,0:T(8,128)(2,1)}, bf16[768,512]{1,0:T(8,128)(2,1)}, u32[]{:S(2)}, u32[]{:S(2)}) collective-permute-start(bf16[768,512]{1,0:T(8,128)(2,1)} %get-tuple-element.41), channel_id=1, source_target_pairs={{0,8},{1,9},{2,10},{3,11},{16,24},{17,25},{18,26},{19,27}} | collective-permute-start | bytes 2359304 | tf_op jit(solution)/shard_map/ppermute | solution.py:686
  24.0 1.3 %collective-permute-start.9 = (f32[40,128]{0,1:T(8,128)S(1)}, f32[40,128]{0,1:T(8,128)S(1)}, u32[]{:S(2)}, u32[]{:S(2)}) collective-permute-start(f32[40,128]{0,1:T(8,128)S(1)} %copy.39), channel_id=1, source_target_pairs={{0,2},{2,0},{1,3},{3,1},{4,6},{6,4},{5,7},{7,5},{8,10},{10,8},{9,1... | collective-permute-start | bytes 61448 | tf_op jit(solution)/shard_map/ppermute | solution.py:831
  26.1 1.0 copy-done.2
  27.7 1.3 %collective-permute-start.4 = (bf16[1152,256]{1,0:T(8,128)(2,1)}, bf16[1152,256]{1,0:T(8,128)(2,1)}, u32[]{:S(2)}, u32[]{:S(2)}) collective-permute-start(bf16[1152,256]{1,0:T(8,128)(2,1)} %get-tuple-element.39), channel_id=1, source_target_pairs={{8,12},{4,0},{9,13},{5,1},{10,14},{6,2},{11,15},{7,3},{24,28},{20,... | collective-permute-start | bytes 1769480 | tf_op jit(solution)/shard_map/ppermute | solution.py:686
  29.2 1.3 %collective-permute-start.6 = (bf16[768,256]{1,0:T(8,128)(2,1)}, bf16[768,256]{1,0:T(8,128)(2,1)}, u32[]{:S(2)}, u32[]{:S(2)}) collective-permute-start(bf16[768,256]{1,0:T(8,128)(2,1)} %get-tuple-element.40), channel_id=1, source_target_pairs={{0,12},{1,13},{2,14},{3,15},{16,28},{17,29},{18,30},{19,31}} | collective-permute-start | bytes 1179656 | tf_op jit(solution)/shard_map/ppermute | solution.py:686
  30.5 1.5 %collective-permute-start.5 = (bf16[768,256]{1,0:T(8,128)(2,1)}, bf16[768,256]{1,0:T(8,128)(2,1)}, u32[]{:S(2)}, u32[]{:S(2)}) collective-permute-start(bf16[768,256]{1,0:T(8,128)(2,1)} %get-tuple-element.40), channel_id=1, source_target_pairs={{4,12},{5,13},{6,14},{7,15},{20,28},{21,29},{22,30},{23,31}} | collective-permute-start | bytes 1179656 | tf_op jit(solution)/shard_map/ppermute | solution.py:686
  32.0 0.9 pad_maximum_fusion
  33.7 1.6 %reshape.33 = f32[16,640]{1,0:T(8,128)} reshape(f32[320,32]{1,0:T(8,128)} %slice.63) | data formatting | bytes 81920 | tf_op jit(solution)/shard_map/reshape | solution.py:1022
  35.3 0.9 fusion.33.constants
  36.2 2.9 %main_heads.1 = (f32[3,40,384]{2,1,0:T(8,128)}, f32[3,40,384]{2,1,0:T(8,128)}) custom-call(s32[12]{0:T(128)S(1)} %bitcast_add_fusion.scalars, s32[16]{0:T(128)S(1)} %reshape.30.mask, bf16[384,2560]{1,0:T(8,128)(2,1)} %refs_0_.7, bf16[192,2560]{1,0:T(8,128)(2,1)} %refs_1_.7, bf16[192,2560]{1,0:T(8,128)(2,1)} %refs_2_.7, ...), custom_call_target="tpu_custom_call" | custom-call | flops 1207959552 | bytes 1179648 | tf_op jit(solution)/shard_map/main_heads/pallas_call | solution.py:655
  39.1 16.8 %collective-permute-done.6.refs_11_ = bf16[768,256]{1,0:T(8,128)(2,1)} collective-permute-done((bf16[768,256]{1,0:T(8,128)(2,1)}, bf16[768,256]{1,0:T(8,128)(2,1)}, u32[]{:S(2)}, u32[]{:S(2)}) %collective-permute-start.6) | collective-permute-done | bytes 393248 | tf_op jit(solution)/shard_map/ppermute | solution.py:686
  55.9 9.3 %collective-permute-done.5.refs_10_ = bf16[768,256]{1,0:T(8,128)(2,1)} collective-permute-done((bf16[768,256]{1,0:T(8,128)(2,1)}, bf16[768,256]{1,0:T(8,128)(2,1)}, u32[]{:S(2)}, u32[]{:S(2)}) %collective-permute-start.5) | collective-permute-done | bytes 393248 | tf_op jit(solution)/shard_map/ppermute | solution.py:686
  65.3 8.9 %final_heads.1 = (f32[3,40,384]{2,1,0:T(8,128)}, f32[3,40,384]{2,1,0:T(8,128)}) custom-call(s32[12]{0:T(128)S(1)} %bitcast_add_fusion.scalars, s32[16]{0:T(128)S(1)} %reshape.30.mask, bf16[384,2560]{1,0:T(8,128)(2,1)} %refs_0_.7, bf16[192,2560]{1,0:T(8,128)(2,1)} %refs_1_.7, ...), custom_call_target="tpu_custom_call", output_to_operand_aliasing={{0}: (14, {}), {1}: (15, {})} | custom-call | flops 4831838208 | bytes 1179648 | tf_op jit(solution)/shard_map/final_heads/pallas_call | solution.py:655
  74.8 1.3 %collective-permute-done.10 = f32[3,40,384]{2,1,0:T(8,128)S(1)} collective-permute-done((f32[3,40,384]{2,1,0:T(8,128)}, f32[3,40,384]{2,1,0:T(8,128)S(1)}, u32[]{:S(2)}, u32[]{:S(2)}) %collective-permute-start.10) | collective-permute-done | bytes 184352 | tf_op jit(solution)/shard_map/ppermute | solution.py:1039
  76.1 1.0 add.84
  77.9 1.3 %collective-permute-start.11 = (f32[56,640]{1,0:T(8,128)S(1)}, f32[56,640]{1,0:T(8,128)S(1)}, u32[]{:S(2)}, u32[]{:S(2)}) collective-permute-start(f32[56,640]{1,0:T(8,128)S(1)} %pad_maximum_fusion.1), channel_id=1, source_target_pairs={{0,4},{4,8},{8,12},{1,5},{5,9},{9,13},{2,6},{6,10},{10,14},{3,7},{... | collective-permute-start | bytes 430088 | tf_op jit(solution)/shard_map/ppermute | solution.py:1043
  79.2 1.3 %collective-permute-start.12 = (f32[40,256]{1,0:T(8,128)S(1)}, f32[40,256]{1,0:T(8,128)S(1)}, u32[]{:S(2)}, u32[]{:S(2)}) collective-permute-start(f32[40,256]{1,0:T(8,128)S(1)} %slice.71), channel_id=1, source_target_pairs={{0,8},{4,12},{1,9},{5,13},{2,10},{6,14},{3,11},{7,15},{16,24},{20,... | collective-permute-start | bytes 122888 | tf_op jit(solution)/shard_map/ppermute | solution.py:1048
  80.5 7.2 %collective-permute-start.13 = (f32[40,384]{1,0:T(8,128)S(1)}, f32[40,384]{1,0:T(8,128)S(1)}, u32[]{:S(2)}, u32[]{:S(2)}) collective-permute-start(f32[40,384]{1,0:T(8,128)S(1)} %get-tuple-element.56), channel_id=1, source_target_pairs={{4,12},{12,8},{5,13},{13,9},{6,14},{14,10},{7,15},{15,11},{20,28},... | collective-permute-start | bytes 184328 | tf_op jit(solution)/shard_map/ppermute | solution.py:1047
  87.7 2.4 %collective-permute-done.12 = f32[40,256]{1,0:T(8,128)S(1)} collective-permute-done((f32[40,256]{1,0:T(8,128)S(1)}, f32[40,256]{1,0:T(8,128)S(1)}, u32[]{:S(2)}, u32[]{:S(2)}) %collective-permute-start.12) | collective-permute-done | bytes 40992 | tf_op jit(solution)/shard_map/ppermute | solution.py:1048
  90.2 2.0 %collective-permute-done.13 = f32[40,384]{1,0:T(8,128)S(1)} collective-permute-done((f32[40,384]{1,0:T(8,128)S(1)}, f32[40,384]{1,0:T(8,128)S(1)}, u32[]{:S(2)}, u32[]{:S(2)}) %collective-permute-start.13) | collective-permute-done | bytes 61472 | tf_op jit(solution)/shard_map/ppermute | solution.py:1047
  92.3 1.2 %collective-permute-start.14 = (f32[40,640]{1,0:T(8,128)S(1)}, f32[40,640]{1,0:T(8,128)S(1)}, u32[]{:S(2)}, u32[]{:S(2)}) collective-permute-start(f32[40,640]{1,0:T(8,128)S(1)} %fusion.32), channel_id=1, source_target_pairs={{0,2},{2,0},{1,3},{3,1},{4,6},{6,4},{5,7},{7,5},{8,10},{10,8},{9,1... | collective-permute-start | bytes 307208 | tf_op jit(solution)/shard_map/ppermute | solution.py:1051
  93.4 2.4 %collective-permute-done.14 = f32[40,640]{1,0:T(8,128)S(1)} collective-permute-done((f32[40,640]{1,0:T(8,128)S(1)}, f32[40,640]{1,0:T(8,128)S(1)}, u32[]{:S(2)}, u32[]{:S(2)}) %collective-permute-start.14) | collective-permute-done | bytes 102432 | tf_op jit(solution)/shard_map/ppermute | solution.py:1051
  95.8 2.4 %collective-permute-start.15 = (f32[40,640]{1,0:T(8,128)S(1)}, f32[40,640]{1,0:T(8,128)S(1)}, u32[]{:S(2)}, u32[]{:S(2)}) collective-permute-start(f32[40,640]{1,0:T(8,128)S(1)} %add.87.mine), channel_id=1, source_target_pairs={{0,1},{1,0},{2,3},{3,2},{4,5},{5,4},{6,7},{7,6},{8,9},{9,8},{10,11... | collective-permute-start | bytes 307208 | tf_op jit(solution)/shard_map/ppermute | solution.py:1052
  98.4 0.8 collective-permute-done.15.other
  99.2 2.4 %finish.1 = (f32[3,8,16,16]{3,2,1,0:T(8,128)}, bf16[3,8,16,384]{3,2,1,0:T(8,128)(2,1)}) custom-call(s32[12]{0:T(128)S(1)} %bitcast_add_fusion.scalars, f32[40,640]{1,0:T(8,128)S(1)} %add.87.mine, f32[40,640]{1,0:T(8,128)S(1)} %collective-permute-done.15.other, f32[320,48]{1,0:T(8,128)S(1)} %bitcast.33, f32[320,32]{1,0:T(8,128)S(1)} %reshape.34.before, ...), custom_call_target="tpu_custom_call" | custom-call | tf_op jit(solution)/shard_map/finish/pallas_call | solution.py:961
  (66 shorter events, 8.2 us)
Async XLA Ops:
  0.6 24.6 %copy-start = (f32[384]{0:T(512)S(1)}, f32[384]{0:T(512)}, u32[]{:S(2)}) copy-start(f32[384]{0:T(512)} %param.21) | copy-start | bytes 4612
  0.6 2.0 %copy-start.10 = (s32[12]{0:T(128)S(1)}, s32[12]{0:T(128)}, u32[]{:S(2)}) copy-start(s32[12]{0:T(128)} %constant.107.clone) | copy-start | bytes 148
  1.9 2.9 %collective-permute-start = (bf16[384,1280]{1,0:T(8,128)(2,1)S(1)}, bf16[384,1280]{1,0:T(8,128)(2,1)S(1)}, u32[]{:S(2)}, u32[]{:S(2)}) collective-permute-start(bf16[384,1280]{1,0:T(8,128)(2,1)S(1)} %pack_handed.1), channel_id=1, source_target_pairs={{0,1},{1,0},{2,3},{3,2},{4,5},{5,4},{6,7},{7,6},{8,9},{9,8},{10,11... | collective-permute-start | bytes 2949128 | tf_op jit(solution)/shard_map/ppermute | solution.py:703
  7.8 28.4 %collective-permute-start.2 = (bf16[1152,512]{1,0:T(8,128)(2,1)}, bf16[1152,512]{1,0:T(8,128)(2,1)}, u32[]{:S(2)}, u32[]{:S(2)}) collective-permute-start(bf16[1152,512]{1,0:T(8,128)(2,1)} %get-tuple-element.32), channel_id=1, source_target_pairs={{4,0},{8,4},{12,8},{5,1},{9,5},{13,9},{6,2},{10,6},{14,10},{7,3},{... | collective-permute-start | bytes 3538952 | tf_op jit(solution)/shard_map/ppermute | solution.py:686
  10.9 8.9 %copy-start.5 = (f32[3,8,16,16]{3,2,1,0:T(8,128)S(1)}, f32[3,8,16,16]{3,2,1,0:T(8,128)}, u32[]{:S(2)}) copy-start(f32[3,8,16,16]{3,2,1,0:T(8,128)} %param.19) | copy-start | bytes 73732
  10.9 12.1 %copy-start.1 = (bf16[2560,64]{0,1:T(8,128)(2,1)S(1)}, bf16[2560,64]{0,1:T(8,128)(2,1)}, u32[]{:S(2)}) copy-start(bf16[2560,64]{0,1:T(8,128)(2,1)} %param.18) | copy-start | bytes 983044
  10.9 12.1 %copy-start.7 = (f32[2560]{0:T(1024)S(1)}, f32[2560]{0:T(1024)}, u32[]{:S(2)}) copy-start(f32[2560]{0:T(1024)} %param.16) | copy-start | bytes 30724
  10.9 12.1 %copy-start.8 = (f32[2560]{0:T(1024)S(1)}, f32[2560]{0:T(1024)}, u32[]{:S(2)}) copy-start(f32[2560]{0:T(1024)} %param.17) | copy-start | bytes 30724
  10.9 18.3 %collective-permute-start.1 = (bf16[768,512]{1,0:T(8,128)(2,1)}, bf16[768,512]{1,0:T(8,128)(2,1)}, u32[]{:S(2)}, u32[]{:S(2)}) collective-permute-start(bf16[768,512]{1,0:T(8,128)(2,1)} %get-tuple-element.38), channel_id=1, source_target_pairs={{0,4},{4,8},{1,5},{5,9},{2,6},{6,10},{3,7},{7,11},{16,20},{20,24},... | collective-permute-start | bytes 2359304 | tf_op jit(solution)/shard_map/ppermute | solution.py:686
  16.1 9.9 %copy-start.9 = (s32[4,4]{1,0:T(4,128)S(1)}, s32[4,4]{1,0:T(4,128)}, u32[]{:S(2)}) copy-start(s32[4,4]{1,0:T(4,128)} %param.15) | copy-start | bytes 196
  16.1 49.2 %collective-permute-start.3 = (bf16[1152,512]{1,0:T(8,128)(2,1)}, bf16[1152,512]{1,0:T(8,128)(2,1)}, u32[]{:S(2)}, u32[]{:S(2)}) collective-permute-start(bf16[1152,512]{1,0:T(8,128)(2,1)} %get-tuple-element.34), channel_id=1, source_target_pairs={{12,4},{13,5},{14,6},{15,7},{28,20},{29,21},{30,22},{31,23}} | collective-permute-start | bytes 3538952 | tf_op jit(solution)/shard_map/ppermute | solution.py:686
  20.1 6.0 %copy-start.3 = (f32[8,16,48]{2,1,0:T(8,128)}, f32[8,16,48]{2,1,0:T(8,128)S(1)}, u32[]{:S(2)}) copy-start(f32[8,16,48]{2,1,0:T(8,128)S(1)} %reshape.31) | copy-start | bytes 73732
  20.1 3.1 %collective-permute-start.8 = (f32[8,48]{1,0:T(8,128)S(1)}, f32[8,48]{1,0:T(8,128)S(1)}, u32[]{:S(2)}, u32[]{:S(2)}) collective-permute-start(f32[8,48]{1,0:T(8,128)S(1)} %bitcast.42), channel_id=1, source_target_pairs={{0,1},{1,0},{2,3},{3,2},{4,5},{5,4},{6,7},{7,6},{8,9},{9,8},{10,11... | collective-permute-start | bytes 4616 | tf_op jit(solution)/shard_map/ppermute | solution.py:816
  21.4 9.1 %collective-permute-start.7 = (bf16[768,512]{1,0:T(8,128)(2,1)}, bf16[768,512]{1,0:T(8,128)(2,1)}, u32[]{:S(2)}, u32[]{:S(2)}) collective-permute-start(bf16[768,512]{1,0:T(8,128)(2,1)} %get-tuple-element.41), channel_id=1, source_target_pairs={{0,8},{1,9},{2,10},{3,11},{16,24},{17,25},{18,26},{19,27}} | collective-permute-start | bytes 2359304 | tf_op jit(solution)/shard_map/ppermute | solution.py:686
  23.2 0.6 copy-start.4
  24.0 3.8 %collective-permute-start.9 = (f32[40,128]{0,1:T(8,128)S(1)}, f32[40,128]{0,1:T(8,128)S(1)}, u32[]{:S(2)}, u32[]{:S(2)}) collective-permute-start(f32[40,128]{0,1:T(8,128)S(1)} %copy.39), channel_id=1, source_target_pairs={{0,2},{2,0},{1,3},{3,1},{4,6},{6,4},{5,7},{7,5},{8,10},{10,8},{9,1... | collective-permute-start | bytes 61448 | tf_op jit(solution)/shard_map/ppermute | solution.py:831
  26.1 1.0 copy-start.2
  27.7 2.8 %copy-start.6 = (f32[40,128]{0,1:T(8,128)}, f32[40,128]{0,1:T(8,128)S(1)}, u32[]{:S(2)}) copy-start(f32[40,128]{0,1:T(8,128)S(1)} %collective-permute-done.9) | copy-start | bytes 61444
  27.7 37.6 %collective-permute-start.4 = (bf16[1152,256]{1,0:T(8,128)(2,1)}, bf16[1152,256]{1,0:T(8,128)(2,1)}, u32[]{:S(2)}, u32[]{:S(2)}) collective-permute-start(bf16[1152,256]{1,0:T(8,128)(2,1)} %get-tuple-element.39), channel_id=1, source_target_pairs={{8,12},{4,0},{9,13},{5,1},{10,14},{6,2},{11,15},{7,3},{24,28},{20,... | collective-permute-start | bytes 1769480 | tf_op jit(solution)/shard_map/ppermute | solution.py:686
  29.2 26.8 %collective-permute-start.6 = (bf16[768,256]{1,0:T(8,128)(2,1)}, bf16[768,256]{1,0:T(8,128)(2,1)}, u32[]{:S(2)}, u32[]{:S(2)}) collective-permute-start(bf16[768,256]{1,0:T(8,128)(2,1)} %get-tuple-element.40), channel_id=1, source_target_pairs={{0,12},{1,13},{2,14},{3,15},{16,28},{17,29},{18,30},{19,31}} | collective-permute-start | bytes 1179656 | tf_op jit(solution)/shard_map/ppermute | solution.py:686
  30.5 34.8 %collective-permute-start.5 = (bf16[768,256]{1,0:T(8,128)(2,1)}, bf16[768,256]{1,0:T(8,128)(2,1)}, u32[]{:S(2)}, u32[]{:S(2)}) collective-permute-start(bf16[768,256]{1,0:T(8,128)(2,1)} %get-tuple-element.40), channel_id=1, source_target_pairs={{4,12},{5,13},{6,14},{7,15},{20,28},{21,29},{22,30},{23,31}} | collective-permute-start | bytes 1179656 | tf_op jit(solution)/shard_map/ppermute | solution.py:686
  74.2 1.8 %collective-permute-start.10 = (f32[3,40,384]{2,1,0:T(8,128)}, f32[3,40,384]{2,1,0:T(8,128)S(1)}, u32[]{:S(2)}, u32[]{:S(2)}) collective-permute-start(f32[3,40,384]{2,1,0:T(8,128)} %get-tuple-element.53), channel_id=1, source_target_pairs={{0,1},{1,0},{2,3},{3,2},{4,5},{5,4},{6,7},{7,6},{8,9},{9,8},{10,11... | collective-permute-start | bytes 552968 | tf_op jit(solution)/shard_map/ppermute | solution.py:1039
  77.9 14.4 %collective-permute-start.11 = (f32[56,640]{1,0:T(8,128)S(1)}, f32[56,640]{1,0:T(8,128)S(1)}, u32[]{:S(2)}, u32[]{:S(2)}) collective-permute-start(f32[56,640]{1,0:T(8,128)S(1)} %pad_maximum_fusion.1), channel_id=1, source_target_pairs={{0,4},{4,8},{8,12},{1,5},{5,9},{9,13},{2,6},{6,10},{10,14},{3,7},{... | collective-permute-start | bytes 430088 | tf_op jit(solution)/shard_map/ppermute | solution.py:1043
  79.2 11.0 %collective-permute-start.12 = (f32[40,256]{1,0:T(8,128)S(1)}, f32[40,256]{1,0:T(8,128)S(1)}, u32[]{:S(2)}, u32[]{:S(2)}) collective-permute-start(f32[40,256]{1,0:T(8,128)S(1)} %slice.71), channel_id=1, source_target_pairs={{0,8},{4,12},{1,9},{5,13},{2,10},{6,14},{3,11},{7,15},{16,24},{20,... | collective-permute-start | bytes 122888 | tf_op jit(solution)/shard_map/ppermute | solution.py:1048
  80.5 11.8 %collective-permute-start.13 = (f32[40,384]{1,0:T(8,128)S(1)}, f32[40,384]{1,0:T(8,128)S(1)}, u32[]{:S(2)}, u32[]{:S(2)}) collective-permute-start(f32[40,384]{1,0:T(8,128)S(1)} %get-tuple-element.56), channel_id=1, source_target_pairs={{4,12},{12,8},{5,13},{13,9},{6,14},{14,10},{7,15},{15,11},{20,28},... | collective-permute-start | bytes 184328 | tf_op jit(solution)/shard_map/ppermute | solution.py:1047
  92.3 3.6 %collective-permute-start.14 = (f32[40,640]{1,0:T(8,128)S(1)}, f32[40,640]{1,0:T(8,128)S(1)}, u32[]{:S(2)}, u32[]{:S(2)}) collective-permute-start(f32[40,640]{1,0:T(8,128)S(1)} %fusion.32), channel_id=1, source_target_pairs={{0,2},{2,0},{1,3},{3,1},{4,6},{6,4},{5,7},{7,5},{8,10},{10,8},{9,1... | collective-permute-start | bytes 307208 | tf_op jit(solution)/shard_map/ppermute | solution.py:1051
  95.8 3.4 %collective-permute-start.15 = (f32[40,640]{1,0:T(8,128)S(1)}, f32[40,640]{1,0:T(8,128)S(1)}, u32[]{:S(2)}, u32[]{:S(2)}) collective-permute-start(f32[40,640]{1,0:T(8,128)S(1)} %add.87.mine), channel_id=1, source_target_pairs={{0,1},{1,0},{2,3},{3,2},{4,5},{5,4},{6,7},{7,6},{8,9},{9,8},{10,11... | collective-permute-start | bytes 307208 | tf_op jit(solution)/shard_map/ppermute | solution.py:1052
